TPU v7x, 256 devices: a whole 4x4x8 slice. The times are simulated.
256 devices in a mesh: seq: 8 (over x, core), dp: 8 (over z), fsdp: 4 (over y).
Axes of the slice: x: 4, y: 4, z: 8, core: 2. Of those that a mesh axis runs over, the one named last changes fastest.
Arguments:
- query_rows: bfloat16 [32, 1024, 4096], P(('dp', 'fsdp'), 'seq'), may hold values from -2.5 to 2.5
- forward_key_rows: bfloat16 [32, 1024, 1024], P(('dp', 'fsdp'), 'seq'), may hold values from -2.5 to 2.5
- forward_value_rows: bfloat16 [32, 1024, 1024], P(('dp', 'fsdp'), 'seq'), may hold values from -4 to 4
- out_cotangent: bfloat16 [32, 1024, 4096], P(('dp', 'fsdp'), 'seq'), may hold values from -12 to 12
- proj_weight: bfloat16 [4096, 4096], P(('dp', 'fsdp'), 'seq'), may hold values from -0.09375 to 0.09375
- sent_lengths: int32 [32, 32], P(('dp', 'fsdp')), may hold values from 1 to 64, 1024 in all within a row
Outputs:
- query_grad: bfloat16 [32, 1024, 4096], P(('dp', 'fsdp'), 'seq')
- key_gradient: bfloat16 [32, 1024, 1024], P(('dp', 'fsdp'), 'seq')
- value_gradient: bfloat16 [32, 1024, 1024], P(('dp', 'fsdp'), 'seq')
- proj_grad: bfloat16 [4096, 4096], P(('dp', 'fsdp'), 'seq')
Inputs may be any that keep to these rules, and one draw needn't show every extreme that they name: `sent_lengths`: each window's 32 lengths sum to 1024, and the longest is exactly 64.
All inputs are finite; a program needn't handle non-finite values.
Results may differ from a plain program's by a relative error of at most 0.0058.
Values may be sent and summed in bfloat16 or wider, within the bound.
No kernel may reach another device: no remote copies, remote signals or barrier semaphores. Data moves between devices by JAX's collectives and lax.ppermute only.
A program may use at most 128 MiB of HBM per device.

v0:
```python
import math

import jax
import jax.numpy as jnp
from jax import lax
from jax.experimental import pallas as pl
from jax.experimental.pallas import tpu as pltpu
from jax.sharding import PartitionSpec as P

HEADS = 4
HEAD = 128
TOK = 128
KW = 448
FACTOR = 1.0 / math.sqrt(HEAD)
F32 = jnp.float32
BF16 = jnp.bfloat16
GROUP = 4
GRID = {"dp": 8, "fsdp": 4}


def window_start(i, blocks):
    return pl.multiple_of(jnp.clip(i * TOK - 256, 0, blocks * TOK - KW), 64)


def probs(i, start, g_ref, lo_ref, hi_ref, key, h0):
    q = jnp.concatenate(
        [g_ref[i, :, (h0 + j) * HEAD : (h0 + j + 1) * HEAD] for j in range(GROUP)], 0
    )
    s = lax.dot_general(key, q, (((1,), (1,)), ((), ())), preferred_element_type=F32)
    place = start + lax.broadcasted_iota(jnp.int32, (KW, GROUP * TOK), 0)
    lo = jnp.concatenate([lo_ref[i]] * GROUP, 1)
    hi = jnp.concatenate([hi_ref[i]] * GROUP, 1)
    p = jnp.where((place >= lo) & (place < hi), jnp.exp(s * FACTOR), 0.0)
    a = p * (1.0 / jnp.sum(p, axis=0, keepdims=True))
    return q, a


def unpack_keys(g_ref, k_ref, v_ref):
    for b in range(g_ref.shape[0]):
        rows = slice(b * TOK, (b + 1) * TOK)
        k_ref[rows, :] = g_ref[b, :, HEADS * HEAD : (HEADS + 1) * HEAD]
        v_ref[rows, :] = g_ref[b, :, (HEADS + 1) * HEAD :]


def fwd_kernel(g_ref, lo_ref, hi_ref, o_ref, k_ref, v_ref):
    blocks = g_ref.shape[0]
    i = pl.program_id(0)

    @pl.when(i == 0)
    def _():
        unpack_keys(g_ref, k_ref, v_ref)

    start = window_start(i, blocks)
    key = k_ref[pl.ds(start, KW), :]
    vt = v_ref[pl.ds(start, KW), :].T
    for h0 in range(0, HEADS, GROUP):
        _, a = probs(i, start, g_ref, lo_ref, hi_ref, key, h0)
        o = jnp.dot(vt, a.astype(BF16), preferred_element_type=F32).astype(BF16)
        for j in range(GROUP):
            o_ref[0, (h0 + j) * HEAD : (h0 + j + 1) * HEAD, :] = o[:, j * TOK : (j + 1) * TOK]


def bwd_kernel(g_ref, u_ref, lo_ref, hi_ref, o_ref, dk_ref, dv_ref, k_ref, v_ref):
    blocks = g_ref.shape[0]
    i = pl.program_id(0)

    @pl.when(i == 0)
    def _():
        unpack_keys(g_ref, k_ref, v_ref)
        dk_ref[...] = jnp.zeros_like(dk_ref)
        dv_ref[...] = jnp.zeros_like(dv_ref)

    start = window_start(i, blocks)
    key = k_ref[pl.ds(start, KW), :]
    val = v_ref[pl.ds(start, KW), :]
    kt = key.T
    dk = None
    for h0 in range(0, HEADS, GROUP):
        q, a = probs(i, start, g_ref, lo_ref, hi_ref, key, h0)
        u = jnp.concatenate(
            [u_ref[i, :, (h0 + j) * HEAD : (h0 + j + 1) * HEAD] for j in range(GROUP)], 0
        )
        g = lax.dot_general(val, u, (((1,), (1,)), ((), ())), preferred_element_type=F32)
        delta = jnp.sum(a * g, axis=0, keepdims=True)
        ds = (a * (g - delta) * FACTOR).astype(BF16)
        dq = jnp.dot(kt, ds, preferred_element_type=F32)
        for j in range(GROUP):
            o_ref[i, :, (h0 + j) * HEAD : (h0 + j + 1) * HEAD] = dq[
                :, j * TOK : (j + 1) * TOK
            ].T.astype(BF16)
        dkh = jnp.dot(ds, q, preferred_element_type=F32)
        dvh = jnp.dot(a.astype(BF16), u, preferred_element_type=F32)
        dk, dv = (dkh, dvh) if dk is None else (dk + dkh, dv + dvh)
    dk_ref[pl.ds(start, KW), :] += dk
    dv_ref[pl.ds(start, KW), :] += dv

    @pl.when(i == blocks - 1)
    def _():
        for b in range(blocks):
            o_ref[b, :, HEADS * HEAD : (HEADS + 1) * HEAD] = dk_ref[
                b * TOK : (b + 1) * TOK, :
            ].astype(BF16)
            o_ref[b, :, (HEADS + 1) * HEAD :] = dv_ref[b * TOK : (b + 1) * TOK, :].astype(BF16)


def whole(shape):
    return pl.BlockSpec(shape, lambda i: (0,) * len(shape))


def limits(sent_lengths, blocks):
    number = sent_lengths.shape[0]
    order = jnp.arange(number, dtype=jnp.int32)
    ends = jnp.sum(jnp.where(order[None, :] <= order[:, None], sent_lengths[None, :], 0), axis=1)
    places = jnp.arange(blocks * TOK, dtype=jnp.int32)
    sentence = jnp.sum((places[:, None] >= ends[None, :]).astype(jnp.int32), axis=1)
    lo = jnp.sum(
        jnp.where(order[None, :] + 3 < sentence[:, None], sent_lengths[None, :], 0), axis=1
    )
    hi = jnp.sum(jnp.where(order[None, :] <= sentence[:, None], sent_lengths[None, :], 0), axis=1)
    return lo.reshape(blocks, 1, TOK), hi.reshape(blocks, 1, TOK)


def attend(g, lo, hi):
    blocks = g.shape[0]
    pairs = blocks * TOK * KW * HEADS
    return pl.pallas_call(
        fwd_kernel,
        grid=(blocks,),
        in_specs=[whole(x.shape) for x in (g, lo, hi)],
        out_specs=pl.BlockSpec((1, HEADS * HEAD, TOK), lambda i: (i, 0, 0)),
        out_shape=jax.ShapeDtypeStruct((blocks, HEADS * HEAD, TOK), BF16),
        scratch_shapes=[pltpu.VMEM((blocks * TOK, HEAD), BF16)] * 2,
        cost_estimate=pl.CostEstimate(
            flops=4 * pairs * HEAD, bytes_accessed=4 * g.size, transcendentals=pairs
        ),
        name="attend",
    )(g, lo, hi)


def attend_grad(g, u, lo, hi):
    blocks = g.shape[0]
    pairs = blocks * TOK * KW * HEADS
    return pl.pallas_call(
        bwd_kernel,
        grid=(blocks,),
        in_specs=[whole(x.shape) for x in (g, u, lo, hi)],
        out_specs=whole(g.shape),
        out_shape=jax.ShapeDtypeStruct(g.shape, BF16),
        scratch_shapes=[pltpu.VMEM((blocks * TOK, HEAD), F32)] * 2
        + [pltpu.VMEM((blocks * TOK, HEAD), BF16)] * 2,
        cost_estimate=pl.CostEstimate(
            flops=10 * pairs * HEAD, bytes_accessed=6 * g.size, transcendentals=pairs
        ),
        name="attend_grad",
    )(g, u, lo, hi)


def head_parts(g):
    wide = HEADS * HEAD
    return (
        (slice(0, wide), slice(g * wide, (g + 1) * wide)),
        (slice(wide, wide + HEAD), slice(g * HEAD, (g + 1) * HEAD)),
        (slice(wide + HEAD, wide + 2 * HEAD), slice(g * HEAD, (g + 1) * HEAD)),
    )


def pack_kernel(q_ref, k_ref, v_ref, o_ref):
    for g in range(o_ref.shape[0]):
        for ref, (inner, outer) in zip((q_ref, k_ref, v_ref), head_parts(g)):
            o_ref[g, :, inner] = ref[0, :, outer]


def pack(q, k, v):
    groups = k.shape[2] // HEAD
    return pl.pallas_call(
        pack_kernel,
        out_shape=jax.ShapeDtypeStruct((groups, TOK, (HEADS + 2) * HEAD), BF16),
        cost_estimate=pl.CostEstimate(flops=0, bytes_accessed=6 * q.size, transcendentals=0),
        name="pack",
    )(q, k, v)


def unpack_kernel(i_ref, q_ref, k_ref, v_ref):
    for g in range(i_ref.shape[0]):
        for ref, (inner, outer) in zip((q_ref, k_ref, v_ref), head_parts(g)):
            ref[0, :, outer] = i_ref[g, :, inner]


def unpack(packed):
    groups = packed.shape[0]
    return pl.pallas_call(
        unpack_kernel,
        out_shape=[
            jax.ShapeDtypeStruct((1, TOK, groups * part), BF16)
            for part in (HEADS * HEAD, HEAD, HEAD)
        ],
        cost_estimate=pl.CostEstimate(flops=0, bytes_accessed=4 * packed.size, transcendentals=0),
        name="unpack",
    )(packed)


def upstream_kernel(ids_ref, *refs):
    pieces, weights, (o_ref, acc_ref, w_ref) = refs[:-8], refs[-8:-3], refs[-3:]
    count = len(pieces)
    near = w_ref.shape[1]
    step = pl.program_id(0)
    last = pl.num_programs(0) - 1
    y = ids_ref[count + 1]
    mine, below, above, far_low, far_high = weights
    w_ref[:, y] = mine[...]
    w_ref[:, lax.rem(y + near - 1, near)] = below[...]
    w_ref[:, lax.rem(y + 1, near)] = above[...]

    @pl.when(step * 2 <= last)
    def _():
        w_ref[:, lax.rem(y + 2, near)] = far_low[...]

    @pl.when(step * 2 > last)
    def _():
        w_ref[:, lax.rem(y + 2, near)] = far_high[...]

    rows = jnp.concatenate([piece[...] for piece in pieces], 0)
    weight = w_ref[...].reshape(rows.shape[1], w_ref.shape[3])
    part = jnp.dot(rows, weight, preferred_element_type=F32)

    @pl.when(step == 0)
    def _():
        acc_ref[...] = part

    @pl.when(step > 0)
    def _():
        acc_ref[...] += part

    @pl.when(step == last)
    def _():
        for p in range(count):
            o_ref[ids_ref[p]] = acc_ref[p * TOK : (p + 1) * TOK, :].astype(BF16)


def upstream(ids, pieces, weights):
    far, rows, width = weights[0].shape
    near = GRID["fsdp"]
    depth = far * near * rows
    planes = 2
    steps = far // planes
    count = len(pieces)
    block = (planes, rows, width)
    return pl.pallas_call(
        upstream_kernel,
        grid_spec=pltpu.PrefetchScalarGridSpec(
            num_scalar_prefetch=1,
            grid=(steps,),
            in_specs=[pl.BlockSpec((TOK, depth // steps), lambda i, ids: (0, i))] * count
            + [pl.BlockSpec(block, lambda i, ids: (i, 0, 0))] * 3
            + [
                pl.BlockSpec(block, lambda i, ids: (jnp.minimum(i, steps // 2 - 1), 0, 0)),
                pl.BlockSpec(block, lambda i, ids: (jnp.maximum(i - steps // 2, 0), 0, 0)),
            ],
            out_specs=pl.BlockSpec((count, TOK, width), lambda i, ids: (0, 0, 0)),
            scratch_shapes=[
                pltpu.VMEM((count * TOK, width), F32),
                pltpu.VMEM((planes, near, rows, width), BF16),
            ],
        ),
        out_shape=jax.ShapeDtypeStruct((count, TOK, width), BF16),
        cost_estimate=pl.CostEstimate(
            flops=2 * count * TOK * width * depth,
            bytes_accessed=2 * (count * TOK * (depth + width) + depth * width),
            transcendentals=0,
        ),
        name="upstream",
    )(ids, *pieces, *weights)


def proj_kernel(ids_ref, *refs):
    pieces, (ot_ref, a_ref, b_ref, lhs_ref) = refs[:-4], refs[-4:]
    count = len(pieces)
    near = a_ref.shape[0]
    split = a_ref.shape[2]

    @pl.when(pl.program_id(0) == 0)
    def _():
        for p in range(count):
            lhs_ref[:, p * TOK : (p + 1) * TOK] = ot_ref[ids_ref[p]]

    rows = jnp.concatenate([piece[...] for piece in pieces], 0)
    out = jnp.dot(lhs_ref[...], rows, preferred_element_type=F32).astype(BF16)
    for t in range(near):
        part = out[:, t * TOK : (t + 1) * TOK]
        a_ref[lax.rem(t + near - ids_ref[count + 1], near), 0] = part[:split]
        b_ref[0, t] = part[split:]


def proj_terms(ids, pieces, ot):
    count, width, _ = ot.shape
    far, near = GRID["dp"], GRID["fsdp"]
    split = width * 3 // 4
    depth = pieces[0].shape[1]

    return pl.pallas_call(
        proj_kernel,
        grid_spec=pltpu.PrefetchScalarGridSpec(
            num_scalar_prefetch=1,
            grid=(far,),
            in_specs=[pl.BlockSpec((TOK, near * TOK), lambda i, ids: (0, i))] * count
            + [pl.BlockSpec(ot.shape, lambda i, ids: (0, 0, 0))],
            out_specs=[
                pl.BlockSpec((near, 1, split, TOK), lambda i, ids: (0, lax.rem(i + far - ids[count], far), 0, 0)),
                pl.BlockSpec((1, near, width - split, TOK), lambda i, ids: (i, 0, 0, 0)),
            ],
            scratch_shapes=[pltpu.VMEM((width, count * TOK), BF16)],
        ),
        out_shape=[
            jax.ShapeDtypeStruct((near, far, split, TOK), BF16),
            jax.ShapeDtypeStruct((far, near, width - split, TOK), BF16),
        ],
        cost_estimate=pl.CostEstimate(
            flops=2 * count * TOK * width * depth,
            bytes_accessed=2 * (count * TOK * (depth + width) + depth * width),
            transcendentals=0,
        ),
        name="proj_terms",
    )(ids, *pieces, ot)


def shift(x, axis, by):
    n = GRID[axis]
    return lax.ppermute(x, axis, [(i, (i + by) % n) for i in range(n)])


def add(a, b):
    return (a.astype(F32) + b.astype(F32)).astype(BF16)


def after(value, done):
    return lax.optimization_barrier((value, done))[0]


def swap(x, axis):
    return lax.all_to_all(x, axis, split_axis=0, concat_axis=0, tiled=True)


def hop(x, chips, core):
    pairs = [(i * 2 + c, ((i + chips) % 4) * 2 + (c ^ core)) for i in range(4) for c in range(2)]
    return lax.ppermute(x, "seq", pairs)


def per_device(
    query_rows, forward_key_rows, forward_value_rows, out_cotangent, proj_weight, sent_lengths
):
    place = lax.axis_index("seq").astype(jnp.int32)
    chip, core = place // 2, place % 2
    offsets = jnp.array([0, 3, 1, 2], jnp.int32)
    chips = (chip + offsets) % 4 * 2
    ids = jnp.concatenate(
        [
            chips + core,
            chips + 1 - core,
            jnp.stack([lax.axis_index("dp"), lax.axis_index("fsdp")]).astype(jnp.int32),
        ]
    )
    far = GRID["dp"] // 2
    half = TOK // 2
    own = out_cotangent[0]
    weight = jnp.broadcast_to(proj_weight, (2 * far, *proj_weight.shape))
    weight = swap(weight, "dp")
    left, right = hop(own, 1, 0), hop(own, -1, 0)
    local = pack(query_rows, forward_key_rows, forward_value_rows)
    partner = hop(own, 0, 1)
    packed = swap(local, "seq")
    below, above = shift(weight, "fsdp", 1), shift(weight, "fsdp", -1)
    lo, hi = limits(sent_lengths[0], packed.shape[0])
    across = [hop(left[:half], 1, 0), hop(right[half:], -1, 0)]
    across = jnp.concatenate(across, 0)
    output = attend(packed, lo, hi)
    pieces = [own, left, right, across, partner]
    pieces += [hop(piece, 0, 1) for piece in (left, right, across)]
    ends = [shift(below[:far], "fsdp", 1), shift(above[far:], "fsdp", -1)]
    first, second = proj_terms(ids, pieces, output)
    second = swap(second, "dp")
    up, down = shift(first[2, :far], "fsdp", 1), shift(first[2, far:], "fsdp", -1)
    arriving = upstream(ids, pieces, [weight, below, above, *ends])
    up, down = after((up, down), arriving)
    up = shift(jnp.concatenate([add(first[1, :far], up), first[1, far:]], 0), "fsdp", 1)
    down = shift(jnp.concatenate([first[3, :far], add(first[3, far:], down)], 0), "fsdp", -1)
    grads = attend_grad(packed, arriving, lo, hi)
    grads_home = swap(grads, "seq")
    up, down, second = after((up, down, second), grads)
    first = (first[0].astype(F32) + up.astype(F32) + down.astype(F32)).astype(BF16)
    part = first.shape[1] // 2
    up, down = shift(first[4, :part], "dp", 1), shift(first[4, part:], "dp", -1)
    up = jnp.concatenate([add(first[3, :part], up), first[3, part:]], 0)
    down = jnp.concatenate([first[5, :part], add(first[5, part:], down)], 0)
    up, down = shift(up, "dp", 1), shift(down, "dp", -1)
    up, down = add(first[2], up), add(first[6], down)
    up, down = shift(up, "dp", 1), shift(down, "dp", -1)
    up, down = add(first[1], up), add(first[7], down)
    up, down = shift(up, "dp", 1), shift(down, "dp", -1)
    second = jnp.sum(second.astype(F32), axis=0).astype(BF16)
    second = swap(second, "fsdp")
    first = first[0].astype(F32) + up.astype(F32) + down.astype(F32)
    proj_grad = jnp.concatenate([first, jnp.sum(second.astype(F32), axis=0)], 0)
    query_grad, key_gradient, value_gradient = unpack(grads_home)
    return (query_grad, key_gradient, value_gradient, proj_grad.T.astype(BF16))


def solution(mesh):
    in_specs = (
        P(("dp", "fsdp"), "seq", None),
        P(("dp", "fsdp"), "seq", None),
        P(("dp", "fsdp"), "seq", None),
        P(("dp", "fsdp"), "seq", None),
        P(("dp", "fsdp"), "seq"),
        P(("dp", "fsdp"), None),
    )
    out_specs = (
        P(("dp", "fsdp"), "seq", None),
        P(("dp", "fsdp"), "seq", None),
        P(("dp", "fsdp"), "seq", None),
        P(("dp", "fsdp"), "seq"),
    )
    return jax.shard_map(
        per_device, mesh=mesh, in_specs=in_specs, out_specs=out_specs, check_vma=False
    )
```

profile of v0, /device:TPU:2, one launch (start us, length us, event | category | flops | bytes accessed | tf_op | source)
XLA Modules:
  0.0 186.3 jit_solution(15861297897243504880)
XLA Ops:
  0.6 2.0 %broadcast_in_dim.41 = bf16[8,128,512]{2,1,0:T(8,128)(2,1)} broadcast(bf16[128,512]{1,0:T(8,128)(2,1)} %param.11), dimensions={1,2} | broadcast | bytes 1179648 | tf_op jit(solution)/shard_map/broadcast_in_dim | solution.py:365
  2.6 8.5 %all-to-all-start.1 = ((bf16[8,128,512]{2,1,0:T(8,128)(2,1)}), bf16[8,128,512]{2,1,0:T(8,128)(2,1)S(1)}, u32[]{:S(2)}, u32[]{:S(2)}) async-start(bf16[8,128,512]{2,1,0:T(8,128)(2,1)} %broadcast_in_dim.41), calls=%async_computation.1 | async-start | bytes 2097152 | tf_op jit(solution)/shard_map/all_to_all | solution.py:340
  11.1 1.5 collective-permute-start
  12.6 0.5 collective-permute-start.1
  13.1 22.8 %collective-permute-done.refs_1_ = bf16[128,4096]{1,0:T(8,128)(2,1)S(1)} collective-permute-done((bf16[128,4096]{1,0:T(8,128)(2,1)}, bf16[128,4096]{1,0:T(8,128)(2,1)S(1)}, u32[]{:S(2)}, u32[]{:S(2)}) %collective-permute-start) | collective-permute-done | bytes 1048608 | tf_op jit(solution)/shard_map/ppermute | solution.py:345
  35.9 0.9 slice.88
  36.8 0.2 copy-done.3
  37.0 1.5 collective-permute-start.2
  38.5 1.3 all-to-all-done.1.refs_8_
  39.8 3.0 %collective-permute-start.9 = (bf16[8,128,512]{2,1,0:T(8,128)(2,1)S(1)}, bf16[8,128,512]{2,1,0:T(8,128)(2,1)}, u32[]{:S(2)}, u32[]{:S(2)}) collective-permute-start(bf16[8,128,512]{2,1,0:T(8,128)(2,1)S(1)} %all-to-all-done.1.refs_8_), channel_id=1, source_target_pairs={{0,3},{1,0},{2,1},{3,2},{4,7},{5,4},{6,5},{7,6},{8,11},{9,8},{10,9... | collective-permute-start | bytes 3145736 | tf_op jit(solution)/shard_map/ppermute | solution.py:328
  42.8 0.9 slice.89
  43.7 0.5 collective-permute-start.3
  44.3 2.7 %pack.1 = bf16[8,128,768]{2,1,0:T(8,128)(2,1)} custom-call(bf16[1,128,4096]{2,1,0:T(8,128)(2,1)} %q_ref.1, bf16[1,128,1024]{2,1,0:T(8,128)(2,1)} %k_ref.1, bf16[1,128,1024]{2,1,0:T(8,128)(2,1)} %v_ref.1), custom_call_target="tpu_custom_call" | custom-call | bytes 3145728 | tf_op jit(solution)/shard_map/pack/pallas_call | solution.py:175
  47.0 6.2 %all-to-all-start = ((bf16[8,128,768]{2,1,0:T(8,128)(2,1)}), bf16[8,128,768]{2,1,0:T(8,128)(2,1)S(1)}, u32[]{:S(2)}, u32[]{:S(2)}) async-start(bf16[8,128,768]{2,1,0:T(8,128)(2,1)} %pack.1), calls=%async_computation | async-start | bytes 3145728 | tf_op jit(solution)/shard_map/all_to_all | solution.py:340
  53.2 0.1 collective-permute-start.6
  53.3 0.4 collective-permute-start.5
  53.7 0.8 constant_dynamic-update-slice_fusion.1
  54.6 5.8 %collective-permute-done.3 = bf16[64,4096]{1,0:T(8,128)(2,1)} collective-permute-done((bf16[64,4096]{1,0:T(8,128)(2,1)}, bf16[64,4096]{1,0:T(8,128)(2,1)}, u32[]{:S(2)}, u32[]{:S(2)}) %collective-permute-start.3) | collective-permute-done | bytes 524320 | tf_op jit(solution)/shard_map/ppermute | solution.py:345
  60.4 1.9 %constant_dynamic-update-slice_fusion.refs_3_ = bf16[128,4096]{1,0:T(8,128)(2,1)} fusion(bf16[128,4096]{1,0:T(8,128)(2,1)} %constant_dynamic-update-slice_fusion.1, bf16[64,4096]{1,0:T(8,128)(2,1)} %collective-permute-done.3), kind=kLoop, calls=%fused_computation.49 | loop fusion | bytes 1048576 | tf_op jit(solution)/shard_map/concatenate | solution.py:374
  62.3 3.2 %collective-permute-done.9.refs_10_ = bf16[8,128,512]{2,1,0:T(8,128)(2,1)} collective-permute-done((bf16[8,128,512]{2,1,0:T(8,128)(2,1)S(1)}, bf16[8,128,512]{2,1,0:T(8,128)(2,1)}, u32[]{:S(2)}, u32[]{:S(2)}) %collective-permute-start.9) | collective-permute-done | bytes 1048608 | tf_op jit(solution)/shard_map/ppermute | solution.py:328
  65.4 1.1 collective-permute-start.8
  66.6 0.6 pad_add_fusion.ids_ref
  67.2 0.1 select_reduce_fusion.2
  67.3 0.1 convert_reduce_fusion
  67.4 0.7 select_reduce_fusion
  68.1 7.2 %all-to-all-done.g_ref = bf16[8,128,768]{2,1,0:T(8,128)(2,1)S(1)} async-done(((bf16[8,128,768]{2,1,0:T(8,128)(2,1)}), bf16[8,128,768]{2,1,0:T(8,128)(2,1)S(1)}, u32[]{:S(2)}, u32[]{:S(2)}) %all-to-all-start) | async-done | bytes 1572896 | tf_op jit(solution)/shard_map/all_to_all | solution.py:340
  75.3 1.2 copy-done.1
  76.5 7.3 %attend.1.refs_8_ = bf16[8,512,128]{2,1,0:T(8,128)(2,1)} custom-call(bf16[8,128,768]{2,1,0:T(8,128)(2,1)} %copy-done.1, s32[8,1,128]{2,1,0:T(1,128)} %bitcast.70, s32[8,1,128]{2,1,0:T(1,128)} %bitcast.68), custom_call_target="tpu_custom_call" | custom-call | flops 939524096 | bytes 3145728 | tf_op jit(solution)/shard_map/attend/pallas_call | solution.py:126
  83.8 1.1 slice.91
  84.9 6.9 %collective-permute-done.8.refs_9_ = bf16[8,128,512]{2,1,0:T(8,128)(2,1)} collective-permute-done((bf16[8,128,512]{2,1,0:T(8,128)(2,1)S(1)}, bf16[8,128,512]{2,1,0:T(8,128)(2,1)}, u32[]{:S(2)}, u32[]{:S(2)}) %collective-permute-start.8) | collective-permute-done | bytes 1048608 | tf_op jit(solution)/shard_map/ppermute | solution.py:328
  91.8 1.7 collective-permute-start.11
  93.5 1.1 slice.90
  94.6 0.4 collective-permute-start.10
  95.0 11.7 %proj_terms.1 = (bf16[4,8,384,128]{3,2,1,0:T(8,128)(2,1)}, bf16[8,4,128,128]{3,2,1,0:T(8,128)(2,1)}) custom-call(s32[10]{0:T(128)} %pad_add_fusion.ids_ref, bf16[128,4096]{1,0:T(8,128)(2,1)} %bitcast.2.refs_0_, bf16[128,4096]{1,0:T(8,128)(2,1)} %copy-done.3, bf16[128,4096]{1,0:T(8,128)(2,1)} %copy-done.4, ...), custom_call_target="tpu_custom_call" | custom-call | flops 4294967296 | bytes 13631488 | tf_op jit(solution)/shard_map/proj_terms/pallas_call | solution.py:300
  106.7 3.6 %all-to-all-start.3 = ((bf16[8,4,128,128]{3,2,1,0:T(8,128)(2,1)}), bf16[8,4,128,128]{3,2,1,0:T(8,128)(2,1)S(1)}, u32[]{:S(2)}, u32[]{:S(2)}) async-start(bf16[8,4,128,128]{3,2,1,0:T(8,128)(2,1)} %get-tuple-element.20), calls=%async_computation.3 | async-start | bytes 2097152 | tf_op jit(solution)/shard_map/all_to_all | solution.py:340
  110.3 2.2 %slice_bitcast_fusion = (bf16[4,384,128]{2,1,0:T(8,128)(2,1)S(1)}, bf16[4,384,128]{2,1,0:T(8,128)(2,1)S(1)}, bf16[4,384,128]{2,1,0:T(8,128)(2,1)}, bf16[4,384,128]{2,1,0:T(8,128)(2,1)S(1)}) fusion(bf16[4,8,384,128]{3,2,1,0:T(8,128)(2,1)} %get-tuple-element.17), kind=kLoop, calls=%fused_computation.9 | loop fusion | bytes 3145728 | tf_op jit(solution)/shard_map/squeeze | solution.py:385
  112.5 3.0 %collective-permute-start.13 = (bf16[4,384,128]{2,1,0:T(8,128)(2,1)}, bf16[4,384,128]{2,1,0:T(8,128)(2,1)}, u32[]{:S(2)}, u32[]{:S(2)}) collective-permute-start(bf16[4,384,128]{2,1,0:T(8,128)(2,1)} %get-tuple-element.38), channel_id=1, source_target_pairs={{0,3},{1,0},{2,1},{3,2},{4,7},{5,4},{6,5},{7,6},{8,11},{9,8},{10,9... | collective-permute-start | bytes 1179656 | tf_op jit(solution)/shard_map/ppermute | solution.py:328
  115.5 10.2 %upstream.1.u_ref = bf16[8,128,512]{2,1,0:T(8,128)(2,1)} custom-call(s32[10]{0:T(128)} %pad_add_fusion.ids_ref, bf16[128,4096]{1,0:T(8,128)(2,1)} %bitcast.2.refs_0_, bf16[128,4096]{1,0:T(8,128)(2,1)} %copy-done.3, bf16[128,4096]{1,0:T(8,128)(2,1)} %copy-done.4, bf16[128,4096]{1,0:T(8,128)(2,1)} %constant_dynamic-update-slice_fusion.refs_3_, ...), custom_call_target="tpu_custom_call" | custom-call | flops 4294967296 | bytes 13631488 | tf_op jit(solution)/shard_map/upstream/pallas_call | solution.py:248
  125.6 1.6 fusion.2
  127.2 0.1 pad_maximum_fusion
  127.3 0.1 collective-permute-start.14
  127.5 3.3 %collective-permute-start.15 = (bf16[8,384,128]{2,1,0:T(8,128)(2,1)S(1)}, bf16[8,384,128]{2,1,0:T(8,128)(2,1)S(1)}, u32[]{:S(2)}, u32[]{:S(2)}) collective-permute-start(bf16[8,384,128]{2,1,0:T(8,128)(2,1)S(1)} %pad_maximum_fusion.1), channel_id=1, source_target_pairs={{0,3},{1,0},{2,1},{3,2},{4,7},{5,4},{6,5},{7,6},{8,11},{9,8},{10,9... | collective-permute-start | bytes 2359304 | tf_op jit(solution)/shard_map/ppermute | solution.py:328
  130.8 12.1 %attend_grad.1 = bf16[8,128,768]{2,1,0:T(8,128)(2,1)} custom-call(bf16[8,128,768]{2,1,0:T(8,128)(2,1)} %copy-done.1, bf16[8,128,512]{2,1,0:T(8,128)(2,1)} %upstream.1.u_ref, s32[8,1,128]{2,1,0:T(1,128)} %bitcast.71, s32[8,1,128]{2,1,0:T(1,128)} %bitcast.69), custom_call_target="tpu_custom_call" | custom-call | flops 2348810240 | bytes 4718592 | tf_op jit(solution)/shard_map/attend_grad/pallas_call | solution.py:143
  142.9 2.7 %collective-permute-done.14 = bf16[8,384,128]{2,1,0:T(8,128)(2,1)} collective-permute-done((bf16[8,384,128]{2,1,0:T(8,128)(2,1)S(1)}, bf16[8,384,128]{2,1,0:T(8,128)(2,1)}, u32[]{:S(2)}, u32[]{:S(2)}) %collective-permute-start.14) | collective-permute-done | bytes 786464 | tf_op jit(solution)/shard_map/ppermute | solution.py:328
  145.6 0.8 reduce_sum.61
  146.4 4.3 %all-to-all-start.4 = ((bf16[4,128,128]{2,1,0:T(8,128)(2,1)}), bf16[4,128,128]{2,1,0:T(8,128)(2,1)S(1)}, u32[]{:S(2)}, u32[]{:S(2)}) async-start(bf16[4,128,128]{2,1,0:T(8,128)(2,1)} %reduce_sum.61), calls=%async_computation.4 | async-start | bytes 262144 | tf_op jit(solution)/shard_map/all_to_all | solution.py:340
  150.7 1.7 fusion.1
  152.4 1.7 collective-permute-start.16
  154.1 1.6 collective-permute-start.20
  155.7 1.0 all-to-all-done.4
  156.7 4.8 %all-to-all-start.2 = ((bf16[8,128,768]{2,1,0:T(8,128)(2,1)}), bf16[8,128,768]{2,1,0:T(8,128)(2,1)S(1)}, u32[]{:S(2)}, u32[]{:S(2)}) async-start(bf16[8,128,768]{2,1,0:T(8,128)(2,1)} %attend_grad.1), calls=%async_computation.2 | async-start | bytes 3145728 | tf_op jit(solution)/shard_map/all_to_all | solution.py:340
  161.6 1.7 collective-permute-start.17
  163.3 1.7 collective-permute-start.21
  165.0 2.7 %collective-permute-done.17 = bf16[384,128]{1,0:T(8,128)(2,1)S(1)} collective-permute-done((bf16[384,128]{1,0:T(8,128)(2,1)S(1)}, bf16[384,128]{1,0:T(8,128)(2,1)S(1)}, u32[]{:S(2)}, u32[]{:S(2)}) %collective-permute-start.17) | collective-permute-done | bytes 98336 | tf_op jit(solution)/shard_map/ppermute | solution.py:328
  167.7 0.5 collective-permute-start.18
  168.2 5.4 %collective-permute-done.18 = bf16[384,128]{1,0:T(8,128)(2,1)S(1)} collective-permute-done((bf16[384,128]{1,0:T(8,128)(2,1)S(1)}, bf16[384,128]{1,0:T(8,128)(2,1)S(1)}, u32[]{:S(2)}, u32[]{:S(2)}) %collective-permute-start.18) | collective-permute-done | bytes 98336 | tf_op jit(solution)/shard_map/ppermute | solution.py:328
  173.7 0.5 collective-permute-start.22
  174.2 1.6 collective-permute-start.19
  175.8 2.6 %collective-permute-done.22 = bf16[384,128]{1,0:T(8,128)(2,1)S(1)} collective-permute-done((bf16[384,128]{1,0:T(8,128)(2,1)S(1)}, bf16[384,128]{1,0:T(8,128)(2,1)S(1)}, u32[]{:S(2)}, u32[]{:S(2)}) %collective-permute-start.22) | collective-permute-done | bytes 98336 | tf_op jit(solution)/shard_map/ppermute | solution.py:328
  178.4 1.7 collective-permute-start.23
  180.2 1.4 all-to-all-done.2.i_ref
  181.6 1.2 copy-done
  182.8 2.7 %unpack.1 = (bf16[1,128,4096]{2,1,0:T(8,128)(2,1)}, bf16[1,128,1024]{2,1,0:T(8,128)(2,1)}, bf16[1,128,1024]{2,1,0:T(8,128)(2,1)}) custom-call(bf16[8,128,768]{2,1,0:T(8,128)(2,1)} %copy-done), custom_call_target="tpu_custom_call" | custom-call | bytes 3145728 | tf_op jit(solution)/shard_map/unpack/pallas_call | solution.py:191
  185.5 0.8 copy.12
  (45 shorter events, 0.4 us)
Async XLA Ops:
  2.6 37.2 %all-to-all-start.1 = ((bf16[8,128,512]{2,1,0:T(8,128)(2,1)}), bf16[8,128,512]{2,1,0:T(8,128)(2,1)S(1)}, u32[]{:S(2)}, u32[]{:S(2)}) async-start(bf16[8,128,512]{2,1,0:T(8,128)(2,1)} %broadcast_in_dim.41), calls=%async_computation.1 | async-start | bytes 2097152 | tf_op jit(solution)/shard_map/all_to_all | solution.py:340
  11.1 24.8 %collective-permute-start = (bf16[128,4096]{1,0:T(8,128)(2,1)}, bf16[128,4096]{1,0:T(8,128)(2,1)S(1)}, u32[]{:S(2)}, u32[]{:S(2)}) collective-permute-start(bf16[128,4096]{1,0:T(8,128)(2,1)} %bitcast.2.refs_0_), channel_id=1, source_target_pairs={{0,64},{32,96},{64,128},{96,160},{128,192},{160,224},{192,0},{224,... | collective-permute-start | bytes 3145736 | tf_op jit(solution)/shard_map/ppermute | solution.py:345
  12.6 30.3 %collective-permute-start.1 = (bf16[128,4096]{1,0:T(8,128)(2,1)}, bf16[128,4096]{1,0:T(8,128)(2,1)S(1)}, u32[]{:S(2)}, u32[]{:S(2)}) collective-permute-start(bf16[128,4096]{1,0:T(8,128)(2,1)} %bitcast.2.refs_0_), channel_id=1, source_target_pairs={{0,192},{32,224},{64,0},{96,32},{128,64},{160,96},{192,128},{224,1... | collective-permute-start | bytes 3145736 | tf_op jit(solution)/shard_map/ppermute | solution.py:345
  35.9 1.1 copy-start.3
  37.0 16.3 %collective-permute-start.2 = (bf16[64,4096]{1,0:T(8,128)(2,1)}, bf16[64,4096]{1,0:T(8,128)(2,1)S(1)}, u32[]{:S(2)}, u32[]{:S(2)}) collective-permute-start(bf16[64,4096]{1,0:T(8,128)(2,1)} %slice.88), channel_id=1, source_target_pairs={{0,64},{32,96},{64,128},{96,160},{128,192},{160,224},{192,0},{224,... | collective-permute-start | bytes 1572872 | tf_op jit(solution)/shard_map/ppermute | solution.py:345
  39.8 25.6 %copy-start.2 = (bf16[8,128,512]{2,1,0:T(8,128)(2,1)}, bf16[8,128,512]{2,1,0:T(8,128)(2,1)S(1)}, u32[]{:S(2)}) copy-start(bf16[8,128,512]{2,1,0:T(8,128)(2,1)S(1)} %all-to-all-done.1.refs_8_) | copy-start | bytes 3145732
  39.8 25.6 %collective-permute-start.9 = (bf16[8,128,512]{2,1,0:T(8,128)(2,1)S(1)}, bf16[8,128,512]{2,1,0:T(8,128)(2,1)}, u32[]{:S(2)}, u32[]{:S(2)}) collective-permute-start(bf16[8,128,512]{2,1,0:T(8,128)(2,1)S(1)} %all-to-all-done.1.refs_8_), channel_id=1, source_target_pairs={{0,3},{1,0},{2,1},{3,2},{4,7},{5,4},{6,5},{7,6},{8,11},{9,8},{10,9... | collective-permute-start | bytes 3145736 | tf_op jit(solution)/shard_map/ppermute | solution.py:328
  42.8 4.2 %copy-start.4 = (bf16[128,4096]{1,0:T(8,128)(2,1)}, bf16[128,4096]{1,0:T(8,128)(2,1)S(1)}, u32[]{:S(2)}) copy-start(bf16[128,4096]{1,0:T(8,128)(2,1)S(1)} %collective-permute-done.1.refs_2_) | copy-start | bytes 3145732
  43.7 16.6 %collective-permute-start.3 = (bf16[64,4096]{1,0:T(8,128)(2,1)}, bf16[64,4096]{1,0:T(8,128)(2,1)}, u32[]{:S(2)}, u32[]{:S(2)}) collective-permute-start(bf16[64,4096]{1,0:T(8,128)(2,1)} %slice.89), channel_id=1, source_target_pairs={{0,192},{32,224},{64,0},{96,32},{128,64},{160,96},{192,128},{224,1... | collective-permute-start | bytes 1572872 | tf_op jit(solution)/shard_map/ppermute | solution.py:345
  44.3 50.3 %collective-permute-start.4 = (bf16[128,4096]{1,0:T(8,128)(2,1)}, bf16[128,4096]{1,0:T(8,128)(2,1)}, u32[]{:S(2)}, u32[]{:S(2)}) collective-permute-start(bf16[128,4096]{1,0:T(8,128)(2,1)} %bitcast.2.refs_0_), channel_id=1, source_target_pairs={{0,32},{32,0},{64,96},{96,64},{128,160},{160,128},{192,224},{224,1... | collective-permute-start | bytes 3145736 | tf_op jit(solution)/shard_map/ppermute | solution.py:345
  47.0 28.3 %all-to-all-start = ((bf16[8,128,768]{2,1,0:T(8,128)(2,1)}), bf16[8,128,768]{2,1,0:T(8,128)(2,1)S(1)}, u32[]{:S(2)}, u32[]{:S(2)}) async-start(bf16[8,128,768]{2,1,0:T(8,128)(2,1)} %pack.1), calls=%async_computation | async-start | bytes 3145728 | tf_op jit(solution)/shard_map/all_to_all | solution.py:340
  53.2 13.4 %copy-start.5 = (s32[4]{0:T(128)S(1)}, s32[4]{0:T(128)}, u32[]{:S(2)}) copy-start(s32[4]{0:T(128)} %constant.61.clone) | copy-start | bytes 52
  53.2 14.0 %copy-start.6 = (s32[1,32]{1,0:T(1,128)S(1)}, s32[1,32]{1,0:T(1,128)}, u32[]{:S(2)}) copy-start(s32[1,32]{1,0:T(1,128)} %param.12) | copy-start | bytes 388
  53.2 41.8 %collective-permute-start.6 = (bf16[128,4096]{1,0:T(8,128)(2,1)}, bf16[128,4096]{1,0:T(8,128)(2,1)}, u32[]{:S(2)}, u32[]{:S(2)}) collective-permute-start(bf16[128,4096]{1,0:T(8,128)(2,1)} %copy-done.4), channel_id=1, source_target_pairs={{0,32},{32,0},{64,96},{96,64},{128,160},{160,128},{192,224},{224,1... | collective-permute-start | bytes 3145736 | tf_op jit(solution)/shard_map/ppermute | solution.py:345
  53.3 41.7 %collective-permute-start.5 = (bf16[128,4096]{1,0:T(8,128)(2,1)}, bf16[128,4096]{1,0:T(8,128)(2,1)}, u32[]{:S(2)}, u32[]{:S(2)}) collective-permute-start(bf16[128,4096]{1,0:T(8,128)(2,1)} %copy-done.3), channel_id=1, source_target_pairs={{0,32},{32,0},{64,96},{96,64},{128,160},{160,128},{192,224},{224,1... | collective-permute-start | bytes 3145736 | tf_op jit(solution)/shard_map/ppermute | solution.py:345
  62.3 32.8 %collective-permute-start.7 = (bf16[128,4096]{1,0:T(8,128)(2,1)}, bf16[128,4096]{1,0:T(8,128)(2,1)}, u32[]{:S(2)}, u32[]{:S(2)}) collective-permute-start(bf16[128,4096]{1,0:T(8,128)(2,1)} %constant_dynamic-update-slice_fusion.refs_3_), channel_id=1, source_target_pairs={{0,32},{32,0},{64,96},{96,64},{128,160},{160,128},{192,224},{224,1... | collective-permute-start | bytes 3145736 | tf_op jit(solution)/shard_map/ppermute | solution.py:345
  65.4 26.4 %collective-permute-start.8 = (bf16[8,128,512]{2,1,0:T(8,128)(2,1)S(1)}, bf16[8,128,512]{2,1,0:T(8,128)(2,1)}, u32[]{:S(2)}, u32[]{:S(2)}) collective-permute-start(bf16[8,128,512]{2,1,0:T(8,128)(2,1)S(1)} %all-to-all-done.1.refs_8_), channel_id=1, source_target_pairs={{0,1},{1,2},{2,3},{3,0},{4,5},{5,6},{6,7},{7,4},{8,9},{9,10},{10,1... | collective-permute-start | bytes 3145736 | tf_op jit(solution)/shard_map/ppermute | solution.py:328
  75.3 1.2 copy-start.1
  91.8 23.7 %collective-permute-start.11 = (bf16[4,128,512]{2,1,0:T(8,128)(2,1)S(1)}, bf16[4,128,512]{2,1,0:T(8,128)(2,1)}, u32[]{:S(2)}, u32[]{:S(2)}) collective-permute-start(bf16[4,128,512]{2,1,0:T(8,128)(2,1)S(1)} %slice.91), channel_id=1, source_target_pairs={{0,3},{1,0},{2,1},{3,2},{4,7},{5,4},{6,5},{7,6},{8,11},{9,8},{10,9... | collective-permute-start | bytes 1572872 | tf_op jit(solution)/shard_map/ppermute | solution.py:328
  94.6 20.8 %collective-permute-start.10 = (bf16[4,128,512]{2,1,0:T(8,128)(2,1)S(1)}, bf16[4,128,512]{2,1,0:T(8,128)(2,1)}, u32[]{:S(2)}, u32[]{:S(2)}) collective-permute-start(bf16[4,128,512]{2,1,0:T(8,128)(2,1)S(1)} %slice.90), channel_id=1, source_target_pairs={{0,1},{1,2},{2,3},{3,0},{4,5},{5,6},{6,7},{7,4},{8,9},{9,10},{10,1... | collective-permute-start | bytes 1572872 | tf_op jit(solution)/shard_map/ppermute | solution.py:328
  106.7 38.9 %all-to-all-start.3 = ((bf16[8,4,128,128]{3,2,1,0:T(8,128)(2,1)}), bf16[8,4,128,128]{3,2,1,0:T(8,128)(2,1)S(1)}, u32[]{:S(2)}, u32[]{:S(2)}) async-start(bf16[8,4,128,128]{3,2,1,0:T(8,128)(2,1)} %get-tuple-element.20), calls=%async_computation.3 | async-start | bytes 2097152 | tf_op jit(solution)/shard_map/all_to_all | solution.py:340
  112.5 13.1 %collective-permute-start.13 = (bf16[4,384,128]{2,1,0:T(8,128)(2,1)}, bf16[4,384,128]{2,1,0:T(8,128)(2,1)}, u32[]{:S(2)}, u32[]{:S(2)}) collective-permute-start(bf16[4,384,128]{2,1,0:T(8,128)(2,1)} %get-tuple-element.38), channel_id=1, source_target_pairs={{0,3},{1,0},{2,1},{3,2},{4,7},{5,4},{6,5},{7,6},{8,11},{9,8},{10,9... | collective-permute-start | bytes 1179656 | tf_op jit(solution)/shard_map/ppermute | solution.py:328
  115.5 10.2 %collective-permute-start.12 = (bf16[4,384,128]{2,1,0:T(8,128)(2,1)S(1)}, bf16[4,384,128]{2,1,0:T(8,128)(2,1)}, u32[]{:S(2)}, u32[]{:S(2)}) collective-permute-start(bf16[4,384,128]{2,1,0:T(8,128)(2,1)S(1)} %get-tuple-element.39), channel_id=1, source_target_pairs={{0,1},{1,2},{2,3},{3,0},{4,5},{5,6},{6,7},{7,4},{8,9},{9,10},{10,1... | collective-permute-start | bytes 1179656 | tf_op jit(solution)/shard_map/ppermute | solution.py:328
  127.3 18.3 %collective-permute-start.14 = (bf16[8,384,128]{2,1,0:T(8,128)(2,1)S(1)}, bf16[8,384,128]{2,1,0:T(8,128)(2,1)}, u32[]{:S(2)}, u32[]{:S(2)}) collective-permute-start(bf16[8,384,128]{2,1,0:T(8,128)(2,1)S(1)} %pad_maximum_fusion), channel_id=1, source_target_pairs={{0,1},{1,2},{2,3},{3,0},{4,5},{5,6},{6,7},{7,4},{8,9},{9,10},{10,1... | collective-permute-start | bytes 2359304 | tf_op jit(solution)/shard_map/ppermute | solution.py:328
  127.5 18.1 %collective-permute-start.15 = (bf16[8,384,128]{2,1,0:T(8,128)(2,1)S(1)}, bf16[8,384,128]{2,1,0:T(8,128)(2,1)S(1)}, u32[]{:S(2)}, u32[]{:S(2)}) collective-permute-start(bf16[8,384,128]{2,1,0:T(8,128)(2,1)S(1)} %pad_maximum_fusion.1), channel_id=1, source_target_pairs={{0,3},{1,0},{2,1},{3,2},{4,7},{5,4},{6,5},{7,6},{8,11},{9,8},{10,9... | collective-permute-start | bytes 2359304 | tf_op jit(solution)/shard_map/ppermute | solution.py:328
  146.4 10.2 %all-to-all-start.4 = ((bf16[4,128,128]{2,1,0:T(8,128)(2,1)}), bf16[4,128,128]{2,1,0:T(8,128)(2,1)S(1)}, u32[]{:S(2)}, u32[]{:S(2)}) async-start(bf16[4,128,128]{2,1,0:T(8,128)(2,1)} %reduce_sum.61), calls=%async_computation.4 | async-start | bytes 262144 | tf_op jit(solution)/shard_map/all_to_all | solution.py:340
  152.4 9.1 %collective-permute-start.16 = (bf16[192,128]{1,0:T(8,128)(2,1)S(1)}, bf16[192,128]{1,0:T(8,128)(2,1)S(1)}, u32[]{:S(2)}, u32[]{:S(2)}) collective-permute-start(bf16[192,128]{1,0:T(8,128)(2,1)S(1)} %get-tuple-element.46), channel_id=1, source_target_pairs={{0,4},{4,8},{8,12},{12,16},{16,20},{20,24},{24,28},{28,0},{1,5},{5... | collective-permute-start | bytes 147464 | tf_op jit(solution)/shard_map/ppermute | solution.py:328
  154.1 7.4 %collective-permute-start.20 = (bf16[192,128]{1,0:T(8,128)(2,1)S(1)}, bf16[192,128]{1,0:T(8,128)(2,1)S(1)}, u32[]{:S(2)}, u32[]{:S(2)}) collective-permute-start(bf16[192,128]{1,0:T(8,128)(2,1)S(1)} %get-tuple-element.47), channel_id=1, source_target_pairs={{0,28},{4,0},{8,4},{12,8},{16,12},{20,16},{24,20},{28,24},{1,29},{... | collective-permute-start | bytes 147464 | tf_op jit(solution)/shard_map/ppermute | solution.py:328
  156.7 24.9 %all-to-all-start.2 = ((bf16[8,128,768]{2,1,0:T(8,128)(2,1)}), bf16[8,128,768]{2,1,0:T(8,128)(2,1)S(1)}, u32[]{:S(2)}, u32[]{:S(2)}) async-start(bf16[8,128,768]{2,1,0:T(8,128)(2,1)} %attend_grad.1), calls=%async_computation.2 | async-start | bytes 3145728 | tf_op jit(solution)/shard_map/all_to_all | solution.py:340
  161.6 6.1 %collective-permute-start.17 = (bf16[384,128]{1,0:T(8,128)(2,1)S(1)}, bf16[384,128]{1,0:T(8,128)(2,1)S(1)}, u32[]{:S(2)}, u32[]{:S(2)}) collective-permute-start(bf16[384,128]{1,0:T(8,128)(2,1)S(1)} %pad_maximum_fusion.2), channel_id=1, source_target_pairs={{0,4},{4,8},{8,12},{12,16},{16,20},{20,24},{24,28},{28,0},{1,5},{5... | collective-permute-start | bytes 294920 | tf_op jit(solution)/shard_map/ppermute | solution.py:328
  163.3 4.9 %collective-permute-start.21 = (bf16[384,128]{1,0:T(8,128)(2,1)S(1)}, bf16[384,128]{1,0:T(8,128)(2,1)S(1)}, u32[]{:S(2)}, u32[]{:S(2)}) collective-permute-start(bf16[384,128]{1,0:T(8,128)(2,1)S(1)} %pad_maximum_fusion.3), channel_id=1, source_target_pairs={{0,28},{4,0},{8,4},{12,8},{16,12},{20,16},{24,20},{28,24},{1,29},{... | collective-permute-start | bytes 294920 | tf_op jit(solution)/shard_map/ppermute | solution.py:328
  167.7 5.9 %collective-permute-start.18 = (bf16[384,128]{1,0:T(8,128)(2,1)S(1)}, bf16[384,128]{1,0:T(8,128)(2,1)S(1)}, u32[]{:S(2)}, u32[]{:S(2)}) collective-permute-start(bf16[384,128]{1,0:T(8,128)(2,1)S(1)} %fusion.6), channel_id=1, source_target_pairs={{0,4},{4,8},{8,12},{12,16},{16,20},{20,24},{24,28},{28,0},{1,5},{5... | collective-permute-start | bytes 294920 | tf_op jit(solution)/shard_map/ppermute | solution.py:328
  173.7 4.7 %collective-permute-start.22 = (bf16[384,128]{1,0:T(8,128)(2,1)S(1)}, bf16[384,128]{1,0:T(8,128)(2,1)S(1)}, u32[]{:S(2)}, u32[]{:S(2)}) collective-permute-start(bf16[384,128]{1,0:T(8,128)(2,1)S(1)} %get-tuple-element.43), channel_id=1, source_target_pairs={{0,28},{4,0},{8,4},{12,8},{16,12},{20,16},{24,20},{28,24},{1,29},{... | collective-permute-start | bytes 294920 | tf_op jit(solution)/shard_map/ppermute | solution.py:328
  174.2 11.2 %collective-permute-start.19 = (bf16[384,128]{1,0:T(8,128)(2,1)S(1)}, bf16[384,128]{1,0:T(8,128)(2,1)S(1)}, u32[]{:S(2)}, u32[]{:S(2)}) collective-permute-start(bf16[384,128]{1,0:T(8,128)(2,1)S(1)} %get-tuple-element.42), channel_id=1, source_target_pairs={{0,4},{4,8},{8,12},{12,16},{16,20},{20,24},{24,28},{28,0},{1,5},{5... | collective-permute-start | bytes 294920 | tf_op jit(solution)/shard_map/ppermute | solution.py:328
  178.4 7.0 %collective-permute-start.23 = (bf16[384,128]{1,0:T(8,128)(2,1)S(1)}, bf16[384,128]{1,0:T(8,128)(2,1)S(1)}, u32[]{:S(2)}, u32[]{:S(2)}) collective-permute-start(bf16[384,128]{1,0:T(8,128)(2,1)S(1)} %fusion.5), channel_id=1, source_target_pairs={{0,28},{4,0},{8,4},{12,8},{16,12},{20,16},{24,20},{28,24},{1,29},{... | collective-permute-start | bytes 294920 | tf_op jit(solution)/shard_map/ppermute | solution.py:328
  181.6 1.2 copy-start
where the time goes:
time: 189 us; the launch traced here: 186 us
  waiting for transfers between devices  63.1 us (33%)
  starting transfers between devices  55.6 us (29%)
  Pallas kernels  46.6 us (25%)
  local copies, waits for them, and re-layouts  14.3 us (8%)
  other arithmetic  5.96 us (3%)
    ppermute x8, waiting for transfers between devices, hop(): return lax.ppermute(x, 'seq', pairs)  28.6 us
    all_to_all x5, starting transfers between devices, swap(): return lax.all_to_all(x, axis, split_axis=0, concat_axis=0, tiled=True)  27.4 us
    ppermute x16, starting transfers between devices, shift(): return lax.ppermute(x, axis, [(i, (i + by) % n) for i in range(n)])  23.6 us
    ppermute x16, waiting for transfers between devices, shift(): return lax.ppermute(x, axis, [(i, (i + by) % n) for i in range(n)])  23.6 us
    pallas_call x1, Pallas kernels, attend_grad(): pl.pallas_call(bwd_kernel, grid=(blocks,), in_specs=[whole(x.shape) for x...  12.1 us
    pallas_call x1, Pallas kernels, proj_terms(): pl.pallas_call(proj_kernel, grid_spec=pltpu.PrefetchScalarGridSpec(num_sc...  11.7 us
    all_to_all x5, waiting for transfers between devices, swap(): return lax.all_to_all(x, axis, split_axis=0, concat_axis=0, tiled=True)  10.8 us
    pallas_call x1, Pallas kernels, upstream(): pl.pallas_call(upstream_kernel, grid_spec=pltpu.PrefetchScalarGridSpec(nu...  10.2 us
  transfers between devices with their start and end apart: 29, of which 12 were waited for; matrix products, arithmetic and copies ran while one was open for 8% of the time, Pallas kernels for 25%

commit v1 on v0

--- a/solution.py
+++ b/solution.py
@@ -22,9 +22,9 @@
     return pl.multiple_of(jnp.clip(i * TOK - 256, 0, blocks * TOK - KW), 64)
 
 
-def probs(i, start, g_ref, lo_ref, hi_ref, key, h0):
+def probs(i, start, q_ref, lo_ref, hi_ref, key, h0):
     q = jnp.concatenate(
-        [g_ref[i, :, (h0 + j) * HEAD : (h0 + j + 1) * HEAD] for j in range(GROUP)], 0
+        [q_ref[i, :, (h0 + j) * HEAD : (h0 + j + 1) * HEAD] for j in range(GROUP)], 0
     )
     s = lax.dot_general(key, q, (((1,), (1,)), ((), ())), preferred_element_type=F32)
     place = start + lax.broadcasted_iota(jnp.int32, (KW, GROUP * TOK), 0)
@@ -35,38 +35,43 @@
     return q, a
 
 
-def unpack_keys(g_ref, k_ref, v_ref):
-    for b in range(g_ref.shape[0]):
-        rows = slice(b * TOK, (b + 1) * TOK)
-        k_ref[rows, :] = g_ref[b, :, HEADS * HEAD : (HEADS + 1) * HEAD]
-        v_ref[rows, :] = g_ref[b, :, (HEADS + 1) * HEAD :]
-
-
-def fwd_kernel(g_ref, lo_ref, hi_ref, o_ref, k_ref, v_ref):
-    blocks = g_ref.shape[0]
+def assemble(ids_ref, pieces, q_ref, k_ref, v_ref):
+    for p, piece in enumerate(pieces):
+        b = ids_ref[p]
+        rows = pl.ds(pl.multiple_of(b * TOK, TOK), TOK)
+        q_ref[b] = piece[:, : HEADS * HEAD]
+        k_ref[rows, :] = piece[:, HEADS * HEAD : (HEADS + 1) * HEAD]
+        v_ref[rows, :] = piece[:, (HEADS + 1) * HEAD :]
+
+
+def fwd_kernel(ids_ref, *refs):
+    pieces, (lo_ref, hi_ref, o_ref, q_ref, k_ref, v_ref) = refs[:-6], refs[-6:]
+    blocks = len(pieces)
     i = pl.program_id(0)
 
     @pl.when(i == 0)
     def _():
-        unpack_keys(g_ref, k_ref, v_ref)
+        assemble(ids_ref, pieces, q_ref, k_ref, v_ref)
 
     start = window_start(i, blocks)
     key = k_ref[pl.ds(start, KW), :]
     vt = v_ref[pl.ds(start, KW), :].T
     for h0 in range(0, HEADS, GROUP):
-        _, a = probs(i, start, g_ref, lo_ref, hi_ref, key, h0)
+        _, a = probs(i, start, q_ref, lo_ref, hi_ref, key, h0)
         o = jnp.dot(vt, a.astype(BF16), preferred_element_type=F32).astype(BF16)
         for j in range(GROUP):
             o_ref[0, (h0 + j) * HEAD : (h0 + j + 1) * HEAD, :] = o[:, j * TOK : (j + 1) * TOK]
 
 
-def bwd_kernel(g_ref, u_ref, lo_ref, hi_ref, o_ref, dk_ref, dv_ref, k_ref, v_ref):
-    blocks = g_ref.shape[0]
+def bwd_kernel(ids_ref, *refs):
+    pieces, refs = refs[:-9], refs[-9:]
+    u_ref, lo_ref, hi_ref, o_ref, dk_ref, dv_ref, q_ref, k_ref, v_ref = refs
+    blocks = len(pieces)
     i = pl.program_id(0)
 
     @pl.when(i == 0)
     def _():
-        unpack_keys(g_ref, k_ref, v_ref)
+        assemble(ids_ref, pieces, q_ref, k_ref, v_ref)
         dk_ref[...] = jnp.zeros_like(dk_ref)
         dv_ref[...] = jnp.zeros_like(dv_ref)
 
@@ -76,7 +81,7 @@
     kt = key.T
     dk = None
     for h0 in range(0, HEADS, GROUP):
-        q, a = probs(i, start, g_ref, lo_ref, hi_ref, key, h0)
+        q, a = probs(i, start, q_ref, lo_ref, hi_ref, key, h0)
         u = jnp.concatenate(
             [u_ref[i, :, (h0 + j) * HEAD : (h0 + j + 1) * HEAD] for j in range(GROUP)], 0
         )
@@ -104,7 +109,7 @@
 
 
 def whole(shape):
-    return pl.BlockSpec(shape, lambda i: (0,) * len(shape))
+    return pl.BlockSpec(shape, lambda i, ids: (0,) * len(shape))
 
 
 def limits(sent_lengths, blocks):
@@ -120,39 +125,54 @@
     return lo.reshape(blocks, 1, TOK), hi.reshape(blocks, 1, TOK)
 
 
-def attend(g, lo, hi):
-    blocks = g.shape[0]
+def head_scratch(blocks):
+    keys = pltpu.VMEM((blocks * TOK, HEAD), BF16)
+    return [pltpu.VMEM((blocks, TOK, HEADS * HEAD), BF16), keys, keys]
+
+
+def attend(ids, pieces, lo, hi):
+    blocks = len(pieces)
     pairs = blocks * TOK * KW * HEADS
     return pl.pallas_call(
         fwd_kernel,
-        grid=(blocks,),
-        in_specs=[whole(x.shape) for x in (g, lo, hi)],
-        out_specs=pl.BlockSpec((1, HEADS * HEAD, TOK), lambda i: (i, 0, 0)),
+        grid_spec=pltpu.PrefetchScalarGridSpec(
+            num_scalar_prefetch=1,
+            grid=(blocks,),
+            in_specs=[whole(x.shape) for x in (*pieces, lo, hi)],
+            out_specs=pl.BlockSpec((1, HEADS * HEAD, TOK), lambda i, ids: (i, 0, 0)),
+            scratch_shapes=head_scratch(blocks),
+        ),
         out_shape=jax.ShapeDtypeStruct((blocks, HEADS * HEAD, TOK), BF16),
-        scratch_shapes=[pltpu.VMEM((blocks * TOK, HEAD), BF16)] * 2,
         cost_estimate=pl.CostEstimate(
-            flops=4 * pairs * HEAD, bytes_accessed=4 * g.size, transcendentals=pairs
+            flops=4 * pairs * HEAD,
+            bytes_accessed=4 * blocks * pieces[0].size,
+            transcendentals=pairs,
         ),
         name="attend",
-    )(g, lo, hi)
-
-
-def attend_grad(g, u, lo, hi):
-    blocks = g.shape[0]
+    )(ids, *pieces, lo, hi)
+
+
+def attend_grad(ids, pieces, u, lo, hi):
+    blocks = len(pieces)
     pairs = blocks * TOK * KW * HEADS
+    shape = (blocks, *pieces[0].shape)
     return pl.pallas_call(
         bwd_kernel,
-        grid=(blocks,),
-        in_specs=[whole(x.shape) for x in (g, u, lo, hi)],
-        out_specs=whole(g.shape),
-        out_shape=jax.ShapeDtypeStruct(g.shape, BF16),
-        scratch_shapes=[pltpu.VMEM((blocks * TOK, HEAD), F32)] * 2
-        + [pltpu.VMEM((blocks * TOK, HEAD), BF16)] * 2,
+        grid_spec=pltpu.PrefetchScalarGridSpec(
+            num_scalar_prefetch=1,
+            grid=(blocks,),
+            in_specs=[whole(x.shape) for x in (*pieces, u, lo, hi)],
+            out_specs=whole(shape),
+            scratch_shapes=[pltpu.VMEM((blocks * TOK, HEAD), F32)] * 2 + head_scratch(blocks),
+        ),
+        out_shape=jax.ShapeDtypeStruct(shape, BF16),
         cost_estimate=pl.CostEstimate(
-            flops=10 * pairs * HEAD, bytes_accessed=6 * g.size, transcendentals=pairs
+            flops=10 * pairs * HEAD,
+            bytes_accessed=6 * blocks * pieces[0].size,
+            transcendentals=pairs,
         ),
         name="attend_grad",
-    )(g, u, lo, hi)
+    )(ids, *pieces, u, lo, hi)
 
 
 def head_parts(g):
@@ -164,20 +184,31 @@
     )
 
 
-def pack_kernel(q_ref, k_ref, v_ref, o_ref):
-    for g in range(o_ref.shape[0]):
-        for ref, (inner, outer) in zip((q_ref, k_ref, v_ref), head_parts(g)):
-            o_ref[g, :, inner] = ref[0, :, outer]
-
-
-def pack(q, k, v):
+def pack_kernel(ids_ref, q_ref, k_ref, v_ref, *o_refs):
+    wide = HEADS * HEAD
+    for p, o_ref in enumerate(o_refs):
+        g = ids_ref[p]
+        heads = pl.ds(pl.multiple_of(g * HEAD, HEAD), HEAD)
+        o_ref[:, :wide] = q_ref[0, :, pl.ds(pl.multiple_of(g * wide, wide), wide)]
+        o_ref[:, wide : wide + HEAD] = k_ref[0, :, heads]
+        o_ref[:, wide + HEAD :] = v_ref[0, :, heads]
+
+
+def pack(ids, q, k, v):
     groups = k.shape[2] // HEAD
+    width = (HEADS + 2) * HEAD
     return pl.pallas_call(
         pack_kernel,
-        out_shape=jax.ShapeDtypeStruct((groups, TOK, (HEADS + 2) * HEAD), BF16),
+        grid_spec=pltpu.PrefetchScalarGridSpec(
+            num_scalar_prefetch=1,
+            grid=(1,),
+            in_specs=[whole(x.shape) for x in (q, k, v)],
+            out_specs=[whole((TOK, width))] * groups,
+        ),
+        out_shape=[jax.ShapeDtypeStruct((TOK, width), BF16)] * groups,
         cost_estimate=pl.CostEstimate(flops=0, bytes_accessed=6 * q.size, transcendentals=0),
         name="pack",
-    )(q, k, v)
+    )(ids, q, k, v)
 
 
 def unpack_kernel(i_ref, q_ref, k_ref, v_ref):
@@ -350,8 +381,7 @@
 ):
     place = lax.axis_index("seq").astype(jnp.int32)
     chip, core = place // 2, place % 2
-    offsets = jnp.array([0, 3, 1, 2], jnp.int32)
-    chips = (chip + offsets) % 4 * 2
+    chips = (chip + jnp.array([0, 3, 1, 2], jnp.int32)) % 4 * 2
     ids = jnp.concatenate(
         [
             chips + core,
@@ -359,20 +389,23 @@
             jnp.stack([lax.axis_index("dp"), lax.axis_index("fsdp")]).astype(jnp.int32),
         ]
     )
+    targets = (chip + jnp.array([0, 1, 3, 2], jnp.int32)) % 4 * 2
+    targets = jnp.concatenate([targets + core, targets + 1 - core])
     far = GRID["dp"] // 2
     half = TOK // 2
     own = out_cotangent[0]
+    left, right = hop(own, 1, 0), hop(own, -1, 0)
     weight = jnp.broadcast_to(proj_weight, (2 * far, *proj_weight.shape))
     weight = swap(weight, "dp")
-    left, right = hop(own, 1, 0), hop(own, -1, 0)
-    local = pack(query_rows, forward_key_rows, forward_value_rows)
+    packed = pack(targets, query_rows, forward_key_rows, forward_value_rows)
+    paths = [(chips, flip) for flip in range(2) for chips in (0, 1, -1, 2)]
+    packed = [packed[0]] + [hop(x, *path) for x, path in zip(packed[1:], paths[1:])]
     partner = hop(own, 0, 1)
-    packed = swap(local, "seq")
     below, above = shift(weight, "fsdp", 1), shift(weight, "fsdp", -1)
-    lo, hi = limits(sent_lengths[0], packed.shape[0])
+    lo, hi = limits(sent_lengths[0], len(packed))
     across = [hop(left[:half], 1, 0), hop(right[half:], -1, 0)]
     across = jnp.concatenate(across, 0)
-    output = attend(packed, lo, hi)
+    output = attend(ids, packed, lo, hi)
     pieces = [own, left, right, across, partner]
     pieces += [hop(piece, 0, 1) for piece in (left, right, across)]
     ends = [shift(below[:far], "fsdp", 1), shift(above[far:], "fsdp", -1)]
@@ -383,7 +416,7 @@
     up, down = after((up, down), arriving)
     up = shift(jnp.concatenate([add(first[1, :far], up), first[1, far:]], 0), "fsdp", 1)
     down = shift(jnp.concatenate([first[3, :far], add(first[3, far:], down)], 0), "fsdp", -1)
-    grads = attend_grad(packed, arriving, lo, hi)
+    grads = attend_grad(ids, packed, arriving, lo, hi)
     grads_home = swap(grads, "seq")
     up, down, second = after((up, down, second), grads)
     first = (first[0].astype(F32) + up.astype(F32) + down.astype(F32)).astype(BF16)

time: 189 us -> 195 us (1.032)
  Pallas kernels: 46.6 us -> 49.2 us
  waiting for transfers between devices: 63.1 us -> 65.7 us
  starting transfers between devices: 55.6 us -> 57.8 us
  local copies, waits for them, and re-layouts: 14.3 us -> 12.2 us
    ppermute x8 -> x15, starting transfers between devices: 4.57 us -> 16.1 us  [hop(): return lax.ppermute(x, 'seq', pairs)]
    ppermute x8 -> x15, waiting for transfers between devices: 28.6 us -> 39.7 us  [hop(): return lax.ppermute(x, 'seq', pairs)]
    all_to_all x5 -> x4, waiting for transfers between devices: 10.8 us -> 3.46 us  [swap(): return lax.all_to_all(x, axis, split_axis=0, concat_axis=0, tiled=True)]
    all_to_all x5 -> x4, starting transfers between devices: 27.4 us -> 20.5 us  [swap(): return lax.all_to_all(x, axis, split_axis=0, concat_axis=0, tiled=True)]
    pallas_call x3, Pallas kernels: 22.1 us -> 24.7 us  [the longest x1 12.9 us: attend_grad(): pl.pallas_call(bwd_kernel, grid_spec=pltpu.PrefetchScalarGridSpec(num_sca...]
    ppermute x16, starting transfers between devices: 23.6 us -> 21.1 us  [shift(): return lax.ppermute(x, axis, [(i, (i + by) % n) for i in range(n)])]
    unnamed x16 -> x26, local copies, waits for them, and re-layouts: 4.22 us -> 2.81 us
  transfers between devices with their start and end apart: 29 -> 35, of which waited for: 12 -> 15; matrix products, arithmetic and copies ran while one was open for 8% -> 7% of each run, Pallas kernels for 25% -> 26%
where the time goes in v1:
time: 195 us; the launch traced here: 192 us
  waiting for transfers between devices  65.7 us (34%)
  starting transfers between devices  57.8 us (30%)
  Pallas kernels  49.2 us (25%)
  local copies, waits for them, and re-layouts  12.2 us (6%)
  other arithmetic  6.54 us (3%)
    ppermute x15, waiting for transfers between devices, hop(): return lax.ppermute(x, 'seq', pairs)  39.7 us
    ppermute x16, waiting for transfers between devices, shift(): return lax.ppermute(x, axis, [(i, (i + by) % n) for i in range(n)])  22.6 us
    ppermute x16, starting transfers between devices, shift(): return lax.ppermute(x, axis, [(i, (i + by) % n) for i in range(n)])  21.1 us
    all_to_all x4, starting transfers between devices, swap(): return lax.all_to_all(x, axis, split_axis=0, concat_axis=0, tiled=True)  20.5 us
    ppermute x15, starting transfers between devices, hop(): return lax.ppermute(x, 'seq', pairs)  16.1 us
    pallas_call x1, Pallas kernels, attend_grad(): pl.pallas_call(bwd_kernel, grid_spec=pltpu.PrefetchScalarGridSpec(num_sca...  12.9 us
    pallas_call x1, Pallas kernels, proj_terms(): pl.pallas_call(proj_kernel, grid_spec=pltpu.PrefetchScalarGridSpec(num_sc...  11.7 us
    pallas_call x1, Pallas kernels, upstream(): pl.pallas_call(upstream_kernel, grid_spec=pltpu.PrefetchScalarGridSpec(nu...  10.2 us
  transfers between devices with their start and end apart: 35, of which 15 were waited for; matrix products, arithmetic and copies ran while one was open for 7% of the time, Pallas kernels for 26%

profile of v1, /device:TPU:2, one launch (start us, length us, event | category | flops | bytes accessed | tf_op | source)
XLA Modules:
  0.0 192.2 jit_solution(14166460408452246379)
XLA Ops:
  0.6 2.0 %broadcast_in_dim.41 = bf16[8,128,512]{2,1,0:T(8,128)(2,1)} broadcast(bf16[128,512]{1,0:T(8,128)(2,1)} %param.12), dimensions={1,2} | broadcast | bytes 1179648 | tf_op jit(solution)/shard_map/broadcast_in_dim | solution.py:398
  2.6 8.6 %all-to-all-start = ((bf16[8,128,512]{2,1,0:T(8,128)(2,1)}), bf16[8,128,512]{2,1,0:T(8,128)(2,1)S(1)}, u32[]{:S(2)}, u32[]{:S(2)}) async-start(bf16[8,128,512]{2,1,0:T(8,128)(2,1)} %broadcast_in_dim.41), calls=%async_computation | async-start | bytes 2097152 | tf_op jit(solution)/shard_map/all_to_all | solution.py:371
  11.2 1.5 collective-permute-start.7
  12.7 0.5 collective-permute-start.8
  13.2 22.9 %collective-permute-done.7.refs_1_ = bf16[128,4096]{1,0:T(8,128)(2,1)} collective-permute-done((bf16[128,4096]{1,0:T(8,128)(2,1)}, bf16[128,4096]{1,0:T(8,128)(2,1)}, u32[]{:S(2)}, u32[]{:S(2)}) %collective-permute-start.7) | collective-permute-done | bytes 1048608 | tf_op jit(solution)/shard_map/ppermute | solution.py:376
  36.1 1.1 slice.88
  37.2 1.6 collective-permute-start.9
  38.8 1.1 all-to-all-done.refs_8_
  39.9 3.0 %collective-permute-start.16 = (bf16[8,128,512]{2,1,0:T(8,128)(2,1)S(1)}, bf16[8,128,512]{2,1,0:T(8,128)(2,1)}, u32[]{:S(2)}, u32[]{:S(2)}) collective-permute-start(bf16[8,128,512]{2,1,0:T(8,128)(2,1)S(1)} %all-to-all-done.refs_8_), channel_id=1, source_target_pairs={{0,3},{1,0},{2,1},{3,2},{4,7},{5,4},{6,5},{7,6},{8,11},{9,8},{10,9... | collective-permute-start | bytes 3145736 | tf_op jit(solution)/shard_map/ppermute | solution.py:359
  43.0 1.1 slice.89
  44.0 0.6 collective-permute-start.10
  44.7 0.6 pad_add_fusion.1.ids_ref
  45.2 3.5 %pack.1 = (bf16[128,768]{1,0:T(8,128)(2,1)}, bf16[128,768]{1,0:T(8,128)(2,1)}, bf16[128,768]{1,0:T(8,128)(2,1)}, bf16[128,768]{1,0:T(8,128)(2,1)}, bf16[128,768]...) custom-call(s32[8]{0:T(128)} %pad_add_fusion.1.ids_ref, ...), custom_call_target="tpu_custom_call" | custom-call | bytes 3145728 | tf_op jit(solution)/shard_map/pack/pallas_call | solution.py:200
  48.7 1.5 collective-permute-start
  50.2 1.3 collective-permute-start.1
  51.5 2.0 %collective-permute-start.2 = (bf16[128,768]{1,0:T(8,128)(2,1)}, bf16[128,768]{1,0:T(8,128)(2,1)S(1)}, u32[]{:S(2)}, u32[]{:S(2)}) collective-permute-start(bf16[128,768]{1,0:T(8,128)(2,1)} %get-tuple-element.25), channel_id=1, source_target_pairs={{0,128},{32,160},{64,192},{96,224},{128,0},{160,32},{192,64},{224,... | collective-permute-start | bytes 589832 | tf_op jit(solution)/shard_map/ppermute | solution.py:376
  53.6 0.8 constant_dynamic-update-slice_fusion.1
  54.4 3.1 %collective-permute-done.refs_1_ = bf16[128,768]{1,0:T(8,128)(2,1)S(1)} collective-permute-done((bf16[128,768]{1,0:T(8,128)(2,1)}, bf16[128,768]{1,0:T(8,128)(2,1)S(1)}, u32[]{:S(2)}, u32[]{:S(2)}) %collective-permute-start) | collective-permute-done | bytes 196640 | tf_op jit(solution)/shard_map/ppermute | solution.py:376
  57.5 4.7 %collective-permute-done.1.refs_2_ = bf16[128,768]{1,0:T(8,128)(2,1)S(1)} collective-permute-done((bf16[128,768]{1,0:T(8,128)(2,1)}, bf16[128,768]{1,0:T(8,128)(2,1)S(1)}, u32[]{:S(2)}, u32[]{:S(2)}) %collective-permute-start.1) | collective-permute-done | bytes 196640 | tf_op jit(solution)/shard_map/ppermute | solution.py:376
  62.2 4.8 %collective-permute-done.2.refs_3_ = bf16[128,768]{1,0:T(8,128)(2,1)S(1)} collective-permute-done((bf16[128,768]{1,0:T(8,128)(2,1)}, bf16[128,768]{1,0:T(8,128)(2,1)S(1)}, u32[]{:S(2)}, u32[]{:S(2)}) %collective-permute-start.2) | collective-permute-done | bytes 196640 | tf_op jit(solution)/shard_map/ppermute | solution.py:376
  67.1 1.9 collective-permute-start.6
  69.0 0.8 constant_dynamic-update-slice_fusion.refs_3_
  70.0 2.4 %collective-permute-start.11 = (bf16[128,4096]{1,0:T(8,128)(2,1)}, bf16[128,4096]{1,0:T(8,128)(2,1)}, u32[]{:S(2)}, u32[]{:S(2)}) collective-permute-start(bf16[128,4096]{1,0:T(8,128)(2,1)} %bitcast.2.refs_0_), channel_id=1, source_target_pairs={{0,32},{32,0},{64,96},{96,64},{128,160},{160,128},{192,224},{224,1... | collective-permute-start | bytes 3145736 | tf_op jit(solution)/shard_map/ppermute | solution.py:376
  72.4 2.8 %collective-permute-done.5.refs_6_ = bf16[128,768]{1,0:T(8,128)(2,1)S(1)} collective-permute-done((bf16[128,768]{1,0:T(8,128)(2,1)}, bf16[128,768]{1,0:T(8,128)(2,1)S(1)}, u32[]{:S(2)}, u32[]{:S(2)}) %collective-permute-start.5) | collective-permute-done | bytes 196640 | tf_op jit(solution)/shard_map/ppermute | solution.py:376
  75.1 1.3 collective-permute-done.6.refs_7_
  76.5 2.5 %collective-permute-start.12 = (bf16[128,4096]{1,0:T(8,128)(2,1)}, bf16[128,4096]{1,0:T(8,128)(2,1)}, u32[]{:S(2)}, u32[]{:S(2)}) collective-permute-start(bf16[128,4096]{1,0:T(8,128)(2,1)} %collective-permute-done.7.refs_1_), channel_id=1, source_target_pairs={{0,32},{32,0},{64,96},{96,64},{128,160},{160,128},{192,224},{224,1... | collective-permute-start | bytes 3145736 | tf_op jit(solution)/shard_map/ppermute | solution.py:376
  79.3 0.6 pad_add_fusion.ids_ref
  80.1 0.7 select_reduce_fusion
  80.8 8.3 %attend.1.refs_8_ = bf16[8,512,128]{2,1,0:T(8,128)(2,1)} custom-call(s32[10]{0:T(128)} %pad_add_fusion.ids_ref, bf16[128,768]{1,0:T(8,128)(2,1)} %get-tuple-element.22.refs_0_, bf16[128,768]{1,0:T(8,128)(2,1)} %copy-done.5, bf16[128,768]{1,0:T(8,128)(2,1)} %copy-done.6, bf16[128,768]{1,0:T(8,128)(2,1)} %copy-done.7, bf16[128,768]{1,0:T(8,128)(2,1)} %copy-done.8, ...), custom_call_target="tpu_custom_call" | custom-call | flops 939524096 | bytes 3145728 | tf_op jit(solution)/shard_map/attend/pallas_call | solution.py:136
  89.1 1.1 slice.91
  90.2 5.7 %collective-permute-done.15.refs_9_ = bf16[8,128,512]{2,1,0:T(8,128)(2,1)} collective-permute-done((bf16[8,128,512]{2,1,0:T(8,128)(2,1)S(1)}, bf16[8,128,512]{2,1,0:T(8,128)(2,1)}, u32[]{:S(2)}, u32[]{:S(2)}) %collective-permute-start.15) | collective-permute-done | bytes 1048608 | tf_op jit(solution)/shard_map/ppermute | solution.py:359
  95.8 1.1 slice.90
  96.9 2.1 %collective-permute-start.17 = (bf16[4,128,512]{2,1,0:T(8,128)(2,1)S(1)}, bf16[4,128,512]{2,1,0:T(8,128)(2,1)}, u32[]{:S(2)}, u32[]{:S(2)}) collective-permute-start(bf16[4,128,512]{2,1,0:T(8,128)(2,1)S(1)} %slice.90), channel_id=1, source_target_pairs={{0,1},{1,2},{2,3},{3,0},{4,5},{5,6},{6,7},{7,4},{8,9},{9,10},{10,1... | collective-permute-start | bytes 1572872 | tf_op jit(solution)/shard_map/ppermute | solution.py:359
  99.0 11.7 %proj_terms.1 = (bf16[4,8,384,128]{3,2,1,0:T(8,128)(2,1)}, bf16[8,4,128,128]{3,2,1,0:T(8,128)(2,1)}) custom-call(s32[10]{0:T(128)} %pad_add_fusion.ids_ref, bf16[128,4096]{1,0:T(8,128)(2,1)} %bitcast.2.refs_0_, bf16[128,4096]{1,0:T(8,128)(2,1)} %collective-permute-done.7.refs_1_, bf16[128,4096]{1,0:T(8,128)(2,1)} %collective-permute-done.8.refs_2_, ...), custom_call_target="tpu_custom_call" | custom-call | flops 4294967296 | bytes 13631488 | tf_op jit(solution)/shard_map/proj_terms/pallas_call | solution.py:331
  110.7 4.1 %all-to-all-start.2 = ((bf16[8,4,128,128]{3,2,1,0:T(8,128)(2,1)}), bf16[8,4,128,128]{3,2,1,0:T(8,128)(2,1)S(1)}, u32[]{:S(2)}, u32[]{:S(2)}) async-start(bf16[8,4,128,128]{3,2,1,0:T(8,128)(2,1)} %get-tuple-element.36), calls=%async_computation.2 | async-start | bytes 2097152 | tf_op jit(solution)/shard_map/all_to_all | solution.py:371
  114.8 2.2 %slice_bitcast_fusion = (bf16[4,384,128]{2,1,0:T(8,128)(2,1)S(1)}, bf16[4,384,128]{2,1,0:T(8,128)(2,1)S(1)}, bf16[4,384,128]{2,1,0:T(8,128)(2,1)}, bf16[4,384,128]{2,1,0:T(8,128)(2,1)S(1)}) fusion(bf16[4,8,384,128]{3,2,1,0:T(8,128)(2,1)} %get-tuple-element.33), kind=kLoop, calls=%fused_computation.9 | loop fusion | bytes 3145728 | tf_op jit(solution)/shard_map/squeeze | solution.py:418
  117.1 1.2 collective-permute-start.20
  118.3 0.8 collective-permute-start.19
  119.1 10.2 %upstream.1.refs_8_ = bf16[8,128,512]{2,1,0:T(8,128)(2,1)} custom-call(s32[10]{0:T(128)} %pad_add_fusion.ids_ref, bf16[128,4096]{1,0:T(8,128)(2,1)} %bitcast.2.refs_0_, bf16[128,4096]{1,0:T(8,128)(2,1)} %collective-permute-done.7.refs_1_, bf16[128,4096]{1,0:T(8,128)(2,1)} %collective-permute-done.8.refs_2_, ...), custom_call_target="tpu_custom_call" | custom-call | flops 4294967296 | bytes 13631488 | tf_op jit(solution)/shard_map/upstream/pallas_call | solution.py:279
  129.3 1.7 collective-permute-done.19
  131.0 1.6 fusion.2
  132.9 3.3 %collective-permute-start.22 = (bf16[8,384,128]{2,1,0:T(8,128)(2,1)S(1)}, bf16[8,384,128]{2,1,0:T(8,128)(2,1)S(1)}, u32[]{:S(2)}, u32[]{:S(2)}) collective-permute-start(bf16[8,384,128]{2,1,0:T(8,128)(2,1)S(1)} %pad_maximum_fusion.1), channel_id=1, source_target_pairs={{0,3},{1,0},{2,1},{3,2},{4,7},{5,4},{6,5},{7,6},{8,11},{9,8},{10,9... | collective-permute-start | bytes 2359304 | tf_op jit(solution)/shard_map/ppermute | solution.py:359
  136.2 12.9 %attend_grad.1 = bf16[8,128,768]{2,1,0:T(8,128)(2,1)} custom-call(s32[10]{0:T(128)} %pad_add_fusion.ids_ref, bf16[128,768]{1,0:T(8,128)(2,1)} %get-tuple-element.22.refs_0_, bf16[128,768]{1,0:T(8,128)(2,1)} %copy-done.5, bf16[128,768]{1,0:T(8,128)(2,1)} %copy-done.6, bf16[128,768]{1,0:T(8,128)(2,1)} %copy-done.7, bf16[128,768]{1,0:T(8,128)(2,1)} %copy-done.8, ...), custom_call_target="tpu_custom_call" | custom-call | flops 2348810240 | bytes 4718592 | tf_op jit(solution)/shard_map/attend_grad/pallas_call | solution.py:159
  149.1 4.0 %collective-permute-done.21 = bf16[8,384,128]{2,1,0:T(8,128)(2,1)} collective-permute-done((bf16[8,384,128]{2,1,0:T(8,128)(2,1)S(1)}, bf16[8,384,128]{2,1,0:T(8,128)(2,1)}, u32[]{:S(2)}, u32[]{:S(2)}) %collective-permute-start.21) | collective-permute-done | bytes 786464 | tf_op jit(solution)/shard_map/ppermute | solution.py:359
  153.1 0.8 reduce_sum.61
  153.9 4.3 %all-to-all-start.3 = ((bf16[4,128,128]{2,1,0:T(8,128)(2,1)}), bf16[4,128,128]{2,1,0:T(8,128)(2,1)S(1)}, u32[]{:S(2)}, u32[]{:S(2)}) async-start(bf16[4,128,128]{2,1,0:T(8,128)(2,1)} %reduce_sum.61), calls=%async_computation.3 | async-start | bytes 262144 | tf_op jit(solution)/shard_map/all_to_all | solution.py:371
  158.2 1.7 fusion.1
  159.9 1.5 collective-permute-start.23
  161.4 1.8 collective-permute-start.27
  163.2 1.0 all-to-all-done.3
  164.2 3.5 %all-to-all-start.1 = ((bf16[8,128,768]{2,1,0:T(8,128)(2,1)}), bf16[8,128,768]{2,1,0:T(8,128)(2,1)S(1)}, u32[]{:S(2)}, u32[]{:S(2)}) async-start(bf16[8,128,768]{2,1,0:T(8,128)(2,1)} %attend_grad.1), calls=%async_computation.1 | async-start | bytes 3145728 | tf_op jit(solution)/shard_map/all_to_all | solution.py:371
  167.8 1.8 collective-permute-start.24
  169.5 1.8 collective-permute-start.28
  171.4 2.5 %collective-permute-done.24 = bf16[384,128]{1,0:T(8,128)(2,1)S(1)} collective-permute-done((bf16[384,128]{1,0:T(8,128)(2,1)S(1)}, bf16[384,128]{1,0:T(8,128)(2,1)S(1)}, u32[]{:S(2)}, u32[]{:S(2)}) %collective-permute-start.24) | collective-permute-done | bytes 98336 | tf_op jit(solution)/shard_map/ppermute | solution.py:359
  173.9 0.3 collective-permute-start.25
  174.3 5.6 %collective-permute-done.25 = bf16[384,128]{1,0:T(8,128)(2,1)S(1)} collective-permute-done((bf16[384,128]{1,0:T(8,128)(2,1)S(1)}, bf16[384,128]{1,0:T(8,128)(2,1)S(1)}, u32[]{:S(2)}, u32[]{:S(2)}) %collective-permute-start.25) | collective-permute-done | bytes 98336 | tf_op jit(solution)/shard_map/ppermute | solution.py:359
  179.9 0.3 collective-permute-start.29
  180.2 1.8 collective-permute-start.26
  182.0 3.0 %collective-permute-done.29 = bf16[384,128]{1,0:T(8,128)(2,1)S(1)} collective-permute-done((bf16[384,128]{1,0:T(8,128)(2,1)S(1)}, bf16[384,128]{1,0:T(8,128)(2,1)S(1)}, u32[]{:S(2)}, u32[]{:S(2)}) %collective-permute-start.29) | collective-permute-done | bytes 98336 | tf_op jit(solution)/shard_map/ppermute | solution.py:359
  185.1 1.1 collective-permute-start.30
  186.2 1.4 all-to-all-done.1.i_ref
  187.5 1.2 copy-done
  188.7 2.7 %unpack.1 = (bf16[1,128,4096]{2,1,0:T(8,128)(2,1)}, bf16[1,128,1024]{2,1,0:T(8,128)(2,1)}, bf16[1,128,1024]{2,1,0:T(8,128)(2,1)}) custom-call(bf16[8,128,768]{2,1,0:T(8,128)(2,1)} %copy-done), custom_call_target="tpu_custom_call" | custom-call | bytes 3145728 | tf_op jit(solution)/shard_map/unpack/pallas_call | solution.py:222
  191.5 0.8 copy.13
  (69 shorter events, 1.3 us)
Async XLA Ops:
  2.6 36.2 %copy-start.3 = (s32[4]{0:T(128)S(1)}, s32[4]{0:T(128)}, u32[]{:S(2)}) copy-start(s32[4]{0:T(128)} %constant.69.clone) | copy-start | bytes 52
  2.6 40.3 %copy-start.2 = (s32[4]{0:T(128)S(1)}, s32[4]{0:T(128)}, u32[]{:S(2)}) copy-start(s32[4]{0:T(128)} %constant.68.clone) | copy-start | bytes 52
  2.6 37.3 %all-to-all-start = ((bf16[8,128,512]{2,1,0:T(8,128)(2,1)}), bf16[8,128,512]{2,1,0:T(8,128)(2,1)S(1)}, u32[]{:S(2)}, u32[]{:S(2)}) async-start(bf16[8,128,512]{2,1,0:T(8,128)(2,1)} %broadcast_in_dim.41), calls=%async_computation | async-start | bytes 2097152 | tf_op jit(solution)/shard_map/all_to_all | solution.py:371
  11.2 24.9 %collective-permute-start.7 = (bf16[128,4096]{1,0:T(8,128)(2,1)}, bf16[128,4096]{1,0:T(8,128)(2,1)}, u32[]{:S(2)}, u32[]{:S(2)}) collective-permute-start(bf16[128,4096]{1,0:T(8,128)(2,1)} %bitcast.2.refs_0_), channel_id=1, source_target_pairs={{0,64},{32,96},{64,128},{96,160},{128,192},{160,224},{192,0},{224,... | collective-permute-start | bytes 3145736 | tf_op jit(solution)/shard_map/ppermute | solution.py:376
  12.7 30.3 %collective-permute-start.8 = (bf16[128,4096]{1,0:T(8,128)(2,1)}, bf16[128,4096]{1,0:T(8,128)(2,1)}, u32[]{:S(2)}, u32[]{:S(2)}) collective-permute-start(bf16[128,4096]{1,0:T(8,128)(2,1)} %bitcast.2.refs_0_), channel_id=1, source_target_pairs={{0,192},{32,224},{64,0},{96,32},{128,64},{160,96},{192,128},{224,1... | collective-permute-start | bytes 3145736 | tf_op jit(solution)/shard_map/ppermute | solution.py:376
  37.2 14.3 %collective-permute-start.9 = (bf16[64,4096]{1,0:T(8,128)(2,1)S(1)}, bf16[64,4096]{1,0:T(8,128)(2,1)S(1)}, u32[]{:S(2)}, u32[]{:S(2)}) collective-permute-start(bf16[64,4096]{1,0:T(8,128)(2,1)S(1)} %slice.88), channel_id=1, source_target_pairs={{0,64},{32,96},{64,128},{96,160},{128,192},{160,224},{192,0},{224,... | collective-permute-start | bytes 1572872 | tf_op jit(solution)/shard_map/ppermute | solution.py:376
  39.9 29.9 %copy-start.1 = (bf16[8,128,512]{2,1,0:T(8,128)(2,1)}, bf16[8,128,512]{2,1,0:T(8,128)(2,1)S(1)}, u32[]{:S(2)}) copy-start(bf16[8,128,512]{2,1,0:T(8,128)(2,1)S(1)} %all-to-all-done.refs_8_) | copy-start | bytes 3145732
  39.9 39.0 %collective-permute-start.16 = (bf16[8,128,512]{2,1,0:T(8,128)(2,1)S(1)}, bf16[8,128,512]{2,1,0:T(8,128)(2,1)}, u32[]{:S(2)}, u32[]{:S(2)}) collective-permute-start(bf16[8,128,512]{2,1,0:T(8,128)(2,1)S(1)} %all-to-all-done.refs_8_), channel_id=1, source_target_pairs={{0,3},{1,0},{2,1},{3,2},{4,7},{5,4},{6,5},{7,6},{8,11},{9,8},{10,9... | collective-permute-start | bytes 3145736 | tf_op jit(solution)/shard_map/ppermute | solution.py:359
  44.0 23.0 %collective-permute-start.10 = (bf16[64,4096]{1,0:T(8,128)(2,1)S(1)}, bf16[64,4096]{1,0:T(8,128)(2,1)S(1)}, u32[]{:S(2)}, u32[]{:S(2)}) collective-permute-start(bf16[64,4096]{1,0:T(8,128)(2,1)S(1)} %slice.89), channel_id=1, source_target_pairs={{0,192},{32,224},{64,0},{96,32},{128,64},{160,96},{192,128},{224,1... | collective-permute-start | bytes 1572872 | tf_op jit(solution)/shard_map/ppermute | solution.py:376
  45.2 34.6 %copy-start.4 = (s32[1,32]{1,0:T(1,128)S(1)}, s32[1,32]{1,0:T(1,128)}, u32[]{:S(2)}) copy-start(s32[1,32]{1,0:T(1,128)} %param.13) | copy-start | bytes 388
  48.7 8.7 %collective-permute-start = (bf16[128,768]{1,0:T(8,128)(2,1)}, bf16[128,768]{1,0:T(8,128)(2,1)S(1)}, u32[]{:S(2)}, u32[]{:S(2)}) collective-permute-start(bf16[128,768]{1,0:T(8,128)(2,1)} %get-tuple-element.23), channel_id=1, source_target_pairs={{0,64},{32,96},{64,128},{96,160},{128,192},{160,224},{192,0},{224,... | collective-permute-start | bytes 589832 | tf_op jit(solution)/shard_map/ppermute | solution.py:376
  50.2 12.0 %collective-permute-start.1 = (bf16[128,768]{1,0:T(8,128)(2,1)}, bf16[128,768]{1,0:T(8,128)(2,1)S(1)}, u32[]{:S(2)}, u32[]{:S(2)}) collective-permute-start(bf16[128,768]{1,0:T(8,128)(2,1)} %get-tuple-element.24), channel_id=1, source_target_pairs={{0,192},{32,224},{64,0},{96,32},{128,64},{160,96},{192,128},{224,1... | collective-permute-start | bytes 589832 | tf_op jit(solution)/shard_map/ppermute | solution.py:376
  51.5 15.5 %collective-permute-start.2 = (bf16[128,768]{1,0:T(8,128)(2,1)}, bf16[128,768]{1,0:T(8,128)(2,1)S(1)}, u32[]{:S(2)}, u32[]{:S(2)}) collective-permute-start(bf16[128,768]{1,0:T(8,128)(2,1)} %get-tuple-element.25), channel_id=1, source_target_pairs={{0,128},{32,160},{64,192},{96,224},{128,0},{160,32},{192,64},{224,... | collective-permute-start | bytes 589832 | tf_op jit(solution)/shard_map/ppermute | solution.py:376
  57.4 23.3 %copy-start.5 = (bf16[128,768]{1,0:T(8,128)(2,1)}, bf16[128,768]{1,0:T(8,128)(2,1)S(1)}, u32[]{:S(2)}) copy-start(bf16[128,768]{1,0:T(8,128)(2,1)S(1)} %collective-permute-done.refs_1_) | copy-start | bytes 589828
  57.5 12.3 %collective-permute-start.3 = (bf16[128,768]{1,0:T(8,128)(2,1)}, bf16[128,768]{1,0:T(8,128)(2,1)S(1)}, u32[]{:S(2)}, u32[]{:S(2)}) collective-permute-start(bf16[128,768]{1,0:T(8,128)(2,1)} %get-tuple-element.26), channel_id=1, source_target_pairs={{0,32},{32,0},{64,96},{96,64},{128,160},{160,128},{192,224},{224,1... | collective-permute-start | bytes 589832 | tf_op jit(solution)/shard_map/ppermute | solution.py:376
  62.2 18.6 %copy-start.6 = (bf16[128,768]{1,0:T(8,128)(2,1)}, bf16[128,768]{1,0:T(8,128)(2,1)S(1)}, u32[]{:S(2)}) copy-start(bf16[128,768]{1,0:T(8,128)(2,1)S(1)} %collective-permute-done.1.refs_2_) | copy-start | bytes 589828
  62.2 7.8 %collective-permute-start.4 = (bf16[128,768]{1,0:T(8,128)(2,1)}, bf16[128,768]{1,0:T(8,128)(2,1)S(1)}, u32[]{:S(2)}, u32[]{:S(2)}) collective-permute-start(bf16[128,768]{1,0:T(8,128)(2,1)} %get-tuple-element.27), channel_id=1, source_target_pairs={{0,96},{32,64},{64,160},{96,128},{128,224},{160,192},{192,32},{224... | collective-permute-start | bytes 589832 | tf_op jit(solution)/shard_map/ppermute | solution.py:376
  67.0 13.7 %copy-start.7 = (bf16[128,768]{1,0:T(8,128)(2,1)}, bf16[128,768]{1,0:T(8,128)(2,1)S(1)}, u32[]{:S(2)}) copy-start(bf16[128,768]{1,0:T(8,128)(2,1)S(1)} %collective-permute-done.2.refs_3_) | copy-start | bytes 589828
  67.0 8.1 %collective-permute-start.5 = (bf16[128,768]{1,0:T(8,128)(2,1)}, bf16[128,768]{1,0:T(8,128)(2,1)S(1)}, u32[]{:S(2)}, u32[]{:S(2)}) collective-permute-start(bf16[128,768]{1,0:T(8,128)(2,1)} %get-tuple-element.28), channel_id=1, source_target_pairs={{0,224},{32,192},{64,32},{96,0},{128,96},{160,64},{192,160},{224,1... | collective-permute-start | bytes 589832 | tf_op jit(solution)/shard_map/ppermute | solution.py:376
  67.1 9.4 %collective-permute-start.6 = (bf16[128,768]{1,0:T(8,128)(2,1)}, bf16[128,768]{1,0:T(8,128)(2,1)S(1)}, u32[]{:S(2)}, u32[]{:S(2)}) collective-permute-start(bf16[128,768]{1,0:T(8,128)(2,1)} %get-tuple-element.29), channel_id=1, source_target_pairs={{0,160},{32,128},{64,224},{96,192},{128,32},{160,0},{192,96},{224,... | collective-permute-start | bytes 589832 | tf_op jit(solution)/shard_map/ppermute | solution.py:376
  69.8 11.0 %copy-start.8 = (bf16[128,768]{1,0:T(8,128)(2,1)}, bf16[128,768]{1,0:T(8,128)(2,1)S(1)}, u32[]{:S(2)}) copy-start(bf16[128,768]{1,0:T(8,128)(2,1)S(1)} %collective-permute-done.3.refs_4_) | copy-start | bytes 589828
  69.8 26.0 %collective-permute-start.15 = (bf16[8,128,512]{2,1,0:T(8,128)(2,1)S(1)}, bf16[8,128,512]{2,1,0:T(8,128)(2,1)}, u32[]{:S(2)}, u32[]{:S(2)}) collective-permute-start(bf16[8,128,512]{2,1,0:T(8,128)(2,1)S(1)} %all-to-all-done.refs_8_), channel_id=1, source_target_pairs={{0,1},{1,2},{2,3},{3,0},{4,5},{5,6},{6,7},{7,4},{8,9},{9,10},{10,1... | collective-permute-start | bytes 3145736 | tf_op jit(solution)/shard_map/ppermute | solution.py:359
  70.0 10.8 %copy-start.9 = (bf16[128,768]{1,0:T(8,128)(2,1)}, bf16[128,768]{1,0:T(8,128)(2,1)S(1)}, u32[]{:S(2)}) copy-start(bf16[128,768]{1,0:T(8,128)(2,1)S(1)} %collective-permute-done.4.refs_5_) | copy-start | bytes 589828
  70.0 26.9 %collective-permute-start.11 = (bf16[128,4096]{1,0:T(8,128)(2,1)}, bf16[128,4096]{1,0:T(8,128)(2,1)}, u32[]{:S(2)}, u32[]{:S(2)}) collective-permute-start(bf16[128,4096]{1,0:T(8,128)(2,1)} %bitcast.2.refs_0_), channel_id=1, source_target_pairs={{0,32},{32,0},{64,96},{96,64},{128,160},{160,128},{192,224},{224,1... | collective-permute-start | bytes 3145736 | tf_op jit(solution)/shard_map/ppermute | solution.py:376
  75.1 5.6 %copy-start.10 = (bf16[128,768]{1,0:T(8,128)(2,1)}, bf16[128,768]{1,0:T(8,128)(2,1)S(1)}, u32[]{:S(2)}) copy-start(bf16[128,768]{1,0:T(8,128)(2,1)S(1)} %collective-permute-done.5.refs_6_) | copy-start | bytes 589828
  75.1 23.9 %collective-permute-start.13 = (bf16[128,4096]{1,0:T(8,128)(2,1)}, bf16[128,4096]{1,0:T(8,128)(2,1)}, u32[]{:S(2)}, u32[]{:S(2)}) collective-permute-start(bf16[128,4096]{1,0:T(8,128)(2,1)} %collective-permute-done.8.refs_2_), channel_id=1, source_target_pairs={{0,32},{32,0},{64,96},{96,64},{128,160},{160,128},{192,224},{224,1... | collective-permute-start | bytes 3145736 | tf_op jit(solution)/shard_map/ppermute | solution.py:376
  76.5 4.3 %copy-start.11 = (bf16[128,768]{1,0:T(8,128)(2,1)}, bf16[128,768]{1,0:T(8,128)(2,1)S(1)}, u32[]{:S(2)}) copy-start(bf16[128,768]{1,0:T(8,128)(2,1)S(1)} %collective-permute-done.6.refs_7_) | copy-start | bytes 589828
  76.5 22.6 %collective-permute-start.12 = (bf16[128,4096]{1,0:T(8,128)(2,1)}, bf16[128,4096]{1,0:T(8,128)(2,1)}, u32[]{:S(2)}, u32[]{:S(2)}) collective-permute-start(bf16[128,4096]{1,0:T(8,128)(2,1)} %collective-permute-done.7.refs_1_), channel_id=1, source_target_pairs={{0,32},{32,0},{64,96},{96,64},{128,160},{160,128},{192,224},{224,1... | collective-permute-start | bytes 3145736 | tf_op jit(solution)/shard_map/ppermute | solution.py:376
  79.0 20.1 %collective-permute-start.14 = (bf16[128,4096]{1,0:T(8,128)(2,1)}, bf16[128,4096]{1,0:T(8,128)(2,1)}, u32[]{:S(2)}, u32[]{:S(2)}) collective-permute-start(bf16[128,4096]{1,0:T(8,128)(2,1)} %constant_dynamic-update-slice_fusion.refs_3_), channel_id=1, source_target_pairs={{0,32},{32,0},{64,96},{96,64},{128,160},{160,128},{192,224},{224,1... | collective-permute-start | bytes 3145736 | tf_op jit(solution)/shard_map/ppermute | solution.py:376
  95.8 23.3 %collective-permute-start.18 = (bf16[4,128,512]{2,1,0:T(8,128)(2,1)S(1)}, bf16[4,128,512]{2,1,0:T(8,128)(2,1)}, u32[]{:S(2)}, u32[]{:S(2)}) collective-permute-start(bf16[4,128,512]{2,1,0:T(8,128)(2,1)S(1)} %slice.91), channel_id=1, source_target_pairs={{0,3},{1,0},{2,1},{3,2},{4,7},{5,4},{6,5},{7,6},{8,11},{9,8},{10,9... | collective-permute-start | bytes 1572872 | tf_op jit(solution)/shard_map/ppermute | solution.py:359
  96.9 22.2 %collective-permute-start.17 = (bf16[4,128,512]{2,1,0:T(8,128)(2,1)S(1)}, bf16[4,128,512]{2,1,0:T(8,128)(2,1)}, u32[]{:S(2)}, u32[]{:S(2)}) collective-permute-start(bf16[4,128,512]{2,1,0:T(8,128)(2,1)S(1)} %slice.90), channel_id=1, source_target_pairs={{0,1},{1,2},{2,3},{3,0},{4,5},{5,6},{6,7},{7,4},{8,9},{9,10},{10,1... | collective-permute-start | bytes 1572872 | tf_op jit(solution)/shard_map/ppermute | solution.py:359
  110.7 42.4 %all-to-all-start.2 = ((bf16[8,4,128,128]{3,2,1,0:T(8,128)(2,1)}), bf16[8,4,128,128]{3,2,1,0:T(8,128)(2,1)S(1)}, u32[]{:S(2)}, u32[]{:S(2)}) async-start(bf16[8,4,128,128]{3,2,1,0:T(8,128)(2,1)} %get-tuple-element.36), calls=%async_computation.2 | async-start | bytes 2097152 | tf_op jit(solution)/shard_map/all_to_all | solution.py:371
  117.1 12.2 %collective-permute-start.20 = (bf16[4,384,128]{2,1,0:T(8,128)(2,1)}, bf16[4,384,128]{2,1,0:T(8,128)(2,1)}, u32[]{:S(2)}, u32[]{:S(2)}) collective-permute-start(bf16[4,384,128]{2,1,0:T(8,128)(2,1)} %get-tuple-element.56), channel_id=1, source_target_pairs={{0,3},{1,0},{2,1},{3,2},{4,7},{5,4},{6,5},{7,6},{8,11},{9,8},{10,9... | collective-permute-start | bytes 1179656 | tf_op jit(solution)/shard_map/ppermute | solution.py:359
  118.3 12.7 %collective-permute-start.19 = (bf16[4,384,128]{2,1,0:T(8,128)(2,1)S(1)}, bf16[4,384,128]{2,1,0:T(8,128)(2,1)}, u32[]{:S(2)}, u32[]{:S(2)}) collective-permute-start(bf16[4,384,128]{2,1,0:T(8,128)(2,1)S(1)} %get-tuple-element.57), channel_id=1, source_target_pairs={{0,1},{1,2},{2,3},{3,0},{4,5},{5,6},{6,7},{7,4},{8,9},{9,10},{10,1... | collective-permute-start | bytes 1179656 | tf_op jit(solution)/shard_map/ppermute | solution.py:359
  132.7 20.4 %collective-permute-start.21 = (bf16[8,384,128]{2,1,0:T(8,128)(2,1)S(1)}, bf16[8,384,128]{2,1,0:T(8,128)(2,1)}, u32[]{:S(2)}, u32[]{:S(2)}) collective-permute-start(bf16[8,384,128]{2,1,0:T(8,128)(2,1)S(1)} %pad_maximum_fusion), channel_id=1, source_target_pairs={{0,1},{1,2},{2,3},{3,0},{4,5},{5,6},{6,7},{7,4},{8,9},{9,10},{10,1... | collective-permute-start | bytes 2359304 | tf_op jit(solution)/shard_map/ppermute | solution.py:359
  132.9 20.2 %collective-permute-start.22 = (bf16[8,384,128]{2,1,0:T(8,128)(2,1)S(1)}, bf16[8,384,128]{2,1,0:T(8,128)(2,1)S(1)}, u32[]{:S(2)}, u32[]{:S(2)}) collective-permute-start(bf16[8,384,128]{2,1,0:T(8,128)(2,1)S(1)} %pad_maximum_fusion.1), channel_id=1, source_target_pairs={{0,3},{1,0},{2,1},{3,2},{4,7},{5,4},{6,5},{7,6},{8,11},{9,8},{10,9... | collective-permute-start | bytes 2359304 | tf_op jit(solution)/shard_map/ppermute | solution.py:359
  153.9 10.2 %all-to-all-start.3 = ((bf16[4,128,128]{2,1,0:T(8,128)(2,1)}), bf16[4,128,128]{2,1,0:T(8,128)(2,1)S(1)}, u32[]{:S(2)}, u32[]{:S(2)}) async-start(bf16[4,128,128]{2,1,0:T(8,128)(2,1)} %reduce_sum.61), calls=%async_computation.3 | async-start | bytes 262144 | tf_op jit(solution)/shard_map/all_to_all | solution.py:371
  159.9 7.8 %collective-permute-start.23 = (bf16[192,128]{1,0:T(8,128)(2,1)S(1)}, bf16[192,128]{1,0:T(8,128)(2,1)S(1)}, u32[]{:S(2)}, u32[]{:S(2)}) collective-permute-start(bf16[192,128]{1,0:T(8,128)(2,1)S(1)} %get-tuple-element.64), channel_id=1, source_target_pairs={{0,4},{4,8},{8,12},{12,16},{16,20},{20,24},{24,28},{28,0},{1,5},{5... | collective-permute-start | bytes 147464 | tf_op jit(solution)/shard_map/ppermute | solution.py:359
  161.4 6.3 %collective-permute-start.27 = (bf16[192,128]{1,0:T(8,128)(2,1)S(1)}, bf16[192,128]{1,0:T(8,128)(2,1)S(1)}, u32[]{:S(2)}, u32[]{:S(2)}) collective-permute-start(bf16[192,128]{1,0:T(8,128)(2,1)S(1)} %get-tuple-element.65), channel_id=1, source_target_pairs={{0,28},{4,0},{8,4},{12,8},{16,12},{20,16},{24,20},{28,24},{1,29},{... | collective-permute-start | bytes 147464 | tf_op jit(solution)/shard_map/ppermute | solution.py:359
  164.2 23.4 %all-to-all-start.1 = ((bf16[8,128,768]{2,1,0:T(8,128)(2,1)}), bf16[8,128,768]{2,1,0:T(8,128)(2,1)S(1)}, u32[]{:S(2)}, u32[]{:S(2)}) async-start(bf16[8,128,768]{2,1,0:T(8,128)(2,1)} %attend_grad.1), calls=%async_computation.1 | async-start | bytes 3145728 | tf_op jit(solution)/shard_map/all_to_all | solution.py:371
  167.8 6.1 %collective-permute-start.24 = (bf16[384,128]{1,0:T(8,128)(2,1)S(1)}, bf16[384,128]{1,0:T(8,128)(2,1)S(1)}, u32[]{:S(2)}, u32[]{:S(2)}) collective-permute-start(bf16[384,128]{1,0:T(8,128)(2,1)S(1)} %pad_maximum_fusion.2), channel_id=1, source_target_pairs={{0,4},{4,8},{8,12},{12,16},{16,20},{20,24},{24,28},{28,0},{1,5},{5... | collective-permute-start | bytes 294920 | tf_op jit(solution)/shard_map/ppermute | solution.py:359
  169.5 4.7 %collective-permute-start.28 = (bf16[384,128]{1,0:T(8,128)(2,1)S(1)}, bf16[384,128]{1,0:T(8,128)(2,1)S(1)}, u32[]{:S(2)}, u32[]{:S(2)}) collective-permute-start(bf16[384,128]{1,0:T(8,128)(2,1)S(1)} %pad_maximum_fusion.3), channel_id=1, source_target_pairs={{0,28},{4,0},{8,4},{12,8},{16,12},{20,16},{24,20},{28,24},{1,29},{... | collective-permute-start | bytes 294920 | tf_op jit(solution)/shard_map/ppermute | solution.py:359
  173.9 5.9 %collective-permute-start.25 = (bf16[384,128]{1,0:T(8,128)(2,1)S(1)}, bf16[384,128]{1,0:T(8,128)(2,1)S(1)}, u32[]{:S(2)}, u32[]{:S(2)}) collective-permute-start(bf16[384,128]{1,0:T(8,128)(2,1)S(1)} %fusion.6), channel_id=1, source_target_pairs={{0,4},{4,8},{8,12},{12,16},{16,20},{20,24},{24,28},{28,0},{1,5},{5... | collective-permute-start | bytes 294920 | tf_op jit(solution)/shard_map/ppermute | solution.py:359
  179.9 5.1 %collective-permute-start.29 = (bf16[384,128]{1,0:T(8,128)(2,1)S(1)}, bf16[384,128]{1,0:T(8,128)(2,1)S(1)}, u32[]{:S(2)}, u32[]{:S(2)}) collective-permute-start(bf16[384,128]{1,0:T(8,128)(2,1)S(1)} %get-tuple-element.61), channel_id=1, source_target_pairs={{0,28},{4,0},{8,4},{12,8},{16,12},{20,16},{24,20},{28,24},{1,29},{... | collective-permute-start | bytes 294920 | tf_op jit(solution)/shard_map/ppermute | solution.py:359
  180.2 11.2 %collective-permute-start.26 = (bf16[384,128]{1,0:T(8,128)(2,1)S(1)}, bf16[384,128]{1,0:T(8,128)(2,1)S(1)}, u32[]{:S(2)}, u32[]{:S(2)}) collective-permute-start(bf16[384,128]{1,0:T(8,128)(2,1)S(1)} %get-tuple-element.60), channel_id=1, source_target_pairs={{0,4},{4,8},{8,12},{12,16},{16,20},{20,24},{24,28},{28,0},{1,5},{5... | collective-permute-start | bytes 294920 | tf_op jit(solution)/shard_map/ppermute | solution.py:359
  185.1 6.3 %collective-permute-start.30 = (bf16[384,128]{1,0:T(8,128)(2,1)S(1)}, bf16[384,128]{1,0:T(8,128)(2,1)S(1)}, u32[]{:S(2)}, u32[]{:S(2)}) collective-permute-start(bf16[384,128]{1,0:T(8,128)(2,1)S(1)} %fusion.5), channel_id=1, source_target_pairs={{0,28},{4,0},{8,4},{12,8},{16,12},{20,16},{24,20},{28,24},{1,29},{... | collective-permute-start | bytes 294920 | tf_op jit(solution)/shard_map/ppermute | solution.py:359
  187.5 1.2 copy-start

commit v2 on v1

--- a/solution.py
+++ b/solution.py
@@ -64,9 +64,10 @@
 
 
 def bwd_kernel(ids_ref, *refs):
-    pieces, refs = refs[:-9], refs[-9:]
-    u_ref, lo_ref, hi_ref, o_ref, dk_ref, dv_ref, q_ref, k_ref, v_ref = refs
-    blocks = len(pieces)
+    blocks = (len(refs) - 9) // 2
+    pieces, (u_ref, lo_ref, hi_ref) = refs[:blocks], refs[blocks : blocks + 3]
+    homes, scratch = refs[blocks + 3 : -6], refs[-6:]
+    o_ref, dk_ref, dv_ref, q_ref, k_ref, v_ref = scratch
     i = pl.program_id(0)
 
     @pl.when(i == 0)
@@ -101,11 +102,12 @@
 
     @pl.when(i == blocks - 1)
     def _():
-        for b in range(blocks):
-            o_ref[b, :, HEADS * HEAD : (HEADS + 1) * HEAD] = dk_ref[
-                b * TOK : (b + 1) * TOK, :
-            ].astype(BF16)
-            o_ref[b, :, (HEADS + 1) * HEAD :] = dv_ref[b * TOK : (b + 1) * TOK, :].astype(BF16)
+        for p, home in enumerate(homes):
+            b = ids_ref[blocks + 2 + p]
+            rows = pl.ds(pl.multiple_of(b * TOK, TOK), TOK)
+            home[:, : HEADS * HEAD] = o_ref[b]
+            home[:, HEADS * HEAD : (HEADS + 1) * HEAD] = dk_ref[rows, :].astype(BF16)
+            home[:, (HEADS + 1) * HEAD :] = dv_ref[rows, :].astype(BF16)
 
 
 def whole(shape):
@@ -155,17 +157,19 @@
 def attend_grad(ids, pieces, u, lo, hi):
     blocks = len(pieces)
     pairs = blocks * TOK * KW * HEADS
-    shape = (blocks, *pieces[0].shape)
+    shape = pieces[0].shape
     return pl.pallas_call(
         bwd_kernel,
         grid_spec=pltpu.PrefetchScalarGridSpec(
             num_scalar_prefetch=1,
             grid=(blocks,),
             in_specs=[whole(x.shape) for x in (*pieces, u, lo, hi)],
-            out_specs=whole(shape),
-            scratch_shapes=[pltpu.VMEM((blocks * TOK, HEAD), F32)] * 2 + head_scratch(blocks),
-        ),
-        out_shape=jax.ShapeDtypeStruct(shape, BF16),
+            out_specs=[whole(shape)] * blocks,
+            scratch_shapes=[pltpu.VMEM((blocks, TOK, HEADS * HEAD), BF16)]
+            + [pltpu.VMEM((blocks * TOK, HEAD), F32)] * 2
+            + head_scratch(blocks),
+        ),
+        out_shape=[jax.ShapeDtypeStruct(shape, BF16)] * blocks,
         cost_estimate=pl.CostEstimate(
             flops=10 * pairs * HEAD,
             bytes_accessed=6 * blocks * pieces[0].size,
@@ -173,15 +177,6 @@
         ),
         name="attend_grad",
     )(ids, *pieces, u, lo, hi)
-
-
-def head_parts(g):
-    wide = HEADS * HEAD
-    return (
-        (slice(0, wide), slice(g * wide, (g + 1) * wide)),
-        (slice(wide, wide + HEAD), slice(g * HEAD, (g + 1) * HEAD)),
-        (slice(wide + HEAD, wide + 2 * HEAD), slice(g * HEAD, (g + 1) * HEAD)),
-    )
 
 
 def pack_kernel(ids_ref, q_ref, k_ref, v_ref, *o_refs):
@@ -211,23 +206,34 @@
     )(ids, q, k, v)
 
 
-def unpack_kernel(i_ref, q_ref, k_ref, v_ref):
-    for g in range(i_ref.shape[0]):
-        for ref, (inner, outer) in zip((q_ref, k_ref, v_ref), head_parts(g)):
-            ref[0, :, outer] = i_ref[g, :, inner]
-
-
-def unpack(packed):
-    groups = packed.shape[0]
+def unpack_kernel(ids_ref, *refs):
+    wide = HEADS * HEAD
+    pieces, (q_ref, k_ref, v_ref) = refs[:-3], refs[-3:]
+    for p, piece in enumerate(pieces):
+        g = ids_ref[p]
+        heads = pl.ds(pl.multiple_of(g * HEAD, HEAD), HEAD)
+        q_ref[0, :, pl.ds(pl.multiple_of(g * wide, wide), wide)] = piece[:, :wide]
+        k_ref[0, :, heads] = piece[:, wide : wide + HEAD]
+        v_ref[0, :, heads] = piece[:, wide + HEAD :]
+
+
+def unpack(ids, pieces):
+    groups = len(pieces)
+    shapes = [(1, TOK, groups * part) for part in (HEADS * HEAD, HEAD, HEAD)]
     return pl.pallas_call(
         unpack_kernel,
-        out_shape=[
-            jax.ShapeDtypeStruct((1, TOK, groups * part), BF16)
-            for part in (HEADS * HEAD, HEAD, HEAD)
-        ],
-        cost_estimate=pl.CostEstimate(flops=0, bytes_accessed=4 * packed.size, transcendentals=0),
+        grid_spec=pltpu.PrefetchScalarGridSpec(
+            num_scalar_prefetch=1,
+            grid=(1,),
+            in_specs=[whole(x.shape) for x in pieces],
+            out_specs=[whole(shape) for shape in shapes],
+        ),
+        out_shape=[jax.ShapeDtypeStruct(shape, BF16) for shape in shapes],
+        cost_estimate=pl.CostEstimate(
+            flops=0, bytes_accessed=4 * groups * pieces[0].size, transcendentals=0
+        ),
         name="unpack",
-    )(packed)
+    )(ids, *pieces)
 
 
 def upstream_kernel(ids_ref, *refs):
@@ -304,30 +310,50 @@
 
 
 def proj_kernel(ids_ref, *refs):
-    pieces, (ot_ref, a_ref, b_ref, lhs_ref) = refs[:-4], refs[-4:]
+    pieces, refs = refs[:-8], refs[-8:]
+    ot_ref, same_ref, next_ref, low_ref, high_ref, last_ref, lhs_ref, out_ref = refs
     count = len(pieces)
-    near = a_ref.shape[0]
-    split = a_ref.shape[2]
-
-    @pl.when(pl.program_id(0) == 0)
+    near = GRID["fsdp"]
+    step = pl.program_id(0)
+    middle = pl.num_programs(0) // 2
+
+    @pl.when(step == 0)
     def _():
         for p in range(count):
             lhs_ref[:, p * TOK : (p + 1) * TOK] = ot_ref[ids_ref[p]]
 
     rows = jnp.concatenate([piece[...] for piece in pieces], 0)
-    out = jnp.dot(lhs_ref[...], rows, preferred_element_type=F32).astype(BF16)
-    for t in range(near):
-        part = out[:, t * TOK : (t + 1) * TOK]
-        a_ref[lax.rem(t + near - ids_ref[count + 1], near), 0] = part[:split]
-        b_ref[0, t] = part[split:]
+    out_ref[...] = jnp.dot(lhs_ref[...], rows, preferred_element_type=F32).astype(BF16)
+
+    def part(offset):
+        t = lax.rem(ids_ref[count + 1] + offset, near)
+        return out_ref[:, pl.ds(pl.multiple_of(t * TOK, TOK), TOK)]
+
+    same_ref[0] = part(0)
+    next_ref[0] = part(1)
+    last_ref[0] = part(3)
+
+    @pl.when(step < middle)
+    def _():
+        low_ref[0] = part(2)
+
+    @pl.when(step >= middle)
+    def _():
+        high_ref[0] = part(2)
 
 
 def proj_terms(ids, pieces, ot):
     count, width, _ = ot.shape
     far, near = GRID["dp"], GRID["fsdp"]
-    split = width * 3 // 4
     depth = pieces[0].shape[1]
-
+    middle = far // 2
+    block = (1, width, TOK)
+
+    def plane(i, ids):
+        return (i, 0, 0)
+
+    full = jax.ShapeDtypeStruct((far, width, TOK), BF16)
+    part = jax.ShapeDtypeStruct((middle, width, TOK), BF16)
     return pl.pallas_call(
         proj_kernel,
         grid_spec=pltpu.PrefetchScalarGridSpec(
@@ -336,15 +362,18 @@
             in_specs=[pl.BlockSpec((TOK, near * TOK), lambda i, ids: (0, i))] * count
             + [pl.BlockSpec(ot.shape, lambda i, ids: (0, 0, 0))],
             out_specs=[
-                pl.BlockSpec((near, 1, split, TOK), lambda i, ids: (0, lax.rem(i + far - ids[count], far), 0, 0)),
-                pl.BlockSpec((1, near, width - split, TOK), lambda i, ids: (i, 0, 0, 0)),
+                pl.BlockSpec(block, plane),
+                pl.BlockSpec(block, plane),
+                pl.BlockSpec(block, lambda i, ids: (jnp.minimum(i, middle - 1), 0, 0)),
+                pl.BlockSpec(block, lambda i, ids: (jnp.maximum(i - middle, 0), 0, 0)),
+                pl.BlockSpec(block, plane),
             ],
-            scratch_shapes=[pltpu.VMEM((width, count * TOK), BF16)],
-        ),
-        out_shape=[
-            jax.ShapeDtypeStruct((near, far, split, TOK), BF16),
-            jax.ShapeDtypeStruct((far, near, width - split, TOK), BF16),
-        ],
+            scratch_shapes=[
+                pltpu.VMEM((width, count * TOK), BF16),
+                pltpu.VMEM((width, near * TOK), BF16),
+            ],
+        ),
+        out_shape=[full, full, part, part, full],
         cost_estimate=pl.CostEstimate(
             flops=2 * count * TOK * width * depth,
             bytes_accessed=2 * (count * TOK * (depth + width) + depth * width),
@@ -352,6 +381,40 @@
         ),
         name="proj_terms",
     )(ids, *pieces, ot)
+
+
+def join_kernel(low_ref, up_ref, high_ref, down_ref, low_out, high_out):
+    low_out[...] = add(low_ref[...], up_ref[...])
+    high_out[...] = add(high_ref[...], down_ref[...])
+
+
+def join(low, up, high, down):
+    planes, width, _ = up.shape
+    block = (planes // 2, width, TOK)
+
+    def front(i):
+        return (i, 0, 0)
+
+    def back(i):
+        return (i + 2, 0, 0)
+
+    return pl.pallas_call(
+        join_kernel,
+        grid=(2,),
+        in_specs=[
+            pl.BlockSpec(block, front),
+            pl.BlockSpec(block, front),
+            pl.BlockSpec(block, back),
+            pl.BlockSpec(block, front),
+        ],
+        out_specs=[pl.BlockSpec(block, front), pl.BlockSpec(block, back)],
+        out_shape=[jax.ShapeDtypeStruct(low.shape, BF16)] * 2,
+        input_output_aliases={0: 0, 2: 1},
+        cost_estimate=pl.CostEstimate(
+            flops=2 * up.size, bytes_accessed=12 * up.size, transcendentals=0
+        ),
+        name="join",
+    )(low, up, high, down)
 
 
 def shift(x, axis, by):
@@ -408,33 +471,21 @@
     output = attend(ids, packed, lo, hi)
     pieces = [own, left, right, across, partner]
     pieces += [hop(piece, 0, 1) for piece in (left, right, across)]
+    same, following, low, high, before = proj_terms(ids, pieces, output)
+    up, down = shift(low, "fsdp", 1), shift(high, "fsdp", -1)
+    below, above = after((below, above), low)
     ends = [shift(below[:far], "fsdp", 1), shift(above[far:], "fsdp", -1)]
-    first, second = proj_terms(ids, pieces, output)
-    second = swap(second, "dp")
-    up, down = shift(first[2, :far], "fsdp", 1), shift(first[2, far:], "fsdp", -1)
+    following, before = join(following, up, before, down)
+    up, down = shift(following, "fsdp", 1), shift(before, "fsdp", -1)
     arriving = upstream(ids, pieces, [weight, below, above, *ends])
-    up, down = after((up, down), arriving)
-    up = shift(jnp.concatenate([add(first[1, :far], up), first[1, far:]], 0), "fsdp", 1)
-    down = shift(jnp.concatenate([first[3, :far], add(first[3, far:], down)], 0), "fsdp", -1)
-    grads = attend_grad(ids, packed, arriving, lo, hi)
-    grads_home = swap(grads, "seq")
-    up, down, second = after((up, down, second), grads)
-    first = (first[0].astype(F32) + up.astype(F32) + down.astype(F32)).astype(BF16)
-    part = first.shape[1] // 2
-    up, down = shift(first[4, :part], "dp", 1), shift(first[4, part:], "dp", -1)
-    up = jnp.concatenate([add(first[3, :part], up), first[3, part:]], 0)
-    down = jnp.concatenate([first[5, :part], add(first[5, part:], down)], 0)
-    up, down = shift(up, "dp", 1), shift(down, "dp", -1)
-    up, down = add(first[2], up), add(first[6], down)
-    up, down = shift(up, "dp", 1), shift(down, "dp", -1)
-    up, down = add(first[1], up), add(first[7], down)
-    up, down = shift(up, "dp", 1), shift(down, "dp", -1)
-    second = jnp.sum(second.astype(F32), axis=0).astype(BF16)
-    second = swap(second, "fsdp")
-    first = first[0].astype(F32) + up.astype(F32) + down.astype(F32)
-    proj_grad = jnp.concatenate([first, jnp.sum(second.astype(F32), axis=0)], 0)
-    query_grad, key_gradient, value_gradient = unpack(grads_home)
-    return (query_grad, key_gradient, value_gradient, proj_grad.T.astype(BF16))
+    grads = attend_grad(jnp.concatenate([ids, targets]), packed, arriving, lo, hi)
+    up, down = after((up, down), grads[0])
+    first = (same.astype(F32) + up.astype(F32) + down.astype(F32)).astype(BF16)
+    first = swap(first, "dp")
+    grads = [grads[0]] + [hop(x, *path) for x, path in zip(grads[1:], paths[1:])]
+    proj_grad = jnp.sum(first.astype(F32), axis=0).T.astype(BF16)
+    query_grad, key_gradient, value_gradient = unpack(ids, grads)
+    return (query_grad, key_gradient, value_gradient, proj_grad)
 
 
 def solution(mesh):

time: 195 us -> 192 us (0.985)
  Pallas kernels: 49.2 us -> 53.3 us
  starting transfers between devices: 57.8 us -> 54.1 us
  other arithmetic: 6.54 us -> 3.68 us
    ppermute x15 -> x22, waiting for transfers between devices: 39.7 us -> 51.9 us  [hop(): return lax.ppermute(x, 'seq', pairs)]
    ppermute x16 -> x8, waiting for transfers between devices: 22.6 us -> 12.5 us  [shift(): return lax.ppermute(x, axis, [(i, (i + by) % n) for i in range(n)])]
    ppermute x15 -> x22, starting transfers between devices: 16.1 us -> 22.9 us  [hop(): return lax.ppermute(x, 'seq', pairs)]
    ppermute x16 -> x8, starting transfers between devices: 21.1 us -> 14.4 us  [shift(): return lax.ppermute(x, axis, [(i, (i + by) % n) for i in range(n)])]
    all_to_all x4 -> x2, starting transfers between devices: 20.5 us -> 16.7 us  [swap(): return lax.all_to_all(x, axis, split_axis=0, concat_axis=0, tiled=True)]
    pallas_call x1 -> x2, Pallas kernels: 2.66 us -> 5.85 us  [the longest x1 3.44 us: unpack(): pl.pallas_call(unpack_kernel, grid_spec=pltpu.PrefetchScalarGridSpec(num_...]
    squeeze x2 -> x0, local copies, waits for them, and re-layouts: 2.26 us -> none  [the longest x1 2.24 us: per_device(): first[3, :far]]
    convert_element_type x7 -> x1, other arithmetic: 3.39 us -> 1.38 us  [per_device(): first = (same.astype(F32) + up.astype(F32) + down.astype(F32)).astype(BF16)]
  transfers between devices with their start and end apart: 35 -> 32, of which waited for: 15 -> 16; matrix products, arithmetic and copies ran while one was open for 7% -> 5% of each run, Pallas kernels for 26% -> 28%
where the time goes in v2:
time: 192 us; the launch traced here: 190 us
  waiting for transfers between devices  67.3 us (35%)
  starting transfers between devices  54.1 us (28%)
  Pallas kernels  53.3 us (28%)
  local copies, waits for them, and re-layouts  10.3 us (5%)
  other arithmetic  3.68 us (2%)
    ppermute x22, waiting for transfers between devices, hop(): return lax.ppermute(x, 'seq', pairs)  51.9 us
    ppermute x22, starting transfers between devices, hop(): return lax.ppermute(x, 'seq', pairs)  22.9 us
    all_to_all x2, starting transfers between devices, swap(): return lax.all_to_all(x, axis, split_axis=0, concat_axis=0, tiled=True)  16.7 us
    ppermute x8, starting transfers between devices, shift(): return lax.ppermute(x, axis, [(i, (i + by) % n) for i in range(n)])  14.4 us
    pallas_call x1, Pallas kernels, attend_grad(): pl.pallas_call(bwd_kernel, grid_spec=pltpu.PrefetchScalarGridSpec(num_sca...  13.3 us
    ppermute x8, waiting for transfers between devices, shift(): return lax.ppermute(x, axis, [(i, (i + by) % n) for i in range(n)])  12.5 us
    pallas_call x1, Pallas kernels, proj_terms(): pl.pallas_call(proj_kernel, grid_spec=pltpu.PrefetchScalarGridSpec(num_sc...  12.4 us
    pallas_call x1, Pallas kernels, upstream(): pl.pallas_call(upstream_kernel, grid_spec=pltpu.PrefetchScalarGridSpec(nu...  10.1 us
  transfers between devices with their start and end apart: 32, of which 16 were waited for; matrix products, arithmetic and copies ran while one was open for 5% of the time, Pallas kernels for 28%

profile of v2, /device:TPU:2, one launch (start us, length us, event | category | flops | bytes accessed | tf_op | source)
XLA Modules:
  0.0 189.6 jit_solution(279980328205058349)
XLA Ops:
  0.6 1.6 collective-permute-start.7
  2.2 0.8 collective-permute-start.8
  3.0 2.0 %broadcast_in_dim.41 = bf16[8,128,512]{2,1,0:T(8,128)(2,1)} broadcast(bf16[128,512]{1,0:T(8,128)(2,1)} %param.12), dimensions={1,2} | broadcast | bytes 1179648 | tf_op jit(solution)/shard_map/broadcast_in_dim | solution.py:461
  5.0 8.2 %all-to-all-start = ((bf16[8,128,512]{2,1,0:T(8,128)(2,1)}), bf16[8,128,512]{2,1,0:T(8,128)(2,1)S(1)}, u32[]{:S(2)}, u32[]{:S(2)}) async-start(bf16[8,128,512]{2,1,0:T(8,128)(2,1)} %broadcast_in_dim.41), calls=%async_computation | async-start | bytes 2097152 | tf_op jit(solution)/shard_map/all_to_all | solution.py:434
  13.2 12.7 %collective-permute-done.7.refs_1_ = bf16[128,4096]{1,0:T(8,128)(2,1)} collective-permute-done((bf16[128,4096]{1,0:T(8,128)(2,1)}, bf16[128,4096]{1,0:T(8,128)(2,1)}, u32[]{:S(2)}, u32[]{:S(2)}) %collective-permute-start.7) | collective-permute-done | bytes 1048608 | tf_op jit(solution)/shard_map/ppermute | solution.py:439
  25.9 1.1 slice.16
  27.0 1.6 collective-permute-start.9
  28.6 1.1 slice.17
  29.7 0.6 collective-permute-start.10
  30.3 0.6 pad_add_fusion.1.ids_ref
  30.9 3.3 %pack.1 = (bf16[128,768]{1,0:T(8,128)(2,1)}, bf16[128,768]{1,0:T(8,128)(2,1)}, bf16[128,768]{1,0:T(8,128)(2,1)}, bf16[128,768]{1,0:T(8,128)(2,1)}, bf16[128,768]...) custom-call(s32[8]{0:T(128)} %pad_add_fusion.1.ids_ref, ...), custom_call_target="tpu_custom_call" | custom-call | bytes 3145728 | tf_op jit(solution)/shard_map/pack/pallas_call | solution.py:195
  34.2 1.5 collective-permute-start
  35.7 1.4 collective-permute-start.1
  37.1 4.7 %collective-permute-done.9 = bf16[64,4096]{1,0:T(8,128)(2,1)S(1)} collective-permute-done((bf16[64,4096]{1,0:T(8,128)(2,1)S(1)}, bf16[64,4096]{1,0:T(8,128)(2,1)S(1)}, u32[]{:S(2)}, u32[]{:S(2)}) %collective-permute-start.9) | collective-permute-done | bytes 524320 | tf_op jit(solution)/shard_map/ppermute | solution.py:439
  41.8 2.2 %collective-permute-start.2 = (bf16[128,768]{1,0:T(8,128)(2,1)}, bf16[128,768]{1,0:T(8,128)(2,1)S(1)}, u32[]{:S(2)}, u32[]{:S(2)}) collective-permute-start(bf16[128,768]{1,0:T(8,128)(2,1)} %get-tuple-element.37), channel_id=1, source_target_pairs={{0,128},{32,160},{64,192},{96,224},{128,0},{160,32},{192,64},{224,... | collective-permute-start | bytes 589832 | tf_op jit(solution)/shard_map/ppermute | solution.py:439
  44.0 0.8 constant_dynamic-update-slice_fusion.1
  44.8 0.8 constant_dynamic-update-slice_fusion.refs_3_
  45.7 0.5 collective-permute-start.12
  46.2 2.1 %collective-permute-done.1.refs_2_ = bf16[128,768]{1,0:T(8,128)(2,1)} collective-permute-done((bf16[128,768]{1,0:T(8,128)(2,1)}, bf16[128,768]{1,0:T(8,128)(2,1)}, u32[]{:S(2)}, u32[]{:S(2)}) %collective-permute-start.1) | collective-permute-done | bytes 196640 | tf_op jit(solution)/shard_map/ppermute | solution.py:439
  48.3 3.1 %collective-permute-done.2.refs_3_ = bf16[128,768]{1,0:T(8,128)(2,1)S(1)} collective-permute-done((bf16[128,768]{1,0:T(8,128)(2,1)}, bf16[128,768]{1,0:T(8,128)(2,1)S(1)}, u32[]{:S(2)}, u32[]{:S(2)}) %collective-permute-start.2) | collective-permute-done | bytes 196640 | tf_op jit(solution)/shard_map/ppermute | solution.py:439
  51.6 6.7 %collective-permute-done.4.refs_5_ = bf16[128,768]{1,0:T(8,128)(2,1)S(1)} collective-permute-done((bf16[128,768]{1,0:T(8,128)(2,1)}, bf16[128,768]{1,0:T(8,128)(2,1)S(1)}, u32[]{:S(2)}, u32[]{:S(2)}) %collective-permute-start.4) | collective-permute-done | bytes 196640 | tf_op jit(solution)/shard_map/ppermute | solution.py:439
  58.3 1.2 collective-permute-start.5
  59.6 5.5 %collective-permute-done.5.refs_6_ = bf16[128,768]{1,0:T(8,128)(2,1)S(1)} collective-permute-done((bf16[128,768]{1,0:T(8,128)(2,1)}, bf16[128,768]{1,0:T(8,128)(2,1)S(1)}, u32[]{:S(2)}, u32[]{:S(2)}) %collective-permute-start.5) | collective-permute-done | bytes 196640 | tf_op jit(solution)/shard_map/ppermute | solution.py:439
  65.1 3.6 %collective-permute-start.6 = (bf16[128,768]{1,0:T(8,128)(2,1)S(1)}, bf16[128,768]{1,0:T(8,128)(2,1)S(1)}, u32[]{:S(2)}, u32[]{:S(2)}) collective-permute-start(bf16[128,768]{1,0:T(8,128)(2,1)S(1)} %copy-done.21), channel_id=1, source_target_pairs={{0,160},{32,128},{64,224},{96,192},{128,32},{160,0},{192,96},{224,... | collective-permute-start | bytes 589832 | tf_op jit(solution)/shard_map/ppermute | solution.py:439
  68.7 5.0 %collective-permute-done.6.refs_7_ = bf16[128,768]{1,0:T(8,128)(2,1)S(1)} collective-permute-done((bf16[128,768]{1,0:T(8,128)(2,1)S(1)}, bf16[128,768]{1,0:T(8,128)(2,1)S(1)}, u32[]{:S(2)}, u32[]{:S(2)}) %collective-permute-start.6) | collective-permute-done | bytes 196640 | tf_op jit(solution)/shard_map/ppermute | solution.py:439
  73.7 3.0 %collective-permute-start.15 = (bf16[8,128,512]{2,1,0:T(8,128)(2,1)S(1)}, bf16[8,128,512]{2,1,0:T(8,128)(2,1)S(1)}, u32[]{:S(2)}, u32[]{:S(2)}) collective-permute-start(bf16[8,128,512]{2,1,0:T(8,128)(2,1)S(1)} %all-to-all-done.refs_8_), channel_id=1, source_target_pairs={{0,1},{1,2},{2,3},{3,0},{4,5},{5,6},{6,7},{7,4},{8,9},{9,10},{10,1... | collective-permute-start | bytes 3145736 | tf_op jit(solution)/shard_map/ppermute | solution.py:422
  76.7 1.7 collective-permute-start.16
  78.5 0.7 pad_add_fusion.ids_ref
  79.1 0.7 select_reduce_fusion
  79.8 8.3 %attend.1.refs_8_ = bf16[8,512,128]{2,1,0:T(8,128)(2,1)} custom-call(s32[10]{0:T(128)} %pad_add_fusion.ids_ref, bf16[128,768]{1,0:T(8,128)(2,1)} %get-tuple-element.34.refs_0_, bf16[128,768]{1,0:T(8,128)(2,1)} %copy-done.15, bf16[128,768]{1,0:T(8,128)(2,1)} %collective-permute-done.1.refs_2_, bf16[128,768]{1,0:T(8,128)(2,1)} %copy-done.16, ...), custom_call_target="tpu_custom_call" | custom-call | flops 939524096 | bytes 3145728 | tf_op jit(solution)/shard_map/attend/pallas_call | solution.py:138
  88.2 12.4 %proj_terms.1 = (bf16[8,512,128]{2,1,0:T(8,128)(2,1)}, bf16[8,512,128]{2,1,0:T(8,128)(2,1)}, bf16[4,512,128]{2,1,0:T(8,128)(2,1)}, bf16[4,512,128]{2,1,0:T(8,128)(2,1)}, bf16[8,512,128]{2,1,0:T(8,128)(2,1)}) custom-call(s32[10]{0:T(128)} %pad_add_fusion.ids_ref, bf16[128,4096]{1,0:T(8,128)(2,1)} %bitcast.17, ...), custom_call_target="tpu_custom_call" | custom-call | flops 4294967296 | bytes 13631488 | tf_op jit(solution)/shard_map/proj_terms/pallas_call | solution.py:357
  100.5 0.4 collective-permute-start.26
  100.9 2.9 %collective-permute-start.27 = (bf16[4,512,128]{2,1,0:T(8,128)(2,1)}, bf16[4,512,128]{2,1,0:T(8,128)(2,1)S(1)}, u32[]{:S(2)}, u32[]{:S(2)}) collective-permute-start(bf16[4,512,128]{2,1,0:T(8,128)(2,1)} %get-tuple-element.59), channel_id=1, source_target_pairs={{0,3},{1,0},{2,1},{3,2},{4,7},{5,4},{6,5},{7,6},{8,11},{9,8},{10,9... | collective-permute-start | bytes 1572872 | tf_op jit(solution)/shard_map/ppermute | solution.py:422
  104.0 1.3 slice.15
  105.3 3.1 %collective-permute-start.18 = (bf16[4,128,512]{2,1,0:T(8,128)(2,1)S(1)}, bf16[4,128,512]{2,1,0:T(8,128)(2,1)}, u32[]{:S(2)}, u32[]{:S(2)}) collective-permute-start(bf16[4,128,512]{2,1,0:T(8,128)(2,1)S(1)} %slice.15), channel_id=1, source_target_pairs={{0,3},{1,0},{2,1},{3,2},{4,7},{5,4},{6,5},{7,6},{8,11},{9,8},{10,9... | collective-permute-start | bytes 1572872 | tf_op jit(solution)/shard_map/ppermute | solution.py:422
  108.4 8.4 %collective-permute-done.26.up_ref = bf16[4,512,128]{2,1,0:T(8,128)(2,1)S(1)} collective-permute-done((bf16[4,512,128]{2,1,0:T(8,128)(2,1)}, bf16[4,512,128]{2,1,0:T(8,128)(2,1)S(1)}, u32[]{:S(2)}, u32[]{:S(2)}) %collective-permute-start.26) | collective-permute-done | bytes 524320 | tf_op jit(solution)/shard_map/ppermute | solution.py:422
  116.8 0.8 copy-done.2
  117.6 0.2 copy-done.3
  117.8 2.4 %join.1 = (bf16[8,512,128]{2,1,0:T(8,128)(2,1)}, bf16[8,512,128]{2,1,0:T(8,128)(2,1)}) custom-call(bf16[8,512,128]{2,1,0:T(8,128)(2,1)} %get-tuple-element.57.low_ref, bf16[4,512,128]{2,1,0:T(8,128)(2,1)} %copy-done.2, bf16[8,512,128]{2,1,0:T(8,128)(2,1)} %get-tuple-element.58.high_ref, ...), custom_call_target="tpu_custom_call", output_to_operand_aliasing={{0}: (0, {}), {1}: (2, {})} | custom-call | flops 524288 | bytes 3145728 | tf_op jit(solution)/shard_map/join/pallas_call | solution.py:401
  120.2 0.5 collective-permute-start.28
  120.7 2.7 %collective-permute-start.29 = (bf16[8,512,128]{2,1,0:T(8,128)(2,1)}, bf16[8,512,128]{2,1,0:T(8,128)(2,1)S(1)}, u32[]{:S(2)}, u32[]{:S(2)}) collective-permute-start(bf16[8,512,128]{2,1,0:T(8,128)(2,1)} %get-tuple-element.61), channel_id=1, source_target_pairs={{0,3},{1,0},{2,1},{3,2},{4,7},{5,4},{6,5},{7,6},{8,11},{9,8},{10,9... | collective-permute-start | bytes 3145736 | tf_op jit(solution)/shard_map/ppermute | solution.py:422
  123.4 0.7 concatenate.14.ids_ref
  124.1 4.1 %collective-permute-done.17.refs_11_ = bf16[4,128,512]{2,1,0:T(8,128)(2,1)} collective-permute-done((bf16[4,128,512]{2,1,0:T(8,128)(2,1)S(1)}, bf16[4,128,512]{2,1,0:T(8,128)(2,1)}, u32[]{:S(2)}, u32[]{:S(2)}) %collective-permute-start.17) | collective-permute-done | bytes 524320 | tf_op jit(solution)/shard_map/ppermute | solution.py:422
  128.2 10.1 %upstream.1.refs_8_ = bf16[8,128,512]{2,1,0:T(8,128)(2,1)} custom-call(s32[10]{0:T(128)} %pad_add_fusion.ids_ref, bf16[128,4096]{1,0:T(8,128)(2,1)} %bitcast.18, bf16[128,4096]{1,0:T(8,128)(2,1)} %collective-permute-done.7.refs_1_, bf16[128,4096]{1,0:T(8,128)(2,1)} %collective-permute-done.8.refs_2_, ...), custom_call_target="tpu_custom_call" | custom-call | flops 4294967296 | bytes 13631488 | tf_op jit(solution)/shard_map/upstream/pallas_call | solution.py:285
  138.3 13.3 %attend_grad.1 = (bf16[128,768]{1,0:T(8,128)(2,1)}, bf16[128,768]{1,0:T(8,128)(2,1)}, bf16[128,768]{1,0:T(8,128)(2,1)}, bf16[128,768]{1,0:T(8,128)(2,1)}, bf16[1...) custom-call(s32[18]{0:T(128)} %concatenate.14.ids_ref, ...), custom_call_target="tpu_custom_call" | custom-call | flops 2348810240 | bytes 4718592 | tf_op jit(solution)/shard_map/attend_grad/pallas_call | solution.py:161
  151.6 1.4 add_convert_fusion
  153.0 8.6 %all-to-all-start.1 = ((bf16[8,512,128]{2,1,0:T(8,128)(2,1)}), bf16[8,512,128]{2,1,0:T(8,128)(2,1)S(1)}, u32[]{:S(2)}, u32[]{:S(2)}) async-start(bf16[8,512,128]{2,1,0:T(8,128)(2,1)} %add_convert_fusion), calls=%async_computation.1 | async-start | bytes 2097152 | tf_op jit(solution)/shard_map/all_to_all | solution.py:434
  161.6 0.5 collective-permute-start.19
  162.2 1.6 collective-permute-start.20
  163.7 3.7 %collective-permute-start.21 = (bf16[128,768]{1,0:T(8,128)(2,1)S(1)}, bf16[128,768]{1,0:T(8,128)(2,1)S(1)}, u32[]{:S(2)}, u32[]{:S(2)}) collective-permute-start(bf16[128,768]{1,0:T(8,128)(2,1)S(1)} %copy-done.26), channel_id=1, source_target_pairs={{0,128},{32,160},{64,192},{96,224},{128,0},{160,32},{192,64},{224,... | collective-permute-start | bytes 589832 | tf_op jit(solution)/shard_map/ppermute | solution.py:439
  167.4 0.9 collective-permute-start.23
  168.4 0.3 collective-permute-done.19.refs_1_
  168.7 0.6 collective-permute-start.24
  169.3 2.3 %collective-permute-done.20.refs_2_ = bf16[128,768]{1,0:T(8,128)(2,1)S(1)} collective-permute-done((bf16[128,768]{1,0:T(8,128)(2,1)S(1)}, bf16[128,768]{1,0:T(8,128)(2,1)S(1)}, u32[]{:S(2)}, u32[]{:S(2)}) %collective-permute-start.20) | collective-permute-done | bytes 196640 | tf_op jit(solution)/shard_map/ppermute | solution.py:439
  171.6 0.4 collective-permute-start.25
  172.1 2.2 %collective-permute-done.21.refs_3_ = bf16[128,768]{1,0:T(8,128)(2,1)S(1)} collective-permute-done((bf16[128,768]{1,0:T(8,128)(2,1)S(1)}, bf16[128,768]{1,0:T(8,128)(2,1)S(1)}, u32[]{:S(2)}, u32[]{:S(2)}) %collective-permute-start.21) | collective-permute-done | bytes 196640 | tf_op jit(solution)/shard_map/ppermute | solution.py:439
  174.2 1.3 collective-permute-done.23.refs_5_
  175.6 2.7 %collective-permute-done.24.refs_6_ = bf16[128,768]{1,0:T(8,128)(2,1)S(1)} collective-permute-done((bf16[128,768]{1,0:T(8,128)(2,1)S(1)}, bf16[128,768]{1,0:T(8,128)(2,1)S(1)}, u32[]{:S(2)}, u32[]{:S(2)}) %collective-permute-start.24) | collective-permute-done | bytes 196640 | tf_op jit(solution)/shard_map/ppermute | solution.py:439
  178.3 3.3 %collective-permute-done.25.refs_7_ = bf16[128,768]{1,0:T(8,128)(2,1)S(1)} collective-permute-done((bf16[128,768]{1,0:T(8,128)(2,1)S(1)}, bf16[128,768]{1,0:T(8,128)(2,1)S(1)}, u32[]{:S(2)}, u32[]{:S(2)}) %collective-permute-start.25) | collective-permute-done | bytes 196640 | tf_op jit(solution)/shard_map/ppermute | solution.py:439
  181.7 0.7 copy-done.11
  182.4 3.4 %unpack.1 = (bf16[1,128,4096]{2,1,0:T(8,128)(2,1)}, bf16[1,128,1024]{2,1,0:T(8,128)(2,1)}, bf16[1,128,1024]{2,1,0:T(8,128)(2,1)}) custom-call(s32[10]{0:T(128)} %pad_add_fusion.ids_ref, bf16[128,768]{1,0:T(8,128)(2,1)} %get-tuple-element.45.refs_0_, bf16[128,768]{1,0:T(8,128)(2,1)} %copy-done.5, bf16[128,768]{1,0:T(8,128)(2,1)} %copy-done.6, ...), custom_call_target="tpu_custom_call" | custom-call | bytes 3145728 | tf_op jit(solution)/shard_map/unpack/pallas_call | solution.py:223
  185.8 2.9 %all-to-all-done.1 = bf16[8,512,128]{2,1,0:T(8,128)(2,1)S(1)} async-done(((bf16[8,512,128]{2,1,0:T(8,128)(2,1)}), bf16[8,512,128]{2,1,0:T(8,128)(2,1)S(1)}, u32[]{:S(2)}, u32[]{:S(2)}) %all-to-all-start.1) | async-done | bytes 1048608 | tf_op jit(solution)/shard_map/all_to_all | solution.py:434
  188.7 0.1 reduce_sum.52
  188.9 0.8 copy.15
  (87 shorter events, 0.6 us)
Async XLA Ops:
  0.6 25.3 %collective-permute-start.7 = (bf16[128,4096]{1,0:T(8,128)(2,1)}, bf16[128,4096]{1,0:T(8,128)(2,1)}, u32[]{:S(2)}, u32[]{:S(2)}) collective-permute-start(bf16[128,4096]{1,0:T(8,128)(2,1)} %bitcast.14), channel_id=1, source_target_pairs={{0,64},{32,96},{64,128},{96,160},{128,192},{160,224},{192,0},{224,... | collective-permute-start | bytes 3145736 | tf_op jit(solution)/shard_map/ppermute | solution.py:439
  2.2 26.4 %collective-permute-start.8 = (bf16[128,4096]{1,0:T(8,128)(2,1)}, bf16[128,4096]{1,0:T(8,128)(2,1)}, u32[]{:S(2)}, u32[]{:S(2)}) collective-permute-start(bf16[128,4096]{1,0:T(8,128)(2,1)} %bitcast.15), channel_id=1, source_target_pairs={{0,192},{32,224},{64,0},{96,32},{128,64},{160,96},{192,128},{224,1... | collective-permute-start | bytes 3145736 | tf_op jit(solution)/shard_map/ppermute | solution.py:439
  3.0 73.7 %collective-permute-start.11 = (bf16[128,4096]{1,0:T(8,128)(2,1)}, bf16[128,4096]{1,0:T(8,128)(2,1)}, u32[]{:S(2)}, u32[]{:S(2)}) collective-permute-start(bf16[128,4096]{1,0:T(8,128)(2,1)} %bitcast.16), channel_id=1, source_target_pairs={{0,32},{32,0},{64,96},{96,64},{128,160},{160,128},{192,224},{224,1... | collective-permute-start | bytes 3145736 | tf_op jit(solution)/shard_map/ppermute | solution.py:439
  5.0 68.7 %all-to-all-start = ((bf16[8,128,512]{2,1,0:T(8,128)(2,1)}), bf16[8,128,512]{2,1,0:T(8,128)(2,1)S(1)}, u32[]{:S(2)}, u32[]{:S(2)}) async-start(bf16[8,128,512]{2,1,0:T(8,128)(2,1)} %broadcast_in_dim.41), calls=%async_computation | async-start | bytes 2097152 | tf_op jit(solution)/shard_map/all_to_all | solution.py:434
  13.2 15.4 %copy-start.12 = (s32[4]{0:T(128)S(1)}, s32[4]{0:T(128)}, u32[]{:S(2)}) copy-start(s32[4]{0:T(128)} %constant.67.clone) | copy-start | bytes 52
  13.2 15.4 %copy-start.13 = (s32[4]{0:T(128)S(1)}, s32[4]{0:T(128)}, u32[]{:S(2)}) copy-start(s32[4]{0:T(128)} %constant.68.clone) | copy-start | bytes 52
  27.0 14.8 %collective-permute-start.9 = (bf16[64,4096]{1,0:T(8,128)(2,1)S(1)}, bf16[64,4096]{1,0:T(8,128)(2,1)S(1)}, u32[]{:S(2)}, u32[]{:S(2)}) collective-permute-start(bf16[64,4096]{1,0:T(8,128)(2,1)S(1)} %slice.16), channel_id=1, source_target_pairs={{0,64},{32,96},{64,128},{96,160},{128,192},{160,224},{192,0},{224,... | collective-permute-start | bytes 1572872 | tf_op jit(solution)/shard_map/ppermute | solution.py:439
  29.7 15.1 %collective-permute-start.10 = (bf16[64,4096]{1,0:T(8,128)(2,1)S(1)}, bf16[64,4096]{1,0:T(8,128)(2,1)S(1)}, u32[]{:S(2)}, u32[]{:S(2)}) collective-permute-start(bf16[64,4096]{1,0:T(8,128)(2,1)S(1)} %slice.17), channel_id=1, source_target_pairs={{0,192},{32,224},{64,0},{96,32},{128,64},{160,96},{192,128},{224,1... | collective-permute-start | bytes 1572872 | tf_op jit(solution)/shard_map/ppermute | solution.py:439
  34.2 10.6 %copy-start.28 = (bf16[128,768]{1,0:T(8,128)(2,1)S(1)}, bf16[128,768]{1,0:T(8,128)(2,1)}, u32[]{:S(2)}) copy-start(bf16[128,768]{1,0:T(8,128)(2,1)} %get-tuple-element.38) | copy-start | bytes 589828
  34.2 11.4 %collective-permute-start = (bf16[128,768]{1,0:T(8,128)(2,1)}, bf16[128,768]{1,0:T(8,128)(2,1)S(1)}, u32[]{:S(2)}, u32[]{:S(2)}) collective-permute-start(bf16[128,768]{1,0:T(8,128)(2,1)} %get-tuple-element.35), channel_id=1, source_target_pairs={{0,64},{32,96},{64,128},{96,160},{128,192},{160,224},{192,0},{224,... | collective-permute-start | bytes 589832 | tf_op jit(solution)/shard_map/ppermute | solution.py:439
  35.7 12.5 %collective-permute-start.1 = (bf16[128,768]{1,0:T(8,128)(2,1)}, bf16[128,768]{1,0:T(8,128)(2,1)}, u32[]{:S(2)}, u32[]{:S(2)}) collective-permute-start(bf16[128,768]{1,0:T(8,128)(2,1)} %get-tuple-element.36), channel_id=1, source_target_pairs={{0,192},{32,224},{64,0},{96,32},{128,64},{160,96},{192,128},{224,1... | collective-permute-start | bytes 589832 | tf_op jit(solution)/shard_map/ppermute | solution.py:439
  41.8 9.7 %copy-start.14 = (s32[1,32]{1,0:T(1,128)S(1)}, s32[1,32]{1,0:T(1,128)}, u32[]{:S(2)}) copy-start(s32[1,32]{1,0:T(1,128)} %param.13) | copy-start | bytes 388
  41.8 23.3 %copy-start.21 = (bf16[128,768]{1,0:T(8,128)(2,1)S(1)}, bf16[128,768]{1,0:T(8,128)(2,1)}, u32[]{:S(2)}) copy-start(bf16[128,768]{1,0:T(8,128)(2,1)} %get-tuple-element.41) | copy-start | bytes 589828
  41.8 9.6 %collective-permute-start.2 = (bf16[128,768]{1,0:T(8,128)(2,1)}, bf16[128,768]{1,0:T(8,128)(2,1)S(1)}, u32[]{:S(2)}, u32[]{:S(2)}) collective-permute-start(bf16[128,768]{1,0:T(8,128)(2,1)} %get-tuple-element.37), channel_id=1, source_target_pairs={{0,128},{32,160},{64,192},{96,224},{128,0},{160,32},{192,64},{224,... | collective-permute-start | bytes 589832 | tf_op jit(solution)/shard_map/ppermute | solution.py:439
  44.8 6.5 %collective-permute-start.3 = (bf16[128,768]{1,0:T(8,128)(2,1)S(1)}, bf16[128,768]{1,0:T(8,128)(2,1)S(1)}, u32[]{:S(2)}, u32[]{:S(2)}) collective-permute-start(bf16[128,768]{1,0:T(8,128)(2,1)S(1)} %copy-done.28), channel_id=1, source_target_pairs={{0,32},{32,0},{64,96},{96,64},{128,160},{160,128},{192,224},{224,1... | collective-permute-start | bytes 589832 | tf_op jit(solution)/shard_map/ppermute | solution.py:439
  45.7 34.1 %copy-start.15 = (bf16[128,768]{1,0:T(8,128)(2,1)}, bf16[128,768]{1,0:T(8,128)(2,1)S(1)}, u32[]{:S(2)}) copy-start(bf16[128,768]{1,0:T(8,128)(2,1)S(1)} %collective-permute-done.refs_1_) | copy-start | bytes 589828
  45.7 42.4 %collective-permute-start.12 = (bf16[128,4096]{1,0:T(8,128)(2,1)}, bf16[128,4096]{1,0:T(8,128)(2,1)}, u32[]{:S(2)}, u32[]{:S(2)}) collective-permute-start(bf16[128,4096]{1,0:T(8,128)(2,1)} %collective-permute-done.7.refs_1_), channel_id=1, source_target_pairs={{0,32},{32,0},{64,96},{96,64},{128,160},{160,128},{192,224},{224,1... | collective-permute-start | bytes 3145736 | tf_op jit(solution)/shard_map/ppermute | solution.py:439
  48.2 39.9 %collective-permute-start.13 = (bf16[128,4096]{1,0:T(8,128)(2,1)}, bf16[128,4096]{1,0:T(8,128)(2,1)}, u32[]{:S(2)}, u32[]{:S(2)}) collective-permute-start(bf16[128,4096]{1,0:T(8,128)(2,1)} %collective-permute-done.8.refs_2_), channel_id=1, source_target_pairs={{0,32},{32,0},{64,96},{96,64},{128,160},{160,128},{192,224},{224,1... | collective-permute-start | bytes 3145736 | tf_op jit(solution)/shard_map/ppermute | solution.py:439
  51.4 22.3 %copy-start.16 = (bf16[128,768]{1,0:T(8,128)(2,1)}, bf16[128,768]{1,0:T(8,128)(2,1)S(1)}, u32[]{:S(2)}) copy-start(bf16[128,768]{1,0:T(8,128)(2,1)S(1)} %collective-permute-done.2.refs_3_) | copy-start | bytes 589828
  51.4 36.8 %collective-permute-start.14 = (bf16[128,4096]{1,0:T(8,128)(2,1)}, bf16[128,4096]{1,0:T(8,128)(2,1)}, u32[]{:S(2)}, u32[]{:S(2)}) collective-permute-start(bf16[128,4096]{1,0:T(8,128)(2,1)} %constant_dynamic-update-slice_fusion.refs_3_), channel_id=1, source_target_pairs={{0,32},{32,0},{64,96},{96,64},{128,160},{160,128},{192,224},{224,1... | collective-permute-start | bytes 3145736 | tf_op jit(solution)/shard_map/ppermute | solution.py:439
  51.4 28.4 %copy-start.17 = (bf16[128,768]{1,0:T(8,128)(2,1)}, bf16[128,768]{1,0:T(8,128)(2,1)S(1)}, u32[]{:S(2)}) copy-start(bf16[128,768]{1,0:T(8,128)(2,1)S(1)} %collective-permute-done.3.refs_4_) | copy-start | bytes 589828
  51.4 6.9 %collective-permute-start.4 = (bf16[128,768]{1,0:T(8,128)(2,1)}, bf16[128,768]{1,0:T(8,128)(2,1)S(1)}, u32[]{:S(2)}, u32[]{:S(2)}) collective-permute-start(bf16[128,768]{1,0:T(8,128)(2,1)} %get-tuple-element.39), channel_id=1, source_target_pairs={{0,96},{32,64},{64,160},{96,128},{128,224},{160,192},{192,32},{224... | collective-permute-start | bytes 589832 | tf_op jit(solution)/shard_map/ppermute | solution.py:439
  58.3 21.6 %copy-start.18 = (bf16[128,768]{1,0:T(8,128)(2,1)}, bf16[128,768]{1,0:T(8,128)(2,1)S(1)}, u32[]{:S(2)}) copy-start(bf16[128,768]{1,0:T(8,128)(2,1)S(1)} %collective-permute-done.4.refs_5_) | copy-start | bytes 589828
  58.3 6.8 %collective-permute-start.5 = (bf16[128,768]{1,0:T(8,128)(2,1)}, bf16[128,768]{1,0:T(8,128)(2,1)S(1)}, u32[]{:S(2)}, u32[]{:S(2)}) collective-permute-start(bf16[128,768]{1,0:T(8,128)(2,1)} %get-tuple-element.40), channel_id=1, source_target_pairs={{0,224},{32,192},{64,32},{96,0},{128,96},{160,64},{192,160},{224,1... | collective-permute-start | bytes 589832 | tf_op jit(solution)/shard_map/ppermute | solution.py:439
  65.1 14.7 %copy-start.19 = (bf16[128,768]{1,0:T(8,128)(2,1)}, bf16[128,768]{1,0:T(8,128)(2,1)S(1)}, u32[]{:S(2)}) copy-start(bf16[128,768]{1,0:T(8,128)(2,1)S(1)} %collective-permute-done.5.refs_6_) | copy-start | bytes 589828
  65.1 8.6 %collective-permute-start.6 = (bf16[128,768]{1,0:T(8,128)(2,1)S(1)}, bf16[128,768]{1,0:T(8,128)(2,1)S(1)}, u32[]{:S(2)}, u32[]{:S(2)}) collective-permute-start(bf16[128,768]{1,0:T(8,128)(2,1)S(1)} %copy-done.21), channel_id=1, source_target_pairs={{0,160},{32,128},{64,224},{96,192},{128,32},{160,0},{192,96},{224,... | collective-permute-start | bytes 589832 | tf_op jit(solution)/shard_map/ppermute | solution.py:439
  73.7 6.1 %copy-start.20 = (bf16[128,768]{1,0:T(8,128)(2,1)}, bf16[128,768]{1,0:T(8,128)(2,1)S(1)}, u32[]{:S(2)}) copy-start(bf16[128,768]{1,0:T(8,128)(2,1)S(1)} %collective-permute-done.6.refs_7_) | copy-start | bytes 589828
  73.7 14.4 %copy-start = (bf16[8,128,512]{2,1,0:T(8,128)(2,1)}, bf16[8,128,512]{2,1,0:T(8,128)(2,1)S(1)}, u32[]{:S(2)}) copy-start(bf16[8,128,512]{2,1,0:T(8,128)(2,1)S(1)} %all-to-all-done.refs_8_) | copy-start | bytes 3145732
  73.7 30.1 %collective-permute-start.15 = (bf16[8,128,512]{2,1,0:T(8,128)(2,1)S(1)}, bf16[8,128,512]{2,1,0:T(8,128)(2,1)S(1)}, u32[]{:S(2)}, u32[]{:S(2)}) collective-permute-start(bf16[8,128,512]{2,1,0:T(8,128)(2,1)S(1)} %all-to-all-done.refs_8_), channel_id=1, source_target_pairs={{0,1},{1,2},{2,3},{3,0},{4,5},{5,6},{6,7},{7,4},{8,9},{9,10},{10,1... | collective-permute-start | bytes 3145736 | tf_op jit(solution)/shard_map/ppermute | solution.py:422
  76.7 27.1 %collective-permute-start.16 = (bf16[8,128,512]{2,1,0:T(8,128)(2,1)S(1)}, bf16[8,128,512]{2,1,0:T(8,128)(2,1)}, u32[]{:S(2)}, u32[]{:S(2)}) collective-permute-start(bf16[8,128,512]{2,1,0:T(8,128)(2,1)S(1)} %all-to-all-done.refs_8_), channel_id=1, source_target_pairs={{0,3},{1,0},{2,1},{3,2},{4,7},{5,4},{6,5},{7,6},{8,11},{9,8},{10,9... | collective-permute-start | bytes 3145736 | tf_op jit(solution)/shard_map/ppermute | solution.py:422
  100.5 16.3 %collective-permute-start.26 = (bf16[4,512,128]{2,1,0:T(8,128)(2,1)}, bf16[4,512,128]{2,1,0:T(8,128)(2,1)S(1)}, u32[]{:S(2)}, u32[]{:S(2)}) collective-permute-start(bf16[4,512,128]{2,1,0:T(8,128)(2,1)} %get-tuple-element.42), channel_id=1, source_target_pairs={{0,1},{1,2},{2,3},{3,0},{4,5},{5,6},{6,7},{7,4},{8,9},{9,10},{10,1... | collective-permute-start | bytes 1572872 | tf_op jit(solution)/shard_map/ppermute | solution.py:422
  100.9 15.9 %collective-permute-start.27 = (bf16[4,512,128]{2,1,0:T(8,128)(2,1)}, bf16[4,512,128]{2,1,0:T(8,128)(2,1)S(1)}, u32[]{:S(2)}, u32[]{:S(2)}) collective-permute-start(bf16[4,512,128]{2,1,0:T(8,128)(2,1)} %get-tuple-element.59), channel_id=1, source_target_pairs={{0,3},{1,0},{2,1},{3,2},{4,7},{5,4},{6,5},{7,6},{8,11},{9,8},{10,9... | collective-permute-start | bytes 1572872 | tf_op jit(solution)/shard_map/ppermute | solution.py:422
  103.9 1.5 copy-start.4
  103.9 24.3 %collective-permute-start.17 = (bf16[4,128,512]{2,1,0:T(8,128)(2,1)S(1)}, bf16[4,128,512]{2,1,0:T(8,128)(2,1)}, u32[]{:S(2)}, u32[]{:S(2)}) collective-permute-start(bf16[4,128,512]{2,1,0:T(8,128)(2,1)S(1)} %slice.14), channel_id=1, source_target_pairs={{0,1},{1,2},{2,3},{3,0},{4,5},{5,6},{6,7},{7,4},{8,9},{9,10},{10,1... | collective-permute-start | bytes 1572872 | tf_op jit(solution)/shard_map/ppermute | solution.py:422
  105.3 22.8 %collective-permute-start.18 = (bf16[4,128,512]{2,1,0:T(8,128)(2,1)S(1)}, bf16[4,128,512]{2,1,0:T(8,128)(2,1)}, u32[]{:S(2)}, u32[]{:S(2)}) collective-permute-start(bf16[4,128,512]{2,1,0:T(8,128)(2,1)S(1)} %slice.15), channel_id=1, source_target_pairs={{0,3},{1,0},{2,1},{3,2},{4,7},{5,4},{6,5},{7,6},{8,11},{9,8},{10,9... | collective-permute-start | bytes 1572872 | tf_op jit(solution)/shard_map/ppermute | solution.py:422
  116.8 0.8 copy-start.2
  116.8 1.0 copy-start.3
  120.2 31.4 %collective-permute-start.28 = (bf16[8,512,128]{2,1,0:T(8,128)(2,1)}, bf16[8,512,128]{2,1,0:T(8,128)(2,1)S(1)}, u32[]{:S(2)}, u32[]{:S(2)}) collective-permute-start(bf16[8,512,128]{2,1,0:T(8,128)(2,1)} %get-tuple-element.60), channel_id=1, source_target_pairs={{0,1},{1,2},{2,3},{3,0},{4,5},{5,6},{6,7},{7,4},{8,9},{9,10},{10,1... | collective-permute-start | bytes 3145736 | tf_op jit(solution)/shard_map/ppermute | solution.py:422
  120.7 30.9 %collective-permute-start.29 = (bf16[8,512,128]{2,1,0:T(8,128)(2,1)}, bf16[8,512,128]{2,1,0:T(8,128)(2,1)S(1)}, u32[]{:S(2)}, u32[]{:S(2)}) collective-permute-start(bf16[8,512,128]{2,1,0:T(8,128)(2,1)} %get-tuple-element.61), channel_id=1, source_target_pairs={{0,3},{1,0},{2,1},{3,2},{4,7},{5,4},{6,5},{7,6},{8,11},{9,8},{10,9... | collective-permute-start | bytes 3145736 | tf_op jit(solution)/shard_map/ppermute | solution.py:422
  138.3 13.3 %copy-start.1 = (bf16[8,512,128]{2,1,0:T(8,128)(2,1)S(1)}, bf16[8,512,128]{2,1,0:T(8,128)(2,1)}, u32[]{:S(2)}) copy-start(bf16[8,512,128]{2,1,0:T(8,128)(2,1)} %get-tuple-element.56) | copy-start | bytes 3145732
  153.0 8.6 %copy-start.29 = (bf16[128,768]{1,0:T(8,128)(2,1)S(1)}, bf16[128,768]{1,0:T(8,128)(2,1)}, u32[]{:S(2)}) copy-start(bf16[128,768]{1,0:T(8,128)(2,1)} %get-tuple-element.46) | copy-start | bytes 589828
  153.0 9.2 %copy-start.27 = (bf16[128,768]{1,0:T(8,128)(2,1)S(1)}, bf16[128,768]{1,0:T(8,128)(2,1)}, u32[]{:S(2)}) copy-start(bf16[128,768]{1,0:T(8,128)(2,1)} %get-tuple-element.47) | copy-start | bytes 589828
  153.0 10.7 %copy-start.26 = (bf16[128,768]{1,0:T(8,128)(2,1)S(1)}, bf16[128,768]{1,0:T(8,128)(2,1)}, u32[]{:S(2)}) copy-start(bf16[128,768]{1,0:T(8,128)(2,1)} %get-tuple-element.48) | copy-start | bytes 589828
  153.0 14.4 %copy-start.25 = (bf16[128,768]{1,0:T(8,128)(2,1)S(1)}, bf16[128,768]{1,0:T(8,128)(2,1)}, u32[]{:S(2)}) copy-start(bf16[128,768]{1,0:T(8,128)(2,1)} %get-tuple-element.49) | copy-start | bytes 589828
  153.0 14.4 %copy-start.24 = (bf16[128,768]{1,0:T(8,128)(2,1)S(1)}, bf16[128,768]{1,0:T(8,128)(2,1)}, u32[]{:S(2)}) copy-start(bf16[128,768]{1,0:T(8,128)(2,1)} %get-tuple-element.50) | copy-start | bytes 589828
  153.0 15.7 %copy-start.23 = (bf16[128,768]{1,0:T(8,128)(2,1)S(1)}, bf16[128,768]{1,0:T(8,128)(2,1)}, u32[]{:S(2)}) copy-start(bf16[128,768]{1,0:T(8,128)(2,1)} %get-tuple-element.51) | copy-start | bytes 589828
  153.0 18.6 %copy-start.22 = (bf16[128,768]{1,0:T(8,128)(2,1)S(1)}, bf16[128,768]{1,0:T(8,128)(2,1)}, u32[]{:S(2)}) copy-start(bf16[128,768]{1,0:T(8,128)(2,1)} %get-tuple-element.52) | copy-start | bytes 589828
  153.0 35.7 %all-to-all-start.1 = ((bf16[8,512,128]{2,1,0:T(8,128)(2,1)}), bf16[8,512,128]{2,1,0:T(8,128)(2,1)S(1)}, u32[]{:S(2)}, u32[]{:S(2)}) async-start(bf16[8,512,128]{2,1,0:T(8,128)(2,1)} %add_convert_fusion), calls=%async_computation.1 | async-start | bytes 2097152 | tf_op jit(solution)/shard_map/all_to_all | solution.py:434
  161.6 7.1 %collective-permute-start.19 = (bf16[128,768]{1,0:T(8,128)(2,1)S(1)}, bf16[128,768]{1,0:T(8,128)(2,1)S(1)}, u32[]{:S(2)}, u32[]{:S(2)}) collective-permute-start(bf16[128,768]{1,0:T(8,128)(2,1)S(1)} %copy-done.29), channel_id=1, source_target_pairs={{0,64},{32,96},{64,128},{96,160},{128,192},{160,224},{192,0},{224,... | collective-permute-start | bytes 589832 | tf_op jit(solution)/shard_map/ppermute | solution.py:439
  162.2 9.5 %collective-permute-start.20 = (bf16[128,768]{1,0:T(8,128)(2,1)S(1)}, bf16[128,768]{1,0:T(8,128)(2,1)S(1)}, u32[]{:S(2)}, u32[]{:S(2)}) collective-permute-start(bf16[128,768]{1,0:T(8,128)(2,1)S(1)} %copy-done.27), channel_id=1, source_target_pairs={{0,192},{32,224},{64,0},{96,32},{128,64},{160,96},{192,128},{224,1... | collective-permute-start | bytes 589832 | tf_op jit(solution)/shard_map/ppermute | solution.py:439
  163.7 10.5 %collective-permute-start.21 = (bf16[128,768]{1,0:T(8,128)(2,1)S(1)}, bf16[128,768]{1,0:T(8,128)(2,1)S(1)}, u32[]{:S(2)}, u32[]{:S(2)}) collective-permute-start(bf16[128,768]{1,0:T(8,128)(2,1)S(1)} %copy-done.26), channel_id=1, source_target_pairs={{0,128},{32,160},{64,192},{96,224},{128,0},{160,32},{192,64},{224,... | collective-permute-start | bytes 589832 | tf_op jit(solution)/shard_map/ppermute | solution.py:439
  167.4 6.8 %collective-permute-start.22 = (bf16[128,768]{1,0:T(8,128)(2,1)S(1)}, bf16[128,768]{1,0:T(8,128)(2,1)S(1)}, u32[]{:S(2)}, u32[]{:S(2)}) collective-permute-start(bf16[128,768]{1,0:T(8,128)(2,1)S(1)} %copy-done.25), channel_id=1, source_target_pairs={{0,32},{32,0},{64,96},{96,64},{128,160},{160,128},{192,224},{224,1... | collective-permute-start | bytes 589832 | tf_op jit(solution)/shard_map/ppermute | solution.py:439
  167.4 8.1 %collective-permute-start.23 = (bf16[128,768]{1,0:T(8,128)(2,1)S(1)}, bf16[128,768]{1,0:T(8,128)(2,1)S(1)}, u32[]{:S(2)}, u32[]{:S(2)}) collective-permute-start(bf16[128,768]{1,0:T(8,128)(2,1)S(1)} %copy-done.24), channel_id=1, source_target_pairs={{0,96},{32,64},{64,160},{96,128},{128,224},{160,192},{192,32},{224... | collective-permute-start | bytes 589832 | tf_op jit(solution)/shard_map/ppermute | solution.py:439
  168.7 12.9 %copy-start.5 = (bf16[128,768]{1,0:T(8,128)(2,1)}, bf16[128,768]{1,0:T(8,128)(2,1)S(1)}, u32[]{:S(2)}) copy-start(bf16[128,768]{1,0:T(8,128)(2,1)S(1)} %collective-permute-done.19.refs_1_) | copy-start | bytes 589828
  168.7 9.6 %collective-permute-start.24 = (bf16[128,768]{1,0:T(8,128)(2,1)S(1)}, bf16[128,768]{1,0:T(8,128)(2,1)S(1)}, u32[]{:S(2)}, u32[]{:S(2)}) collective-permute-start(bf16[128,768]{1,0:T(8,128)(2,1)S(1)} %copy-done.23), channel_id=1, source_target_pairs={{0,224},{32,192},{64,32},{96,0},{128,96},{160,64},{192,160},{224,1... | collective-permute-start | bytes 589832 | tf_op jit(solution)/shard_map/ppermute | solution.py:439
  171.6 10.0 %copy-start.6 = (bf16[128,768]{1,0:T(8,128)(2,1)}, bf16[128,768]{1,0:T(8,128)(2,1)S(1)}, u32[]{:S(2)}) copy-start(bf16[128,768]{1,0:T(8,128)(2,1)S(1)} %collective-permute-done.20.refs_2_) | copy-start | bytes 589828
  171.6 10.0 %collective-permute-start.25 = (bf16[128,768]{1,0:T(8,128)(2,1)S(1)}, bf16[128,768]{1,0:T(8,128)(2,1)S(1)}, u32[]{:S(2)}, u32[]{:S(2)}) collective-permute-start(bf16[128,768]{1,0:T(8,128)(2,1)S(1)} %copy-done.22), channel_id=1, source_target_pairs={{0,160},{32,128},{64,224},{96,192},{128,32},{160,0},{192,96},{224,... | collective-permute-start | bytes 589832 | tf_op jit(solution)/shard_map/ppermute | solution.py:439
  174.2 7.4 %copy-start.7 = (bf16[128,768]{1,0:T(8,128)(2,1)}, bf16[128,768]{1,0:T(8,128)(2,1)S(1)}, u32[]{:S(2)}) copy-start(bf16[128,768]{1,0:T(8,128)(2,1)S(1)} %collective-permute-done.21.refs_3_) | copy-start | bytes 589828
  174.2 7.4 %copy-start.8 = (bf16[128,768]{1,0:T(8,128)(2,1)}, bf16[128,768]{1,0:T(8,128)(2,1)S(1)}, u32[]{:S(2)}) copy-start(bf16[128,768]{1,0:T(8,128)(2,1)S(1)} %collective-permute-done.22.refs_4_) | copy-start | bytes 589828
  175.6 6.1 %copy-start.9 = (bf16[128,768]{1,0:T(8,128)(2,1)}, bf16[128,768]{1,0:T(8,128)(2,1)S(1)}, u32[]{:S(2)}) copy-start(bf16[128,768]{1,0:T(8,128)(2,1)S(1)} %collective-permute-done.23.refs_5_) | copy-start | bytes 589828
  178.3 3.3 %copy-start.10 = (bf16[128,768]{1,0:T(8,128)(2,1)}, bf16[128,768]{1,0:T(8,128)(2,1)S(1)}, u32[]{:S(2)}) copy-start(bf16[128,768]{1,0:T(8,128)(2,1)S(1)} %collective-permute-done.24.refs_6_) | copy-start | bytes 589828
  181.7 0.7 copy-start.11

commit v3 on v2

--- a/solution.py
+++ b/solution.py
@@ -237,24 +237,18 @@
 
 
 def upstream_kernel(ids_ref, *refs):
-    pieces, weights, (o_ref, acc_ref, w_ref) = refs[:-8], refs[-8:-3], refs[-3:]
+    weights, (o_ref, acc_ref, w_ref) = refs[-11:-3], refs[-3:]
+    pieces = refs[:-11]
     count = len(pieces)
     near = w_ref.shape[1]
     step = pl.program_id(0)
     last = pl.num_programs(0) - 1
-    y = ids_ref[count + 1]
-    mine, below, above, far_low, far_high = weights
-    w_ref[:, y] = mine[...]
-    w_ref[:, lax.rem(y + near - 1, near)] = below[...]
-    w_ref[:, lax.rem(y + 1, near)] = above[...]
-
-    @pl.when(step * 2 <= last)
-    def _():
-        w_ref[:, lax.rem(y + 2, near)] = far_low[...]
-
-    @pl.when(step * 2 > last)
-    def _():
-        w_ref[:, lax.rem(y + 2, near)] = far_high[...]
+    for offset in range(near):
+        t = lax.rem(ids_ref[count + 1] + offset, near)
+        left, right = weights[2 * offset], weights[2 * offset + 1]
+        cut = left.shape[2]
+        w_ref[:, t, :, :cut] = left[...]
+        w_ref[:, t, :, cut:] = right[...]
 
     rows = jnp.concatenate([piece[...] for piece in pieces], 0)
     weight = w_ref[...].reshape(rows.shape[1], w_ref.shape[3])
@@ -275,24 +269,20 @@
 
 
 def upstream(ids, pieces, weights):
-    far, rows, width = weights[0].shape
+    far, rows, cut = weights[0].shape
+    width = 2 * cut
     near = GRID["fsdp"]
     depth = far * near * rows
     planes = 2
     steps = far // planes
     count = len(pieces)
-    block = (planes, rows, width)
     return pl.pallas_call(
         upstream_kernel,
         grid_spec=pltpu.PrefetchScalarGridSpec(
             num_scalar_prefetch=1,
             grid=(steps,),
             in_specs=[pl.BlockSpec((TOK, depth // steps), lambda i, ids: (0, i))] * count
-            + [pl.BlockSpec(block, lambda i, ids: (i, 0, 0))] * 3
-            + [
-                pl.BlockSpec(block, lambda i, ids: (jnp.minimum(i, steps // 2 - 1), 0, 0)),
-                pl.BlockSpec(block, lambda i, ids: (jnp.maximum(i - steps // 2, 0), 0, 0)),
-            ],
+            + [pl.BlockSpec((planes, rows, cut), lambda i, ids: (i, 0, 0))] * (2 * near),
             out_specs=pl.BlockSpec((count, TOK, width), lambda i, ids: (0, 0, 0)),
             scratch_shapes=[
                 pltpu.VMEM((count * TOK, width), F32),
@@ -458,13 +448,19 @@
     half = TOK // 2
     own = out_cotangent[0]
     left, right = hop(own, 1, 0), hop(own, -1, 0)
-    weight = jnp.broadcast_to(proj_weight, (2 * far, *proj_weight.shape))
-    weight = swap(weight, "dp")
+    cut = proj_weight.shape[1] // 2
+    left_half, right_half = (
+        jnp.broadcast_to(x, (2 * far, *x.shape)) for x in jnp.split(proj_weight, [cut], axis=1)
+    )
+    left_half = swap(left_half, "dp")
     packed = pack(targets, query_rows, forward_key_rows, forward_value_rows)
     paths = [(chips, flip) for flip in range(2) for chips in (0, 1, -1, 2)]
     packed = [packed[0]] + [hop(x, *path) for x, path in zip(packed[1:], paths[1:])]
     partner = hop(own, 0, 1)
-    below, above = shift(weight, "fsdp", 1), shift(weight, "fsdp", -1)
+    right_half = swap(right_half, "dp")
+    weights_left = [left_half] + [shift(left_half, "fsdp", -by) for by in (1, 2, 3)]
+    weights_right = [right_half] + [shift(right_half, "fsdp", -by) for by in (1, 2, 3)]
+    weights = [x for pair in zip(weights_left, weights_right) for x in pair]
     lo, hi = limits(sent_lengths[0], len(packed))
     across = [hop(left[:half], 1, 0), hop(right[half:], -1, 0)]
     across = jnp.concatenate(across, 0)
@@ -473,11 +469,9 @@
     pieces += [hop(piece, 0, 1) for piece in (left, right, across)]
     same, following, low, high, before = proj_terms(ids, pieces, output)
     up, down = shift(low, "fsdp", 1), shift(high, "fsdp", -1)
-    below, above = after((below, above), low)
-    ends = [shift(below[:far], "fsdp", 1), shift(above[far:], "fsdp", -1)]
     following, before = join(following, up, before, down)
     up, down = shift(following, "fsdp", 1), shift(before, "fsdp", -1)
-    arriving = upstream(ids, pieces, [weight, below, above, *ends])
+    arriving = upstream(ids, pieces, weights)
     grads = attend_grad(jnp.concatenate([ids, targets]), packed, arriving, lo, hi)
     up, down = after((up, down), grads[0])
     first = (same.astype(F32) + up.astype(F32) + down.astype(F32)).astype(BF16)

time: 192 us -> 238 us (1.24)
  waiting for transfers between devices: 67.3 us -> 103 us
  starting transfers between devices: 54.1 us -> 65.4 us
    ppermute x8 -> x10, waiting for transfers between devices: 12.5 us -> 42.9 us  [shift(): return lax.ppermute(x, axis, [(i, (i + by) % n) for i in range(n)])]
    ppermute x22, waiting for transfers between devices: 51.9 us -> 58.4 us  [hop(): return lax.ppermute(x, 'seq', pairs)]
    all_to_all x2 -> x3, starting transfers between devices: 16.7 us -> 22.7 us  [swap(): return lax.all_to_all(x, axis, split_axis=0, concat_axis=0, tiled=True)]
    ppermute x22, starting transfers between devices: 22.9 us -> 26.1 us  [hop(): return lax.ppermute(x, 'seq', pairs)]
    ppermute x8 -> x10, starting transfers between devices: 14.4 us -> 16.6 us  [shift(): return lax.ppermute(x, axis, [(i, (i + by) % n) for i in range(n)])]
    unnamed x62 -> x68, local copies, waits for them, and re-layouts: 3.35 us -> 4.9 us
  transfers between devices with their start and end apart: 32 -> 35, of which waited for: 16 -> 17; matrix products, arithmetic and copies ran while one was open for 5% -> 3% of each run, Pallas kernels for 28% -> 23%
where the time goes in v3:
time: 238 us; the launch traced here: 236 us
  waiting for transfers between devices  103 us (43%)
  starting transfers between devices  65.4 us (27%)
  Pallas kernels  53 us (22%)
  local copies, waits for them, and re-layouts  9.31 us (4%)
  other arithmetic  3.69 us (2%)
    ppermute x22, waiting for transfers between devices, hop(): return lax.ppermute(x, 'seq', pairs)  58.4 us
    ppermute x10, waiting for transfers between devices, shift(): return lax.ppermute(x, axis, [(i, (i + by) % n) for i in range(n)])  42.9 us
    ppermute x22, starting transfers between devices, hop(): return lax.ppermute(x, 'seq', pairs)  26.1 us
    all_to_all x3, starting transfers between devices, swap(): return lax.all_to_all(x, axis, split_axis=0, concat_axis=0, tiled=True)  22.7 us
    ppermute x10, starting transfers between devices, shift(): return lax.ppermute(x, axis, [(i, (i + by) % n) for i in range(n)])  16.6 us
    pallas_call x1, Pallas kernels, attend_grad(): pl.pallas_call(bwd_kernel, grid_spec=pltpu.PrefetchScalarGridSpec(num_sca...  13.2 us
    pallas_call x1, Pallas kernels, proj_terms(): pl.pallas_call(proj_kernel, grid_spec=pltpu.PrefetchScalarGridSpec(num_sc...  12.3 us
    pallas_call x1, Pallas kernels, upstream(): pl.pallas_call(upstream_kernel, grid_spec=pltpu.PrefetchScalarGridSpec(nu...  10.1 us
  transfers between devices with their start and end apart: 35, of which 17 were waited for; matrix products, arithmetic and copies ran while one was open for 3% of the time, Pallas kernels for 23%

profile of v3, /device:TPU:2, one launch (start us, length us, event | category | flops | bytes accessed | tf_op | source)
XLA Modules:
  0.0 235.7 jit_solution(14405249659580560020)
XLA Ops:
  0.7 1.6 collective-permute-start.7
  2.2 0.8 collective-permute-start.8
  3.1 22.8 %collective-permute-done.7.refs_1_ = bf16[128,4096]{1,0:T(8,128)(2,1)S(1)} collective-permute-done((bf16[128,4096]{1,0:T(8,128)(2,1)}, bf16[128,4096]{1,0:T(8,128)(2,1)S(1)}, u32[]{:S(2)}, u32[]{:S(2)}) %collective-permute-start.7) | collective-permute-done | bytes 1048608 | tf_op jit(solution)/shard_map/ppermute | solution.py:429
  25.9 1.6 collective-permute-start.9
  27.5 1.1 slice.9
  28.6 0.6 collective-permute-start.10
  29.2 0.6 pad_add_fusion.1.ids_ref
  29.8 3.3 %pack.1 = (bf16[128,768]{1,0:T(8,128)(2,1)}, bf16[128,768]{1,0:T(8,128)(2,1)}, bf16[128,768]{1,0:T(8,128)(2,1)}, bf16[128,768]{1,0:T(8,128)(2,1)}, bf16[128,768]...) custom-call(s32[8]{0:T(128)} %pad_add_fusion.1.ids_ref, ...), custom_call_target="tpu_custom_call" | custom-call | bytes 3145728 | tf_op jit(solution)/shard_map/pack/pallas_call | solution.py:195
  33.1 1.5 collective-permute-start
  34.6 1.3 collective-permute-start.1
  35.9 4.9 %collective-permute-done.9 = bf16[64,4096]{1,0:T(8,128)(2,1)S(1)} collective-permute-done((bf16[64,4096]{1,0:T(8,128)(2,1)S(1)}, bf16[64,4096]{1,0:T(8,128)(2,1)S(1)}, u32[]{:S(2)}, u32[]{:S(2)}) %collective-permute-start.9) | collective-permute-done | bytes 524320 | tf_op jit(solution)/shard_map/ppermute | solution.py:429
  40.8 2.1 collective-permute-start.2
  42.9 0.9 constant_dynamic-update-slice_fusion.1
  43.8 0.8 constant_dynamic-update-slice_fusion.refs_3_
  45.1 1.9 collective-permute-done.1.refs_2_
  47.0 3.3 %collective-permute-done.2.refs_3_ = bf16[128,768]{1,0:T(8,128)(2,1)S(1)} collective-permute-done((bf16[128,768]{1,0:T(8,128)(2,1)}, bf16[128,768]{1,0:T(8,128)(2,1)S(1)}, u32[]{:S(2)}, u32[]{:S(2)}) %collective-permute-start.2) | collective-permute-done | bytes 196640 | tf_op jit(solution)/shard_map/ppermute | solution.py:429
  50.4 0.8 broadcast_in_dim.44
  51.2 8.5 %all-to-all-start = ((bf16[8,128,256]{2,1,0:T(8,128)(2,1)}), bf16[8,128,256]{2,1,0:T(8,128)(2,1)S(1)}, u32[]{:S(2)}, u32[]{:S(2)}) async-start(bf16[8,128,256]{2,1,0:T(8,128)(2,1)} %broadcast_in_dim.44), calls=%async_computation | async-start | bytes 1048576 | tf_op jit(solution)/shard_map/all_to_all | solution.py:424
  60.0 6.9 %collective-permute-done.4.refs_5_ = bf16[128,768]{1,0:T(8,128)(2,1)S(1)} collective-permute-done((bf16[128,768]{1,0:T(8,128)(2,1)}, bf16[128,768]{1,0:T(8,128)(2,1)S(1)}, u32[]{:S(2)}, u32[]{:S(2)}) %collective-permute-start.4) | collective-permute-done | bytes 196640 | tf_op jit(solution)/shard_map/ppermute | solution.py:429
  66.9 2.4 %collective-permute-start.5 = (bf16[128,768]{1,0:T(8,128)(2,1)}, bf16[128,768]{1,0:T(8,128)(2,1)S(1)}, u32[]{:S(2)}, u32[]{:S(2)}) collective-permute-start(bf16[128,768]{1,0:T(8,128)(2,1)} %get-tuple-element.38), channel_id=1, source_target_pairs={{0,224},{32,192},{64,32},{96,0},{128,96},{160,64},{192,160},{224,1... | collective-permute-start | bytes 589832 | tf_op jit(solution)/shard_map/ppermute | solution.py:429
  69.3 4.4 %collective-permute-done.5.refs_6_ = bf16[128,768]{1,0:T(8,128)(2,1)S(1)} collective-permute-done((bf16[128,768]{1,0:T(8,128)(2,1)}, bf16[128,768]{1,0:T(8,128)(2,1)S(1)}, u32[]{:S(2)}, u32[]{:S(2)}) %collective-permute-start.5) | collective-permute-done | bytes 196640 | tf_op jit(solution)/shard_map/ppermute | solution.py:429
  73.7 5.3 %collective-permute-start.6 = (bf16[128,768]{1,0:T(8,128)(2,1)}, bf16[128,768]{1,0:T(8,128)(2,1)S(1)}, u32[]{:S(2)}, u32[]{:S(2)}) collective-permute-start(bf16[128,768]{1,0:T(8,128)(2,1)} %get-tuple-element.39), channel_id=1, source_target_pairs={{0,160},{32,128},{64,224},{96,192},{128,32},{160,0},{192,96},{224,... | collective-permute-start | bytes 589832 | tf_op jit(solution)/shard_map/ppermute | solution.py:429
  79.0 0.6 pad_add_fusion.ids_ref
  79.5 0.7 select_reduce_fusion
  80.2 4.0 %collective-permute-done.6.refs_7_ = bf16[128,768]{1,0:T(8,128)(2,1)S(1)} collective-permute-done((bf16[128,768]{1,0:T(8,128)(2,1)}, bf16[128,768]{1,0:T(8,128)(2,1)S(1)}, u32[]{:S(2)}, u32[]{:S(2)}) %collective-permute-start.6) | collective-permute-done | bytes 196640 | tf_op jit(solution)/shard_map/ppermute | solution.py:429
  84.2 0.7 copy-done.25
  84.9 8.3 %attend.1.refs_8_ = bf16[8,512,128]{2,1,0:T(8,128)(2,1)} custom-call(s32[10]{0:T(128)} %pad_add_fusion.ids_ref, bf16[128,768]{1,0:T(8,128)(2,1)} %get-tuple-element.32.refs_0_, bf16[128,768]{1,0:T(8,128)(2,1)} %copy-done.20, bf16[128,768]{1,0:T(8,128)(2,1)} %copy-done.21, bf16[128,768]{1,0:T(8,128)(2,1)} %copy-done.22, ...), custom_call_target="tpu_custom_call" | custom-call | flops 939524096 | bytes 3145728 | tf_op jit(solution)/shard_map/attend/pallas_call | solution.py:138
  93.2 0.9 broadcast_in_dim.45
  94.1 6.9 %all-to-all-start.1 = ((bf16[8,128,256]{2,1,0:T(8,128)(2,1)}), bf16[8,128,256]{2,1,0:T(8,128)(2,1)S(1)}, u32[]{:S(2)}, u32[]{:S(2)}) async-start(bf16[8,128,256]{2,1,0:T(8,128)(2,1)} %broadcast_in_dim.45), calls=%async_computation.1 | async-start | bytes 1048576 | tf_op jit(solution)/shard_map/all_to_all | solution.py:424
  101.0 1.6 collective-permute-start.19
  102.6 1.0 copy-done.17
  103.6 12.3 %proj_terms.1 = (bf16[8,512,128]{2,1,0:T(8,128)(2,1)}, bf16[8,512,128]{2,1,0:T(8,128)(2,1)}, bf16[4,512,128]{2,1,0:T(8,128)(2,1)}, bf16[4,512,128]{2,1,0:T(8,128)(2,1)}, bf16[8,512,128]{2,1,0:T(8,128)(2,1)}) custom-call(s32[10]{0:T(128)} %pad_add_fusion.ids_ref, bf16[128,4096]{1,0:T(8,128)(2,1)} %bitcast.17, bf16[128,4096]{1,0:T(8,128)(2,1)} %copy-done.5, ...), custom_call_target="tpu_custom_call" | custom-call | flops 4294967296 | bytes 13631488 | tf_op jit(solution)/shard_map/proj_terms/pallas_call | solution.py:347
  115.9 1.7 collective-permute-start.28
  117.6 1.6 collective-permute-start.29
  119.2 1.8 collective-permute-start.17
  121.0 1.3 collective-permute-start.15
  122.3 0.8 collective-permute-start.20
  123.1 20.3 %collective-permute-done.28.up_ref = bf16[4,512,128]{2,1,0:T(8,128)(2,1)S(1)} collective-permute-done((bf16[4,512,128]{2,1,0:T(8,128)(2,1)}, bf16[4,512,128]{2,1,0:T(8,128)(2,1)S(1)}, u32[]{:S(2)}, u32[]{:S(2)}) %collective-permute-start.28) | collective-permute-done | bytes 524320 | tf_op jit(solution)/shard_map/ppermute | solution.py:412
  143.5 1.6 collective-permute-start.18
  145.1 1.6 collective-permute-start.16
  146.7 2.4 %join.1 = (bf16[8,512,128]{2,1,0:T(8,128)(2,1)}, bf16[8,512,128]{2,1,0:T(8,128)(2,1)}) custom-call(bf16[8,512,128]{2,1,0:T(8,128)(2,1)} %get-tuple-element.52.low_ref, bf16[4,512,128]{2,1,0:T(8,128)(2,1)} %copy-done.3, bf16[8,512,128]{2,1,0:T(8,128)(2,1)} %get-tuple-element.54.high_ref, ...), custom_call_target="tpu_custom_call", output_to_operand_aliasing={{0}: (0, {}), {1}: (2, {})} | custom-call | flops 524288 | bytes 3145728 | tf_op jit(solution)/shard_map/join/pallas_call | solution.py:391
  149.6 15.5 %collective-permute-done.15.refs_10_ = bf16[8,128,256]{2,1,0:T(8,128)(2,1)S(1)} collective-permute-done((bf16[8,128,256]{2,1,0:T(8,128)(2,1)S(1)}, bf16[8,128,256]{2,1,0:T(8,128)(2,1)S(1)}, u32[]{:S(2)}, u32[]{:S(2)}) %collective-permute-start.15) | collective-permute-done | bytes 524320 | tf_op jit(solution)/shard_map/ppermute | solution.py:412
  165.1 0.8 copy-done.19
  165.9 4.1 %collective-permute-start.31 = (bf16[8,512,128]{2,1,0:T(8,128)(2,1)}, bf16[8,512,128]{2,1,0:T(8,128)(2,1)S(1)}, u32[]{:S(2)}, u32[]{:S(2)}) collective-permute-start(bf16[8,512,128]{2,1,0:T(8,128)(2,1)} %get-tuple-element.57), channel_id=1, source_target_pairs={{0,3},{1,0},{2,1},{3,2},{4,7},{5,4},{6,5},{7,6},{8,11},{9,8},{10,9... | collective-permute-start | bytes 3145736 | tf_op jit(solution)/shard_map/ppermute | solution.py:412
  170.0 0.7 concatenate.14.ids_ref
  170.7 7.1 %collective-permute-done.16.refs_11_ = bf16[8,128,256]{2,1,0:T(8,128)(2,1)} collective-permute-done((bf16[8,128,256]{2,1,0:T(8,128)(2,1)S(1)}, bf16[8,128,256]{2,1,0:T(8,128)(2,1)}, u32[]{:S(2)}, u32[]{:S(2)}) %collective-permute-start.16) | collective-permute-done | bytes 524320 | tf_op jit(solution)/shard_map/ppermute | solution.py:412
  177.7 10.1 %upstream.1.refs_8_ = bf16[8,128,512]{2,1,0:T(8,128)(2,1)} custom-call(s32[10]{0:T(128)} %pad_add_fusion.ids_ref, bf16[128,4096]{1,0:T(8,128)(2,1)} %bitcast.18, bf16[128,4096]{1,0:T(8,128)(2,1)} %copy-done.5, bf16[128,4096]{1,0:T(8,128)(2,1)} %collective-permute-done.8.refs_2_, bf16[128,4096]{1,0:T(8,128)(2,1)} %constant_dynamic-update-slice_fusion.refs_3_, ...), custom_call_target="tpu_custom_call" | custom-call | flops 4294967296 | bytes 13631488 | tf_op jit(solution)/shard_map/upstream/pallas_call | solution.py:279
  187.8 13.2 %attend_grad.1 = (bf16[128,768]{1,0:T(8,128)(2,1)}, bf16[128,768]{1,0:T(8,128)(2,1)}, bf16[128,768]{1,0:T(8,128)(2,1)}, bf16[128,768]{1,0:T(8,128)(2,1)}, bf16[1...) custom-call(s32[18]{0:T(128)} %concatenate.14.ids_ref, ...), custom_call_target="tpu_custom_call" | custom-call | flops 2348810240 | bytes 4718592 | tf_op jit(solution)/shard_map/attend_grad/pallas_call | solution.py:161
  201.0 1.4 add_convert_fusion
  202.5 7.3 %all-to-all-start.2 = ((bf16[8,512,128]{2,1,0:T(8,128)(2,1)}), bf16[8,512,128]{2,1,0:T(8,128)(2,1)S(1)}, u32[]{:S(2)}, u32[]{:S(2)}) async-start(bf16[8,512,128]{2,1,0:T(8,128)(2,1)} %add_convert_fusion), calls=%async_computation.2 | async-start | bytes 2097152 | tf_op jit(solution)/shard_map/all_to_all | solution.py:424
  210.0 2.0 collective-permute-start.22
  212.0 3.7 %collective-permute-start.23 = (bf16[128,768]{1,0:T(8,128)(2,1)S(1)}, bf16[128,768]{1,0:T(8,128)(2,1)S(1)}, u32[]{:S(2)}, u32[]{:S(2)}) collective-permute-start(bf16[128,768]{1,0:T(8,128)(2,1)S(1)} %copy-done.30), channel_id=1, source_target_pairs={{0,128},{32,160},{64,192},{96,224},{128,0},{160,32},{192,64},{224,... | collective-permute-start | bytes 589832 | tf_op jit(solution)/shard_map/ppermute | solution.py:429
  215.7 1.0 collective-permute-start.25
  216.8 0.8 collective-permute-start.26
  217.6 0.6 collective-permute-done.22.refs_2_
  218.2 0.8 collective-permute-start.27
  219.0 3.7 %collective-permute-done.23.refs_3_ = bf16[128,768]{1,0:T(8,128)(2,1)S(1)} collective-permute-done((bf16[128,768]{1,0:T(8,128)(2,1)S(1)}, bf16[128,768]{1,0:T(8,128)(2,1)S(1)}, u32[]{:S(2)}, u32[]{:S(2)}) %collective-permute-start.23) | collective-permute-done | bytes 196640 | tf_op jit(solution)/shard_map/ppermute | solution.py:429
  222.7 1.6 collective-permute-done.25.refs_5_
  224.3 2.5 %collective-permute-done.26.refs_6_ = bf16[128,768]{1,0:T(8,128)(2,1)S(1)} collective-permute-done((bf16[128,768]{1,0:T(8,128)(2,1)S(1)}, bf16[128,768]{1,0:T(8,128)(2,1)S(1)}, u32[]{:S(2)}, u32[]{:S(2)}) %collective-permute-start.26) | collective-permute-done | bytes 196640 | tf_op jit(solution)/shard_map/ppermute | solution.py:429
  226.8 1.7 collective-permute-done.27.refs_7_
  228.6 0.7 copy-done.12
  229.3 3.4 %unpack.1 = (bf16[1,128,4096]{2,1,0:T(8,128)(2,1)}, bf16[1,128,1024]{2,1,0:T(8,128)(2,1)}, bf16[1,128,1024]{2,1,0:T(8,128)(2,1)}) custom-call(s32[10]{0:T(128)} %pad_add_fusion.ids_ref, bf16[128,768]{1,0:T(8,128)(2,1)} %get-tuple-element.40.refs_0_, bf16[128,768]{1,0:T(8,128)(2,1)} %copy-done.6, bf16[128,768]{1,0:T(8,128)(2,1)} %copy-done.7, ...), custom_call_target="tpu_custom_call" | custom-call | bytes 3145728 | tf_op jit(solution)/shard_map/unpack/pallas_call | solution.py:223
  232.7 2.0 all-to-all-done.2
  234.9 0.8 copy.15
  (99 shorter events, 1.8 us)
Async XLA Ops:
  0.6 26.8 %copy-start.14 = (s32[4]{0:T(128)S(1)}, s32[4]{0:T(128)}, u32[]{:S(2)}) copy-start(s32[4]{0:T(128)} %constant.68.clone) | copy-start | bytes 52
  0.6 26.8 %copy-start.15 = (s32[4]{0:T(128)S(1)}, s32[4]{0:T(128)}, u32[]{:S(2)}) copy-start(s32[4]{0:T(128)} %constant.67.clone) | copy-start | bytes 52
  0.7 25.2 %collective-permute-start.7 = (bf16[128,4096]{1,0:T(8,128)(2,1)}, bf16[128,4096]{1,0:T(8,128)(2,1)S(1)}, u32[]{:S(2)}, u32[]{:S(2)}) collective-permute-start(bf16[128,4096]{1,0:T(8,128)(2,1)} %bitcast.14), channel_id=1, source_target_pairs={{0,64},{32,96},{64,128},{96,160},{128,192},{160,224},{192,0},{224,... | collective-permute-start | bytes 3145736 | tf_op jit(solution)/shard_map/ppermute | solution.py:429
  2.2 25.3 %collective-permute-start.8 = (bf16[128,4096]{1,0:T(8,128)(2,1)}, bf16[128,4096]{1,0:T(8,128)(2,1)}, u32[]{:S(2)}, u32[]{:S(2)}) collective-permute-start(bf16[128,4096]{1,0:T(8,128)(2,1)} %bitcast.15), channel_id=1, source_target_pairs={{0,192},{32,224},{64,0},{96,32},{128,64},{160,96},{192,128},{224,1... | collective-permute-start | bytes 3145736 | tf_op jit(solution)/shard_map/ppermute | solution.py:429
  3.1 99.5 %collective-permute-start.11 = (bf16[128,4096]{1,0:T(8,128)(2,1)}, bf16[128,4096]{1,0:T(8,128)(2,1)}, u32[]{:S(2)}, u32[]{:S(2)}) collective-permute-start(bf16[128,4096]{1,0:T(8,128)(2,1)} %bitcast.16), channel_id=1, source_target_pairs={{0,32},{32,0},{64,96},{96,64},{128,160},{160,128},{192,224},{224,1... | collective-permute-start | bytes 3145736 | tf_op jit(solution)/shard_map/ppermute | solution.py:429
  25.8 21.2 %copy-start.5 = (bf16[128,4096]{1,0:T(8,128)(2,1)}, bf16[128,4096]{1,0:T(8,128)(2,1)S(1)}, u32[]{:S(2)}) copy-start(bf16[128,4096]{1,0:T(8,128)(2,1)S(1)} %collective-permute-done.7.refs_1_) | copy-start | bytes 3145732
  25.9 14.9 %collective-permute-start.9 = (bf16[64,4096]{1,0:T(8,128)(2,1)S(1)}, bf16[64,4096]{1,0:T(8,128)(2,1)S(1)}, u32[]{:S(2)}, u32[]{:S(2)}) collective-permute-start(bf16[64,4096]{1,0:T(8,128)(2,1)S(1)} %slice.8), channel_id=1, source_target_pairs={{0,64},{32,96},{64,128},{96,160},{128,192},{160,224},{192,0},{224,... | collective-permute-start | bytes 1572872 | tf_op jit(solution)/shard_map/ppermute | solution.py:429
  28.6 15.2 %collective-permute-start.10 = (bf16[64,4096]{1,0:T(8,128)(2,1)S(1)}, bf16[64,4096]{1,0:T(8,128)(2,1)S(1)}, u32[]{:S(2)}, u32[]{:S(2)}) collective-permute-start(bf16[64,4096]{1,0:T(8,128)(2,1)S(1)} %slice.9), channel_id=1, source_target_pairs={{0,192},{32,224},{64,0},{96,32},{128,64},{160,96},{192,128},{224,1... | collective-permute-start | bytes 1572872 | tf_op jit(solution)/shard_map/ppermute | solution.py:429
  33.1 11.5 %collective-permute-start = (bf16[128,768]{1,0:T(8,128)(2,1)}, bf16[128,768]{1,0:T(8,128)(2,1)S(1)}, u32[]{:S(2)}, u32[]{:S(2)}) collective-permute-start(bf16[128,768]{1,0:T(8,128)(2,1)} %get-tuple-element.33), channel_id=1, source_target_pairs={{0,64},{32,96},{64,128},{96,160},{128,192},{160,224},{192,0},{224,... | collective-permute-start | bytes 589832 | tf_op jit(solution)/shard_map/ppermute | solution.py:429
  34.6 12.4 %collective-permute-start.1 = (bf16[128,768]{1,0:T(8,128)(2,1)}, bf16[128,768]{1,0:T(8,128)(2,1)S(1)}, u32[]{:S(2)}, u32[]{:S(2)}) collective-permute-start(bf16[128,768]{1,0:T(8,128)(2,1)} %get-tuple-element.34), channel_id=1, source_target_pairs={{0,192},{32,224},{64,0},{96,32},{128,64},{160,96},{192,128},{224,1... | collective-permute-start | bytes 589832 | tf_op jit(solution)/shard_map/ppermute | solution.py:429
  40.8 9.6 %copy-start.13 = (bf16[128,512]{1,0:T(8,128)(2,1)S(1)}, bf16[128,512]{1,0:T(8,128)(2,1)}, u32[]{:S(2)}) copy-start(bf16[128,512]{1,0:T(8,128)(2,1)} %param.12) | copy-start | bytes 393220
  40.8 9.6 %collective-permute-start.2 = (bf16[128,768]{1,0:T(8,128)(2,1)}, bf16[128,768]{1,0:T(8,128)(2,1)S(1)}, u32[]{:S(2)}, u32[]{:S(2)}) collective-permute-start(bf16[128,768]{1,0:T(8,128)(2,1)} %get-tuple-element.35), channel_id=1, source_target_pairs={{0,128},{32,160},{64,192},{96,224},{128,0},{160,32},{192,64},{224,... | collective-permute-start | bytes 589832 | tf_op jit(solution)/shard_map/ppermute | solution.py:429
  43.7 16.1 %collective-permute-start.3 = (bf16[128,768]{1,0:T(8,128)(2,1)}, bf16[128,768]{1,0:T(8,128)(2,1)}, u32[]{:S(2)}, u32[]{:S(2)}) collective-permute-start(bf16[128,768]{1,0:T(8,128)(2,1)} %get-tuple-element.36), channel_id=1, source_target_pairs={{0,32},{32,0},{64,96},{96,64},{128,160},{160,128},{192,224},{224,1... | collective-permute-start | bytes 589832 | tf_op jit(solution)/shard_map/ppermute | solution.py:429
  44.6 15.1 %copy-start.16 = (s32[1,32]{1,0:T(1,128)S(1)}, s32[1,32]{1,0:T(1,128)}, u32[]{:S(2)}) copy-start(s32[1,32]{1,0:T(1,128)} %param.13) | copy-start | bytes 388
  44.6 40.3 %copy-start.20 = (bf16[128,768]{1,0:T(8,128)(2,1)}, bf16[128,768]{1,0:T(8,128)(2,1)S(1)}, u32[]{:S(2)}) copy-start(bf16[128,768]{1,0:T(8,128)(2,1)S(1)} %collective-permute-done.refs_1_) | copy-start | bytes 589828
  44.6 58.0 %collective-permute-start.13 = (bf16[128,4096]{1,0:T(8,128)(2,1)}, bf16[128,4096]{1,0:T(8,128)(2,1)S(1)}, u32[]{:S(2)}, u32[]{:S(2)}) collective-permute-start(bf16[128,4096]{1,0:T(8,128)(2,1)} %collective-permute-done.8.refs_2_), channel_id=1, source_target_pairs={{0,32},{32,0},{64,96},{96,64},{128,160},{160,128},{192,224},{224,1... | collective-permute-start | bytes 3145736 | tf_op jit(solution)/shard_map/ppermute | solution.py:429
  47.0 3.4 %copy-start.21 = (bf16[128,768]{1,0:T(8,128)(2,1)}, bf16[128,768]{1,0:T(8,128)(2,1)S(1)}, u32[]{:S(2)}) copy-start(bf16[128,768]{1,0:T(8,128)(2,1)S(1)} %collective-permute-done.1.refs_2_) | copy-start | bytes 589828
  47.0 55.5 %collective-permute-start.12 = (bf16[128,4096]{1,0:T(8,128)(2,1)S(1)}, bf16[128,4096]{1,0:T(8,128)(2,1)}, u32[]{:S(2)}, u32[]{:S(2)}) collective-permute-start(bf16[128,4096]{1,0:T(8,128)(2,1)S(1)} %collective-permute-done.7.refs_1_), channel_id=1, source_target_pairs={{0,32},{32,0},{64,96},{96,64},{128,160},{160,128},{192,224},{224,1... | collective-permute-start | bytes 3145736 | tf_op jit(solution)/shard_map/ppermute | solution.py:429
  50.3 34.5 %copy-start.22 = (bf16[128,768]{1,0:T(8,128)(2,1)}, bf16[128,768]{1,0:T(8,128)(2,1)S(1)}, u32[]{:S(2)}) copy-start(bf16[128,768]{1,0:T(8,128)(2,1)S(1)} %collective-permute-done.2.refs_3_) | copy-start | bytes 589828
  50.4 52.2 %collective-permute-start.14 = (bf16[128,4096]{1,0:T(8,128)(2,1)}, bf16[128,4096]{1,0:T(8,128)(2,1)}, u32[]{:S(2)}, u32[]{:S(2)}) collective-permute-start(bf16[128,4096]{1,0:T(8,128)(2,1)} %constant_dynamic-update-slice_fusion.refs_3_), channel_id=1, source_target_pairs={{0,32},{32,0},{64,96},{96,64},{128,160},{160,128},{192,224},{224,1... | collective-permute-start | bytes 3145736 | tf_op jit(solution)/shard_map/ppermute | solution.py:429
  51.2 41.9 %all-to-all-start = ((bf16[8,128,256]{2,1,0:T(8,128)(2,1)}), bf16[8,128,256]{2,1,0:T(8,128)(2,1)S(1)}, u32[]{:S(2)}, u32[]{:S(2)}) async-start(bf16[8,128,256]{2,1,0:T(8,128)(2,1)} %broadcast_in_dim.44), calls=%async_computation | async-start | bytes 1048576 | tf_op jit(solution)/shard_map/all_to_all | solution.py:424
  59.8 7.1 %collective-permute-start.4 = (bf16[128,768]{1,0:T(8,128)(2,1)}, bf16[128,768]{1,0:T(8,128)(2,1)S(1)}, u32[]{:S(2)}, u32[]{:S(2)}) collective-permute-start(bf16[128,768]{1,0:T(8,128)(2,1)} %get-tuple-element.37), channel_id=1, source_target_pairs={{0,96},{32,64},{64,160},{96,128},{128,224},{160,192},{192,32},{224... | collective-permute-start | bytes 589832 | tf_op jit(solution)/shard_map/ppermute | solution.py:429
  66.9 13.3 %copy-start.23 = (bf16[128,768]{1,0:T(8,128)(2,1)}, bf16[128,768]{1,0:T(8,128)(2,1)S(1)}, u32[]{:S(2)}) copy-start(bf16[128,768]{1,0:T(8,128)(2,1)S(1)} %collective-permute-done.4.refs_5_) | copy-start | bytes 589828
  66.9 6.8 %collective-permute-start.5 = (bf16[128,768]{1,0:T(8,128)(2,1)}, bf16[128,768]{1,0:T(8,128)(2,1)S(1)}, u32[]{:S(2)}, u32[]{:S(2)}) collective-permute-start(bf16[128,768]{1,0:T(8,128)(2,1)} %get-tuple-element.38), channel_id=1, source_target_pairs={{0,224},{32,192},{64,32},{96,0},{128,96},{160,64},{192,160},{224,1... | collective-permute-start | bytes 589832 | tf_op jit(solution)/shard_map/ppermute | solution.py:429
  73.7 10.5 %copy-start.24 = (bf16[128,768]{1,0:T(8,128)(2,1)}, bf16[128,768]{1,0:T(8,128)(2,1)S(1)}, u32[]{:S(2)}) copy-start(bf16[128,768]{1,0:T(8,128)(2,1)S(1)} %collective-permute-done.5.refs_6_) | copy-start | bytes 589828
  73.7 10.5 %collective-permute-start.6 = (bf16[128,768]{1,0:T(8,128)(2,1)}, bf16[128,768]{1,0:T(8,128)(2,1)S(1)}, u32[]{:S(2)}, u32[]{:S(2)}) collective-permute-start(bf16[128,768]{1,0:T(8,128)(2,1)} %get-tuple-element.39), channel_id=1, source_target_pairs={{0,160},{32,128},{64,224},{96,192},{128,32},{160,0},{192,96},{224,... | collective-permute-start | bytes 589832 | tf_op jit(solution)/shard_map/ppermute | solution.py:429
  93.2 27.8 %copy-start.1 = (bf16[8,128,256]{2,1,0:T(8,128)(2,1)}, bf16[8,128,256]{2,1,0:T(8,128)(2,1)S(1)}, u32[]{:S(2)}) copy-start(bf16[8,128,256]{2,1,0:T(8,128)(2,1)S(1)} %all-to-all-done.refs_8_) | copy-start | bytes 1572868
  94.1 28.2 %all-to-all-start.1 = ((bf16[8,128,256]{2,1,0:T(8,128)(2,1)}), bf16[8,128,256]{2,1,0:T(8,128)(2,1)S(1)}, u32[]{:S(2)}, u32[]{:S(2)}) async-start(bf16[8,128,256]{2,1,0:T(8,128)(2,1)} %broadcast_in_dim.45), calls=%async_computation.1 | async-start | bytes 1048576 | tf_op jit(solution)/shard_map/all_to_all | solution.py:424
  101.0 21.3 %collective-permute-start.19 = (bf16[8,128,256]{2,1,0:T(8,128)(2,1)S(1)}, bf16[8,128,256]{2,1,0:T(8,128)(2,1)}, u32[]{:S(2)}, u32[]{:S(2)}) collective-permute-start(bf16[8,128,256]{2,1,0:T(8,128)(2,1)S(1)} %all-to-all-done.refs_8_), channel_id=1, source_target_pairs={{0,1},{1,2},{2,3},{3,0},{4,5},{5,6},{6,7},{7,4},{8,9},{9,10},{10,1... | collective-permute-start | bytes 1572872 | tf_op jit(solution)/shard_map/ppermute | solution.py:412
  115.9 27.5 %collective-permute-start.28 = (bf16[4,512,128]{2,1,0:T(8,128)(2,1)}, bf16[4,512,128]{2,1,0:T(8,128)(2,1)S(1)}, u32[]{:S(2)}, u32[]{:S(2)}) collective-permute-start(bf16[4,512,128]{2,1,0:T(8,128)(2,1)} %get-tuple-element.53), channel_id=1, source_target_pairs={{0,1},{1,2},{2,3},{3,0},{4,5},{5,6},{6,7},{7,4},{8,9},{9,10},{10,1... | collective-permute-start | bytes 1572872 | tf_op jit(solution)/shard_map/ppermute | solution.py:412
  117.6 27.5 %collective-permute-start.29 = (bf16[4,512,128]{2,1,0:T(8,128)(2,1)}, bf16[4,512,128]{2,1,0:T(8,128)(2,1)S(1)}, u32[]{:S(2)}, u32[]{:S(2)}) collective-permute-start(bf16[4,512,128]{2,1,0:T(8,128)(2,1)} %get-tuple-element.55), channel_id=1, source_target_pairs={{0,3},{1,0},{2,1},{3,2},{4,7},{5,4},{6,5},{7,6},{8,11},{9,8},{10,9... | collective-permute-start | bytes 1572872 | tf_op jit(solution)/shard_map/ppermute | solution.py:412
  119.2 29.8 %collective-permute-start.17 = (bf16[8,128,256]{2,1,0:T(8,128)(2,1)S(1)}, bf16[8,128,256]{2,1,0:T(8,128)(2,1)S(1)}, u32[]{:S(2)}, u32[]{:S(2)}) collective-permute-start(bf16[8,128,256]{2,1,0:T(8,128)(2,1)S(1)} %all-to-all-done.refs_8_), channel_id=1, source_target_pairs={{0,2},{1,3},{2,0},{3,1},{4,6},{5,7},{6,4},{7,5},{8,10},{9,11},{10,... | collective-permute-start | bytes 1572872 | tf_op jit(solution)/shard_map/ppermute | solution.py:412
  121.0 44.1 %collective-permute-start.15 = (bf16[8,128,256]{2,1,0:T(8,128)(2,1)S(1)}, bf16[8,128,256]{2,1,0:T(8,128)(2,1)S(1)}, u32[]{:S(2)}, u32[]{:S(2)}) collective-permute-start(bf16[8,128,256]{2,1,0:T(8,128)(2,1)S(1)} %all-to-all-done.refs_8_), channel_id=1, source_target_pairs={{0,3},{1,0},{2,1},{3,2},{4,7},{5,4},{6,5},{7,6},{8,11},{9,8},{10,9... | collective-permute-start | bytes 1572872 | tf_op jit(solution)/shard_map/ppermute | solution.py:412
  122.3 26.8 %copy-start.2 = (bf16[8,128,256]{2,1,0:T(8,128)(2,1)}, bf16[8,128,256]{2,1,0:T(8,128)(2,1)S(1)}, u32[]{:S(2)}) copy-start(bf16[8,128,256]{2,1,0:T(8,128)(2,1)S(1)} %all-to-all-done.1.refs_9_) | copy-start | bytes 1572868
  122.3 48.4 %collective-permute-start.20 = (bf16[8,128,256]{2,1,0:T(8,128)(2,1)S(1)}, bf16[8,128,256]{2,1,0:T(8,128)(2,1)}, u32[]{:S(2)}, u32[]{:S(2)}) collective-permute-start(bf16[8,128,256]{2,1,0:T(8,128)(2,1)S(1)} %all-to-all-done.1.refs_9_), channel_id=1, source_target_pairs={{0,1},{1,2},{2,3},{3,0},{4,5},{5,6},{6,7},{7,4},{8,9},{9,10},{10,1... | collective-permute-start | bytes 1572872 | tf_op jit(solution)/shard_map/ppermute | solution.py:412
  143.4 3.2 %copy-start.3 = (bf16[4,512,128]{2,1,0:T(8,128)(2,1)}, bf16[4,512,128]{2,1,0:T(8,128)(2,1)S(1)}, u32[]{:S(2)}) copy-start(bf16[4,512,128]{2,1,0:T(8,128)(2,1)S(1)} %collective-permute-done.28.up_ref) | copy-start | bytes 1572868
  143.5 27.2 %collective-permute-start.18 = (bf16[8,128,256]{2,1,0:T(8,128)(2,1)S(1)}, bf16[8,128,256]{2,1,0:T(8,128)(2,1)}, u32[]{:S(2)}, u32[]{:S(2)}) collective-permute-start(bf16[8,128,256]{2,1,0:T(8,128)(2,1)S(1)} %all-to-all-done.1.refs_9_), channel_id=1, source_target_pairs={{0,2},{1,3},{2,0},{3,1},{4,6},{5,7},{6,4},{7,5},{8,10},{9,11},{10,... | collective-permute-start | bytes 1572872 | tf_op jit(solution)/shard_map/ppermute | solution.py:412
  145.0 1.6 copy-start.4
  145.1 32.7 %collective-permute-start.16 = (bf16[8,128,256]{2,1,0:T(8,128)(2,1)S(1)}, bf16[8,128,256]{2,1,0:T(8,128)(2,1)}, u32[]{:S(2)}, u32[]{:S(2)}) collective-permute-start(bf16[8,128,256]{2,1,0:T(8,128)(2,1)S(1)} %all-to-all-done.1.refs_9_), channel_id=1, source_target_pairs={{0,3},{1,0},{2,1},{3,2},{4,7},{5,4},{6,5},{7,6},{8,11},{9,8},{10,9... | collective-permute-start | bytes 1572872 | tf_op jit(solution)/shard_map/ppermute | solution.py:412
  149.1 16.0 %copy-start.18 = (bf16[8,128,256]{2,1,0:T(8,128)(2,1)}, bf16[8,128,256]{2,1,0:T(8,128)(2,1)S(1)}, u32[]{:S(2)}) copy-start(bf16[8,128,256]{2,1,0:T(8,128)(2,1)S(1)} %collective-permute-done.17.refs_12_) | copy-start | bytes 1572868
  149.1 51.9 %collective-permute-start.30 = (bf16[8,512,128]{2,1,0:T(8,128)(2,1)}, bf16[8,512,128]{2,1,0:T(8,128)(2,1)S(1)}, u32[]{:S(2)}, u32[]{:S(2)}) collective-permute-start(bf16[8,512,128]{2,1,0:T(8,128)(2,1)} %get-tuple-element.56), channel_id=1, source_target_pairs={{0,1},{1,2},{2,3},{3,0},{4,5},{5,6},{6,7},{7,4},{8,9},{9,10},{10,1... | collective-permute-start | bytes 3145736 | tf_op jit(solution)/shard_map/ppermute | solution.py:412
  165.9 35.1 %collective-permute-start.31 = (bf16[8,512,128]{2,1,0:T(8,128)(2,1)}, bf16[8,512,128]{2,1,0:T(8,128)(2,1)S(1)}, u32[]{:S(2)}, u32[]{:S(2)}) collective-permute-start(bf16[8,512,128]{2,1,0:T(8,128)(2,1)} %get-tuple-element.57), channel_id=1, source_target_pairs={{0,3},{1,0},{2,1},{3,2},{4,7},{5,4},{6,5},{7,6},{8,11},{9,8},{10,9... | collective-permute-start | bytes 3145736 | tf_op jit(solution)/shard_map/ppermute | solution.py:412
  187.8 13.2 %copy-start = (bf16[8,512,128]{2,1,0:T(8,128)(2,1)S(1)}, bf16[8,512,128]{2,1,0:T(8,128)(2,1)}, u32[]{:S(2)}) copy-start(bf16[8,512,128]{2,1,0:T(8,128)(2,1)} %get-tuple-element.51) | copy-start | bytes 3145732
  202.5 7.4 %copy-start.32 = (bf16[128,768]{1,0:T(8,128)(2,1)S(1)}, bf16[128,768]{1,0:T(8,128)(2,1)}, u32[]{:S(2)}) copy-start(bf16[128,768]{1,0:T(8,128)(2,1)} %get-tuple-element.41) | copy-start | bytes 589828
  202.5 7.5 %copy-start.31 = (bf16[128,768]{1,0:T(8,128)(2,1)S(1)}, bf16[128,768]{1,0:T(8,128)(2,1)}, u32[]{:S(2)}) copy-start(bf16[128,768]{1,0:T(8,128)(2,1)} %get-tuple-element.42) | copy-start | bytes 589828
  202.5 9.5 %copy-start.30 = (bf16[128,768]{1,0:T(8,128)(2,1)S(1)}, bf16[128,768]{1,0:T(8,128)(2,1)}, u32[]{:S(2)}) copy-start(bf16[128,768]{1,0:T(8,128)(2,1)} %get-tuple-element.43) | copy-start | bytes 589828
  202.5 13.2 %copy-start.29 = (bf16[128,768]{1,0:T(8,128)(2,1)S(1)}, bf16[128,768]{1,0:T(8,128)(2,1)}, u32[]{:S(2)}) copy-start(bf16[128,768]{1,0:T(8,128)(2,1)} %get-tuple-element.44) | copy-start | bytes 589828
  202.5 13.2 %copy-start.28 = (bf16[128,768]{1,0:T(8,128)(2,1)S(1)}, bf16[128,768]{1,0:T(8,128)(2,1)}, u32[]{:S(2)}) copy-start(bf16[128,768]{1,0:T(8,128)(2,1)} %get-tuple-element.45) | copy-start | bytes 589828
  202.5 14.3 %copy-start.27 = (bf16[128,768]{1,0:T(8,128)(2,1)S(1)}, bf16[128,768]{1,0:T(8,128)(2,1)}, u32[]{:S(2)}) copy-start(bf16[128,768]{1,0:T(8,128)(2,1)} %get-tuple-element.46) | copy-start | bytes 589828
  202.5 15.7 %copy-start.26 = (bf16[128,768]{1,0:T(8,128)(2,1)S(1)}, bf16[128,768]{1,0:T(8,128)(2,1)}, u32[]{:S(2)}) copy-start(bf16[128,768]{1,0:T(8,128)(2,1)} %get-tuple-element.47) | copy-start | bytes 589828
  202.5 32.3 %all-to-all-start.2 = ((bf16[8,512,128]{2,1,0:T(8,128)(2,1)}), bf16[8,512,128]{2,1,0:T(8,128)(2,1)S(1)}, u32[]{:S(2)}, u32[]{:S(2)}) async-start(bf16[8,512,128]{2,1,0:T(8,128)(2,1)} %add_convert_fusion), calls=%async_computation.2 | async-start | bytes 2097152 | tf_op jit(solution)/shard_map/all_to_all | solution.py:424
  209.9 6.9 %collective-permute-start.21 = (bf16[128,768]{1,0:T(8,128)(2,1)S(1)}, bf16[128,768]{1,0:T(8,128)(2,1)S(1)}, u32[]{:S(2)}, u32[]{:S(2)}) collective-permute-start(bf16[128,768]{1,0:T(8,128)(2,1)S(1)} %copy-done.32), channel_id=1, source_target_pairs={{0,64},{32,96},{64,128},{96,160},{128,192},{160,224},{192,0},{224,... | collective-permute-start | bytes 589832 | tf_op jit(solution)/shard_map/ppermute | solution.py:429
  210.0 8.2 %collective-permute-start.22 = (bf16[128,768]{1,0:T(8,128)(2,1)S(1)}, bf16[128,768]{1,0:T(8,128)(2,1)S(1)}, u32[]{:S(2)}, u32[]{:S(2)}) collective-permute-start(bf16[128,768]{1,0:T(8,128)(2,1)S(1)} %copy-done.31), channel_id=1, source_target_pairs={{0,192},{32,224},{64,0},{96,32},{128,64},{160,96},{192,128},{224,1... | collective-permute-start | bytes 589832 | tf_op jit(solution)/shard_map/ppermute | solution.py:429
  212.0 10.7 %collective-permute-start.23 = (bf16[128,768]{1,0:T(8,128)(2,1)S(1)}, bf16[128,768]{1,0:T(8,128)(2,1)S(1)}, u32[]{:S(2)}, u32[]{:S(2)}) collective-permute-start(bf16[128,768]{1,0:T(8,128)(2,1)S(1)} %copy-done.30), channel_id=1, source_target_pairs={{0,128},{32,160},{64,192},{96,224},{128,0},{160,32},{192,64},{224,... | collective-permute-start | bytes 589832 | tf_op jit(solution)/shard_map/ppermute | solution.py:429
  215.7 7.0 %collective-permute-start.24 = (bf16[128,768]{1,0:T(8,128)(2,1)S(1)}, bf16[128,768]{1,0:T(8,128)(2,1)S(1)}, u32[]{:S(2)}, u32[]{:S(2)}) collective-permute-start(bf16[128,768]{1,0:T(8,128)(2,1)S(1)} %copy-done.29), channel_id=1, source_target_pairs={{0,32},{32,0},{64,96},{96,64},{128,160},{160,128},{192,224},{224,1... | collective-permute-start | bytes 589832 | tf_op jit(solution)/shard_map/ppermute | solution.py:429
  215.7 8.6 %collective-permute-start.25 = (bf16[128,768]{1,0:T(8,128)(2,1)S(1)}, bf16[128,768]{1,0:T(8,128)(2,1)S(1)}, u32[]{:S(2)}, u32[]{:S(2)}) collective-permute-start(bf16[128,768]{1,0:T(8,128)(2,1)S(1)} %copy-done.28), channel_id=1, source_target_pairs={{0,96},{32,64},{64,160},{96,128},{128,224},{160,192},{192,32},{224... | collective-permute-start | bytes 589832 | tf_op jit(solution)/shard_map/ppermute | solution.py:429
  216.8 11.8 %copy-start.6 = (bf16[128,768]{1,0:T(8,128)(2,1)}, bf16[128,768]{1,0:T(8,128)(2,1)S(1)}, u32[]{:S(2)}) copy-start(bf16[128,768]{1,0:T(8,128)(2,1)S(1)} %collective-permute-done.21.refs_1_) | copy-start | bytes 589828
  216.8 10.0 %collective-permute-start.26 = (bf16[128,768]{1,0:T(8,128)(2,1)S(1)}, bf16[128,768]{1,0:T(8,128)(2,1)S(1)}, u32[]{:S(2)}, u32[]{:S(2)}) collective-permute-start(bf16[128,768]{1,0:T(8,128)(2,1)S(1)} %copy-done.27), channel_id=1, source_target_pairs={{0,224},{32,192},{64,32},{96,0},{128,96},{160,64},{192,160},{224,1... | collective-permute-start | bytes 589832 | tf_op jit(solution)/shard_map/ppermute | solution.py:429
  218.2 10.4 %copy-start.7 = (bf16[128,768]{1,0:T(8,128)(2,1)}, bf16[128,768]{1,0:T(8,128)(2,1)S(1)}, u32[]{:S(2)}) copy-start(bf16[128,768]{1,0:T(8,128)(2,1)S(1)} %collective-permute-done.22.refs_2_) | copy-start | bytes 589828
  218.2 10.4 %collective-permute-start.27 = (bf16[128,768]{1,0:T(8,128)(2,1)S(1)}, bf16[128,768]{1,0:T(8,128)(2,1)S(1)}, u32[]{:S(2)}, u32[]{:S(2)}) collective-permute-start(bf16[128,768]{1,0:T(8,128)(2,1)S(1)} %copy-done.26), channel_id=1, source_target_pairs={{0,160},{32,128},{64,224},{96,192},{128,32},{160,0},{192,96},{224,... | collective-permute-start | bytes 589832 | tf_op jit(solution)/shard_map/ppermute | solution.py:429
  222.7 5.9 %copy-start.8 = (bf16[128,768]{1,0:T(8,128)(2,1)}, bf16[128,768]{1,0:T(8,128)(2,1)S(1)}, u32[]{:S(2)}) copy-start(bf16[128,768]{1,0:T(8,128)(2,1)S(1)} %collective-permute-done.23.refs_3_) | copy-start | bytes 589828
  222.7 5.9 %copy-start.9 = (bf16[128,768]{1,0:T(8,128)(2,1)}, bf16[128,768]{1,0:T(8,128)(2,1)S(1)}, u32[]{:S(2)}) copy-start(bf16[128,768]{1,0:T(8,128)(2,1)S(1)} %collective-permute-done.24.refs_4_) | copy-start | bytes 589828
  224.3 4.3 %copy-start.10 = (bf16[128,768]{1,0:T(8,128)(2,1)}, bf16[128,768]{1,0:T(8,128)(2,1)S(1)}, u32[]{:S(2)}) copy-start(bf16[128,768]{1,0:T(8,128)(2,1)S(1)} %collective-permute-done.25.refs_5_) | copy-start | bytes 589828
  226.8 1.8 copy-start.11
  (4 other events, 3.2 us)

commit v4 on v2

--- a/solution.py
+++ b/solution.py
@@ -310,8 +310,9 @@
 
 
 def proj_kernel(ids_ref, *refs):
-    pieces, refs = refs[:-8], refs[-8:]
-    ot_ref, same_ref, next_ref, low_ref, high_ref, last_ref, lhs_ref, out_ref = refs
+    pieces, refs = refs[:-9], refs[-9:]
+    ot_ref, same_ref, next_ref, low_ref, high_ref, last_ref, side_ref, lhs_ref, out_ref = refs
+    split = same_ref.shape[1]
     count = len(pieces)
     near = GRID["fsdp"]
     step = pl.program_id(0)
@@ -325,9 +326,15 @@
     rows = jnp.concatenate([piece[...] for piece in pieces], 0)
     out_ref[...] = jnp.dot(lhs_ref[...], rows, preferred_element_type=F32).astype(BF16)
 
+    def columns(offset):
+        t = lax.rem(ids_ref[count + 1] + offset, near)
+        return pl.ds(pl.multiple_of(t * TOK, TOK), TOK)
+
     def part(offset):
-        t = lax.rem(ids_ref[count + 1] + offset, near)
-        return out_ref[:, pl.ds(pl.multiple_of(t * TOK, TOK), TOK)]
+        return out_ref[:split, columns(offset)]
+
+    for offset in range(near):
+        side_ref[0, offset] = out_ref[split:, columns(offset)]
 
     same_ref[0] = part(0)
     next_ref[0] = part(1)
@@ -347,13 +354,15 @@
     far, near = GRID["dp"], GRID["fsdp"]
     depth = pieces[0].shape[1]
     middle = far // 2
-    block = (1, width, TOK)
+    split = width * 3 // 4
+    block = (1, split, TOK)
 
     def plane(i, ids):
         return (i, 0, 0)
 
-    full = jax.ShapeDtypeStruct((far, width, TOK), BF16)
-    part = jax.ShapeDtypeStruct((middle, width, TOK), BF16)
+    full = jax.ShapeDtypeStruct((far, split, TOK), BF16)
+    part = jax.ShapeDtypeStruct((middle, split, TOK), BF16)
+    side = jax.ShapeDtypeStruct((far, near, width - split, TOK), BF16)
     return pl.pallas_call(
         proj_kernel,
         grid_spec=pltpu.PrefetchScalarGridSpec(
@@ -367,13 +376,14 @@
                 pl.BlockSpec(block, lambda i, ids: (jnp.minimum(i, middle - 1), 0, 0)),
                 pl.BlockSpec(block, lambda i, ids: (jnp.maximum(i - middle, 0), 0, 0)),
                 pl.BlockSpec(block, plane),
+                pl.BlockSpec((1, near, width - split, TOK), lambda i, ids: (i, 0, 0, 0)),
             ],
             scratch_shapes=[
                 pltpu.VMEM((width, count * TOK), BF16),
                 pltpu.VMEM((width, near * TOK), BF16),
             ],
         ),
-        out_shape=[full, full, part, part, full],
+        out_shape=[full, full, part, part, full, side],
         cost_estimate=pl.CostEstimate(
             flops=2 * count * TOK * width * depth,
             bytes_accessed=2 * (count * TOK * (depth + width) + depth * width),
@@ -471,7 +481,8 @@
     output = attend(ids, packed, lo, hi)
     pieces = [own, left, right, across, partner]
     pieces += [hop(piece, 0, 1) for piece in (left, right, across)]
-    same, following, low, high, before = proj_terms(ids, pieces, output)
+    same, following, low, high, before, side = proj_terms(ids, pieces, output)
+    side = swap(side, "dp")
     up, down = shift(low, "fsdp", 1), shift(high, "fsdp", -1)
     below, above = after((below, above), low)
     ends = [shift(below[:far], "fsdp", 1), shift(above[far:], "fsdp", -1)]
@@ -479,11 +490,15 @@
     up, down = shift(following, "fsdp", 1), shift(before, "fsdp", -1)
     arriving = upstream(ids, pieces, [weight, below, above, *ends])
     grads = attend_grad(jnp.concatenate([ids, targets]), packed, arriving, lo, hi)
-    up, down = after((up, down), grads[0])
+    side = after(side, arriving)
     first = (same.astype(F32) + up.astype(F32) + down.astype(F32)).astype(BF16)
     first = swap(first, "dp")
     grads = [grads[0]] + [hop(x, *path) for x, path in zip(grads[1:], paths[1:])]
-    proj_grad = jnp.sum(first.astype(F32), axis=0).T.astype(BF16)
+    side = jnp.sum(side.astype(F32), axis=0)
+    own_side, side = side[0], side.astype(BF16)
+    side = [shift(side[by], "fsdp", by).astype(F32) for by in (1, 2, 3)]
+    proj_grad = [jnp.sum(first.astype(F32), axis=0), own_side + side[0] + side[1] + side[2]]
+    proj_grad = jnp.concatenate(proj_grad, 0).T.astype(BF16)
     query_grad, key_gradient, value_gradient = unpack(ids, grads)
     return (query_grad, key_gradient, value_gradient, proj_grad)
 

time: 192 us -> 234 us (1.22)
  the two profiles are of different devices: /device:TPU:2 before, /device:TPU:1 now
where the time goes in v4:
time: 234 us; the launch traced here: 233 us
  waiting for transfers between devices  87.7 us (37%)
  starting transfers between devices  76.5 us (33%)
  Pallas kernels  52.8 us (23%)
  local copies, waits for them, and re-layouts  11.7 us (5%)
  other arithmetic  3.6 us (2%)
    ppermute x22, waiting for transfers between devices, hop(): return lax.ppermute(x, 'seq', pairs)  43.9 us
    ppermute x11, waiting for transfers between devices, shift(): return lax.ppermute(x, axis, [(i, (i + by) % n) for i in range(n)])  43.8 us
    ppermute x22, starting transfers between devices, hop(): return lax.ppermute(x, 'seq', pairs)  32.1 us
    all_to_all x3, starting transfers between devices, swap(): return lax.all_to_all(x, axis, split_axis=0, concat_axis=0, tiled=True)  22.7 us
    ppermute x11, starting transfers between devices, shift(): return lax.ppermute(x, axis, [(i, (i + by) % n) for i in range(n)])  21.7 us
    pallas_call x1, Pallas kernels, attend_grad(): pl.pallas_call(bwd_kernel, grid_spec=pltpu.PrefetchScalarGridSpec(num_sca...  13.1 us
    pallas_call x1, Pallas kernels, proj_terms(): pl.pallas_call(proj_kernel, grid_spec=pltpu.PrefetchScalarGridSpec(num_sc...  12.3 us
    pallas_call x1, Pallas kernels, upstream(): pl.pallas_call(upstream_kernel, grid_spec=pltpu.PrefetchScalarGridSpec(nu...  10.1 us
  transfers between devices with their start and end apart: 36, of which 10 were waited for; matrix products, arithmetic and copies ran while one was open for 5% of the time, Pallas kernels for 23%

profile of v4, /device:TPU:1, one launch (start us, length us, event | category | flops | bytes accessed | tf_op | source)
XLA Modules:
  0.0 233.3 jit_solution(10854749510440754661)
XLA Ops:
  0.7 2.1 collective-permute-start.7
  2.8 1.4 collective-permute-start.8
  4.1 3.0 %collective-permute-start.11 = (bf16[128,4096]{1,0:T(8,128)(2,1)}, bf16[128,4096]{1,0:T(8,128)(2,1)}, u32[]{:S(2)}, u32[]{:S(2)}) collective-permute-start(bf16[128,4096]{1,0:T(8,128)(2,1)} %bitcast.32), channel_id=1, source_target_pairs={{0,32},{32,0},{64,96},{96,64},{128,160},{160,128},{192,224},{224,1... | collective-permute-start | bytes 3145736 | tf_op jit(solution)/shard_map/ppermute | solution.py:449
  7.2 17.9 %collective-permute-done.7.refs_1_ = bf16[128,4096]{1,0:T(8,128)(2,1)} collective-permute-done((bf16[128,4096]{1,0:T(8,128)(2,1)}, bf16[128,4096]{1,0:T(8,128)(2,1)}, u32[]{:S(2)}, u32[]{:S(2)}) %collective-permute-start.7) | collective-permute-done | bytes 1048608 | tf_op jit(solution)/shard_map/ppermute | solution.py:449
  25.0 1.1 slice.32
  26.1 1.9 collective-permute-start.9
  28.1 1.1 slice.33
  29.2 1.6 collective-permute-start.10
  30.8 0.6 pad_add_fusion.1.ids_ref
  31.4 3.4 %pack.1 = (bf16[128,768]{1,0:T(8,128)(2,1)}, bf16[128,768]{1,0:T(8,128)(2,1)}, bf16[128,768]{1,0:T(8,128)(2,1)}, bf16[128,768]{1,0:T(8,128)(2,1)}, bf16[128,768]...) custom-call(s32[8]{0:T(128)} %pad_add_fusion.1.ids_ref, ...), custom_call_target="tpu_custom_call" | custom-call | bytes 3145728 | tf_op jit(solution)/shard_map/pack/pallas_call | solution.py:195
  34.7 2.7 %collective-permute-start.1 = (bf16[128,768]{1,0:T(8,128)(2,1)}, bf16[128,768]{1,0:T(8,128)(2,1)}, u32[]{:S(2)}, u32[]{:S(2)}) collective-permute-start(bf16[128,768]{1,0:T(8,128)(2,1)} %get-tuple-element.36), channel_id=1, source_target_pairs={{0,192},{32,224},{64,0},{96,32},{128,64},{160,96},{192,128},{224,1... | collective-permute-start | bytes 589832 | tf_op jit(solution)/shard_map/ppermute | solution.py:449
  37.4 1.1 broadcast_in_dim.41
  38.5 9.6 %all-to-all-start = ((bf16[8,128,512]{2,1,0:T(8,128)(2,1)}), bf16[8,128,512]{2,1,0:T(8,128)(2,1)S(1)}, u32[]{:S(2)}, u32[]{:S(2)}) async-start(bf16[8,128,512]{2,1,0:T(8,128)(2,1)} %broadcast_in_dim.41), calls=%async_computation | async-start | bytes 2097152 | tf_op jit(solution)/shard_map/all_to_all | solution.py:444
  48.2 0.8 constant_dynamic-update-slice_fusion.1
  49.0 2.9 %collective-permute-start.12 = (bf16[128,4096]{1,0:T(8,128)(2,1)}, bf16[128,4096]{1,0:T(8,128)(2,1)}, u32[]{:S(2)}, u32[]{:S(2)}) collective-permute-start(bf16[128,4096]{1,0:T(8,128)(2,1)} %collective-permute-done.7.refs_1_), channel_id=1, source_target_pairs={{0,32},{32,0},{64,96},{96,64},{128,160},{160,128},{192,224},{224,1... | collective-permute-start | bytes 3145736 | tf_op jit(solution)/shard_map/ppermute | solution.py:449
  51.9 0.8 constant_dynamic-update-slice_fusion.refs_3_
  52.8 0.5 collective-permute-start.14
  53.3 1.2 collective-permute-done.2.refs_3_
  54.5 4.1 %collective-permute-start.3 = (bf16[128,768]{1,0:T(8,128)(2,1)}, bf16[128,768]{1,0:T(8,128)(2,1)S(1)}, u32[]{:S(2)}, u32[]{:S(2)}) collective-permute-start(bf16[128,768]{1,0:T(8,128)(2,1)} %get-tuple-element.38), channel_id=1, source_target_pairs={{0,32},{32,0},{64,96},{96,64},{128,160},{160,128},{192,224},{224,1... | collective-permute-start | bytes 589832 | tf_op jit(solution)/shard_map/ppermute | solution.py:449
  58.6 0.1 select_reduce_fusion.2
  58.7 1.2 collective-permute-done.3.refs_4_
  59.9 8.5 %collective-permute-done.4.refs_5_ = bf16[128,768]{1,0:T(8,128)(2,1)S(1)} collective-permute-done((bf16[128,768]{1,0:T(8,128)(2,1)}, bf16[128,768]{1,0:T(8,128)(2,1)S(1)}, u32[]{:S(2)}, u32[]{:S(2)}) %collective-permute-start.4) | collective-permute-done | bytes 196640 | tf_op jit(solution)/shard_map/ppermute | solution.py:449
  68.5 7.1 %collective-permute-done.5.refs_6_ = bf16[128,768]{1,0:T(8,128)(2,1)S(1)} collective-permute-done((bf16[128,768]{1,0:T(8,128)(2,1)}, bf16[128,768]{1,0:T(8,128)(2,1)S(1)}, u32[]{:S(2)}, u32[]{:S(2)}) %collective-permute-start.5) | collective-permute-done | bytes 196640 | tf_op jit(solution)/shard_map/ppermute | solution.py:449
  75.5 0.6 pad_add_fusion.ids_ref
  76.1 0.7 select_reduce_fusion
  76.8 6.7 %collective-permute-done.6.refs_7_ = bf16[128,768]{1,0:T(8,128)(2,1)S(1)} collective-permute-done((bf16[128,768]{1,0:T(8,128)(2,1)}, bf16[128,768]{1,0:T(8,128)(2,1)S(1)}, u32[]{:S(2)}, u32[]{:S(2)}) %collective-permute-start.6) | collective-permute-done | bytes 196640 | tf_op jit(solution)/shard_map/ppermute | solution.py:449
  83.6 0.7 copy-done.21
  84.2 8.2 %attend.1.refs_8_ = bf16[8,512,128]{2,1,0:T(8,128)(2,1)} custom-call(s32[10]{0:T(128)} %pad_add_fusion.ids_ref, bf16[128,768]{1,0:T(8,128)(2,1)} %get-tuple-element.34.refs_0_, bf16[128,768]{1,0:T(8,128)(2,1)} %copy-done.17, bf16[128,768]{1,0:T(8,128)(2,1)} %collective-permute-done.1.refs_2_, bf16[128,768]{1,0:T(8,128)(2,1)} %collective-permute-done.2.refs_3_, ...), custom_call_target="tpu_custom_call" | custom-call | flops 939524096 | bytes 3145728 | tf_op jit(solution)/shard_map/attend/pallas_call | solution.py:138
  92.5 1.0 copy-done.15
  93.5 12.3 %proj_terms.1 = (bf16[8,384,128]{2,1,0:T(8,128)(2,1)}, bf16[8,384,128]{2,1,0:T(8,128)(2,1)}, bf16[4,384,128]{2,1,0:T(8,128)(2,1)}, bf16[4,384,128]{2,1,0:T(8,128...) custom-call(s32[10]{0:T(128)} %pad_add_fusion.ids_ref, bf16[128,4096]{1,0:T(8,128)(2,1)} %bitcast.33, ...), custom_call_target="tpu_custom_call" | custom-call | flops 4294967296 | bytes 13631488 | tf_op jit(solution)/shard_map/proj_terms/pallas_call | solution.py:366
  105.8 7.1 %all-to-all-start.2 = ((bf16[8,4,128,128]{3,2,1,0:T(8,128)(2,1)}), bf16[8,4,128,128]{3,2,1,0:T(8,128)(2,1)S(1)}, u32[]{:S(2)}, u32[]{:S(2)}) async-start(bf16[8,4,128,128]{3,2,1,0:T(8,128)(2,1)} %get-tuple-element.62), calls=%async_computation.2 | async-start | bytes 2097152 | tf_op jit(solution)/shard_map/all_to_all | solution.py:444
  112.9 1.3 collective-permute-start.15
  114.2 1.5 collective-permute-start.16
  115.8 2.7 %collective-permute-start.27 = (bf16[4,384,128]{2,1,0:T(8,128)(2,1)S(1)}, bf16[4,384,128]{2,1,0:T(8,128)(2,1)S(1)}, u32[]{:S(2)}, u32[]{:S(2)}) collective-permute-start(bf16[4,384,128]{2,1,0:T(8,128)(2,1)S(1)} %copy-done.16), channel_id=1, source_target_pairs={{0,3},{1,0},{2,1},{3,2},{4,7},{5,4},{6,5},{7,6},{8,11},{9,8},{10,9... | collective-permute-start | bytes 1179656 | tf_op jit(solution)/shard_map/ppermute | solution.py:432
  118.4 28.6 %collective-permute-done.26.up_ref = bf16[4,384,128]{2,1,0:T(8,128)(2,1)S(1)} collective-permute-done((bf16[4,384,128]{2,1,0:T(8,128)(2,1)}, bf16[4,384,128]{2,1,0:T(8,128)(2,1)S(1)}, u32[]{:S(2)}, u32[]{:S(2)}) %collective-permute-start.26) | collective-permute-done | bytes 393248 | tf_op jit(solution)/shard_map/ppermute | solution.py:432
  147.1 0.7 copy-done.2
  147.8 0.2 copy-done.3
  148.0 2.3 join.1
  150.2 0.9 collective-permute-start.28
  151.1 1.8 collective-permute-start.29
  152.9 1.1 slice.26
  154.1 1.1 slice.27
  155.2 2.7 %collective-permute-start.18 = (bf16[4,128,512]{2,1,0:T(8,128)(2,1)S(1)}, bf16[4,128,512]{2,1,0:T(8,128)(2,1)}, u32[]{:S(2)}, u32[]{:S(2)}) collective-permute-start(bf16[4,128,512]{2,1,0:T(8,128)(2,1)S(1)} %slice.27), channel_id=1, source_target_pairs={{0,3},{1,0},{2,1},{3,2},{4,7},{5,4},{6,5},{7,6},{8,11},{9,8},{10,9... | collective-permute-start | bytes 1572872 | tf_op jit(solution)/shard_map/ppermute | solution.py:432
  157.9 11.7 %collective-permute-done.28 = bf16[8,384,128]{2,1,0:T(8,128)(2,1)S(1)} collective-permute-done((bf16[8,384,128]{2,1,0:T(8,128)(2,1)}, bf16[8,384,128]{2,1,0:T(8,128)(2,1)S(1)}, u32[]{:S(2)}, u32[]{:S(2)}) %collective-permute-start.28) | collective-permute-done | bytes 786464 | tf_op jit(solution)/shard_map/ppermute | solution.py:432
  169.6 1.2 add_convert_fusion
  170.8 6.1 %all-to-all-start.1 = ((bf16[8,384,128]{2,1,0:T(8,128)(2,1)}), bf16[8,384,128]{2,1,0:T(8,128)(2,1)S(1)}, u32[]{:S(2)}, u32[]{:S(2)}) async-start(bf16[8,384,128]{2,1,0:T(8,128)(2,1)} %add_convert_fusion), calls=%async_computation.1 | async-start | bytes 1572864 | tf_op jit(solution)/shard_map/all_to_all | solution.py:444
  176.9 0.6 concatenate.18.ids_ref
  177.5 3.5 %collective-permute-done.17.refs_11_ = bf16[4,128,512]{2,1,0:T(8,128)(2,1)} collective-permute-done((bf16[4,128,512]{2,1,0:T(8,128)(2,1)S(1)}, bf16[4,128,512]{2,1,0:T(8,128)(2,1)}, u32[]{:S(2)}, u32[]{:S(2)}) %collective-permute-start.17) | collective-permute-done | bytes 524320 | tf_op jit(solution)/shard_map/ppermute | solution.py:432
  181.0 10.1 %upstream.1.refs_8_ = bf16[8,128,512]{2,1,0:T(8,128)(2,1)} custom-call(s32[10]{0:T(128)} %pad_add_fusion.ids_ref, bf16[128,4096]{1,0:T(8,128)(2,1)} %bitcast.34, bf16[128,4096]{1,0:T(8,128)(2,1)} %collective-permute-done.7.refs_1_, bf16[128,4096]{1,0:T(8,128)(2,1)} %collective-permute-done.8.refs_2_, ...), custom_call_target="tpu_custom_call" | custom-call | flops 4294967296 | bytes 13631488 | tf_op jit(solution)/shard_map/upstream/pallas_call | solution.py:285
  191.1 13.1 %attend_grad.1 = (bf16[128,768]{1,0:T(8,128)(2,1)}, bf16[128,768]{1,0:T(8,128)(2,1)}, bf16[128,768]{1,0:T(8,128)(2,1)}, bf16[128,768]{1,0:T(8,128)(2,1)}, bf16[1...) custom-call(s32[18]{0:T(128)} %concatenate.18.ids_ref, ...), custom_call_target="tpu_custom_call" | custom-call | flops 2348810240 | bytes 4718592 | tf_op jit(solution)/shard_map/attend_grad/pallas_call | solution.py:161
  204.2 2.7 %collective-permute-start.20 = (bf16[128,768]{1,0:T(8,128)(2,1)}, bf16[128,768]{1,0:T(8,128)(2,1)S(1)}, u32[]{:S(2)}, u32[]{:S(2)}) collective-permute-start(bf16[128,768]{1,0:T(8,128)(2,1)} %get-tuple-element.47), channel_id=1, source_target_pairs={{0,192},{32,224},{64,0},{96,32},{128,64},{160,96},{192,128},{224,1... | collective-permute-start | bytes 589832 | tf_op jit(solution)/shard_map/ppermute | solution.py:449
  206.9 2.6 %collective-permute-start.22 = (bf16[128,768]{1,0:T(8,128)(2,1)}, bf16[128,768]{1,0:T(8,128)(2,1)S(1)}, u32[]{:S(2)}, u32[]{:S(2)}) collective-permute-start(bf16[128,768]{1,0:T(8,128)(2,1)} %get-tuple-element.49), channel_id=1, source_target_pairs={{0,32},{32,0},{64,96},{96,64},{128,160},{160,128},{192,224},{224,1... | collective-permute-start | bytes 589832 | tf_op jit(solution)/shard_map/ppermute | solution.py:449
  209.5 0.9 collective-permute-start.23
  210.3 0.1 convert_reduce_fusion
  210.5 5.3 %collective-permute-start.24 = (bf16[128,768]{1,0:T(8,128)(2,1)S(1)}, bf16[128,768]{1,0:T(8,128)(2,1)S(1)}, u32[]{:S(2)}, u32[]{:S(2)}) collective-permute-start(bf16[128,768]{1,0:T(8,128)(2,1)S(1)} %copy-done.23), channel_id=1, source_target_pairs={{0,224},{32,192},{64,32},{96,0},{128,96},{160,64},{192,160},{224,1... | collective-permute-start | bytes 589832 | tf_op jit(solution)/shard_map/ppermute | solution.py:449
  215.8 0.3 collective-permute-start.25
  216.2 0.5 collective-permute-start.30
  216.7 3.4 %collective-permute-start.31 = (bf16[128,128]{1,0:T(8,128)(2,1)S(1)}, bf16[128,128]{1,0:T(8,128)(2,1)S(1)}, u32[]{:S(2)}, u32[]{:S(2)}) collective-permute-start(bf16[128,128]{1,0:T(8,128)(2,1)S(1)} %get-tuple-element.80), channel_id=1, source_target_pairs={{0,2},{1,3},{2,0},{3,1},{4,6},{5,7},{6,4},{7,5},{8,10},{9,11},{10,... | collective-permute-start | bytes 98312 | tf_op jit(solution)/shard_map/ppermute | solution.py:432
  220.1 1.3 collective-permute-done.23.refs_5_
  221.4 6.8 %collective-permute-start.32 = (bf16[128,128]{1,0:T(8,128)(2,1)S(1)}, bf16[128,128]{1,0:T(8,128)(2,1)S(1)}, u32[]{:S(2)}, u32[]{:S(2)}) collective-permute-start(bf16[128,128]{1,0:T(8,128)(2,1)S(1)} %get-tuple-element.79), channel_id=1, source_target_pairs={{0,3},{1,0},{2,1},{3,2},{4,7},{5,4},{6,5},{7,6},{8,11},{9,8},{10,9... | collective-permute-start | bytes 98312 | tf_op jit(solution)/shard_map/ppermute | solution.py:432
  228.2 0.6 copy-done.9
  228.9 3.4 %unpack.1 = (bf16[1,128,4096]{2,1,0:T(8,128)(2,1)}, bf16[1,128,1024]{2,1,0:T(8,128)(2,1)}, bf16[1,128,1024]{2,1,0:T(8,128)(2,1)}) custom-call(s32[10]{0:T(128)} %pad_add_fusion.ids_ref, bf16[128,768]{1,0:T(8,128)(2,1)} %get-tuple-element.45.refs_0_, bf16[128,768]{1,0:T(8,128)(2,1)} %copy-done.4, bf16[128,768]{1,0:T(8,128)(2,1)} %copy-done.5, ...), custom_call_target="tpu_custom_call" | custom-call | bytes 3145728 | tf_op jit(solution)/shard_map/unpack/pallas_call | solution.py:223
  232.4 0.1 reduce
  232.5 0.8 copy.15
  (88 shorter events, 0.7 us)
Async XLA Ops:
  0.6 27.4 %copy-start.12 = (s32[4]{0:T(128)S(1)}, s32[4]{0:T(128)}, u32[]{:S(2)}) copy-start(s32[4]{0:T(128)} %constant.66.clone) | copy-start | bytes 52
  0.6 27.4 %copy-start.13 = (s32[4]{0:T(128)S(1)}, s32[4]{0:T(128)}, u32[]{:S(2)}) copy-start(s32[4]{0:T(128)} %constant.67.clone) | copy-start | bytes 52
  0.7 24.4 %collective-permute-start.7 = (bf16[128,4096]{1,0:T(8,128)(2,1)}, bf16[128,4096]{1,0:T(8,128)(2,1)}, u32[]{:S(2)}, u32[]{:S(2)}) collective-permute-start(bf16[128,4096]{1,0:T(8,128)(2,1)} %bitcast.30), channel_id=1, source_target_pairs={{0,64},{32,96},{64,128},{96,160},{128,192},{160,224},{192,0},{224,... | collective-permute-start | bytes 3145736 | tf_op jit(solution)/shard_map/ppermute | solution.py:449
  2.8 25.3 %collective-permute-start.8 = (bf16[128,4096]{1,0:T(8,128)(2,1)}, bf16[128,4096]{1,0:T(8,128)(2,1)}, u32[]{:S(2)}, u32[]{:S(2)}) collective-permute-start(bf16[128,4096]{1,0:T(8,128)(2,1)} %bitcast.31), channel_id=1, source_target_pairs={{0,192},{32,224},{64,0},{96,32},{128,64},{160,96},{192,128},{224,1... | collective-permute-start | bytes 3145736 | tf_op jit(solution)/shard_map/ppermute | solution.py:449
  4.1 88.3 %collective-permute-start.11 = (bf16[128,4096]{1,0:T(8,128)(2,1)}, bf16[128,4096]{1,0:T(8,128)(2,1)}, u32[]{:S(2)}, u32[]{:S(2)}) collective-permute-start(bf16[128,4096]{1,0:T(8,128)(2,1)} %bitcast.32), channel_id=1, source_target_pairs={{0,32},{32,0},{64,96},{96,64},{128,160},{160,128},{192,224},{224,1... | collective-permute-start | bytes 3145736 | tf_op jit(solution)/shard_map/ppermute | solution.py:449
  26.1 21.9 %collective-permute-start.9 = (bf16[64,4096]{1,0:T(8,128)(2,1)S(1)}, bf16[64,4096]{1,0:T(8,128)(2,1)S(1)}, u32[]{:S(2)}, u32[]{:S(2)}) collective-permute-start(bf16[64,4096]{1,0:T(8,128)(2,1)S(1)} %slice.32), channel_id=1, source_target_pairs={{0,64},{32,96},{64,128},{96,160},{128,192},{160,224},{192,0},{224,... | collective-permute-start | bytes 1572872 | tf_op jit(solution)/shard_map/ppermute | solution.py:449
  29.2 8.2 %copy-start.11 = (bf16[128,512]{1,0:T(8,128)(2,1)S(1)}, bf16[128,512]{1,0:T(8,128)(2,1)}, u32[]{:S(2)}) copy-start(bf16[128,512]{1,0:T(8,128)(2,1)} %param.12) | copy-start | bytes 393220
  29.2 19.8 %collective-permute-start.10 = (bf16[64,4096]{1,0:T(8,128)(2,1)S(1)}, bf16[64,4096]{1,0:T(8,128)(2,1)S(1)}, u32[]{:S(2)}, u32[]{:S(2)}) collective-permute-start(bf16[64,4096]{1,0:T(8,128)(2,1)S(1)} %slice.33), channel_id=1, source_target_pairs={{0,192},{32,224},{64,0},{96,32},{128,64},{160,96},{192,128},{224,1... | collective-permute-start | bytes 1572872 | tf_op jit(solution)/shard_map/ppermute | solution.py:449
  34.7 18.0 %collective-permute-start = (bf16[128,768]{1,0:T(8,128)(2,1)}, bf16[128,768]{1,0:T(8,128)(2,1)S(1)}, u32[]{:S(2)}, u32[]{:S(2)}) collective-permute-start(bf16[128,768]{1,0:T(8,128)(2,1)} %get-tuple-element.35), channel_id=1, source_target_pairs={{0,64},{32,96},{64,128},{96,160},{128,192},{160,224},{192,0},{224,... | collective-permute-start | bytes 589832 | tf_op jit(solution)/shard_map/ppermute | solution.py:449
  34.7 18.0 %collective-permute-start.1 = (bf16[128,768]{1,0:T(8,128)(2,1)}, bf16[128,768]{1,0:T(8,128)(2,1)}, u32[]{:S(2)}, u32[]{:S(2)}) collective-permute-start(bf16[128,768]{1,0:T(8,128)(2,1)} %get-tuple-element.36), channel_id=1, source_target_pairs={{0,192},{32,224},{64,0},{96,32},{128,64},{160,96},{192,128},{224,1... | collective-permute-start | bytes 589832 | tf_op jit(solution)/shard_map/ppermute | solution.py:449
  38.5 67.3 %all-to-all-start = ((bf16[8,128,512]{2,1,0:T(8,128)(2,1)}), bf16[8,128,512]{2,1,0:T(8,128)(2,1)S(1)}, u32[]{:S(2)}, u32[]{:S(2)}) async-start(bf16[8,128,512]{2,1,0:T(8,128)(2,1)} %broadcast_in_dim.41), calls=%async_computation | async-start | bytes 2097152 | tf_op jit(solution)/shard_map/all_to_all | solution.py:444
  48.0 10.5 %copy-start.14 = (s32[1,32]{1,0:T(1,128)S(1)}, s32[1,32]{1,0:T(1,128)}, u32[]{:S(2)}) copy-start(s32[1,32]{1,0:T(1,128)} %param.13) | copy-start | bytes 388
  48.1 6.4 %collective-permute-start.2 = (bf16[128,768]{1,0:T(8,128)(2,1)}, bf16[128,768]{1,0:T(8,128)(2,1)}, u32[]{:S(2)}, u32[]{:S(2)}) collective-permute-start(bf16[128,768]{1,0:T(8,128)(2,1)} %get-tuple-element.37), channel_id=1, source_target_pairs={{0,128},{32,160},{64,192},{96,224},{128,0},{160,32},{192,64},{224,... | collective-permute-start | bytes 589832 | tf_op jit(solution)/shard_map/ppermute | solution.py:449
  49.0 43.5 %collective-permute-start.12 = (bf16[128,4096]{1,0:T(8,128)(2,1)}, bf16[128,4096]{1,0:T(8,128)(2,1)}, u32[]{:S(2)}, u32[]{:S(2)}) collective-permute-start(bf16[128,4096]{1,0:T(8,128)(2,1)} %collective-permute-done.7.refs_1_), channel_id=1, source_target_pairs={{0,32},{32,0},{64,96},{96,64},{128,160},{160,128},{192,224},{224,1... | collective-permute-start | bytes 3145736 | tf_op jit(solution)/shard_map/ppermute | solution.py:449
  52.8 30.8 %copy-start.17 = (bf16[128,768]{1,0:T(8,128)(2,1)}, bf16[128,768]{1,0:T(8,128)(2,1)S(1)}, u32[]{:S(2)}) copy-start(bf16[128,768]{1,0:T(8,128)(2,1)S(1)} %collective-permute-done.refs_1_) | copy-start | bytes 589828
  52.8 39.7 %collective-permute-start.13 = (bf16[128,4096]{1,0:T(8,128)(2,1)}, bf16[128,4096]{1,0:T(8,128)(2,1)S(1)}, u32[]{:S(2)}, u32[]{:S(2)}) collective-permute-start(bf16[128,4096]{1,0:T(8,128)(2,1)} %collective-permute-done.8.refs_2_), channel_id=1, source_target_pairs={{0,32},{32,0},{64,96},{96,64},{128,160},{160,128},{192,224},{224,1... | collective-permute-start | bytes 3145736 | tf_op jit(solution)/shard_map/ppermute | solution.py:449
  52.8 39.7 %collective-permute-start.14 = (bf16[128,4096]{1,0:T(8,128)(2,1)}, bf16[128,4096]{1,0:T(8,128)(2,1)}, u32[]{:S(2)}, u32[]{:S(2)}) collective-permute-start(bf16[128,4096]{1,0:T(8,128)(2,1)} %constant_dynamic-update-slice_fusion.refs_3_), channel_id=1, source_target_pairs={{0,32},{32,0},{64,96},{96,64},{128,160},{160,128},{192,224},{224,1... | collective-permute-start | bytes 3145736 | tf_op jit(solution)/shard_map/ppermute | solution.py:449
  54.5 5.4 %collective-permute-start.3 = (bf16[128,768]{1,0:T(8,128)(2,1)}, bf16[128,768]{1,0:T(8,128)(2,1)S(1)}, u32[]{:S(2)}, u32[]{:S(2)}) collective-permute-start(bf16[128,768]{1,0:T(8,128)(2,1)} %get-tuple-element.38), channel_id=1, source_target_pairs={{0,32},{32,0},{64,96},{96,64},{128,160},{160,128},{192,224},{224,1... | collective-permute-start | bytes 589832 | tf_op jit(solution)/shard_map/ppermute | solution.py:449
  59.8 23.7 %copy-start.18 = (bf16[128,768]{1,0:T(8,128)(2,1)}, bf16[128,768]{1,0:T(8,128)(2,1)S(1)}, u32[]{:S(2)}) copy-start(bf16[128,768]{1,0:T(8,128)(2,1)S(1)} %collective-permute-done.3.refs_4_) | copy-start | bytes 589828
  59.8 8.6 %collective-permute-start.4 = (bf16[128,768]{1,0:T(8,128)(2,1)}, bf16[128,768]{1,0:T(8,128)(2,1)S(1)}, u32[]{:S(2)}, u32[]{:S(2)}) collective-permute-start(bf16[128,768]{1,0:T(8,128)(2,1)} %get-tuple-element.39), channel_id=1, source_target_pairs={{0,96},{32,64},{64,160},{96,128},{128,224},{160,192},{192,32},{224... | collective-permute-start | bytes 589832 | tf_op jit(solution)/shard_map/ppermute | solution.py:449
  68.4 15.1 %copy-start.19 = (bf16[128,768]{1,0:T(8,128)(2,1)}, bf16[128,768]{1,0:T(8,128)(2,1)S(1)}, u32[]{:S(2)}) copy-start(bf16[128,768]{1,0:T(8,128)(2,1)S(1)} %collective-permute-done.4.refs_5_) | copy-start | bytes 589828
  68.5 7.1 %collective-permute-start.5 = (bf16[128,768]{1,0:T(8,128)(2,1)}, bf16[128,768]{1,0:T(8,128)(2,1)S(1)}, u32[]{:S(2)}, u32[]{:S(2)}) collective-permute-start(bf16[128,768]{1,0:T(8,128)(2,1)} %get-tuple-element.40), channel_id=1, source_target_pairs={{0,224},{32,192},{64,32},{96,0},{128,96},{160,64},{192,160},{224,1... | collective-permute-start | bytes 589832 | tf_op jit(solution)/shard_map/ppermute | solution.py:449
  75.5 8.0 %copy-start.20 = (bf16[128,768]{1,0:T(8,128)(2,1)}, bf16[128,768]{1,0:T(8,128)(2,1)S(1)}, u32[]{:S(2)}) copy-start(bf16[128,768]{1,0:T(8,128)(2,1)S(1)} %collective-permute-done.5.refs_6_) | copy-start | bytes 589828
  75.5 8.0 %collective-permute-start.6 = (bf16[128,768]{1,0:T(8,128)(2,1)}, bf16[128,768]{1,0:T(8,128)(2,1)S(1)}, u32[]{:S(2)}, u32[]{:S(2)}) collective-permute-start(bf16[128,768]{1,0:T(8,128)(2,1)} %get-tuple-element.41), channel_id=1, source_target_pairs={{0,160},{32,128},{64,224},{96,192},{128,32},{160,0},{192,96},{224,... | collective-permute-start | bytes 589832 | tf_op jit(solution)/shard_map/ppermute | solution.py:449
  83.5 0.7 copy-start.21
  92.5 1.0 copy-start.15
  105.8 8.4 %copy-start = (bf16[8,128,512]{2,1,0:T(8,128)(2,1)}, bf16[8,128,512]{2,1,0:T(8,128)(2,1)S(1)}, u32[]{:S(2)}) copy-start(bf16[8,128,512]{2,1,0:T(8,128)(2,1)S(1)} %all-to-all-done.refs_8_) | copy-start | bytes 3145732
  105.8 9.9 %copy-start.16 = (bf16[4,384,128]{2,1,0:T(8,128)(2,1)S(1)}, bf16[4,384,128]{2,1,0:T(8,128)(2,1)}, u32[]{:S(2)}) copy-start(bf16[4,384,128]{2,1,0:T(8,128)(2,1)} %get-tuple-element.59) | copy-start | bytes 1179652
  105.8 65.0 %all-to-all-start.2 = ((bf16[8,4,128,128]{3,2,1,0:T(8,128)(2,1)}), bf16[8,4,128,128]{3,2,1,0:T(8,128)(2,1)S(1)}, u32[]{:S(2)}, u32[]{:S(2)}) async-start(bf16[8,4,128,128]{3,2,1,0:T(8,128)(2,1)} %get-tuple-element.62), calls=%async_computation.2 | async-start | bytes 2097152 | tf_op jit(solution)/shard_map/all_to_all | solution.py:444
  112.9 40.0 %collective-permute-start.15 = (bf16[8,128,512]{2,1,0:T(8,128)(2,1)S(1)}, bf16[8,128,512]{2,1,0:T(8,128)(2,1)}, u32[]{:S(2)}, u32[]{:S(2)}) collective-permute-start(bf16[8,128,512]{2,1,0:T(8,128)(2,1)S(1)} %all-to-all-done.refs_8_), channel_id=1, source_target_pairs={{0,1},{1,2},{2,3},{3,0},{4,5},{5,6},{6,7},{7,4},{8,9},{9,10},{10,1... | collective-permute-start | bytes 3145736 | tf_op jit(solution)/shard_map/ppermute | solution.py:432
  114.2 38.7 %collective-permute-start.16 = (bf16[8,128,512]{2,1,0:T(8,128)(2,1)S(1)}, bf16[8,128,512]{2,1,0:T(8,128)(2,1)}, u32[]{:S(2)}, u32[]{:S(2)}) collective-permute-start(bf16[8,128,512]{2,1,0:T(8,128)(2,1)S(1)} %all-to-all-done.refs_8_), channel_id=1, source_target_pairs={{0,3},{1,0},{2,1},{3,2},{4,7},{5,4},{6,5},{7,6},{8,11},{9,8},{10,9... | collective-permute-start | bytes 3145736 | tf_op jit(solution)/shard_map/ppermute | solution.py:432
  115.7 31.3 %collective-permute-start.26 = (bf16[4,384,128]{2,1,0:T(8,128)(2,1)}, bf16[4,384,128]{2,1,0:T(8,128)(2,1)S(1)}, u32[]{:S(2)}, u32[]{:S(2)}) collective-permute-start(bf16[4,384,128]{2,1,0:T(8,128)(2,1)} %get-tuple-element.42), channel_id=1, source_target_pairs={{0,1},{1,2},{2,3},{3,0},{4,5},{5,6},{6,7},{7,4},{8,9},{9,10},{10,1... | collective-permute-start | bytes 1179656 | tf_op jit(solution)/shard_map/ppermute | solution.py:432
  115.8 31.3 %collective-permute-start.27 = (bf16[4,384,128]{2,1,0:T(8,128)(2,1)S(1)}, bf16[4,384,128]{2,1,0:T(8,128)(2,1)S(1)}, u32[]{:S(2)}, u32[]{:S(2)}) collective-permute-start(bf16[4,384,128]{2,1,0:T(8,128)(2,1)S(1)} %copy-done.16), channel_id=1, source_target_pairs={{0,3},{1,0},{2,1},{3,2},{4,7},{5,4},{6,5},{7,6},{8,11},{9,8},{10,9... | collective-permute-start | bytes 1179656 | tf_op jit(solution)/shard_map/ppermute | solution.py:432
  147.1 0.7 copy-start.2
  147.1 0.9 copy-start.3
  150.2 19.4 %collective-permute-start.28 = (bf16[8,384,128]{2,1,0:T(8,128)(2,1)}, bf16[8,384,128]{2,1,0:T(8,128)(2,1)S(1)}, u32[]{:S(2)}, u32[]{:S(2)}) collective-permute-start(bf16[8,384,128]{2,1,0:T(8,128)(2,1)} %get-tuple-element.60), channel_id=1, source_target_pairs={{0,1},{1,2},{2,3},{3,0},{4,5},{5,6},{6,7},{7,4},{8,9},{9,10},{10,1... | collective-permute-start | bytes 2359304 | tf_op jit(solution)/shard_map/ppermute | solution.py:432
  151.1 18.5 %copy-start.1 = (bf16[8,384,128]{2,1,0:T(8,128)(2,1)S(1)}, bf16[8,384,128]{2,1,0:T(8,128)(2,1)}, u32[]{:S(2)}) copy-start(bf16[8,384,128]{2,1,0:T(8,128)(2,1)} %get-tuple-element.56) | copy-start | bytes 2359300
  151.1 18.5 %collective-permute-start.29 = (bf16[8,384,128]{2,1,0:T(8,128)(2,1)}, bf16[8,384,128]{2,1,0:T(8,128)(2,1)S(1)}, u32[]{:S(2)}, u32[]{:S(2)}) collective-permute-start(bf16[8,384,128]{2,1,0:T(8,128)(2,1)} %get-tuple-element.61), channel_id=1, source_target_pairs={{0,3},{1,0},{2,1},{3,2},{4,7},{5,4},{6,5},{7,6},{8,11},{9,8},{10,9... | collective-permute-start | bytes 2359304 | tf_op jit(solution)/shard_map/ppermute | solution.py:432
  154.0 27.0 %collective-permute-start.17 = (bf16[4,128,512]{2,1,0:T(8,128)(2,1)S(1)}, bf16[4,128,512]{2,1,0:T(8,128)(2,1)}, u32[]{:S(2)}, u32[]{:S(2)}) collective-permute-start(bf16[4,128,512]{2,1,0:T(8,128)(2,1)S(1)} %slice.26), channel_id=1, source_target_pairs={{0,1},{1,2},{2,3},{3,0},{4,5},{5,6},{6,7},{7,4},{8,9},{9,10},{10,1... | collective-permute-start | bytes 1572872 | tf_op jit(solution)/shard_map/ppermute | solution.py:432
  155.2 25.8 %collective-permute-start.18 = (bf16[4,128,512]{2,1,0:T(8,128)(2,1)S(1)}, bf16[4,128,512]{2,1,0:T(8,128)(2,1)}, u32[]{:S(2)}, u32[]{:S(2)}) collective-permute-start(bf16[4,128,512]{2,1,0:T(8,128)(2,1)S(1)} %slice.27), channel_id=1, source_target_pairs={{0,3},{1,0},{2,1},{3,2},{4,7},{5,4},{6,5},{7,6},{8,11},{9,8},{10,9... | collective-permute-start | bytes 1572872 | tf_op jit(solution)/shard_map/ppermute | solution.py:432
  170.8 61.6 %all-to-all-start.1 = ((bf16[8,384,128]{2,1,0:T(8,128)(2,1)}), bf16[8,384,128]{2,1,0:T(8,128)(2,1)S(1)}, u32[]{:S(2)}, u32[]{:S(2)}) async-start(bf16[8,384,128]{2,1,0:T(8,128)(2,1)} %add_convert_fusion), calls=%async_computation.1 | async-start | bytes 1572864 | tf_op jit(solution)/shard_map/all_to_all | solution.py:444
  204.1 6.4 %copy-start.23 = (bf16[128,768]{1,0:T(8,128)(2,1)S(1)}, bf16[128,768]{1,0:T(8,128)(2,1)}, u32[]{:S(2)}) copy-start(bf16[128,768]{1,0:T(8,128)(2,1)} %get-tuple-element.51) | copy-start | bytes 589828
  204.1 11.7 %copy-start.22 = (bf16[128,768]{1,0:T(8,128)(2,1)S(1)}, bf16[128,768]{1,0:T(8,128)(2,1)}, u32[]{:S(2)}) copy-start(bf16[128,768]{1,0:T(8,128)(2,1)} %get-tuple-element.52) | copy-start | bytes 589828
  204.1 6.4 %collective-permute-start.19 = (bf16[128,768]{1,0:T(8,128)(2,1)}, bf16[128,768]{1,0:T(8,128)(2,1)S(1)}, u32[]{:S(2)}, u32[]{:S(2)}) collective-permute-start(bf16[128,768]{1,0:T(8,128)(2,1)} %get-tuple-element.46), channel_id=1, source_target_pairs={{0,64},{32,96},{64,128},{96,160},{128,192},{160,224},{192,0},{224,... | collective-permute-start | bytes 589832 | tf_op jit(solution)/shard_map/ppermute | solution.py:449
  204.2 11.6 %collective-permute-start.20 = (bf16[128,768]{1,0:T(8,128)(2,1)}, bf16[128,768]{1,0:T(8,128)(2,1)S(1)}, u32[]{:S(2)}, u32[]{:S(2)}) collective-permute-start(bf16[128,768]{1,0:T(8,128)(2,1)} %get-tuple-element.47), channel_id=1, source_target_pairs={{0,192},{32,224},{64,0},{96,32},{128,64},{160,96},{192,128},{224,1... | collective-permute-start | bytes 589832 | tf_op jit(solution)/shard_map/ppermute | solution.py:449
  206.9 9.3 %collective-permute-start.21 = (bf16[128,768]{1,0:T(8,128)(2,1)}, bf16[128,768]{1,0:T(8,128)(2,1)S(1)}, u32[]{:S(2)}, u32[]{:S(2)}) collective-permute-start(bf16[128,768]{1,0:T(8,128)(2,1)} %get-tuple-element.48), channel_id=1, source_target_pairs={{0,128},{32,160},{64,192},{96,224},{128,0},{160,32},{192,64},{224,... | collective-permute-start | bytes 589832 | tf_op jit(solution)/shard_map/ppermute | solution.py:449
  206.9 9.7 %collective-permute-start.22 = (bf16[128,768]{1,0:T(8,128)(2,1)}, bf16[128,768]{1,0:T(8,128)(2,1)S(1)}, u32[]{:S(2)}, u32[]{:S(2)}) collective-permute-start(bf16[128,768]{1,0:T(8,128)(2,1)} %get-tuple-element.49), channel_id=1, source_target_pairs={{0,32},{32,0},{64,96},{96,64},{128,160},{160,128},{192,224},{224,1... | collective-permute-start | bytes 589832 | tf_op jit(solution)/shard_map/ppermute | solution.py:449
  209.5 11.9 %collective-permute-start.23 = (bf16[128,768]{1,0:T(8,128)(2,1)}, bf16[128,768]{1,0:T(8,128)(2,1)S(1)}, u32[]{:S(2)}, u32[]{:S(2)}) collective-permute-start(bf16[128,768]{1,0:T(8,128)(2,1)} %get-tuple-element.50), channel_id=1, source_target_pairs={{0,96},{32,64},{64,160},{96,128},{128,224},{160,192},{192,32},{224... | collective-permute-start | bytes 589832 | tf_op jit(solution)/shard_map/ppermute | solution.py:449
  210.5 17.6 %copy-start.4 = (bf16[128,768]{1,0:T(8,128)(2,1)}, bf16[128,768]{1,0:T(8,128)(2,1)S(1)}, u32[]{:S(2)}) copy-start(bf16[128,768]{1,0:T(8,128)(2,1)S(1)} %collective-permute-done.19.refs_1_) | copy-start | bytes 589828
  210.5 17.6 %collective-permute-start.24 = (bf16[128,768]{1,0:T(8,128)(2,1)S(1)}, bf16[128,768]{1,0:T(8,128)(2,1)S(1)}, u32[]{:S(2)}, u32[]{:S(2)}) collective-permute-start(bf16[128,768]{1,0:T(8,128)(2,1)S(1)} %copy-done.23), channel_id=1, source_target_pairs={{0,224},{32,192},{64,32},{96,0},{128,96},{160,64},{192,160},{224,1... | collective-permute-start | bytes 589832 | tf_op jit(solution)/shard_map/ppermute | solution.py:449
  215.8 12.3 %copy-start.5 = (bf16[128,768]{1,0:T(8,128)(2,1)}, bf16[128,768]{1,0:T(8,128)(2,1)S(1)}, u32[]{:S(2)}) copy-start(bf16[128,768]{1,0:T(8,128)(2,1)S(1)} %collective-permute-done.20.refs_2_) | copy-start | bytes 589828
  215.8 12.3 %collective-permute-start.25 = (bf16[128,768]{1,0:T(8,128)(2,1)S(1)}, bf16[128,768]{1,0:T(8,128)(2,1)S(1)}, u32[]{:S(2)}, u32[]{:S(2)}) collective-permute-start(bf16[128,768]{1,0:T(8,128)(2,1)S(1)} %copy-done.22), channel_id=1, source_target_pairs={{0,160},{32,128},{64,224},{96,192},{128,32},{160,0},{192,96},{224,... | collective-permute-start | bytes 589832 | tf_op jit(solution)/shard_map/ppermute | solution.py:449
  216.2 12.0 %copy-start.6 = (bf16[128,768]{1,0:T(8,128)(2,1)}, bf16[128,768]{1,0:T(8,128)(2,1)S(1)}, u32[]{:S(2)}) copy-start(bf16[128,768]{1,0:T(8,128)(2,1)S(1)} %collective-permute-done.21.refs_3_) | copy-start | bytes 589828
  216.2 16.2 %collective-permute-start.30 = (bf16[128,128]{1,0:T(8,128)(2,1)S(1)}, bf16[128,128]{1,0:T(8,128)(2,1)S(1)}, u32[]{:S(2)}, u32[]{:S(2)}) collective-permute-start(bf16[128,128]{1,0:T(8,128)(2,1)S(1)} %get-tuple-element.78), channel_id=1, source_target_pairs={{0,1},{1,2},{2,3},{3,0},{4,5},{5,6},{6,7},{7,4},{8,9},{9,10},{10,1... | collective-permute-start | bytes 98312 | tf_op jit(solution)/shard_map/ppermute | solution.py:432
  216.7 11.5 %copy-start.7 = (bf16[128,768]{1,0:T(8,128)(2,1)}, bf16[128,768]{1,0:T(8,128)(2,1)S(1)}, u32[]{:S(2)}) copy-start(bf16[128,768]{1,0:T(8,128)(2,1)S(1)} %collective-permute-done.22.refs_4_) | copy-start | bytes 589828
  216.7 15.7 %collective-permute-start.31 = (bf16[128,128]{1,0:T(8,128)(2,1)S(1)}, bf16[128,128]{1,0:T(8,128)(2,1)S(1)}, u32[]{:S(2)}, u32[]{:S(2)}) collective-permute-start(bf16[128,128]{1,0:T(8,128)(2,1)S(1)} %get-tuple-element.80), channel_id=1, source_target_pairs={{0,2},{1,3},{2,0},{3,1},{4,6},{5,7},{6,4},{7,5},{8,10},{9,11},{10,... | collective-permute-start | bytes 98312 | tf_op jit(solution)/shard_map/ppermute | solution.py:432
  221.3 6.8 %copy-start.8 = (bf16[128,768]{1,0:T(8,128)(2,1)}, bf16[128,768]{1,0:T(8,128)(2,1)S(1)}, u32[]{:S(2)}) copy-start(bf16[128,768]{1,0:T(8,128)(2,1)S(1)} %collective-permute-done.23.refs_5_) | copy-start | bytes 589828
  221.4 11.0 %collective-permute-start.32 = (bf16[128,128]{1,0:T(8,128)(2,1)S(1)}, bf16[128,128]{1,0:T(8,128)(2,1)S(1)}, u32[]{:S(2)}, u32[]{:S(2)}) collective-permute-start(bf16[128,128]{1,0:T(8,128)(2,1)S(1)} %get-tuple-element.79), channel_id=1, source_target_pairs={{0,3},{1,0},{2,1},{3,2},{4,7},{5,4},{6,5},{7,6},{8,11},{9,8},{10,9... | collective-permute-start | bytes 98312 | tf_op jit(solution)/shard_map/ppermute | solution.py:432
  228.1 0.7 copy-start.9
  228.1 0.7 copy-start.10

commit v5 on v2

--- a/solution.py
+++ b/solution.py
@@ -236,33 +236,55 @@
     )(ids, *pieces)
 
 
-def upstream_kernel(ids_ref, *refs):
-    pieces, weights, (o_ref, acc_ref, w_ref) = refs[:-8], refs[-8:-3], refs[-3:]
-    count = len(pieces)
-    near = w_ref.shape[1]
+def gathered_rows(ids_ref, pieces, offsets):
+    near = GRID["fsdp"]
+    planes = pieces[0].shape[1] // (near * TOK)
+    turn = ids_ref[len(pieces) + 1]
+    starts = [
+        pl.multiple_of((plane * near + lax.rem(turn + offset, near)) * TOK, TOK)
+        for offset in offsets
+        for plane in range(planes)
+    ]
+    return jnp.concatenate(
+        [
+            jnp.concatenate([piece[:, pl.ds(start, TOK)] for start in starts], 1)
+            for piece in pieces
+        ],
+        0,
+    )
+
+
+def most_kernel(ids_ref, *refs):
+    pieces, (mine_ref, below_ref, above_ref, o_ref) = refs[:-4], refs[-4:]
+    near = GRID["fsdp"]
+    rows = gathered_rows(ids_ref, pieces, (0, near - 1, 1))
+    width = mine_ref.shape[2]
+    weight = jnp.concatenate(
+        [x[...].reshape(-1, width) for x in (mine_ref, below_ref, above_ref)], 0
+    )
+    part = jnp.dot(rows, weight, preferred_element_type=F32)
+    first = pl.program_id(0) == 0
+
+    @pl.when(first)
+    def _():
+        o_ref[...] = part
+
+    @pl.when(jnp.logical_not(first))
+    def _():
+        o_ref[...] += part
+
+
+def rest_kernel(ids_ref, *refs):
+    pieces, (low_ref, high_ref, sum_ref, o_ref, acc_ref) = refs[:-5], refs[-5:]
     step = pl.program_id(0)
     last = pl.num_programs(0) - 1
-    y = ids_ref[count + 1]
-    mine, below, above, far_low, far_high = weights
-    w_ref[:, y] = mine[...]
-    w_ref[:, lax.rem(y + near - 1, near)] = below[...]
-    w_ref[:, lax.rem(y + 1, near)] = above[...]
-
-    @pl.when(step * 2 <= last)
-    def _():
-        w_ref[:, lax.rem(y + 2, near)] = far_low[...]
-
-    @pl.when(step * 2 > last)
-    def _():
-        w_ref[:, lax.rem(y + 2, near)] = far_high[...]
-
-    rows = jnp.concatenate([piece[...] for piece in pieces], 0)
-    weight = w_ref[...].reshape(rows.shape[1], w_ref.shape[3])
-    part = jnp.dot(rows, weight, preferred_element_type=F32)
+    rows = gathered_rows(ids_ref, pieces, (2,))
+    weight = jnp.where(step * 2 <= last, low_ref[...], high_ref[...])
+    part = jnp.dot(rows, weight.reshape(-1, weight.shape[2]), preferred_element_type=F32)
 
     @pl.when(step == 0)
     def _():
-        acc_ref[...] = part
+        acc_ref[...] = sum_ref[...] + part
 
     @pl.when(step > 0)
     def _():
@@ -270,43 +292,70 @@
 
     @pl.when(step == last)
     def _():
-        for p in range(count):
+        for p in range(len(pieces)):
             o_ref[ids_ref[p]] = acc_ref[p * TOK : (p + 1) * TOK, :].astype(BF16)
 
 
-def upstream(ids, pieces, weights):
+PLANES = 2
+
+
+def chunk_specs(pieces):
+    near = GRID["fsdp"]
+    return [pl.BlockSpec((TOK, PLANES * near * TOK), lambda i, ids: (0, i))] * len(pieces)
+
+
+def upstream_most(ids, pieces, weights):
     far, rows, width = weights[0].shape
-    near = GRID["fsdp"]
-    depth = far * near * rows
-    planes = 2
-    steps = far // planes
     count = len(pieces)
-    block = (planes, rows, width)
-    return pl.pallas_call(
-        upstream_kernel,
+    tokens = count * TOK
+    depth = 3 * far * rows
+    return pl.pallas_call(
+        most_kernel,
+        grid_spec=pltpu.PrefetchScalarGridSpec(
+            num_scalar_prefetch=1,
+            grid=(far // PLANES,),
+            in_specs=chunk_specs(pieces)
+            + [pl.BlockSpec((PLANES, rows, width), lambda i, ids: (i, 0, 0))] * 3,
+            out_specs=whole((tokens, width)),
+        ),
+        out_shape=jax.ShapeDtypeStruct((tokens, width), F32),
+        cost_estimate=pl.CostEstimate(
+            flops=2 * tokens * width * depth,
+            bytes_accessed=2 * (tokens * (depth + 2 * width) + depth * width),
+            transcendentals=0,
+        ),
+        name="upstream_most",
+    )(ids, *pieces, *weights)
+
+
+def upstream_rest(ids, pieces, ends, sums):
+    middle, rows, width = ends[0].shape
+    count = len(pieces)
+    steps = 2 * middle // PLANES
+    block = (PLANES, rows, width)
+    depth = 2 * middle * rows
+    return pl.pallas_call(
+        rest_kernel,
         grid_spec=pltpu.PrefetchScalarGridSpec(
             num_scalar_prefetch=1,
             grid=(steps,),
-            in_specs=[pl.BlockSpec((TOK, depth // steps), lambda i, ids: (0, i))] * count
-            + [pl.BlockSpec(block, lambda i, ids: (i, 0, 0))] * 3
+            in_specs=chunk_specs(pieces)
             + [
                 pl.BlockSpec(block, lambda i, ids: (jnp.minimum(i, steps // 2 - 1), 0, 0)),
                 pl.BlockSpec(block, lambda i, ids: (jnp.maximum(i - steps // 2, 0), 0, 0)),
+                whole(sums.shape),
             ],
-            out_specs=pl.BlockSpec((count, TOK, width), lambda i, ids: (0, 0, 0)),
-            scratch_shapes=[
-                pltpu.VMEM((count * TOK, width), F32),
-                pltpu.VMEM((planes, near, rows, width), BF16),
-            ],
+            out_specs=whole((count, TOK, width)),
+            scratch_shapes=[pltpu.VMEM(sums.shape, F32)],
         ),
         out_shape=jax.ShapeDtypeStruct((count, TOK, width), BF16),
         cost_estimate=pl.CostEstimate(
             flops=2 * count * TOK * width * depth,
-            bytes_accessed=2 * (count * TOK * (depth + width) + depth * width),
+            bytes_accessed=2 * count * TOK * (4 * depth + 3 * width),
             transcendentals=0,
         ),
-        name="upstream",
-    )(ids, *pieces, *weights)
+        name="upstream_rest",
+    )(ids, *pieces, *ends, sums)
 
 
 def proj_kernel(ids_ref, *refs):
@@ -475,9 +524,10 @@
     up, down = shift(low, "fsdp", 1), shift(high, "fsdp", -1)
     below, above = after((below, above), low)
     ends = [shift(below[:far], "fsdp", 1), shift(above[far:], "fsdp", -1)]
+    sums = upstream_most(ids, pieces, [weight, below, above])
     following, before = join(following, up, before, down)
     up, down = shift(following, "fsdp", 1), shift(before, "fsdp", -1)
-    arriving = upstream(ids, pieces, [weight, below, above, *ends])
+    arriving = upstream_rest(ids, pieces, ends, sums)
     grads = attend_grad(jnp.concatenate([ids, targets]), packed, arriving, lo, hi)
     up, down = after((up, down), grads[0])
     first = (same.astype(F32) + up.astype(F32) + down.astype(F32)).astype(BF16)

time: 192 us -> 233 us (1.21); the launches traced: 190 us -> 228 us
  waiting for transfers between devices: 67.3 us -> 91.4 us
  Pallas kernels: 53.3 us -> 60.3 us
  local copies, waits for them, and re-layouts: 10.3 us -> 14.1 us
  starting transfers between devices: 54.1 us -> 56.9 us
    ppermute x8, waiting for transfers between devices: 12.5 us -> 35.5 us  [shift(): return lax.ppermute(x, axis, [(i, (i + by) % n) for i in range(n)])]
    pallas_call x1 -> x2, Pallas kernels: 10.1 us -> 17.4 us  [the longest x1 9.15 us: upstream_most(): pl.pallas_call(most_kernel, grid_spec=pltpu.PrefetchScalarGridSpec(num_sc...]
    ppermute x22, starting transfers between devices: 22.9 us -> 27.7 us  [hop(): return lax.ppermute(x, 'seq', pairs)]
    unnamed x62 -> x60, local copies, waits for them, and re-layouts: 3.35 us -> 6.63 us
    slice x2, local copies, waits for them, and re-layouts: 1.36 us -> 3.76 us  [per_device(): ends = [shift(below[:far], 'fsdp', 1), shift(above[far:], 'fsdp', -1)]]
  transfers between devices with their start and end apart: 32 -> 32, of which waited for: 16 -> 15; matrix products, arithmetic and copies ran while one was open for 5% -> 5% of each run, Pallas kernels for 28% -> 26%
where the time goes in v5:
time: 233 us; the launch traced here: 228 us
  waiting for transfers between devices  91.4 us (39%)
  Pallas kernels  60.3 us (26%)
  starting transfers between devices  56.9 us (24%)
  local copies, waits for them, and re-layouts  14.1 us (6%)
  other arithmetic  4.41 us (2%)
    ppermute x22, waiting for transfers between devices, hop(): return lax.ppermute(x, 'seq', pairs)  52.4 us
    ppermute x8, waiting for transfers between devices, shift(): return lax.ppermute(x, axis, [(i, (i + by) % n) for i in range(n)])  35.5 us
    ppermute x22, starting transfers between devices, hop(): return lax.ppermute(x, 'seq', pairs)  27.7 us
    all_to_all x2, starting transfers between devices, swap(): return lax.all_to_all(x, axis, split_axis=0, concat_axis=0, tiled=True)  16.1 us
    pallas_call x1, Pallas kernels, attend_grad(): pl.pallas_call(bwd_kernel, grid_spec=pltpu.PrefetchScalarGridSpec(num_sca...  13.2 us
    ppermute x8, starting transfers between devices, shift(): return lax.ppermute(x, axis, [(i, (i + by) % n) for i in range(n)])  13 us
    pallas_call x1, Pallas kernels, proj_terms(): pl.pallas_call(proj_kernel, grid_spec=pltpu.PrefetchScalarGridSpec(num_sc...  12.3 us
    pallas_call x1, Pallas kernels, upstream_most(): pl.pallas_call(most_kernel, grid_spec=pltpu.PrefetchScalarGridSpec(num_sc...  9.15 us
  transfers between devices with their start and end apart: 32, of which 15 were waited for; matrix products, arithmetic and copies ran while one was open for 5% of the time, Pallas kernels for 26%

profile of v5, /device:TPU:2, one launch (start us, length us, event | category | flops | bytes accessed | tf_op | source)
XLA Modules:
  0.0 228.1 jit_solution(16104464271671665996)
XLA Ops:
  0.6 1.6 collective-permute-start.7
  2.2 0.8 collective-permute-start.8
  3.1 22.8 %collective-permute-done.7.refs_1_ = bf16[128,4096]{1,0:T(8,128)(2,1)S(1)} collective-permute-done((bf16[128,4096]{1,0:T(8,128)(2,1)}, bf16[128,4096]{1,0:T(8,128)(2,1)S(1)}, u32[]{:S(2)}, u32[]{:S(2)}) %collective-permute-start.7) | collective-permute-done | bytes 1048608 | tf_op jit(solution)/shard_map/ppermute | solution.py:488
  25.9 1.6 collective-permute-start.9
  27.4 0.7 add_subtract_fusion
  28.2 0.9 slice.17
  29.6 0.6 pad_add_fusion.1.ids_ref
  30.2 3.3 %pack.1 = (bf16[128,768]{1,0:T(8,128)(2,1)}, bf16[128,768]{1,0:T(8,128)(2,1)}, bf16[128,768]{1,0:T(8,128)(2,1)}, bf16[128,768]{1,0:T(8,128)(2,1)}, bf16[128,768]...) custom-call(s32[8]{0:T(128)} %pad_add_fusion.1.ids_ref, ...), custom_call_target="tpu_custom_call" | custom-call | bytes 3145728 | tf_op jit(solution)/shard_map/pack/pallas_call | solution.py:195
  33.5 1.5 collective-permute-start
  35.0 1.3 collective-permute-start.1
  36.3 1.0 broadcast_in_dim.41
  37.3 8.8 %all-to-all-start = ((bf16[8,128,512]{2,1,0:T(8,128)(2,1)}), bf16[8,128,512]{2,1,0:T(8,128)(2,1)}, u32[]{:S(2)}, u32[]{:S(2)}) async-start(bf16[8,128,512]{2,1,0:T(8,128)(2,1)} %broadcast_in_dim.41), calls=%async_computation | async-start | bytes 2097152 | tf_op jit(solution)/shard_map/all_to_all | solution.py:483
  46.1 0.8 copy-done.6
  46.9 2.1 collective-permute-start.2
  49.0 1.1 constant_dynamic-update-slice_fusion.1
  50.2 1.1 constant_dynamic-update-slice_fusion.refs_3_
  51.3 0.6 collective-permute-start.13
  52.0 2.4 %collective-permute-done.2.refs_3_ = bf16[128,768]{1,0:T(8,128)(2,1)} collective-permute-done((bf16[128,768]{1,0:T(8,128)(2,1)}, bf16[128,768]{1,0:T(8,128)(2,1)}, u32[]{:S(2)}, u32[]{:S(2)}) %collective-permute-start.2) | collective-permute-done | bytes 196640 | tf_op jit(solution)/shard_map/ppermute | solution.py:488
  54.6 1.7 collective-permute-done.3.refs_4_
  56.3 2.5 %collective-permute-start.4 = (bf16[128,768]{1,0:T(8,128)(2,1)}, bf16[128,768]{1,0:T(8,128)(2,1)S(1)}, u32[]{:S(2)}, u32[]{:S(2)}) collective-permute-start(bf16[128,768]{1,0:T(8,128)(2,1)} %get-tuple-element.39), channel_id=1, source_target_pairs={{0,96},{32,64},{64,160},{96,128},{128,224},{160,192},{192,32},{224... | collective-permute-start | bytes 589832 | tf_op jit(solution)/shard_map/ppermute | solution.py:488
  58.8 5.5 %collective-permute-done.4.refs_5_ = bf16[128,768]{1,0:T(8,128)(2,1)S(1)} collective-permute-done((bf16[128,768]{1,0:T(8,128)(2,1)}, bf16[128,768]{1,0:T(8,128)(2,1)S(1)}, u32[]{:S(2)}, u32[]{:S(2)}) %collective-permute-start.4) | collective-permute-done | bytes 196640 | tf_op jit(solution)/shard_map/ppermute | solution.py:488
  64.3 3.6 %collective-permute-start.5 = (bf16[128,768]{1,0:T(8,128)(2,1)}, bf16[128,768]{1,0:T(8,128)(2,1)S(1)}, u32[]{:S(2)}, u32[]{:S(2)}) collective-permute-start(bf16[128,768]{1,0:T(8,128)(2,1)} %get-tuple-element.40), channel_id=1, source_target_pairs={{0,224},{32,192},{64,32},{96,0},{128,96},{160,64},{192,160},{224,1... | collective-permute-start | bytes 589832 | tf_op jit(solution)/shard_map/ppermute | solution.py:488
  67.9 4.9 %collective-permute-done.5.refs_6_ = bf16[128,768]{1,0:T(8,128)(2,1)S(1)} collective-permute-done((bf16[128,768]{1,0:T(8,128)(2,1)}, bf16[128,768]{1,0:T(8,128)(2,1)S(1)}, u32[]{:S(2)}, u32[]{:S(2)}) %collective-permute-start.5) | collective-permute-done | bytes 196640 | tf_op jit(solution)/shard_map/ppermute | solution.py:488
  72.8 2.4 %collective-permute-start.6 = (bf16[128,768]{1,0:T(8,128)(2,1)}, bf16[128,768]{1,0:T(8,128)(2,1)S(1)}, u32[]{:S(2)}, u32[]{:S(2)}) collective-permute-start(bf16[128,768]{1,0:T(8,128)(2,1)} %get-tuple-element.41), channel_id=1, source_target_pairs={{0,160},{32,128},{64,224},{96,192},{128,32},{160,0},{192,96},{224,... | collective-permute-start | bytes 589832 | tf_op jit(solution)/shard_map/ppermute | solution.py:488
  75.2 0.7 pad_add_fusion.ids_ref
  75.9 0.7 select_reduce_fusion
  76.6 4.9 %collective-permute-done.6.refs_7_ = bf16[128,768]{1,0:T(8,128)(2,1)S(1)} collective-permute-done((bf16[128,768]{1,0:T(8,128)(2,1)}, bf16[128,768]{1,0:T(8,128)(2,1)S(1)}, u32[]{:S(2)}, u32[]{:S(2)}) %collective-permute-start.6) | collective-permute-done | bytes 196640 | tf_op jit(solution)/shard_map/ppermute | solution.py:488
  81.5 0.7 copy-done.21
  82.1 8.2 %attend.1.refs_8_ = bf16[8,512,128]{2,1,0:T(8,128)(2,1)} custom-call(s32[10]{0:T(128)} %pad_add_fusion.ids_ref, bf16[128,768]{1,0:T(8,128)(2,1)} %get-tuple-element.34.refs_0_, bf16[128,768]{1,0:T(8,128)(2,1)} %copy-done.18, bf16[128,768]{1,0:T(8,128)(2,1)} %collective-permute-done.1.refs_2_, bf16[128,768]{1,0:T(8,128)(2,1)} %collective-permute-done.2.refs_3_, ...), custom_call_target="tpu_custom_call" | custom-call | flops 939524096 | bytes 3145728 | tf_op jit(solution)/shard_map/attend/pallas_call | solution.py:138
  90.4 1.6 collective-permute-start.15
  91.9 1.7 collective-permute-start.16
  93.6 12.3 %proj_terms.1 = (bf16[8,512,128]{2,1,0:T(8,128)(2,1)}, bf16[8,512,128]{2,1,0:T(8,128)(2,1)}, bf16[4,512,128]{2,1,0:T(8,128)(2,1)}, bf16[4,512,128]{2,1,0:T(8,128)(2,1)}, bf16[8,512,128]{2,1,0:T(8,128)(2,1)}) custom-call(s32[10]{0:T(128)} %pad_add_fusion.ids_ref, bf16[128,4096]{1,0:T(8,128)(2,1)} %bitcast.10, bf16[128,4096]{1,0:T(8,128)(2,1)} %copy-done, ...), custom_call_target="tpu_custom_call" | custom-call | flops 4294967296 | bytes 13631488 | tf_op jit(solution)/shard_map/proj_terms/pallas_call | solution.py:406
  106.4 2.9 %collective-permute-start.27 = (bf16[4,512,128]{2,1,0:T(8,128)(2,1)}, bf16[4,512,128]{2,1,0:T(8,128)(2,1)S(1)}, u32[]{:S(2)}, u32[]{:S(2)}) collective-permute-start(bf16[4,512,128]{2,1,0:T(8,128)(2,1)} %get-tuple-element.59), channel_id=1, source_target_pairs={{0,3},{1,0},{2,1},{3,2},{4,7},{5,4},{6,5},{7,6},{8,11},{9,8},{10,9... | collective-permute-start | bytes 1572872 | tf_op jit(solution)/shard_map/ppermute | solution.py:471
  109.3 18.7 %collective-permute-done.26.up_ref = bf16[4,512,128]{2,1,0:T(8,128)(2,1)S(1)} collective-permute-done((bf16[4,512,128]{2,1,0:T(8,128)(2,1)}, bf16[4,512,128]{2,1,0:T(8,128)(2,1)S(1)}, u32[]{:S(2)}, u32[]{:S(2)}) %collective-permute-start.26) | collective-permute-done | bytes 524320 | tf_op jit(solution)/shard_map/ppermute | solution.py:471
  128.0 0.8 copy-done.7
  129.0 2.4 %join.1 = (bf16[8,512,128]{2,1,0:T(8,128)(2,1)}, bf16[8,512,128]{2,1,0:T(8,128)(2,1)}) custom-call(bf16[8,512,128]{2,1,0:T(8,128)(2,1)} %get-tuple-element.57.low_ref, bf16[4,512,128]{2,1,0:T(8,128)(2,1)} %copy-done.7, bf16[8,512,128]{2,1,0:T(8,128)(2,1)} %get-tuple-element.58.high_ref, ...), custom_call_target="tpu_custom_call", output_to_operand_aliasing={{0}: (0, {}), {1}: (2, {})} | custom-call | flops 524288 | bytes 3145728 | tf_op jit(solution)/shard_map/join/pallas_call | solution.py:450
  131.4 1.4 collective-permute-start.28
  132.8 1.8 collective-permute-start.29
  134.6 1.9 slice.14
  136.7 1.9 slice.15
  138.6 3.0 %collective-permute-start.18 = (bf16[4,128,512]{2,1,0:T(8,128)(2,1)}, bf16[4,128,512]{2,1,0:T(8,128)(2,1)S(1)}, u32[]{:S(2)}, u32[]{:S(2)}) collective-permute-start(bf16[4,128,512]{2,1,0:T(8,128)(2,1)} %slice.15), channel_id=1, source_target_pairs={{0,3},{1,0},{2,1},{3,2},{4,7},{5,4},{6,5},{7,6},{8,11},{9,8},{10,9... | collective-permute-start | bytes 1572872 | tf_op jit(solution)/shard_map/ppermute | solution.py:471
  141.6 0.7 concatenate.14.ids_ref
  142.3 9.1 %upstream_most.1.refs_10_ = f32[1024,512]{1,0:T(8,128)} custom-call(s32[10]{0:T(128)} %pad_add_fusion.ids_ref, bf16[128,4096]{1,0:T(8,128)(2,1)} %bitcast.11, bf16[128,4096]{1,0:T(8,128)(2,1)} %copy-done, bf16[128,4096]{1,0:T(8,128)(2,1)} %copy-done.1, bf16[128,4096]{1,0:T(8,128)(2,1)} %copy-done.2, bf16[128,4096]{1,0:T(8,128)(2,1)} %collective-permute-done.11.refs_4_, ...), custom_call_target="tpu_custom_call" | custom-call | flops 3221225472 | bytes 11534336 | tf_op jit(solution)/shard_map/upstream_most/pallas_call | solution.py:312
  151.4 16.8 %collective-permute-done.17.refs_8_ = bf16[4,128,512]{2,1,0:T(8,128)(2,1)S(1)} collective-permute-done((bf16[4,128,512]{2,1,0:T(8,128)(2,1)}, bf16[4,128,512]{2,1,0:T(8,128)(2,1)S(1)}, u32[]{:S(2)}, u32[]{:S(2)}) %collective-permute-start.17) | collective-permute-done | bytes 524320 | tf_op jit(solution)/shard_map/ppermute | solution.py:471
  168.2 0.8 copy-done.4
  169.0 0.8 copy-done.5
  169.8 8.2 %upstream_rest.1.refs_8_ = bf16[8,128,512]{2,1,0:T(8,128)(2,1)} custom-call(s32[10]{0:T(128)} %pad_add_fusion.ids_ref, bf16[128,4096]{1,0:T(8,128)(2,1)} %bitcast.12, bf16[128,4096]{1,0:T(8,128)(2,1)} %copy-done, bf16[128,4096]{1,0:T(8,128)(2,1)} %copy-done.1, bf16[128,4096]{1,0:T(8,128)(2,1)} %copy-done.2, ...), custom_call_target="tpu_custom_call" | custom-call | flops 1073741824 | bytes 11534336 | tf_op jit(solution)/shard_map/upstream_rest/pallas_call | solution.py:337
  178.0 13.2 %attend_grad.1 = (bf16[128,768]{1,0:T(8,128)(2,1)}, bf16[128,768]{1,0:T(8,128)(2,1)}, bf16[128,768]{1,0:T(8,128)(2,1)}, bf16[128,768]{1,0:T(8,128)(2,1)}, bf16[1...) custom-call(s32[18]{0:T(128)} %concatenate.14.ids_ref, ...), custom_call_target="tpu_custom_call" | custom-call | flops 2348810240 | bytes 4718592 | tf_op jit(solution)/shard_map/attend_grad/pallas_call | solution.py:161
  191.2 1.4 add_convert_fusion
  192.7 7.3 %all-to-all-start.1 = ((bf16[8,512,128]{2,1,0:T(8,128)(2,1)}), bf16[8,512,128]{2,1,0:T(8,128)(2,1)S(1)}, u32[]{:S(2)}, u32[]{:S(2)}) async-start(bf16[8,512,128]{2,1,0:T(8,128)(2,1)} %add_convert_fusion), calls=%async_computation.1 | async-start | bytes 2097152 | tf_op jit(solution)/shard_map/all_to_all | solution.py:483
  200.0 0.8 collective-permute-start.19
  200.8 1.9 collective-permute-start.20
  202.7 2.6 %collective-permute-start.21 = (bf16[128,768]{1,0:T(8,128)(2,1)S(1)}, bf16[128,768]{1,0:T(8,128)(2,1)S(1)}, u32[]{:S(2)}, u32[]{:S(2)}) collective-permute-start(bf16[128,768]{1,0:T(8,128)(2,1)S(1)} %copy-done.26), channel_id=1, source_target_pairs={{0,128},{32,160},{64,192},{96,224},{128,0},{160,32},{192,64},{224,... | collective-permute-start | bytes 589832 | tf_op jit(solution)/shard_map/ppermute | solution.py:488
  205.3 2.1 collective-permute-start.23
  207.8 1.7 collective-permute-done.20.refs_2_
  209.6 1.7 collective-permute-start.25
  211.3 2.3 %collective-permute-done.21.refs_3_ = bf16[128,768]{1,0:T(8,128)(2,1)S(1)} collective-permute-done((bf16[128,768]{1,0:T(8,128)(2,1)S(1)}, bf16[128,768]{1,0:T(8,128)(2,1)S(1)}, u32[]{:S(2)}, u32[]{:S(2)}) %collective-permute-start.21) | collective-permute-done | bytes 196640 | tf_op jit(solution)/shard_map/ppermute | solution.py:488
  213.6 0.9 collective-permute-done.23.refs_5_
  214.5 3.3 %collective-permute-done.24.refs_6_ = bf16[128,768]{1,0:T(8,128)(2,1)S(1)} collective-permute-done((bf16[128,768]{1,0:T(8,128)(2,1)S(1)}, bf16[128,768]{1,0:T(8,128)(2,1)S(1)}, u32[]{:S(2)}, u32[]{:S(2)}) %collective-permute-start.24) | collective-permute-done | bytes 196640 | tf_op jit(solution)/shard_map/ppermute | solution.py:488
  217.8 1.6 collective-permute-done.25.refs_7_
  219.5 0.7 copy-done.15
  220.1 3.4 %unpack.1 = (bf16[1,128,4096]{2,1,0:T(8,128)(2,1)}, bf16[1,128,1024]{2,1,0:T(8,128)(2,1)}, bf16[1,128,1024]{2,1,0:T(8,128)(2,1)}) custom-call(s32[10]{0:T(128)} %pad_add_fusion.ids_ref, bf16[128,768]{1,0:T(8,128)(2,1)} %get-tuple-element.45.refs_0_, bf16[128,768]{1,0:T(8,128)(2,1)} %copy-done.9, bf16[128,768]{1,0:T(8,128)(2,1)} %copy-done.10, ...), custom_call_target="tpu_custom_call" | custom-call | bytes 3145728 | tf_op jit(solution)/shard_map/unpack/pallas_call | solution.py:223
  223.6 3.6 %all-to-all-done.1 = bf16[8,512,128]{2,1,0:T(8,128)(2,1)S(1)} async-done(((bf16[8,512,128]{2,1,0:T(8,128)(2,1)}), bf16[8,512,128]{2,1,0:T(8,128)(2,1)S(1)}, u32[]{:S(2)}, u32[]{:S(2)}) %all-to-all-start.1) | async-done | bytes 1048608 | tf_op jit(solution)/shard_map/all_to_all | solution.py:483
  227.3 0.8 copy.15
  (86 shorter events, 2.5 us)
Async XLA Ops:
  0.6 35.7 %copy-start.16 = (bf16[128,512]{1,0:T(8,128)(2,1)S(1)}, bf16[128,512]{1,0:T(8,128)(2,1)}, u32[]{:S(2)}) copy-start(bf16[128,512]{1,0:T(8,128)(2,1)} %param.12) | copy-start | bytes 393220
  0.6 25.2 %collective-permute-start.7 = (bf16[128,4096]{1,0:T(8,128)(2,1)}, bf16[128,4096]{1,0:T(8,128)(2,1)S(1)}, u32[]{:S(2)}, u32[]{:S(2)}) collective-permute-start(bf16[128,4096]{1,0:T(8,128)(2,1)} %bitcast.7), channel_id=1, source_target_pairs={{0,64},{32,96},{64,128},{96,160},{128,192},{160,224},{192,0},{224,... | collective-permute-start | bytes 3145736 | tf_op jit(solution)/shard_map/ppermute | solution.py:488
  2.2 25.9 %collective-permute-start.8 = (bf16[128,4096]{1,0:T(8,128)(2,1)}, bf16[128,4096]{1,0:T(8,128)(2,1)S(1)}, u32[]{:S(2)}, u32[]{:S(2)}) collective-permute-start(bf16[128,4096]{1,0:T(8,128)(2,1)} %bitcast.8), channel_id=1, source_target_pairs={{0,192},{32,224},{64,0},{96,32},{128,64},{160,96},{192,128},{224,1... | collective-permute-start | bytes 3145736 | tf_op jit(solution)/shard_map/ppermute | solution.py:488
  3.1 88.9 %collective-permute-start.11 = (bf16[128,4096]{1,0:T(8,128)(2,1)}, bf16[128,4096]{1,0:T(8,128)(2,1)}, u32[]{:S(2)}, u32[]{:S(2)}) collective-permute-start(bf16[128,4096]{1,0:T(8,128)(2,1)} %bitcast.9), channel_id=1, source_target_pairs={{0,32},{32,0},{64,96},{96,64},{128,160},{160,128},{192,224},{224,1... | collective-permute-start | bytes 3145736 | tf_op jit(solution)/shard_map/ppermute | solution.py:488
  25.8 24.3 %copy-start = (bf16[128,4096]{1,0:T(8,128)(2,1)}, bf16[128,4096]{1,0:T(8,128)(2,1)S(1)}, u32[]{:S(2)}) copy-start(bf16[128,4096]{1,0:T(8,128)(2,1)S(1)} %collective-permute-done.7.refs_1_) | copy-start | bytes 3145732
  25.9 20.3 %collective-permute-start.9 = (bf16[64,4096]{1,0:T(8,128)(2,1)S(1)}, bf16[64,4096]{1,0:T(8,128)(2,1)S(1)}, u32[]{:S(2)}, u32[]{:S(2)}) collective-permute-start(bf16[64,4096]{1,0:T(8,128)(2,1)S(1)} %slice.16), channel_id=1, source_target_pairs={{0,64},{32,96},{64,128},{96,160},{128,192},{160,224},{192,0},{224,... | collective-permute-start | bytes 1572872 | tf_op jit(solution)/shard_map/ppermute | solution.py:488
  28.1 23.2 %copy-start.1 = (bf16[128,4096]{1,0:T(8,128)(2,1)}, bf16[128,4096]{1,0:T(8,128)(2,1)S(1)}, u32[]{:S(2)}) copy-start(bf16[128,4096]{1,0:T(8,128)(2,1)S(1)} %collective-permute-done.8.refs_2_) | copy-start | bytes 3145732
  29.0 21.0 %collective-permute-start.10 = (bf16[64,4096]{1,0:T(8,128)(2,1)}, bf16[64,4096]{1,0:T(8,128)(2,1)}, u32[]{:S(2)}, u32[]{:S(2)}) collective-permute-start(bf16[64,4096]{1,0:T(8,128)(2,1)} %slice.17), channel_id=1, source_target_pairs={{0,192},{32,224},{64,0},{96,32},{128,64},{160,96},{192,128},{224,1... | collective-permute-start | bytes 1572872 | tf_op jit(solution)/shard_map/ppermute | solution.py:488
  33.5 17.8 %collective-permute-start = (bf16[128,768]{1,0:T(8,128)(2,1)}, bf16[128,768]{1,0:T(8,128)(2,1)S(1)}, u32[]{:S(2)}, u32[]{:S(2)}) collective-permute-start(bf16[128,768]{1,0:T(8,128)(2,1)} %get-tuple-element.35), channel_id=1, source_target_pairs={{0,64},{32,96},{64,128},{96,160},{128,192},{160,224},{192,0},{224,... | collective-permute-start | bytes 589832 | tf_op jit(solution)/shard_map/ppermute | solution.py:488
  35.0 16.9 %collective-permute-start.1 = (bf16[128,768]{1,0:T(8,128)(2,1)}, bf16[128,768]{1,0:T(8,128)(2,1)}, u32[]{:S(2)}, u32[]{:S(2)}) collective-permute-start(bf16[128,768]{1,0:T(8,128)(2,1)} %get-tuple-element.36), channel_id=1, source_target_pairs={{0,192},{32,224},{64,0},{96,32},{128,64},{160,96},{192,128},{224,1... | collective-permute-start | bytes 589832 | tf_op jit(solution)/shard_map/ppermute | solution.py:488
  37.3 17.1 %copy-start.17 = (s32[1,32]{1,0:T(1,128)S(1)}, s32[1,32]{1,0:T(1,128)}, u32[]{:S(2)}) copy-start(s32[1,32]{1,0:T(1,128)} %param.13) | copy-start | bytes 388
  37.3 53.0 %all-to-all-start = ((bf16[8,128,512]{2,1,0:T(8,128)(2,1)}), bf16[8,128,512]{2,1,0:T(8,128)(2,1)}, u32[]{:S(2)}, u32[]{:S(2)}) async-start(bf16[8,128,512]{2,1,0:T(8,128)(2,1)} %broadcast_in_dim.41), calls=%async_computation | async-start | bytes 2097152 | tf_op jit(solution)/shard_map/all_to_all | solution.py:483
  46.1 0.8 copy-start.6
  46.9 7.5 %collective-permute-start.2 = (bf16[128,768]{1,0:T(8,128)(2,1)}, bf16[128,768]{1,0:T(8,128)(2,1)}, u32[]{:S(2)}, u32[]{:S(2)}) collective-permute-start(bf16[128,768]{1,0:T(8,128)(2,1)} %get-tuple-element.37), channel_id=1, source_target_pairs={{0,128},{32,160},{64,192},{96,224},{128,0},{160,32},{192,64},{224,... | collective-permute-start | bytes 589832 | tf_op jit(solution)/shard_map/ppermute | solution.py:488
  50.1 43.5 %collective-permute-start.12 = (bf16[128,4096]{1,0:T(8,128)(2,1)S(1)}, bf16[128,4096]{1,0:T(8,128)(2,1)}, u32[]{:S(2)}, u32[]{:S(2)}) collective-permute-start(bf16[128,4096]{1,0:T(8,128)(2,1)S(1)} %collective-permute-done.7.refs_1_), channel_id=1, source_target_pairs={{0,32},{32,0},{64,96},{96,64},{128,160},{160,128},{192,224},{224,1... | collective-permute-start | bytes 3145736 | tf_op jit(solution)/shard_map/ppermute | solution.py:488
  51.3 42.3 %copy-start.2 = (bf16[128,4096]{1,0:T(8,128)(2,1)}, bf16[128,4096]{1,0:T(8,128)(2,1)S(1)}, u32[]{:S(2)}) copy-start(bf16[128,4096]{1,0:T(8,128)(2,1)S(1)} %constant_dynamic-update-slice_fusion.refs_3_) | copy-start | bytes 3145732
  51.3 30.8 %copy-start.18 = (bf16[128,768]{1,0:T(8,128)(2,1)}, bf16[128,768]{1,0:T(8,128)(2,1)S(1)}, u32[]{:S(2)}) copy-start(bf16[128,768]{1,0:T(8,128)(2,1)S(1)} %collective-permute-done.refs_1_) | copy-start | bytes 589828
  51.3 42.3 %collective-permute-start.13 = (bf16[128,4096]{1,0:T(8,128)(2,1)S(1)}, bf16[128,4096]{1,0:T(8,128)(2,1)}, u32[]{:S(2)}, u32[]{:S(2)}) collective-permute-start(bf16[128,4096]{1,0:T(8,128)(2,1)S(1)} %collective-permute-done.8.refs_2_), channel_id=1, source_target_pairs={{0,32},{32,0},{64,96},{96,64},{128,160},{160,128},{192,224},{224,1... | collective-permute-start | bytes 3145736 | tf_op jit(solution)/shard_map/ppermute | solution.py:488
  51.9 41.7 %collective-permute-start.14 = (bf16[128,4096]{1,0:T(8,128)(2,1)S(1)}, bf16[128,4096]{1,0:T(8,128)(2,1)}, u32[]{:S(2)}, u32[]{:S(2)}) collective-permute-start(bf16[128,4096]{1,0:T(8,128)(2,1)S(1)} %constant_dynamic-update-slice_fusion.refs_3_), channel_id=1, source_target_pairs={{0,32},{32,0},{64,96},{96,64},{128,160},{160,128},{192,224},{224,1... | collective-permute-start | bytes 3145736 | tf_op jit(solution)/shard_map/ppermute | solution.py:488
  54.4 1.8 collective-permute-start.3
  56.3 8.0 %collective-permute-start.4 = (bf16[128,768]{1,0:T(8,128)(2,1)}, bf16[128,768]{1,0:T(8,128)(2,1)S(1)}, u32[]{:S(2)}, u32[]{:S(2)}) collective-permute-start(bf16[128,768]{1,0:T(8,128)(2,1)} %get-tuple-element.39), channel_id=1, source_target_pairs={{0,96},{32,64},{64,160},{96,128},{128,224},{160,192},{192,32},{224... | collective-permute-start | bytes 589832 | tf_op jit(solution)/shard_map/ppermute | solution.py:488
  64.3 12.3 %copy-start.19 = (bf16[128,768]{1,0:T(8,128)(2,1)}, bf16[128,768]{1,0:T(8,128)(2,1)S(1)}, u32[]{:S(2)}) copy-start(bf16[128,768]{1,0:T(8,128)(2,1)S(1)} %collective-permute-done.4.refs_5_) | copy-start | bytes 589828
  64.3 8.5 %collective-permute-start.5 = (bf16[128,768]{1,0:T(8,128)(2,1)}, bf16[128,768]{1,0:T(8,128)(2,1)S(1)}, u32[]{:S(2)}, u32[]{:S(2)}) collective-permute-start(bf16[128,768]{1,0:T(8,128)(2,1)} %get-tuple-element.40), channel_id=1, source_target_pairs={{0,224},{32,192},{64,32},{96,0},{128,96},{160,64},{192,160},{224,1... | collective-permute-start | bytes 589832 | tf_op jit(solution)/shard_map/ppermute | solution.py:488
  72.8 8.7 %copy-start.20 = (bf16[128,768]{1,0:T(8,128)(2,1)}, bf16[128,768]{1,0:T(8,128)(2,1)S(1)}, u32[]{:S(2)}) copy-start(bf16[128,768]{1,0:T(8,128)(2,1)S(1)} %collective-permute-done.5.refs_6_) | copy-start | bytes 589828
  72.8 8.7 %collective-permute-start.6 = (bf16[128,768]{1,0:T(8,128)(2,1)}, bf16[128,768]{1,0:T(8,128)(2,1)S(1)}, u32[]{:S(2)}, u32[]{:S(2)}) collective-permute-start(bf16[128,768]{1,0:T(8,128)(2,1)} %get-tuple-element.41), channel_id=1, source_target_pairs={{0,160},{32,128},{64,224},{96,192},{128,32},{160,0},{192,96},{224,... | collective-permute-start | bytes 589832 | tf_op jit(solution)/shard_map/ppermute | solution.py:488
  81.4 0.7 copy-start.21
  90.4 44.3 %collective-permute-start.15 = (bf16[8,128,512]{2,1,0:T(8,128)(2,1)}, bf16[8,128,512]{2,1,0:T(8,128)(2,1)}, u32[]{:S(2)}, u32[]{:S(2)}) collective-permute-start(bf16[8,128,512]{2,1,0:T(8,128)(2,1)} %all-to-all-done.refs_8_), channel_id=1, source_target_pairs={{0,1},{1,2},{2,3},{3,0},{4,5},{5,6},{6,7},{7,4},{8,9},{9,10},{10,1... | collective-permute-start | bytes 3145736 | tf_op jit(solution)/shard_map/ppermute | solution.py:471
  91.9 42.7 %collective-permute-start.16 = (bf16[8,128,512]{2,1,0:T(8,128)(2,1)}, bf16[8,128,512]{2,1,0:T(8,128)(2,1)}, u32[]{:S(2)}, u32[]{:S(2)}) collective-permute-start(bf16[8,128,512]{2,1,0:T(8,128)(2,1)} %all-to-all-done.refs_8_), channel_id=1, source_target_pairs={{0,3},{1,0},{2,1},{3,2},{4,7},{5,4},{6,5},{7,6},{8,11},{9,8},{10,9... | collective-permute-start | bytes 3145736 | tf_op jit(solution)/shard_map/ppermute | solution.py:471
  106.0 22.1 %collective-permute-start.26 = (bf16[4,512,128]{2,1,0:T(8,128)(2,1)}, bf16[4,512,128]{2,1,0:T(8,128)(2,1)S(1)}, u32[]{:S(2)}, u32[]{:S(2)}) collective-permute-start(bf16[4,512,128]{2,1,0:T(8,128)(2,1)} %get-tuple-element.42), channel_id=1, source_target_pairs={{0,1},{1,2},{2,3},{3,0},{4,5},{5,6},{6,7},{7,4},{8,9},{9,10},{10,1... | collective-permute-start | bytes 1572872 | tf_op jit(solution)/shard_map/ppermute | solution.py:471
  106.4 21.6 %collective-permute-start.27 = (bf16[4,512,128]{2,1,0:T(8,128)(2,1)}, bf16[4,512,128]{2,1,0:T(8,128)(2,1)S(1)}, u32[]{:S(2)}, u32[]{:S(2)}) collective-permute-start(bf16[4,512,128]{2,1,0:T(8,128)(2,1)} %get-tuple-element.59), channel_id=1, source_target_pairs={{0,3},{1,0},{2,1},{3,2},{4,7},{5,4},{6,5},{7,6},{8,11},{9,8},{10,9... | collective-permute-start | bytes 1572872 | tf_op jit(solution)/shard_map/ppermute | solution.py:471
  128.0 0.8 copy-start.7
  128.0 1.0 copy-start.8
  131.4 59.8 %collective-permute-start.28 = (bf16[8,512,128]{2,1,0:T(8,128)(2,1)}, bf16[8,512,128]{2,1,0:T(8,128)(2,1)S(1)}, u32[]{:S(2)}, u32[]{:S(2)}) collective-permute-start(bf16[8,512,128]{2,1,0:T(8,128)(2,1)} %get-tuple-element.60), channel_id=1, source_target_pairs={{0,1},{1,2},{2,3},{3,0},{4,5},{5,6},{6,7},{7,4},{8,9},{9,10},{10,1... | collective-permute-start | bytes 3145736 | tf_op jit(solution)/shard_map/ppermute | solution.py:471
  132.8 58.4 %collective-permute-start.29 = (bf16[8,512,128]{2,1,0:T(8,128)(2,1)}, bf16[8,512,128]{2,1,0:T(8,128)(2,1)S(1)}, u32[]{:S(2)}, u32[]{:S(2)}) collective-permute-start(bf16[8,512,128]{2,1,0:T(8,128)(2,1)} %get-tuple-element.61), channel_id=1, source_target_pairs={{0,3},{1,0},{2,1},{3,2},{4,7},{5,4},{6,5},{7,6},{8,11},{9,8},{10,9... | collective-permute-start | bytes 3145736 | tf_op jit(solution)/shard_map/ppermute | solution.py:471
  136.5 31.7 %collective-permute-start.17 = (bf16[4,128,512]{2,1,0:T(8,128)(2,1)}, bf16[4,128,512]{2,1,0:T(8,128)(2,1)S(1)}, u32[]{:S(2)}, u32[]{:S(2)}) collective-permute-start(bf16[4,128,512]{2,1,0:T(8,128)(2,1)} %slice.14), channel_id=1, source_target_pairs={{0,1},{1,2},{2,3},{3,0},{4,5},{5,6},{6,7},{7,4},{8,9},{9,10},{10,1... | collective-permute-start | bytes 1572872 | tf_op jit(solution)/shard_map/ppermute | solution.py:471
  138.6 29.6 %collective-permute-start.18 = (bf16[4,128,512]{2,1,0:T(8,128)(2,1)}, bf16[4,128,512]{2,1,0:T(8,128)(2,1)S(1)}, u32[]{:S(2)}, u32[]{:S(2)}) collective-permute-start(bf16[4,128,512]{2,1,0:T(8,128)(2,1)} %slice.15), channel_id=1, source_target_pairs={{0,3},{1,0},{2,1},{3,2},{4,7},{5,4},{6,5},{7,6},{8,11},{9,8},{10,9... | collective-permute-start | bytes 1572872 | tf_op jit(solution)/shard_map/ppermute | solution.py:471
  168.2 0.8 copy-start.4
  169.0 0.8 copy-start.5
  178.0 13.2 %copy-start.3 = (bf16[8,512,128]{2,1,0:T(8,128)(2,1)S(1)}, bf16[8,512,128]{2,1,0:T(8,128)(2,1)}, u32[]{:S(2)}) copy-start(bf16[8,512,128]{2,1,0:T(8,128)(2,1)} %get-tuple-element.56) | copy-start | bytes 3145732
  192.7 7.4 %copy-start.28 = (bf16[128,768]{1,0:T(8,128)(2,1)S(1)}, bf16[128,768]{1,0:T(8,128)(2,1)}, u32[]{:S(2)}) copy-start(bf16[128,768]{1,0:T(8,128)(2,1)} %get-tuple-element.46) | copy-start | bytes 589828
  192.7 8.2 %copy-start.27 = (bf16[128,768]{1,0:T(8,128)(2,1)S(1)}, bf16[128,768]{1,0:T(8,128)(2,1)}, u32[]{:S(2)}) copy-start(bf16[128,768]{1,0:T(8,128)(2,1)} %get-tuple-element.47) | copy-start | bytes 589828
  192.7 10.1 %copy-start.26 = (bf16[128,768]{1,0:T(8,128)(2,1)S(1)}, bf16[128,768]{1,0:T(8,128)(2,1)}, u32[]{:S(2)}) copy-start(bf16[128,768]{1,0:T(8,128)(2,1)} %get-tuple-element.48) | copy-start | bytes 589828
  192.7 12.7 %copy-start.25 = (bf16[128,768]{1,0:T(8,128)(2,1)S(1)}, bf16[128,768]{1,0:T(8,128)(2,1)}, u32[]{:S(2)}) copy-start(bf16[128,768]{1,0:T(8,128)(2,1)} %get-tuple-element.49) | copy-start | bytes 589828
  192.7 12.7 %copy-start.24 = (bf16[128,768]{1,0:T(8,128)(2,1)S(1)}, bf16[128,768]{1,0:T(8,128)(2,1)}, u32[]{:S(2)}) copy-start(bf16[128,768]{1,0:T(8,128)(2,1)} %get-tuple-element.50) | copy-start | bytes 589828
  192.7 15.2 %copy-start.23 = (bf16[128,768]{1,0:T(8,128)(2,1)S(1)}, bf16[128,768]{1,0:T(8,128)(2,1)}, u32[]{:S(2)}) copy-start(bf16[128,768]{1,0:T(8,128)(2,1)} %get-tuple-element.51) | copy-start | bytes 589828
  192.7 16.9 %copy-start.22 = (bf16[128,768]{1,0:T(8,128)(2,1)S(1)}, bf16[128,768]{1,0:T(8,128)(2,1)}, u32[]{:S(2)}) copy-start(bf16[128,768]{1,0:T(8,128)(2,1)} %get-tuple-element.52) | copy-start | bytes 589828
  192.7 34.4 %all-to-all-start.1 = ((bf16[8,512,128]{2,1,0:T(8,128)(2,1)}), bf16[8,512,128]{2,1,0:T(8,128)(2,1)S(1)}, u32[]{:S(2)}, u32[]{:S(2)}) async-start(bf16[8,512,128]{2,1,0:T(8,128)(2,1)} %add_convert_fusion), calls=%async_computation.1 | async-start | bytes 2097152 | tf_op jit(solution)/shard_map/all_to_all | solution.py:483
  200.0 7.8 %collective-permute-start.19 = (bf16[128,768]{1,0:T(8,128)(2,1)S(1)}, bf16[128,768]{1,0:T(8,128)(2,1)S(1)}, u32[]{:S(2)}, u32[]{:S(2)}) collective-permute-start(bf16[128,768]{1,0:T(8,128)(2,1)S(1)} %copy-done.28), channel_id=1, source_target_pairs={{0,64},{32,96},{64,128},{96,160},{128,192},{160,224},{192,0},{224,... | collective-permute-start | bytes 589832 | tf_op jit(solution)/shard_map/ppermute | solution.py:488
  200.8 8.8 %collective-permute-start.20 = (bf16[128,768]{1,0:T(8,128)(2,1)S(1)}, bf16[128,768]{1,0:T(8,128)(2,1)S(1)}, u32[]{:S(2)}, u32[]{:S(2)}) collective-permute-start(bf16[128,768]{1,0:T(8,128)(2,1)S(1)} %copy-done.27), channel_id=1, source_target_pairs={{0,192},{32,224},{64,0},{96,32},{128,64},{160,96},{192,128},{224,1... | collective-permute-start | bytes 589832 | tf_op jit(solution)/shard_map/ppermute | solution.py:488
  202.7 10.9 %collective-permute-start.21 = (bf16[128,768]{1,0:T(8,128)(2,1)S(1)}, bf16[128,768]{1,0:T(8,128)(2,1)S(1)}, u32[]{:S(2)}, u32[]{:S(2)}) collective-permute-start(bf16[128,768]{1,0:T(8,128)(2,1)S(1)} %copy-done.26), channel_id=1, source_target_pairs={{0,128},{32,160},{64,192},{96,224},{128,0},{160,32},{192,64},{224,... | collective-permute-start | bytes 589832 | tf_op jit(solution)/shard_map/ppermute | solution.py:488
  205.3 8.3 %collective-permute-start.22 = (bf16[128,768]{1,0:T(8,128)(2,1)S(1)}, bf16[128,768]{1,0:T(8,128)(2,1)S(1)}, u32[]{:S(2)}, u32[]{:S(2)}) collective-permute-start(bf16[128,768]{1,0:T(8,128)(2,1)S(1)} %copy-done.25), channel_id=1, source_target_pairs={{0,32},{32,0},{64,96},{96,64},{128,160},{160,128},{192,224},{224,1... | collective-permute-start | bytes 589832 | tf_op jit(solution)/shard_map/ppermute | solution.py:488
  205.3 9.2 %collective-permute-start.23 = (bf16[128,768]{1,0:T(8,128)(2,1)S(1)}, bf16[128,768]{1,0:T(8,128)(2,1)S(1)}, u32[]{:S(2)}, u32[]{:S(2)}) collective-permute-start(bf16[128,768]{1,0:T(8,128)(2,1)S(1)} %copy-done.24), channel_id=1, source_target_pairs={{0,96},{32,64},{64,160},{96,128},{128,224},{160,192},{192,32},{224... | collective-permute-start | bytes 589832 | tf_op jit(solution)/shard_map/ppermute | solution.py:488
  207.8 11.6 %copy-start.9 = (bf16[128,768]{1,0:T(8,128)(2,1)}, bf16[128,768]{1,0:T(8,128)(2,1)S(1)}, u32[]{:S(2)}) copy-start(bf16[128,768]{1,0:T(8,128)(2,1)S(1)} %collective-permute-done.19.refs_1_) | copy-start | bytes 589828
  207.8 10.0 %collective-permute-start.24 = (bf16[128,768]{1,0:T(8,128)(2,1)S(1)}, bf16[128,768]{1,0:T(8,128)(2,1)S(1)}, u32[]{:S(2)}, u32[]{:S(2)}) collective-permute-start(bf16[128,768]{1,0:T(8,128)(2,1)S(1)} %copy-done.23), channel_id=1, source_target_pairs={{0,224},{32,192},{64,32},{96,0},{128,96},{160,64},{192,160},{224,1... | collective-permute-start | bytes 589832 | tf_op jit(solution)/shard_map/ppermute | solution.py:488
  209.6 9.8 %copy-start.10 = (bf16[128,768]{1,0:T(8,128)(2,1)}, bf16[128,768]{1,0:T(8,128)(2,1)S(1)}, u32[]{:S(2)}) copy-start(bf16[128,768]{1,0:T(8,128)(2,1)S(1)} %collective-permute-done.20.refs_2_) | copy-start | bytes 589828
  209.6 9.8 %collective-permute-start.25 = (bf16[128,768]{1,0:T(8,128)(2,1)S(1)}, bf16[128,768]{1,0:T(8,128)(2,1)S(1)}, u32[]{:S(2)}, u32[]{:S(2)}) collective-permute-start(bf16[128,768]{1,0:T(8,128)(2,1)S(1)} %copy-done.22), channel_id=1, source_target_pairs={{0,160},{32,128},{64,224},{96,192},{128,32},{160,0},{192,96},{224,... | collective-permute-start | bytes 589832 | tf_op jit(solution)/shard_map/ppermute | solution.py:488
  213.6 5.8 %copy-start.11 = (bf16[128,768]{1,0:T(8,128)(2,1)}, bf16[128,768]{1,0:T(8,128)(2,1)S(1)}, u32[]{:S(2)}) copy-start(bf16[128,768]{1,0:T(8,128)(2,1)S(1)} %collective-permute-done.21.refs_3_) | copy-start | bytes 589828
  213.6 5.8 %copy-start.12 = (bf16[128,768]{1,0:T(8,128)(2,1)}, bf16[128,768]{1,0:T(8,128)(2,1)S(1)}, u32[]{:S(2)}) copy-start(bf16[128,768]{1,0:T(8,128)(2,1)S(1)} %collective-permute-done.22.refs_4_) | copy-start | bytes 589828
  214.5 4.9 %copy-start.13 = (bf16[128,768]{1,0:T(8,128)(2,1)}, bf16[128,768]{1,0:T(8,128)(2,1)S(1)}, u32[]{:S(2)}) copy-start(bf16[128,768]{1,0:T(8,128)(2,1)S(1)} %collective-permute-done.23.refs_5_) | copy-start | bytes 589828
  217.8 1.6 copy-start.14
  219.4 0.7 copy-start.15

commit v6 on v5

--- a/solution.py
+++ b/solution.py
@@ -255,8 +255,9 @@
 
 
 def most_kernel(ids_ref, *refs):
-    pieces, (mine_ref, below_ref, above_ref, o_ref) = refs[:-4], refs[-4:]
+    pieces, (mine_ref, below_ref, above_ref, o_ref, left_ref) = refs[:-5], refs[-5:]
     near = GRID["fsdp"]
+    left_ref[...] = gathered_rows(ids_ref, pieces, (2,))
     rows = gathered_rows(ids_ref, pieces, (0, near - 1, 1))
     width = mine_ref.shape[2]
     weight = jnp.concatenate(
@@ -274,26 +275,14 @@
         o_ref[...] += part
 
 
-def rest_kernel(ids_ref, *refs):
-    pieces, (low_ref, high_ref, sum_ref, o_ref, acc_ref) = refs[:-5], refs[-5:]
-    step = pl.program_id(0)
-    last = pl.num_programs(0) - 1
-    rows = gathered_rows(ids_ref, pieces, (2,))
-    weight = jnp.where(step * 2 <= last, low_ref[...], high_ref[...])
-    part = jnp.dot(rows, weight.reshape(-1, weight.shape[2]), preferred_element_type=F32)
-
-    @pl.when(step == 0)
-    def _():
-        acc_ref[...] = sum_ref[...] + part
-
-    @pl.when(step > 0)
-    def _():
-        acc_ref[...] += part
-
-    @pl.when(step == last)
-    def _():
-        for p in range(len(pieces)):
-            o_ref[ids_ref[p]] = acc_ref[p * TOK : (p + 1) * TOK, :].astype(BF16)
+def rest_kernel(ids_ref, rows_ref, low_ref, high_ref, sum_ref, o_ref):
+    width = low_ref.shape[2]
+    weight = jnp.concatenate([x[...].reshape(-1, width) for x in (low_ref, high_ref)], 0)
+    total = sum_ref[...] + jnp.dot(rows_ref[...], weight, preferred_element_type=F32)
+    count = rows_ref.shape[0] // TOK
+    first = pl.program_id(0) * count
+    for p in range(count):
+        o_ref[ids_ref[first + p]] = total[p * TOK : (p + 1) * TOK, :].astype(BF16)
 
 
 PLANES = 2
@@ -316,9 +305,15 @@
             grid=(far // PLANES,),
             in_specs=chunk_specs(pieces)
             + [pl.BlockSpec((PLANES, rows, width), lambda i, ids: (i, 0, 0))] * 3,
-            out_specs=whole((tokens, width)),
-        ),
-        out_shape=jax.ShapeDtypeStruct((tokens, width), F32),
+            out_specs=[
+                whole((tokens, width)),
+                pl.BlockSpec((tokens, PLANES * TOK), lambda i, ids: (0, i)),
+            ],
+        ),
+        out_shape=[
+            jax.ShapeDtypeStruct((tokens, width), F32),
+            jax.ShapeDtypeStruct((tokens, far * TOK), BF16),
+        ],
         cost_estimate=pl.CostEstimate(
             flops=2 * tokens * width * depth,
             bytes_accessed=2 * (tokens * (depth + 2 * width) + depth * width),
@@ -328,34 +323,31 @@
     )(ids, *pieces, *weights)
 
 
-def upstream_rest(ids, pieces, ends, sums):
-    middle, rows, width = ends[0].shape
-    count = len(pieces)
-    steps = 2 * middle // PLANES
-    block = (PLANES, rows, width)
-    depth = 2 * middle * rows
+def upstream_rest(ids, rows, ends, sums):
+    tokens, depth = rows.shape
+    width = sums.shape[1]
+    steps = 2
     return pl.pallas_call(
         rest_kernel,
         grid_spec=pltpu.PrefetchScalarGridSpec(
             num_scalar_prefetch=1,
             grid=(steps,),
-            in_specs=chunk_specs(pieces)
-            + [
-                pl.BlockSpec(block, lambda i, ids: (jnp.minimum(i, steps // 2 - 1), 0, 0)),
-                pl.BlockSpec(block, lambda i, ids: (jnp.maximum(i - steps // 2, 0), 0, 0)),
-                whole(sums.shape),
+            in_specs=[
+                pl.BlockSpec((tokens // steps, depth), lambda i, ids: (i, 0)),
+                whole(ends[0].shape),
+                whole(ends[1].shape),
+                pl.BlockSpec((tokens // steps, width), lambda i, ids: (i, 0)),
             ],
-            out_specs=whole((count, TOK, width)),
-            scratch_shapes=[pltpu.VMEM(sums.shape, F32)],
-        ),
-        out_shape=jax.ShapeDtypeStruct((count, TOK, width), BF16),
-        cost_estimate=pl.CostEstimate(
-            flops=2 * count * TOK * width * depth,
-            bytes_accessed=2 * count * TOK * (4 * depth + 3 * width),
+            out_specs=whole((tokens // TOK, TOK, width)),
+        ),
+        out_shape=jax.ShapeDtypeStruct((tokens // TOK, TOK, width), BF16),
+        cost_estimate=pl.CostEstimate(
+            flops=2 * tokens * width * depth,
+            bytes_accessed=2 * (tokens * (depth + 3 * width) + depth * width),
             transcendentals=0,
         ),
         name="upstream_rest",
-    )(ids, *pieces, *ends, sums)
+    )(ids, rows, *ends, sums)
 
 
 def proj_kernel(ids_ref, *refs):
@@ -524,10 +516,10 @@
     up, down = shift(low, "fsdp", 1), shift(high, "fsdp", -1)
     below, above = after((below, above), low)
     ends = [shift(below[:far], "fsdp", 1), shift(above[far:], "fsdp", -1)]
-    sums = upstream_most(ids, pieces, [weight, below, above])
+    sums, rows = upstream_most(ids, pieces, [weight, below, above])
     following, before = join(following, up, before, down)
     up, down = shift(following, "fsdp", 1), shift(before, "fsdp", -1)
-    arriving = upstream_rest(ids, pieces, ends, sums)
+    arriving = upstream_rest(ids, rows, ends, sums)
     grads = attend_grad(jnp.concatenate([ids, targets]), packed, arriving, lo, hi)
     up, down = after((up, down), grads[0])
     first = (same.astype(F32) + up.astype(F32) + down.astype(F32)).astype(BF16)

time: 233 us -> 228 us (0.979)
  Pallas kernels: 60.3 us -> 57.8 us
    pallas_call x1, Pallas kernels: 8.25 us -> 4.91 us  [upstream_rest(): pl.pallas_call(rest_kernel, grid_spec=pltpu.PrefetchScalarGridSpec(num_sc...]
where the time goes in v6:
time: 228 us; the launch traced here: 224 us
  waiting for transfers between devices  89.1 us (39%)
  Pallas kernels  57.8 us (25%)
  starting transfers between devices  57.5 us (25%)
  local copies, waits for them, and re-layouts  14.1 us (6%)
  other arithmetic  4.33 us (2%)
    ppermute x22, waiting for transfers between devices, hop(): return lax.ppermute(x, 'seq', pairs)  54.2 us
    ppermute x8, waiting for transfers between devices, shift(): return lax.ppermute(x, axis, [(i, (i + by) % n) for i in range(n)])  33.3 us
    ppermute x22, starting transfers between devices, hop(): return lax.ppermute(x, 'seq', pairs)  28.1 us
    all_to_all x2, starting transfers between devices, swap(): return lax.all_to_all(x, axis, split_axis=0, concat_axis=0, tiled=True)  16.1 us
    ppermute x8, starting transfers between devices, shift(): return lax.ppermute(x, axis, [(i, (i + by) % n) for i in range(n)])  13.3 us
    pallas_call x1, Pallas kernels, attend_grad(): pl.pallas_call(bwd_kernel, grid_spec=pltpu.PrefetchScalarGridSpec(num_sca...  13.2 us
    pallas_call x1, Pallas kernels, proj_terms(): pl.pallas_call(proj_kernel, grid_spec=pltpu.PrefetchScalarGridSpec(num_sc...  12.3 us
    pallas_call x1, Pallas kernels, upstream_most(): pl.pallas_call(most_kernel, grid_spec=pltpu.PrefetchScalarGridSpec(num_sc...  9.93 us
  transfers between devices with their start and end apart: 32, of which 15 were waited for; matrix products, arithmetic and copies ran while one was open for 5% of the time, Pallas kernels for 26%

profile of v6, /device:TPU:2, one launch (start us, length us, event | category | flops | bytes accessed | tf_op | source)
XLA Modules:
  0.0 223.6 jit_solution(11724013363885225002)
XLA Ops:
  0.6 1.6 collective-permute-start.7
  2.2 0.8 collective-permute-start.8
  3.1 22.8 %collective-permute-done.7.refs_1_ = bf16[128,4096]{1,0:T(8,128)(2,1)S(1)} collective-permute-done((bf16[128,4096]{1,0:T(8,128)(2,1)}, bf16[128,4096]{1,0:T(8,128)(2,1)S(1)}, u32[]{:S(2)}, u32[]{:S(2)}) %collective-permute-start.7) | collective-permute-done | bytes 1048608 | tf_op jit(solution)/shard_map/ppermute | solution.py:480
  25.9 1.6 collective-permute-start.9
  27.4 0.7 add_subtract_fusion
  28.1 1.1 slice.17
  29.2 0.6 collective-permute-start.10
  29.8 0.6 pad_add_fusion.1.ids_ref
  30.4 3.3 %pack.1 = (bf16[128,768]{1,0:T(8,128)(2,1)}, bf16[128,768]{1,0:T(8,128)(2,1)}, bf16[128,768]{1,0:T(8,128)(2,1)}, bf16[128,768]{1,0:T(8,128)(2,1)}, bf16[128,768]...) custom-call(s32[8]{0:T(128)} %pad_add_fusion.1.ids_ref, ...), custom_call_target="tpu_custom_call" | custom-call | bytes 3145728 | tf_op jit(solution)/shard_map/pack/pallas_call | solution.py:195
  33.8 1.5 collective-permute-start
  35.3 1.3 collective-permute-start.1
  36.6 1.1 broadcast_in_dim.41
  37.6 8.8 %all-to-all-start = ((bf16[8,128,512]{2,1,0:T(8,128)(2,1)}), bf16[8,128,512]{2,1,0:T(8,128)(2,1)S(1)}, u32[]{:S(2)}, u32[]{:S(2)}) async-start(bf16[8,128,512]{2,1,0:T(8,128)(2,1)} %broadcast_in_dim.41), calls=%async_computation | async-start | bytes 2097152 | tf_op jit(solution)/shard_map/all_to_all | solution.py:475
  46.4 2.1 collective-permute-start.2
  48.6 0.8 constant_dynamic-update-slice_fusion.1
  49.4 0.9 constant_dynamic-update-slice_fusion.refs_3_
  50.3 0.5 collective-permute-start.13
  50.9 3.1 %collective-permute-done.2.refs_3_ = bf16[128,768]{1,0:T(8,128)(2,1)} collective-permute-done((bf16[128,768]{1,0:T(8,128)(2,1)}, bf16[128,768]{1,0:T(8,128)(2,1)}, u32[]{:S(2)}, u32[]{:S(2)}) %collective-permute-start.2) | collective-permute-done | bytes 196640 | tf_op jit(solution)/shard_map/ppermute | solution.py:480
  54.1 1.5 collective-permute-done.3.refs_4_
  55.7 2.3 %collective-permute-start.4 = (bf16[128,768]{1,0:T(8,128)(2,1)}, bf16[128,768]{1,0:T(8,128)(2,1)S(1)}, u32[]{:S(2)}, u32[]{:S(2)}) collective-permute-start(bf16[128,768]{1,0:T(8,128)(2,1)} %get-tuple-element.41), channel_id=1, source_target_pairs={{0,96},{32,64},{64,160},{96,128},{128,224},{160,192},{192,32},{224... | collective-permute-start | bytes 589832 | tf_op jit(solution)/shard_map/ppermute | solution.py:480
  58.0 5.7 %collective-permute-done.4.refs_5_ = bf16[128,768]{1,0:T(8,128)(2,1)S(1)} collective-permute-done((bf16[128,768]{1,0:T(8,128)(2,1)}, bf16[128,768]{1,0:T(8,128)(2,1)S(1)}, u32[]{:S(2)}, u32[]{:S(2)}) %collective-permute-start.4) | collective-permute-done | bytes 196640 | tf_op jit(solution)/shard_map/ppermute | solution.py:480
  63.7 3.5 %collective-permute-start.5 = (bf16[128,768]{1,0:T(8,128)(2,1)}, bf16[128,768]{1,0:T(8,128)(2,1)S(1)}, u32[]{:S(2)}, u32[]{:S(2)}) collective-permute-start(bf16[128,768]{1,0:T(8,128)(2,1)} %get-tuple-element.42), channel_id=1, source_target_pairs={{0,224},{32,192},{64,32},{96,0},{128,96},{160,64},{192,160},{224,1... | collective-permute-start | bytes 589832 | tf_op jit(solution)/shard_map/ppermute | solution.py:480
  67.2 5.0 %collective-permute-done.5.refs_6_ = bf16[128,768]{1,0:T(8,128)(2,1)S(1)} collective-permute-done((bf16[128,768]{1,0:T(8,128)(2,1)}, bf16[128,768]{1,0:T(8,128)(2,1)S(1)}, u32[]{:S(2)}, u32[]{:S(2)}) %collective-permute-start.5) | collective-permute-done | bytes 196640 | tf_op jit(solution)/shard_map/ppermute | solution.py:480
  72.2 2.5 %collective-permute-start.6 = (bf16[128,768]{1,0:T(8,128)(2,1)}, bf16[128,768]{1,0:T(8,128)(2,1)S(1)}, u32[]{:S(2)}, u32[]{:S(2)}) collective-permute-start(bf16[128,768]{1,0:T(8,128)(2,1)} %get-tuple-element.43), channel_id=1, source_target_pairs={{0,160},{32,128},{64,224},{96,192},{128,32},{160,0},{192,96},{224,... | collective-permute-start | bytes 589832 | tf_op jit(solution)/shard_map/ppermute | solution.py:480
  74.7 0.6 pad_add_fusion.ids_ref
  75.3 0.7 select_reduce_fusion
  76.0 4.8 %collective-permute-done.6.refs_7_ = bf16[128,768]{1,0:T(8,128)(2,1)S(1)} collective-permute-done((bf16[128,768]{1,0:T(8,128)(2,1)}, bf16[128,768]{1,0:T(8,128)(2,1)S(1)}, u32[]{:S(2)}, u32[]{:S(2)}) %collective-permute-start.6) | collective-permute-done | bytes 196640 | tf_op jit(solution)/shard_map/ppermute | solution.py:480
  80.8 0.7 copy-done.21
  81.5 8.3 %attend.1.refs_8_ = bf16[8,512,128]{2,1,0:T(8,128)(2,1)} custom-call(s32[10]{0:T(128)} %pad_add_fusion.ids_ref, bf16[128,768]{1,0:T(8,128)(2,1)} %get-tuple-element.36.refs_0_, bf16[128,768]{1,0:T(8,128)(2,1)} %copy-done.17, bf16[128,768]{1,0:T(8,128)(2,1)} %collective-permute-done.1.refs_2_, bf16[128,768]{1,0:T(8,128)(2,1)} %collective-permute-done.2.refs_3_, ...), custom_call_target="tpu_custom_call" | custom-call | flops 939524096 | bytes 3145728 | tf_op jit(solution)/shard_map/attend/pallas_call | solution.py:138
  89.8 1.8 collective-permute-start.15
  91.6 1.7 collective-permute-start.16
  93.3 1.0 copy-done.16
  94.3 12.3 %proj_terms.1 = (bf16[8,512,128]{2,1,0:T(8,128)(2,1)}, bf16[8,512,128]{2,1,0:T(8,128)(2,1)}, bf16[4,512,128]{2,1,0:T(8,128)(2,1)}, bf16[4,512,128]{2,1,0:T(8,128)(2,1)}, bf16[8,512,128]{2,1,0:T(8,128)(2,1)}) custom-call(s32[10]{0:T(128)} %pad_add_fusion.ids_ref, bf16[128,4096]{1,0:T(8,128)(2,1)} %bitcast.17, bf16[128,4096]{1,0:T(8,128)(2,1)} %copy-done.6, ...), custom_call_target="tpu_custom_call" | custom-call | flops 4294967296 | bytes 13631488 | tf_op jit(solution)/shard_map/proj_terms/pallas_call | solution.py:398
  107.1 2.9 %collective-permute-start.27 = (bf16[4,512,128]{2,1,0:T(8,128)(2,1)}, bf16[4,512,128]{2,1,0:T(8,128)(2,1)S(1)}, u32[]{:S(2)}, u32[]{:S(2)}) collective-permute-start(bf16[4,512,128]{2,1,0:T(8,128)(2,1)} %get-tuple-element.63), channel_id=1, source_target_pairs={{0,3},{1,0},{2,1},{3,2},{4,7},{5,4},{6,5},{7,6},{8,11},{9,8},{10,9... | collective-permute-start | bytes 1572872 | tf_op jit(solution)/shard_map/ppermute | solution.py:463
  109.9 17.4 %collective-permute-done.26.up_ref = bf16[4,512,128]{2,1,0:T(8,128)(2,1)S(1)} collective-permute-done((bf16[4,512,128]{2,1,0:T(8,128)(2,1)}, bf16[4,512,128]{2,1,0:T(8,128)(2,1)S(1)}, u32[]{:S(2)}, u32[]{:S(2)}) %collective-permute-start.26) | collective-permute-done | bytes 524320 | tf_op jit(solution)/shard_map/ppermute | solution.py:463
  127.4 0.8 copy-done.4
  128.4 2.4 %join.1 = (bf16[8,512,128]{2,1,0:T(8,128)(2,1)}, bf16[8,512,128]{2,1,0:T(8,128)(2,1)}) custom-call(bf16[8,512,128]{2,1,0:T(8,128)(2,1)} %get-tuple-element.61.low_ref, bf16[4,512,128]{2,1,0:T(8,128)(2,1)} %copy-done.4, bf16[8,512,128]{2,1,0:T(8,128)(2,1)} %get-tuple-element.62.high_ref, ...), custom_call_target="tpu_custom_call", output_to_operand_aliasing={{0}: (0, {}), {1}: (2, {})} | custom-call | flops 524288 | bytes 3145728 | tf_op jit(solution)/shard_map/join/pallas_call | solution.py:442
  130.7 1.4 collective-permute-start.28
  132.1 1.8 collective-permute-start.29
  134.0 1.9 slice.14
  136.0 1.9 slice.15
  137.9 3.1 %collective-permute-start.18 = (bf16[4,128,512]{2,1,0:T(8,128)(2,1)}, bf16[4,128,512]{2,1,0:T(8,128)(2,1)S(1)}, u32[]{:S(2)}, u32[]{:S(2)}) collective-permute-start(bf16[4,128,512]{2,1,0:T(8,128)(2,1)} %slice.15), channel_id=1, source_target_pairs={{0,3},{1,0},{2,1},{3,2},{4,7},{5,4},{6,5},{7,6},{8,11},{9,8},{10,9... | collective-permute-start | bytes 1572872 | tf_op jit(solution)/shard_map/ppermute | solution.py:463
  141.0 0.7 concatenate.14.ids_ref
  141.7 9.9 %upstream_most.1 = (f32[1024,512]{1,0:T(8,128)}, bf16[1024,1024]{1,0:T(8,128)(2,1)}) custom-call(s32[10]{0:T(128)} %pad_add_fusion.ids_ref, bf16[128,4096]{1,0:T(8,128)(2,1)} %bitcast.18, bf16[128,4096]{1,0:T(8,128)(2,1)} %copy-done.6, bf16[128,4096]{1,0:T(8,128)(2,1)} %collective-permute-done.8.refs_2_, ...), custom_call_target="tpu_custom_call" | custom-call | flops 3221225472 | bytes 11534336 | tf_op jit(solution)/shard_map/upstream_most/pallas_call | solution.py:301
  151.6 15.8 %collective-permute-done.17.low_ref = bf16[4,128,512]{2,1,0:T(8,128)(2,1)S(1)} collective-permute-done((bf16[4,128,512]{2,1,0:T(8,128)(2,1)}, bf16[4,128,512]{2,1,0:T(8,128)(2,1)S(1)}, u32[]{:S(2)}, u32[]{:S(2)}) %collective-permute-start.17) | collective-permute-done | bytes 524320 | tf_op jit(solution)/shard_map/ppermute | solution.py:463
  167.4 0.8 copy-done.2
  168.4 4.9 %upstream_rest.1.refs_8_ = bf16[8,128,512]{2,1,0:T(8,128)(2,1)} custom-call(s32[10]{0:T(128)} %pad_add_fusion.ids_ref, bf16[1024,1024]{1,0:T(8,128)(2,1)} %get-tuple-element.47.rows_ref, bf16[4,128,512]{2,1,0:T(8,128)(2,1)} %copy-done.2, bf16[4,128,512]{2,1,0:T(8,128)(2,1)} %copy-done.3, f32[1024,512]{1,0:T(8,128)} %get-tuple-element.48.sum_ref), custom_call_target="tpu_custom_call" | custom-call | flops 1073741824 | bytes 6291456 | tf_op jit(solution)/shard_map/upstream_rest/pallas_call | solution.py:330
  173.4 13.2 %attend_grad.1 = (bf16[128,768]{1,0:T(8,128)(2,1)}, bf16[128,768]{1,0:T(8,128)(2,1)}, bf16[128,768]{1,0:T(8,128)(2,1)}, bf16[128,768]{1,0:T(8,128)(2,1)}, bf16[1...) custom-call(s32[18]{0:T(128)} %concatenate.14.ids_ref, ...), custom_call_target="tpu_custom_call" | custom-call | flops 2348810240 | bytes 4718592 | tf_op jit(solution)/shard_map/attend_grad/pallas_call | solution.py:161
  186.6 1.4 add_convert_fusion
  188.0 7.3 %all-to-all-start.1 = ((bf16[8,512,128]{2,1,0:T(8,128)(2,1)}), bf16[8,512,128]{2,1,0:T(8,128)(2,1)S(1)}, u32[]{:S(2)}, u32[]{:S(2)}) async-start(bf16[8,512,128]{2,1,0:T(8,128)(2,1)} %add_convert_fusion), calls=%async_computation.1 | async-start | bytes 2097152 | tf_op jit(solution)/shard_map/all_to_all | solution.py:475
  195.4 0.9 collective-permute-start.19
  196.3 2.0 collective-permute-start.20
  198.3 2.3 %collective-permute-start.21 = (bf16[128,768]{1,0:T(8,128)(2,1)S(1)}, bf16[128,768]{1,0:T(8,128)(2,1)S(1)}, u32[]{:S(2)}, u32[]{:S(2)}) collective-permute-start(bf16[128,768]{1,0:T(8,128)(2,1)S(1)} %copy-done.26), channel_id=1, source_target_pairs={{0,128},{32,160},{64,192},{96,224},{128,0},{160,32},{192,64},{224,... | collective-permute-start | bytes 589832 | tf_op jit(solution)/shard_map/ppermute | solution.py:480
  200.6 2.4 %collective-permute-start.23 = (bf16[128,768]{1,0:T(8,128)(2,1)S(1)}, bf16[128,768]{1,0:T(8,128)(2,1)S(1)}, u32[]{:S(2)}, u32[]{:S(2)}) collective-permute-start(bf16[128,768]{1,0:T(8,128)(2,1)S(1)} %copy-done.24), channel_id=1, source_target_pairs={{0,96},{32,64},{64,160},{96,128},{128,224},{160,192},{192,32},{224... | collective-permute-start | bytes 589832 | tf_op jit(solution)/shard_map/ppermute | solution.py:480
  203.5 1.2 collective-permute-done.20.refs_2_
  204.7 2.1 collective-permute-start.25
  206.8 2.7 %collective-permute-done.21.refs_3_ = bf16[128,768]{1,0:T(8,128)(2,1)S(1)} collective-permute-done((bf16[128,768]{1,0:T(8,128)(2,1)S(1)}, bf16[128,768]{1,0:T(8,128)(2,1)S(1)}, u32[]{:S(2)}, u32[]{:S(2)}) %collective-permute-start.21) | collective-permute-done | bytes 196640 | tf_op jit(solution)/shard_map/ppermute | solution.py:480
  209.5 0.7 collective-permute-done.23.refs_5_
  210.2 6.2 %collective-permute-done.24.refs_6_ = bf16[128,768]{1,0:T(8,128)(2,1)S(1)} collective-permute-done((bf16[128,768]{1,0:T(8,128)(2,1)S(1)}, bf16[128,768]{1,0:T(8,128)(2,1)S(1)}, u32[]{:S(2)}, u32[]{:S(2)}) %collective-permute-start.24) | collective-permute-done | bytes 196640 | tf_op jit(solution)/shard_map/ppermute | solution.py:480
  216.4 0.7 copy-done.12
  217.1 0.7 copy-done.13
  217.8 3.4 %unpack.1 = (bf16[1,128,4096]{2,1,0:T(8,128)(2,1)}, bf16[1,128,1024]{2,1,0:T(8,128)(2,1)}, bf16[1,128,1024]{2,1,0:T(8,128)(2,1)}) custom-call(s32[10]{0:T(128)} %pad_add_fusion.ids_ref, bf16[128,768]{1,0:T(8,128)(2,1)} %get-tuple-element.49.refs_0_, bf16[128,768]{1,0:T(8,128)(2,1)} %copy-done.7, bf16[128,768]{1,0:T(8,128)(2,1)} %copy-done.8, ...), custom_call_target="tpu_custom_call" | custom-call | bytes 3145728 | tf_op jit(solution)/shard_map/unpack/pallas_call | solution.py:223
  221.2 1.5 all-to-all-done.1
  222.9 0.8 copy.15
  (86 shorter events, 2.2 us)
Async XLA Ops:
  0.6 35.9 %copy-start.14 = (bf16[128,512]{1,0:T(8,128)(2,1)S(1)}, bf16[128,512]{1,0:T(8,128)(2,1)}, u32[]{:S(2)}) copy-start(bf16[128,512]{1,0:T(8,128)(2,1)} %param.12) | copy-start | bytes 393220
  0.6 25.2 %collective-permute-start.7 = (bf16[128,4096]{1,0:T(8,128)(2,1)}, bf16[128,4096]{1,0:T(8,128)(2,1)S(1)}, u32[]{:S(2)}, u32[]{:S(2)}) collective-permute-start(bf16[128,4096]{1,0:T(8,128)(2,1)} %bitcast.14), channel_id=1, source_target_pairs={{0,64},{32,96},{64,128},{96,160},{128,192},{160,224},{192,0},{224,... | collective-permute-start | bytes 3145736 | tf_op jit(solution)/shard_map/ppermute | solution.py:480
  2.2 25.9 %collective-permute-start.8 = (bf16[128,4096]{1,0:T(8,128)(2,1)}, bf16[128,4096]{1,0:T(8,128)(2,1)}, u32[]{:S(2)}, u32[]{:S(2)}) collective-permute-start(bf16[128,4096]{1,0:T(8,128)(2,1)} %bitcast.15), channel_id=1, source_target_pairs={{0,192},{32,224},{64,0},{96,32},{128,64},{160,96},{192,128},{224,1... | collective-permute-start | bytes 3145736 | tf_op jit(solution)/shard_map/ppermute | solution.py:480
  3.1 88.6 %collective-permute-start.11 = (bf16[128,4096]{1,0:T(8,128)(2,1)}, bf16[128,4096]{1,0:T(8,128)(2,1)}, u32[]{:S(2)}, u32[]{:S(2)}) collective-permute-start(bf16[128,4096]{1,0:T(8,128)(2,1)} %bitcast.16), channel_id=1, source_target_pairs={{0,32},{32,0},{64,96},{96,64},{128,160},{160,128},{192,224},{224,1... | collective-permute-start | bytes 3145736 | tf_op jit(solution)/shard_map/ppermute | solution.py:480
  25.8 11.8 %copy-start.6 = (bf16[128,4096]{1,0:T(8,128)(2,1)}, bf16[128,4096]{1,0:T(8,128)(2,1)S(1)}, u32[]{:S(2)}) copy-start(bf16[128,4096]{1,0:T(8,128)(2,1)S(1)} %collective-permute-done.7.refs_1_) | copy-start | bytes 3145732
  25.9 20.6 %collective-permute-start.9 = (bf16[64,4096]{1,0:T(8,128)(2,1)S(1)}, bf16[64,4096]{1,0:T(8,128)(2,1)S(1)}, u32[]{:S(2)}, u32[]{:S(2)}) collective-permute-start(bf16[64,4096]{1,0:T(8,128)(2,1)S(1)} %slice.16), channel_id=1, source_target_pairs={{0,64},{32,96},{64,128},{96,160},{128,192},{160,224},{192,0},{224,... | collective-permute-start | bytes 1572872 | tf_op jit(solution)/shard_map/ppermute | solution.py:480
  29.2 20.2 %collective-permute-start.10 = (bf16[64,4096]{1,0:T(8,128)(2,1)S(1)}, bf16[64,4096]{1,0:T(8,128)(2,1)S(1)}, u32[]{:S(2)}, u32[]{:S(2)}) collective-permute-start(bf16[64,4096]{1,0:T(8,128)(2,1)S(1)} %slice.17), channel_id=1, source_target_pairs={{0,192},{32,224},{64,0},{96,32},{128,64},{160,96},{192,128},{224,1... | collective-permute-start | bytes 1572872 | tf_op jit(solution)/shard_map/ppermute | solution.py:480
  33.8 16.5 %collective-permute-start = (bf16[128,768]{1,0:T(8,128)(2,1)}, bf16[128,768]{1,0:T(8,128)(2,1)S(1)}, u32[]{:S(2)}, u32[]{:S(2)}) collective-permute-start(bf16[128,768]{1,0:T(8,128)(2,1)} %get-tuple-element.37), channel_id=1, source_target_pairs={{0,64},{32,96},{64,128},{96,160},{128,192},{160,224},{192,0},{224,... | collective-permute-start | bytes 589832 | tf_op jit(solution)/shard_map/ppermute | solution.py:480
  35.3 15.5 %collective-permute-start.1 = (bf16[128,768]{1,0:T(8,128)(2,1)}, bf16[128,768]{1,0:T(8,128)(2,1)}, u32[]{:S(2)}, u32[]{:S(2)}) collective-permute-start(bf16[128,768]{1,0:T(8,128)(2,1)} %get-tuple-element.38), channel_id=1, source_target_pairs={{0,192},{32,224},{64,0},{96,32},{128,64},{160,96},{192,128},{224,1... | collective-permute-start | bytes 589832 | tf_op jit(solution)/shard_map/ppermute | solution.py:480
  37.6 16.4 %copy-start.15 = (s32[1,32]{1,0:T(1,128)S(1)}, s32[1,32]{1,0:T(1,128)}, u32[]{:S(2)}) copy-start(s32[1,32]{1,0:T(1,128)} %param.13) | copy-start | bytes 388
  37.6 52.1 %all-to-all-start = ((bf16[8,128,512]{2,1,0:T(8,128)(2,1)}), bf16[8,128,512]{2,1,0:T(8,128)(2,1)S(1)}, u32[]{:S(2)}, u32[]{:S(2)}) async-start(bf16[8,128,512]{2,1,0:T(8,128)(2,1)} %broadcast_in_dim.41), calls=%async_computation | async-start | bytes 2097152 | tf_op jit(solution)/shard_map/all_to_all | solution.py:475
  46.4 7.6 %collective-permute-start.2 = (bf16[128,768]{1,0:T(8,128)(2,1)}, bf16[128,768]{1,0:T(8,128)(2,1)}, u32[]{:S(2)}, u32[]{:S(2)}) collective-permute-start(bf16[128,768]{1,0:T(8,128)(2,1)} %get-tuple-element.39), channel_id=1, source_target_pairs={{0,128},{32,160},{64,192},{96,224},{128,0},{160,32},{192,64},{224,... | collective-permute-start | bytes 589832 | tf_op jit(solution)/shard_map/ppermute | solution.py:480
  49.4 43.9 %collective-permute-start.12 = (bf16[128,4096]{1,0:T(8,128)(2,1)}, bf16[128,4096]{1,0:T(8,128)(2,1)}, u32[]{:S(2)}, u32[]{:S(2)}) collective-permute-start(bf16[128,4096]{1,0:T(8,128)(2,1)} %copy-done.6), channel_id=1, source_target_pairs={{0,32},{32,0},{64,96},{96,64},{128,160},{160,128},{192,224},{224,1... | collective-permute-start | bytes 3145736 | tf_op jit(solution)/shard_map/ppermute | solution.py:480
  50.3 30.6 %copy-start.17 = (bf16[128,768]{1,0:T(8,128)(2,1)}, bf16[128,768]{1,0:T(8,128)(2,1)S(1)}, u32[]{:S(2)}) copy-start(bf16[128,768]{1,0:T(8,128)(2,1)S(1)} %collective-permute-done.refs_1_) | copy-start | bytes 589828
  50.3 43.0 %collective-permute-start.13 = (bf16[128,4096]{1,0:T(8,128)(2,1)}, bf16[128,4096]{1,0:T(8,128)(2,1)S(1)}, u32[]{:S(2)}, u32[]{:S(2)}) collective-permute-start(bf16[128,4096]{1,0:T(8,128)(2,1)} %collective-permute-done.8.refs_2_), channel_id=1, source_target_pairs={{0,32},{32,0},{64,96},{96,64},{128,160},{160,128},{192,224},{224,1... | collective-permute-start | bytes 3145736 | tf_op jit(solution)/shard_map/ppermute | solution.py:480
  50.8 42.5 %collective-permute-start.14 = (bf16[128,4096]{1,0:T(8,128)(2,1)}, bf16[128,4096]{1,0:T(8,128)(2,1)}, u32[]{:S(2)}, u32[]{:S(2)}) collective-permute-start(bf16[128,4096]{1,0:T(8,128)(2,1)} %constant_dynamic-update-slice_fusion.refs_3_), channel_id=1, source_target_pairs={{0,32},{32,0},{64,96},{96,64},{128,160},{160,128},{192,224},{224,1... | collective-permute-start | bytes 3145736 | tf_op jit(solution)/shard_map/ppermute | solution.py:480
  54.0 1.7 collective-permute-start.3
  55.7 25.2 %copy-start.18 = (bf16[128,768]{1,0:T(8,128)(2,1)}, bf16[128,768]{1,0:T(8,128)(2,1)S(1)}, u32[]{:S(2)}) copy-start(bf16[128,768]{1,0:T(8,128)(2,1)S(1)} %collective-permute-done.3.refs_4_) | copy-start | bytes 589828
  55.7 8.1 %collective-permute-start.4 = (bf16[128,768]{1,0:T(8,128)(2,1)}, bf16[128,768]{1,0:T(8,128)(2,1)S(1)}, u32[]{:S(2)}, u32[]{:S(2)}) collective-permute-start(bf16[128,768]{1,0:T(8,128)(2,1)} %get-tuple-element.41), channel_id=1, source_target_pairs={{0,96},{32,64},{64,160},{96,128},{128,224},{160,192},{192,32},{224... | collective-permute-start | bytes 589832 | tf_op jit(solution)/shard_map/ppermute | solution.py:480
  63.7 17.1 %copy-start.19 = (bf16[128,768]{1,0:T(8,128)(2,1)}, bf16[128,768]{1,0:T(8,128)(2,1)S(1)}, u32[]{:S(2)}) copy-start(bf16[128,768]{1,0:T(8,128)(2,1)S(1)} %collective-permute-done.4.refs_5_) | copy-start | bytes 589828
  63.7 8.5 %collective-permute-start.5 = (bf16[128,768]{1,0:T(8,128)(2,1)}, bf16[128,768]{1,0:T(8,128)(2,1)S(1)}, u32[]{:S(2)}, u32[]{:S(2)}) collective-permute-start(bf16[128,768]{1,0:T(8,128)(2,1)} %get-tuple-element.42), channel_id=1, source_target_pairs={{0,224},{32,192},{64,32},{96,0},{128,96},{160,64},{192,160},{224,1... | collective-permute-start | bytes 589832 | tf_op jit(solution)/shard_map/ppermute | solution.py:480
  72.2 8.6 %copy-start.20 = (bf16[128,768]{1,0:T(8,128)(2,1)}, bf16[128,768]{1,0:T(8,128)(2,1)S(1)}, u32[]{:S(2)}) copy-start(bf16[128,768]{1,0:T(8,128)(2,1)S(1)} %collective-permute-done.5.refs_6_) | copy-start | bytes 589828
  72.2 8.6 %collective-permute-start.6 = (bf16[128,768]{1,0:T(8,128)(2,1)}, bf16[128,768]{1,0:T(8,128)(2,1)S(1)}, u32[]{:S(2)}, u32[]{:S(2)}) collective-permute-start(bf16[128,768]{1,0:T(8,128)(2,1)} %get-tuple-element.43), channel_id=1, source_target_pairs={{0,160},{32,128},{64,224},{96,192},{128,32},{160,0},{192,96},{224,... | collective-permute-start | bytes 589832 | tf_op jit(solution)/shard_map/ppermute | solution.py:480
  80.8 0.7 copy-start.21
  89.8 16.8 %copy-start = (bf16[8,128,512]{2,1,0:T(8,128)(2,1)}, bf16[8,128,512]{2,1,0:T(8,128)(2,1)S(1)}, u32[]{:S(2)}) copy-start(bf16[8,128,512]{2,1,0:T(8,128)(2,1)S(1)} %all-to-all-done.refs_8_) | copy-start | bytes 3145732
  89.8 44.2 %collective-permute-start.15 = (bf16[8,128,512]{2,1,0:T(8,128)(2,1)S(1)}, bf16[8,128,512]{2,1,0:T(8,128)(2,1)}, u32[]{:S(2)}, u32[]{:S(2)}) collective-permute-start(bf16[8,128,512]{2,1,0:T(8,128)(2,1)S(1)} %all-to-all-done.refs_8_), channel_id=1, source_target_pairs={{0,1},{1,2},{2,3},{3,0},{4,5},{5,6},{6,7},{7,4},{8,9},{9,10},{10,1... | collective-permute-start | bytes 3145736 | tf_op jit(solution)/shard_map/ppermute | solution.py:463
  91.6 42.4 %collective-permute-start.16 = (bf16[8,128,512]{2,1,0:T(8,128)(2,1)S(1)}, bf16[8,128,512]{2,1,0:T(8,128)(2,1)}, u32[]{:S(2)}, u32[]{:S(2)}) collective-permute-start(bf16[8,128,512]{2,1,0:T(8,128)(2,1)S(1)} %all-to-all-done.refs_8_), channel_id=1, source_target_pairs={{0,3},{1,0},{2,1},{3,2},{4,7},{5,4},{6,5},{7,6},{8,11},{9,8},{10,9... | collective-permute-start | bytes 3145736 | tf_op jit(solution)/shard_map/ppermute | solution.py:463
  93.3 1.0 copy-start.16
  106.6 20.8 %collective-permute-start.26 = (bf16[4,512,128]{2,1,0:T(8,128)(2,1)}, bf16[4,512,128]{2,1,0:T(8,128)(2,1)S(1)}, u32[]{:S(2)}, u32[]{:S(2)}) collective-permute-start(bf16[4,512,128]{2,1,0:T(8,128)(2,1)} %get-tuple-element.44), channel_id=1, source_target_pairs={{0,1},{1,2},{2,3},{3,0},{4,5},{5,6},{6,7},{7,4},{8,9},{9,10},{10,1... | collective-permute-start | bytes 1572872 | tf_op jit(solution)/shard_map/ppermute | solution.py:463
  107.1 20.4 %collective-permute-start.27 = (bf16[4,512,128]{2,1,0:T(8,128)(2,1)}, bf16[4,512,128]{2,1,0:T(8,128)(2,1)S(1)}, u32[]{:S(2)}, u32[]{:S(2)}) collective-permute-start(bf16[4,512,128]{2,1,0:T(8,128)(2,1)} %get-tuple-element.63), channel_id=1, source_target_pairs={{0,3},{1,0},{2,1},{3,2},{4,7},{5,4},{6,5},{7,6},{8,11},{9,8},{10,9... | collective-permute-start | bytes 1572872 | tf_op jit(solution)/shard_map/ppermute | solution.py:463
  127.4 0.8 copy-start.4
  127.4 0.9 copy-start.5
  130.7 55.8 %collective-permute-start.28 = (bf16[8,512,128]{2,1,0:T(8,128)(2,1)}, bf16[8,512,128]{2,1,0:T(8,128)(2,1)S(1)}, u32[]{:S(2)}, u32[]{:S(2)}) collective-permute-start(bf16[8,512,128]{2,1,0:T(8,128)(2,1)} %get-tuple-element.64), channel_id=1, source_target_pairs={{0,1},{1,2},{2,3},{3,0},{4,5},{5,6},{6,7},{7,4},{8,9},{9,10},{10,1... | collective-permute-start | bytes 3145736 | tf_op jit(solution)/shard_map/ppermute | solution.py:463
  132.1 54.4 %collective-permute-start.29 = (bf16[8,512,128]{2,1,0:T(8,128)(2,1)}, bf16[8,512,128]{2,1,0:T(8,128)(2,1)S(1)}, u32[]{:S(2)}, u32[]{:S(2)}) collective-permute-start(bf16[8,512,128]{2,1,0:T(8,128)(2,1)} %get-tuple-element.65), channel_id=1, source_target_pairs={{0,3},{1,0},{2,1},{3,2},{4,7},{5,4},{6,5},{7,6},{8,11},{9,8},{10,9... | collective-permute-start | bytes 3145736 | tf_op jit(solution)/shard_map/ppermute | solution.py:463
  135.9 31.6 %collective-permute-start.17 = (bf16[4,128,512]{2,1,0:T(8,128)(2,1)}, bf16[4,128,512]{2,1,0:T(8,128)(2,1)S(1)}, u32[]{:S(2)}, u32[]{:S(2)}) collective-permute-start(bf16[4,128,512]{2,1,0:T(8,128)(2,1)} %slice.14), channel_id=1, source_target_pairs={{0,1},{1,2},{2,3},{3,0},{4,5},{5,6},{6,7},{7,4},{8,9},{9,10},{10,1... | collective-permute-start | bytes 1572872 | tf_op jit(solution)/shard_map/ppermute | solution.py:463
  137.9 29.5 %collective-permute-start.18 = (bf16[4,128,512]{2,1,0:T(8,128)(2,1)}, bf16[4,128,512]{2,1,0:T(8,128)(2,1)S(1)}, u32[]{:S(2)}, u32[]{:S(2)}) collective-permute-start(bf16[4,128,512]{2,1,0:T(8,128)(2,1)} %slice.15), channel_id=1, source_target_pairs={{0,3},{1,0},{2,1},{3,2},{4,7},{5,4},{6,5},{7,6},{8,11},{9,8},{10,9... | collective-permute-start | bytes 1572872 | tf_op jit(solution)/shard_map/ppermute | solution.py:463
  167.4 0.8 copy-start.2
  167.4 1.0 copy-start.3
  173.3 13.2 %copy-start.1 = (bf16[8,512,128]{2,1,0:T(8,128)(2,1)S(1)}, bf16[8,512,128]{2,1,0:T(8,128)(2,1)}, u32[]{:S(2)}) copy-start(bf16[8,512,128]{2,1,0:T(8,128)(2,1)} %get-tuple-element.60) | copy-start | bytes 3145732
  188.0 7.4 %copy-start.28 = (bf16[128,768]{1,0:T(8,128)(2,1)S(1)}, bf16[128,768]{1,0:T(8,128)(2,1)}, u32[]{:S(2)}) copy-start(bf16[128,768]{1,0:T(8,128)(2,1)} %get-tuple-element.50) | copy-start | bytes 589828
  188.0 8.3 %copy-start.27 = (bf16[128,768]{1,0:T(8,128)(2,1)S(1)}, bf16[128,768]{1,0:T(8,128)(2,1)}, u32[]{:S(2)}) copy-start(bf16[128,768]{1,0:T(8,128)(2,1)} %get-tuple-element.51) | copy-start | bytes 589828
  188.0 10.3 %copy-start.26 = (bf16[128,768]{1,0:T(8,128)(2,1)S(1)}, bf16[128,768]{1,0:T(8,128)(2,1)}, u32[]{:S(2)}) copy-start(bf16[128,768]{1,0:T(8,128)(2,1)} %get-tuple-element.52) | copy-start | bytes 589828
  188.0 12.6 %copy-start.25 = (bf16[128,768]{1,0:T(8,128)(2,1)S(1)}, bf16[128,768]{1,0:T(8,128)(2,1)}, u32[]{:S(2)}) copy-start(bf16[128,768]{1,0:T(8,128)(2,1)} %get-tuple-element.53) | copy-start | bytes 589828
  188.0 12.6 %copy-start.24 = (bf16[128,768]{1,0:T(8,128)(2,1)S(1)}, bf16[128,768]{1,0:T(8,128)(2,1)}, u32[]{:S(2)}) copy-start(bf16[128,768]{1,0:T(8,128)(2,1)} %get-tuple-element.54) | copy-start | bytes 589828
  188.0 15.5 %copy-start.23 = (bf16[128,768]{1,0:T(8,128)(2,1)S(1)}, bf16[128,768]{1,0:T(8,128)(2,1)}, u32[]{:S(2)}) copy-start(bf16[128,768]{1,0:T(8,128)(2,1)} %get-tuple-element.55) | copy-start | bytes 589828
  188.0 16.7 %copy-start.22 = (bf16[128,768]{1,0:T(8,128)(2,1)S(1)}, bf16[128,768]{1,0:T(8,128)(2,1)}, u32[]{:S(2)}) copy-start(bf16[128,768]{1,0:T(8,128)(2,1)} %get-tuple-element.56) | copy-start | bytes 589828
  188.0 34.7 %all-to-all-start.1 = ((bf16[8,512,128]{2,1,0:T(8,128)(2,1)}), bf16[8,512,128]{2,1,0:T(8,128)(2,1)S(1)}, u32[]{:S(2)}, u32[]{:S(2)}) async-start(bf16[8,512,128]{2,1,0:T(8,128)(2,1)} %add_convert_fusion), calls=%async_computation.1 | async-start | bytes 2097152 | tf_op jit(solution)/shard_map/all_to_all | solution.py:475
  195.4 8.1 %collective-permute-start.19 = (bf16[128,768]{1,0:T(8,128)(2,1)S(1)}, bf16[128,768]{1,0:T(8,128)(2,1)S(1)}, u32[]{:S(2)}, u32[]{:S(2)}) collective-permute-start(bf16[128,768]{1,0:T(8,128)(2,1)S(1)} %copy-done.28), channel_id=1, source_target_pairs={{0,64},{32,96},{64,128},{96,160},{128,192},{160,224},{192,0},{224,... | collective-permute-start | bytes 589832 | tf_op jit(solution)/shard_map/ppermute | solution.py:480
  196.3 8.4 %collective-permute-start.20 = (bf16[128,768]{1,0:T(8,128)(2,1)S(1)}, bf16[128,768]{1,0:T(8,128)(2,1)S(1)}, u32[]{:S(2)}, u32[]{:S(2)}) collective-permute-start(bf16[128,768]{1,0:T(8,128)(2,1)S(1)} %copy-done.27), channel_id=1, source_target_pairs={{0,192},{32,224},{64,0},{96,32},{128,64},{160,96},{192,128},{224,1... | collective-permute-start | bytes 589832 | tf_op jit(solution)/shard_map/ppermute | solution.py:480
  198.3 11.2 %collective-permute-start.21 = (bf16[128,768]{1,0:T(8,128)(2,1)S(1)}, bf16[128,768]{1,0:T(8,128)(2,1)S(1)}, u32[]{:S(2)}, u32[]{:S(2)}) collective-permute-start(bf16[128,768]{1,0:T(8,128)(2,1)S(1)} %copy-done.26), channel_id=1, source_target_pairs={{0,128},{32,160},{64,192},{96,224},{128,0},{160,32},{192,64},{224,... | collective-permute-start | bytes 589832 | tf_op jit(solution)/shard_map/ppermute | solution.py:480
  200.6 8.9 %collective-permute-start.22 = (bf16[128,768]{1,0:T(8,128)(2,1)S(1)}, bf16[128,768]{1,0:T(8,128)(2,1)S(1)}, u32[]{:S(2)}, u32[]{:S(2)}) collective-permute-start(bf16[128,768]{1,0:T(8,128)(2,1)S(1)} %copy-done.25), channel_id=1, source_target_pairs={{0,32},{32,0},{64,96},{96,64},{128,160},{160,128},{192,224},{224,1... | collective-permute-start | bytes 589832 | tf_op jit(solution)/shard_map/ppermute | solution.py:480
  200.6 9.6 %collective-permute-start.23 = (bf16[128,768]{1,0:T(8,128)(2,1)S(1)}, bf16[128,768]{1,0:T(8,128)(2,1)S(1)}, u32[]{:S(2)}, u32[]{:S(2)}) collective-permute-start(bf16[128,768]{1,0:T(8,128)(2,1)S(1)} %copy-done.24), channel_id=1, source_target_pairs={{0,96},{32,64},{64,160},{96,128},{128,224},{160,192},{192,32},{224... | collective-permute-start | bytes 589832 | tf_op jit(solution)/shard_map/ppermute | solution.py:480
  203.5 12.9 %copy-start.7 = (bf16[128,768]{1,0:T(8,128)(2,1)}, bf16[128,768]{1,0:T(8,128)(2,1)S(1)}, u32[]{:S(2)}) copy-start(bf16[128,768]{1,0:T(8,128)(2,1)S(1)} %collective-permute-done.19.refs_1_) | copy-start | bytes 589828
  203.5 12.9 %collective-permute-start.24 = (bf16[128,768]{1,0:T(8,128)(2,1)S(1)}, bf16[128,768]{1,0:T(8,128)(2,1)S(1)}, u32[]{:S(2)}, u32[]{:S(2)}) collective-permute-start(bf16[128,768]{1,0:T(8,128)(2,1)S(1)} %copy-done.23), channel_id=1, source_target_pairs={{0,224},{32,192},{64,32},{96,0},{128,96},{160,64},{192,160},{224,1... | collective-permute-start | bytes 589832 | tf_op jit(solution)/shard_map/ppermute | solution.py:480
  204.7 11.7 %copy-start.8 = (bf16[128,768]{1,0:T(8,128)(2,1)}, bf16[128,768]{1,0:T(8,128)(2,1)S(1)}, u32[]{:S(2)}) copy-start(bf16[128,768]{1,0:T(8,128)(2,1)S(1)} %collective-permute-done.20.refs_2_) | copy-start | bytes 589828
  204.7 11.7 %collective-permute-start.25 = (bf16[128,768]{1,0:T(8,128)(2,1)S(1)}, bf16[128,768]{1,0:T(8,128)(2,1)S(1)}, u32[]{:S(2)}, u32[]{:S(2)}) collective-permute-start(bf16[128,768]{1,0:T(8,128)(2,1)S(1)} %copy-done.22), channel_id=1, source_target_pairs={{0,160},{32,128},{64,224},{96,192},{128,32},{160,0},{192,96},{224,... | collective-permute-start | bytes 589832 | tf_op jit(solution)/shard_map/ppermute | solution.py:480
  209.5 6.9 %copy-start.9 = (bf16[128,768]{1,0:T(8,128)(2,1)}, bf16[128,768]{1,0:T(8,128)(2,1)S(1)}, u32[]{:S(2)}) copy-start(bf16[128,768]{1,0:T(8,128)(2,1)S(1)} %collective-permute-done.21.refs_3_) | copy-start | bytes 589828
  209.5 6.9 %copy-start.10 = (bf16[128,768]{1,0:T(8,128)(2,1)}, bf16[128,768]{1,0:T(8,128)(2,1)S(1)}, u32[]{:S(2)}) copy-start(bf16[128,768]{1,0:T(8,128)(2,1)S(1)} %collective-permute-done.22.refs_4_) | copy-start | bytes 589828
  210.2 6.2 %copy-start.11 = (bf16[128,768]{1,0:T(8,128)(2,1)}, bf16[128,768]{1,0:T(8,128)(2,1)S(1)}, u32[]{:S(2)}) copy-start(bf16[128,768]{1,0:T(8,128)(2,1)S(1)} %collective-permute-done.23.refs_5_) | copy-start | bytes 589828
  216.4 0.7 copy-start.12
  217.1 0.7 copy-start.13

commit v7 on v6

--- a/solution.py
+++ b/solution.py
@@ -366,41 +366,44 @@
     rows = jnp.concatenate([piece[...] for piece in pieces], 0)
     out_ref[...] = jnp.dot(lhs_ref[...], rows, preferred_element_type=F32).astype(BF16)
 
-    def part(offset):
+    def fill(ref, offset):
         t = lax.rem(ids_ref[count + 1] + offset, near)
-        return out_ref[:, pl.ds(pl.multiple_of(t * TOK, TOK), TOK)]
-
-    same_ref[0] = part(0)
-    next_ref[0] = part(1)
-    last_ref[0] = part(3)
+        for plane in range(PLANES):
+            start = pl.multiple_of((plane * near + t) * TOK, TOK)
+            ref[plane] = out_ref[:, pl.ds(start, TOK)]
+
+    fill(same_ref, 0)
+    fill(next_ref, 1)
+    fill(last_ref, 3)
 
     @pl.when(step < middle)
     def _():
-        low_ref[0] = part(2)
+        fill(low_ref, 2)
 
     @pl.when(step >= middle)
     def _():
-        high_ref[0] = part(2)
+        fill(high_ref, 2)
 
 
 def proj_terms(ids, pieces, ot):
     count, width, _ = ot.shape
     far, near = GRID["dp"], GRID["fsdp"]
     depth = pieces[0].shape[1]
-    middle = far // 2
-    block = (1, width, TOK)
+    steps = far // PLANES
+    middle = steps // 2
+    block = (PLANES, width, TOK)
 
     def plane(i, ids):
         return (i, 0, 0)
 
     full = jax.ShapeDtypeStruct((far, width, TOK), BF16)
-    part = jax.ShapeDtypeStruct((middle, width, TOK), BF16)
+    part = jax.ShapeDtypeStruct((far // 2, width, TOK), BF16)
     return pl.pallas_call(
         proj_kernel,
         grid_spec=pltpu.PrefetchScalarGridSpec(
             num_scalar_prefetch=1,
-            grid=(far,),
-            in_specs=[pl.BlockSpec((TOK, near * TOK), lambda i, ids: (0, i))] * count
+            grid=(steps,),
+            in_specs=chunk_specs(pieces)
             + [pl.BlockSpec(ot.shape, lambda i, ids: (0, 0, 0))],
             out_specs=[
                 pl.BlockSpec(block, plane),
@@ -411,7 +414,7 @@
             ],
             scratch_shapes=[
                 pltpu.VMEM((width, count * TOK), BF16),
-                pltpu.VMEM((width, near * TOK), BF16),
+                pltpu.VMEM((width, PLANES * near * TOK), BF16),
             ],
         ),
         out_shape=[full, full, part, part, full],

time: 228 us -> 228 us (level)
  transfers between devices with their start and end apart: 32 -> 32, of which waited for: 15 -> 15; matrix products, arithmetic and copies ran while one was open for 5% -> 5% of each run, Pallas kernels for 26% -> 25%
where the time goes in v7:
time: 228 us; the launch traced here: 224 us
  waiting for transfers between devices  91 us (40%)
  starting transfers between devices  57.3 us (25%)
  Pallas kernels  56.1 us (25%)
  local copies, waits for them, and re-layouts  14.1 us (6%)
  other arithmetic  4.33 us (2%)
    ppermute x22, waiting for transfers between devices, hop(): return lax.ppermute(x, 'seq', pairs)  54.5 us
    ppermute x8, waiting for transfers between devices, shift(): return lax.ppermute(x, axis, [(i, (i + by) % n) for i in range(n)])  35.1 us
    ppermute x22, starting transfers between devices, hop(): return lax.ppermute(x, 'seq', pairs)  27.9 us
    all_to_all x2, starting transfers between devices, swap(): return lax.all_to_all(x, axis, split_axis=0, concat_axis=0, tiled=True)  16.1 us
    ppermute x8, starting transfers between devices, shift(): return lax.ppermute(x, axis, [(i, (i + by) % n) for i in range(n)])  13.3 us
    pallas_call x1, Pallas kernels, attend_grad(): pl.pallas_call(bwd_kernel, grid_spec=pltpu.PrefetchScalarGridSpec(num_sca...  13.2 us
    pallas_call x1, Pallas kernels, proj_terms(): pl.pallas_call(proj_kernel, grid_spec=pltpu.PrefetchScalarGridSpec(num_sc...  10.6 us
    pallas_call x1, Pallas kernels, upstream_most(): pl.pallas_call(most_kernel, grid_spec=pltpu.PrefetchScalarGridSpec(num_sc...  9.93 us
  transfers between devices with their start and end apart: 32, of which 15 were waited for; matrix products, arithmetic and copies ran while one was open for 5% of the time, Pallas kernels for 25%

profile of v7, /device:TPU:2, one launch (start us, length us, event | category | flops | bytes accessed | tf_op | source)
XLA Modules:
  0.0 223.6 jit_solution(14154374128983043867)
XLA Ops:
  0.6 1.6 collective-permute-start.7
  2.2 0.8 collective-permute-start.8
  3.1 22.8 %collective-permute-done.7.refs_1_ = bf16[128,4096]{1,0:T(8,128)(2,1)S(1)} collective-permute-done((bf16[128,4096]{1,0:T(8,128)(2,1)}, bf16[128,4096]{1,0:T(8,128)(2,1)S(1)}, u32[]{:S(2)}, u32[]{:S(2)}) %collective-permute-start.7) | collective-permute-done | bytes 1048608 | tf_op jit(solution)/shard_map/ppermute | solution.py:483
  25.9 1.6 collective-permute-start.9
  27.4 0.7 add_subtract_fusion
  28.1 1.1 slice.17
  29.2 0.6 collective-permute-start.10
  29.8 0.6 pad_add_fusion.1.ids_ref
  30.4 3.3 %pack.1 = (bf16[128,768]{1,0:T(8,128)(2,1)}, bf16[128,768]{1,0:T(8,128)(2,1)}, bf16[128,768]{1,0:T(8,128)(2,1)}, bf16[128,768]{1,0:T(8,128)(2,1)}, bf16[128,768]...) custom-call(s32[8]{0:T(128)} %pad_add_fusion.1.ids_ref, ...), custom_call_target="tpu_custom_call" | custom-call | bytes 3145728 | tf_op jit(solution)/shard_map/pack/pallas_call | solution.py:195
  33.8 1.5 collective-permute-start
  35.3 1.3 collective-permute-start.1
  36.6 1.1 broadcast_in_dim.41
  37.6 8.8 %all-to-all-start = ((bf16[8,128,512]{2,1,0:T(8,128)(2,1)}), bf16[8,128,512]{2,1,0:T(8,128)(2,1)S(1)}, u32[]{:S(2)}, u32[]{:S(2)}) async-start(bf16[8,128,512]{2,1,0:T(8,128)(2,1)} %broadcast_in_dim.41), calls=%async_computation | async-start | bytes 2097152 | tf_op jit(solution)/shard_map/all_to_all | solution.py:478
  46.4 2.1 collective-permute-start.2
  48.6 0.8 constant_dynamic-update-slice_fusion.1
  49.4 0.9 constant_dynamic-update-slice_fusion.refs_3_
  50.3 0.5 collective-permute-start.13
  50.9 3.1 %collective-permute-done.2.refs_3_ = bf16[128,768]{1,0:T(8,128)(2,1)} collective-permute-done((bf16[128,768]{1,0:T(8,128)(2,1)}, bf16[128,768]{1,0:T(8,128)(2,1)}, u32[]{:S(2)}, u32[]{:S(2)}) %collective-permute-start.2) | collective-permute-done | bytes 196640 | tf_op jit(solution)/shard_map/ppermute | solution.py:483
  54.1 1.5 collective-permute-done.3.refs_4_
  55.7 2.3 %collective-permute-start.4 = (bf16[128,768]{1,0:T(8,128)(2,1)}, bf16[128,768]{1,0:T(8,128)(2,1)S(1)}, u32[]{:S(2)}, u32[]{:S(2)}) collective-permute-start(bf16[128,768]{1,0:T(8,128)(2,1)} %get-tuple-element.41), channel_id=1, source_target_pairs={{0,96},{32,64},{64,160},{96,128},{128,224},{160,192},{192,32},{224... | collective-permute-start | bytes 589832 | tf_op jit(solution)/shard_map/ppermute | solution.py:483
  58.0 5.7 %collective-permute-done.4.refs_5_ = bf16[128,768]{1,0:T(8,128)(2,1)S(1)} collective-permute-done((bf16[128,768]{1,0:T(8,128)(2,1)}, bf16[128,768]{1,0:T(8,128)(2,1)S(1)}, u32[]{:S(2)}, u32[]{:S(2)}) %collective-permute-start.4) | collective-permute-done | bytes 196640 | tf_op jit(solution)/shard_map/ppermute | solution.py:483
  63.7 3.5 %collective-permute-start.5 = (bf16[128,768]{1,0:T(8,128)(2,1)}, bf16[128,768]{1,0:T(8,128)(2,1)S(1)}, u32[]{:S(2)}, u32[]{:S(2)}) collective-permute-start(bf16[128,768]{1,0:T(8,128)(2,1)} %get-tuple-element.42), channel_id=1, source_target_pairs={{0,224},{32,192},{64,32},{96,0},{128,96},{160,64},{192,160},{224,1... | collective-permute-start | bytes 589832 | tf_op jit(solution)/shard_map/ppermute | solution.py:483
  67.2 5.0 %collective-permute-done.5.refs_6_ = bf16[128,768]{1,0:T(8,128)(2,1)S(1)} collective-permute-done((bf16[128,768]{1,0:T(8,128)(2,1)}, bf16[128,768]{1,0:T(8,128)(2,1)S(1)}, u32[]{:S(2)}, u32[]{:S(2)}) %collective-permute-start.5) | collective-permute-done | bytes 196640 | tf_op jit(solution)/shard_map/ppermute | solution.py:483
  72.2 2.5 %collective-permute-start.6 = (bf16[128,768]{1,0:T(8,128)(2,1)}, bf16[128,768]{1,0:T(8,128)(2,1)S(1)}, u32[]{:S(2)}, u32[]{:S(2)}) collective-permute-start(bf16[128,768]{1,0:T(8,128)(2,1)} %get-tuple-element.43), channel_id=1, source_target_pairs={{0,160},{32,128},{64,224},{96,192},{128,32},{160,0},{192,96},{224,... | collective-permute-start | bytes 589832 | tf_op jit(solution)/shard_map/ppermute | solution.py:483
  74.7 0.6 pad_add_fusion.ids_ref
  75.3 0.7 select_reduce_fusion
  76.0 4.8 %collective-permute-done.6.refs_7_ = bf16[128,768]{1,0:T(8,128)(2,1)S(1)} collective-permute-done((bf16[128,768]{1,0:T(8,128)(2,1)}, bf16[128,768]{1,0:T(8,128)(2,1)S(1)}, u32[]{:S(2)}, u32[]{:S(2)}) %collective-permute-start.6) | collective-permute-done | bytes 196640 | tf_op jit(solution)/shard_map/ppermute | solution.py:483
  80.8 0.7 copy-done.21
  81.5 8.3 %attend.1.refs_8_ = bf16[8,512,128]{2,1,0:T(8,128)(2,1)} custom-call(s32[10]{0:T(128)} %pad_add_fusion.ids_ref, bf16[128,768]{1,0:T(8,128)(2,1)} %get-tuple-element.36.refs_0_, bf16[128,768]{1,0:T(8,128)(2,1)} %copy-done.17, bf16[128,768]{1,0:T(8,128)(2,1)} %collective-permute-done.1.refs_2_, bf16[128,768]{1,0:T(8,128)(2,1)} %collective-permute-done.2.refs_3_, ...), custom_call_target="tpu_custom_call" | custom-call | flops 939524096 | bytes 3145728 | tf_op jit(solution)/shard_map/attend/pallas_call | solution.py:138
  89.8 1.8 collective-permute-start.15
  91.6 1.7 collective-permute-start.16
  93.3 1.0 copy-done.16
  94.3 10.6 %proj_terms.1 = (bf16[8,512,128]{2,1,0:T(8,128)(2,1)}, bf16[8,512,128]{2,1,0:T(8,128)(2,1)}, bf16[4,512,128]{2,1,0:T(8,128)(2,1)}, bf16[4,512,128]{2,1,0:T(8,128)(2,1)}, bf16[8,512,128]{2,1,0:T(8,128)(2,1)}) custom-call(s32[10]{0:T(128)} %pad_add_fusion.ids_ref, bf16[128,4096]{1,0:T(8,128)(2,1)} %bitcast.17, bf16[128,4096]{1,0:T(8,128)(2,1)} %copy-done.6, ...), custom_call_target="tpu_custom_call" | custom-call | flops 4294967296 | bytes 13631488 | tf_op jit(solution)/shard_map/proj_terms/pallas_call | solution.py:401
  105.3 2.9 %collective-permute-start.27 = (bf16[4,512,128]{2,1,0:T(8,128)(2,1)}, bf16[4,512,128]{2,1,0:T(8,128)(2,1)S(1)}, u32[]{:S(2)}, u32[]{:S(2)}) collective-permute-start(bf16[4,512,128]{2,1,0:T(8,128)(2,1)} %get-tuple-element.63), channel_id=1, source_target_pairs={{0,3},{1,0},{2,1},{3,2},{4,7},{5,4},{6,5},{7,6},{8,11},{9,8},{10,9... | collective-permute-start | bytes 1572872 | tf_op jit(solution)/shard_map/ppermute | solution.py:466
  108.2 19.2 %collective-permute-done.26.up_ref = bf16[4,512,128]{2,1,0:T(8,128)(2,1)S(1)} collective-permute-done((bf16[4,512,128]{2,1,0:T(8,128)(2,1)}, bf16[4,512,128]{2,1,0:T(8,128)(2,1)S(1)}, u32[]{:S(2)}, u32[]{:S(2)}) %collective-permute-start.26) | collective-permute-done | bytes 524320 | tf_op jit(solution)/shard_map/ppermute | solution.py:466
  127.4 0.8 copy-done.4
  128.4 2.4 %join.1 = (bf16[8,512,128]{2,1,0:T(8,128)(2,1)}, bf16[8,512,128]{2,1,0:T(8,128)(2,1)}) custom-call(bf16[8,512,128]{2,1,0:T(8,128)(2,1)} %get-tuple-element.61.low_ref, bf16[4,512,128]{2,1,0:T(8,128)(2,1)} %copy-done.4, bf16[8,512,128]{2,1,0:T(8,128)(2,1)} %get-tuple-element.62.high_ref, ...), custom_call_target="tpu_custom_call", output_to_operand_aliasing={{0}: (0, {}), {1}: (2, {})} | custom-call | flops 524288 | bytes 3145728 | tf_op jit(solution)/shard_map/join/pallas_call | solution.py:445
  130.7 1.4 collective-permute-start.28
  132.1 1.8 collective-permute-start.29
  134.0 1.9 slice.14
  136.0 1.9 slice.15
  137.9 3.1 %collective-permute-start.18 = (bf16[4,128,512]{2,1,0:T(8,128)(2,1)}, bf16[4,128,512]{2,1,0:T(8,128)(2,1)S(1)}, u32[]{:S(2)}, u32[]{:S(2)}) collective-permute-start(bf16[4,128,512]{2,1,0:T(8,128)(2,1)} %slice.15), channel_id=1, source_target_pairs={{0,3},{1,0},{2,1},{3,2},{4,7},{5,4},{6,5},{7,6},{8,11},{9,8},{10,9... | collective-permute-start | bytes 1572872 | tf_op jit(solution)/shard_map/ppermute | solution.py:466
  141.0 0.7 concatenate.14.ids_ref
  141.7 9.9 %upstream_most.1 = (f32[1024,512]{1,0:T(8,128)}, bf16[1024,1024]{1,0:T(8,128)(2,1)}) custom-call(s32[10]{0:T(128)} %pad_add_fusion.ids_ref, bf16[128,4096]{1,0:T(8,128)(2,1)} %bitcast.18, bf16[128,4096]{1,0:T(8,128)(2,1)} %copy-done.6, bf16[128,4096]{1,0:T(8,128)(2,1)} %collective-permute-done.8.refs_2_, ...), custom_call_target="tpu_custom_call" | custom-call | flops 3221225472 | bytes 11534336 | tf_op jit(solution)/shard_map/upstream_most/pallas_call | solution.py:301
  151.6 15.8 %collective-permute-done.17.low_ref = bf16[4,128,512]{2,1,0:T(8,128)(2,1)S(1)} collective-permute-done((bf16[4,128,512]{2,1,0:T(8,128)(2,1)}, bf16[4,128,512]{2,1,0:T(8,128)(2,1)S(1)}, u32[]{:S(2)}, u32[]{:S(2)}) %collective-permute-start.17) | collective-permute-done | bytes 524320 | tf_op jit(solution)/shard_map/ppermute | solution.py:466
  167.4 0.8 copy-done.2
  168.4 4.9 %upstream_rest.1.refs_8_ = bf16[8,128,512]{2,1,0:T(8,128)(2,1)} custom-call(s32[10]{0:T(128)} %pad_add_fusion.ids_ref, bf16[1024,1024]{1,0:T(8,128)(2,1)} %get-tuple-element.47.rows_ref, bf16[4,128,512]{2,1,0:T(8,128)(2,1)} %copy-done.2, bf16[4,128,512]{2,1,0:T(8,128)(2,1)} %copy-done.3, f32[1024,512]{1,0:T(8,128)} %get-tuple-element.48.sum_ref), custom_call_target="tpu_custom_call" | custom-call | flops 1073741824 | bytes 6291456 | tf_op jit(solution)/shard_map/upstream_rest/pallas_call | solution.py:330
  173.4 13.2 %attend_grad.1 = (bf16[128,768]{1,0:T(8,128)(2,1)}, bf16[128,768]{1,0:T(8,128)(2,1)}, bf16[128,768]{1,0:T(8,128)(2,1)}, bf16[128,768]{1,0:T(8,128)(2,1)}, bf16[1...) custom-call(s32[18]{0:T(128)} %concatenate.14.ids_ref, ...), custom_call_target="tpu_custom_call" | custom-call | flops 2348810240 | bytes 4718592 | tf_op jit(solution)/shard_map/attend_grad/pallas_call | solution.py:161
  186.6 1.4 add_convert_fusion
  188.0 7.3 %all-to-all-start.1 = ((bf16[8,512,128]{2,1,0:T(8,128)(2,1)}), bf16[8,512,128]{2,1,0:T(8,128)(2,1)S(1)}, u32[]{:S(2)}, u32[]{:S(2)}) async-start(bf16[8,512,128]{2,1,0:T(8,128)(2,1)} %add_convert_fusion), calls=%async_computation.1 | async-start | bytes 2097152 | tf_op jit(solution)/shard_map/all_to_all | solution.py:478
  195.4 0.9 collective-permute-start.19
  196.3 2.2 %collective-permute-start.20 = (bf16[128,768]{1,0:T(8,128)(2,1)S(1)}, bf16[128,768]{1,0:T(8,128)(2,1)S(1)}, u32[]{:S(2)}, u32[]{:S(2)}) collective-permute-start(bf16[128,768]{1,0:T(8,128)(2,1)S(1)} %copy-done.27), channel_id=1, source_target_pairs={{0,192},{32,224},{64,0},{96,32},{128,64},{160,96},{192,128},{224,1... | collective-permute-start | bytes 589832 | tf_op jit(solution)/shard_map/ppermute | solution.py:483
  198.5 2.1 collective-permute-start.21
  200.6 2.4 %collective-permute-start.23 = (bf16[128,768]{1,0:T(8,128)(2,1)S(1)}, bf16[128,768]{1,0:T(8,128)(2,1)S(1)}, u32[]{:S(2)}, u32[]{:S(2)}) collective-permute-start(bf16[128,768]{1,0:T(8,128)(2,1)S(1)} %copy-done.24), channel_id=1, source_target_pairs={{0,96},{32,64},{64,160},{96,128},{128,224},{160,192},{192,32},{224... | collective-permute-start | bytes 589832 | tf_op jit(solution)/shard_map/ppermute | solution.py:483
  203.5 1.2 collective-permute-done.20.refs_2_
  204.7 1.8 collective-permute-start.25
  206.6 3.0 %collective-permute-done.21.refs_3_ = bf16[128,768]{1,0:T(8,128)(2,1)S(1)} collective-permute-done((bf16[128,768]{1,0:T(8,128)(2,1)S(1)}, bf16[128,768]{1,0:T(8,128)(2,1)S(1)}, u32[]{:S(2)}, u32[]{:S(2)}) %collective-permute-start.21) | collective-permute-done | bytes 196640 | tf_op jit(solution)/shard_map/ppermute | solution.py:483
  209.5 0.7 collective-permute-done.23.refs_5_
  210.2 6.2 %collective-permute-done.24.refs_6_ = bf16[128,768]{1,0:T(8,128)(2,1)S(1)} collective-permute-done((bf16[128,768]{1,0:T(8,128)(2,1)S(1)}, bf16[128,768]{1,0:T(8,128)(2,1)S(1)}, u32[]{:S(2)}, u32[]{:S(2)}) %collective-permute-start.24) | collective-permute-done | bytes 196640 | tf_op jit(solution)/shard_map/ppermute | solution.py:483
  216.4 0.7 copy-done.12
  217.1 0.7 copy-done.13
  217.8 3.4 %unpack.1 = (bf16[1,128,4096]{2,1,0:T(8,128)(2,1)}, bf16[1,128,1024]{2,1,0:T(8,128)(2,1)}, bf16[1,128,1024]{2,1,0:T(8,128)(2,1)}) custom-call(s32[10]{0:T(128)} %pad_add_fusion.ids_ref, bf16[128,768]{1,0:T(8,128)(2,1)} %get-tuple-element.49.refs_0_, bf16[128,768]{1,0:T(8,128)(2,1)} %copy-done.7, bf16[128,768]{1,0:T(8,128)(2,1)} %copy-done.8, ...), custom_call_target="tpu_custom_call" | custom-call | bytes 3145728 | tf_op jit(solution)/shard_map/unpack/pallas_call | solution.py:223
  221.2 1.5 all-to-all-done.1
  222.9 0.8 copy.15
  (86 shorter events, 2.2 us)
Async XLA Ops:
  0.6 35.9 %copy-start.14 = (bf16[128,512]{1,0:T(8,128)(2,1)S(1)}, bf16[128,512]{1,0:T(8,128)(2,1)}, u32[]{:S(2)}) copy-start(bf16[128,512]{1,0:T(8,128)(2,1)} %param.12) | copy-start | bytes 393220
  0.6 25.2 %collective-permute-start.7 = (bf16[128,4096]{1,0:T(8,128)(2,1)}, bf16[128,4096]{1,0:T(8,128)(2,1)S(1)}, u32[]{:S(2)}, u32[]{:S(2)}) collective-permute-start(bf16[128,4096]{1,0:T(8,128)(2,1)} %bitcast.14), channel_id=1, source_target_pairs={{0,64},{32,96},{64,128},{96,160},{128,192},{160,224},{192,0},{224,... | collective-permute-start | bytes 3145736 | tf_op jit(solution)/shard_map/ppermute | solution.py:483
  2.2 25.9 %collective-permute-start.8 = (bf16[128,4096]{1,0:T(8,128)(2,1)}, bf16[128,4096]{1,0:T(8,128)(2,1)}, u32[]{:S(2)}, u32[]{:S(2)}) collective-permute-start(bf16[128,4096]{1,0:T(8,128)(2,1)} %bitcast.15), channel_id=1, source_target_pairs={{0,192},{32,224},{64,0},{96,32},{128,64},{160,96},{192,128},{224,1... | collective-permute-start | bytes 3145736 | tf_op jit(solution)/shard_map/ppermute | solution.py:483
  3.1 88.6 %collective-permute-start.11 = (bf16[128,4096]{1,0:T(8,128)(2,1)}, bf16[128,4096]{1,0:T(8,128)(2,1)}, u32[]{:S(2)}, u32[]{:S(2)}) collective-permute-start(bf16[128,4096]{1,0:T(8,128)(2,1)} %bitcast.16), channel_id=1, source_target_pairs={{0,32},{32,0},{64,96},{96,64},{128,160},{160,128},{192,224},{224,1... | collective-permute-start | bytes 3145736 | tf_op jit(solution)/shard_map/ppermute | solution.py:483
  25.8 11.8 %copy-start.6 = (bf16[128,4096]{1,0:T(8,128)(2,1)}, bf16[128,4096]{1,0:T(8,128)(2,1)S(1)}, u32[]{:S(2)}) copy-start(bf16[128,4096]{1,0:T(8,128)(2,1)S(1)} %collective-permute-done.7.refs_1_) | copy-start | bytes 3145732
  25.9 20.6 %collective-permute-start.9 = (bf16[64,4096]{1,0:T(8,128)(2,1)S(1)}, bf16[64,4096]{1,0:T(8,128)(2,1)S(1)}, u32[]{:S(2)}, u32[]{:S(2)}) collective-permute-start(bf16[64,4096]{1,0:T(8,128)(2,1)S(1)} %slice.16), channel_id=1, source_target_pairs={{0,64},{32,96},{64,128},{96,160},{128,192},{160,224},{192,0},{224,... | collective-permute-start | bytes 1572872 | tf_op jit(solution)/shard_map/ppermute | solution.py:483
  29.2 20.2 %collective-permute-start.10 = (bf16[64,4096]{1,0:T(8,128)(2,1)S(1)}, bf16[64,4096]{1,0:T(8,128)(2,1)S(1)}, u32[]{:S(2)}, u32[]{:S(2)}) collective-permute-start(bf16[64,4096]{1,0:T(8,128)(2,1)S(1)} %slice.17), channel_id=1, source_target_pairs={{0,192},{32,224},{64,0},{96,32},{128,64},{160,96},{192,128},{224,1... | collective-permute-start | bytes 1572872 | tf_op jit(solution)/shard_map/ppermute | solution.py:483
  33.8 16.5 %collective-permute-start = (bf16[128,768]{1,0:T(8,128)(2,1)}, bf16[128,768]{1,0:T(8,128)(2,1)S(1)}, u32[]{:S(2)}, u32[]{:S(2)}) collective-permute-start(bf16[128,768]{1,0:T(8,128)(2,1)} %get-tuple-element.37), channel_id=1, source_target_pairs={{0,64},{32,96},{64,128},{96,160},{128,192},{160,224},{192,0},{224,... | collective-permute-start | bytes 589832 | tf_op jit(solution)/shard_map/ppermute | solution.py:483
  35.3 15.5 %collective-permute-start.1 = (bf16[128,768]{1,0:T(8,128)(2,1)}, bf16[128,768]{1,0:T(8,128)(2,1)}, u32[]{:S(2)}, u32[]{:S(2)}) collective-permute-start(bf16[128,768]{1,0:T(8,128)(2,1)} %get-tuple-element.38), channel_id=1, source_target_pairs={{0,192},{32,224},{64,0},{96,32},{128,64},{160,96},{192,128},{224,1... | collective-permute-start | bytes 589832 | tf_op jit(solution)/shard_map/ppermute | solution.py:483
  37.6 16.4 %copy-start.15 = (s32[1,32]{1,0:T(1,128)S(1)}, s32[1,32]{1,0:T(1,128)}, u32[]{:S(2)}) copy-start(s32[1,32]{1,0:T(1,128)} %param.13) | copy-start | bytes 388
  37.6 52.1 %all-to-all-start = ((bf16[8,128,512]{2,1,0:T(8,128)(2,1)}), bf16[8,128,512]{2,1,0:T(8,128)(2,1)S(1)}, u32[]{:S(2)}, u32[]{:S(2)}) async-start(bf16[8,128,512]{2,1,0:T(8,128)(2,1)} %broadcast_in_dim.41), calls=%async_computation | async-start | bytes 2097152 | tf_op jit(solution)/shard_map/all_to_all | solution.py:478
  46.4 7.6 %collective-permute-start.2 = (bf16[128,768]{1,0:T(8,128)(2,1)}, bf16[128,768]{1,0:T(8,128)(2,1)}, u32[]{:S(2)}, u32[]{:S(2)}) collective-permute-start(bf16[128,768]{1,0:T(8,128)(2,1)} %get-tuple-element.39), channel_id=1, source_target_pairs={{0,128},{32,160},{64,192},{96,224},{128,0},{160,32},{192,64},{224,... | collective-permute-start | bytes 589832 | tf_op jit(solution)/shard_map/ppermute | solution.py:483
  49.4 43.9 %collective-permute-start.12 = (bf16[128,4096]{1,0:T(8,128)(2,1)}, bf16[128,4096]{1,0:T(8,128)(2,1)}, u32[]{:S(2)}, u32[]{:S(2)}) collective-permute-start(bf16[128,4096]{1,0:T(8,128)(2,1)} %copy-done.6), channel_id=1, source_target_pairs={{0,32},{32,0},{64,96},{96,64},{128,160},{160,128},{192,224},{224,1... | collective-permute-start | bytes 3145736 | tf_op jit(solution)/shard_map/ppermute | solution.py:483
  50.3 30.6 %copy-start.17 = (bf16[128,768]{1,0:T(8,128)(2,1)}, bf16[128,768]{1,0:T(8,128)(2,1)S(1)}, u32[]{:S(2)}) copy-start(bf16[128,768]{1,0:T(8,128)(2,1)S(1)} %collective-permute-done.refs_1_) | copy-start | bytes 589828
  50.3 43.0 %collective-permute-start.13 = (bf16[128,4096]{1,0:T(8,128)(2,1)}, bf16[128,4096]{1,0:T(8,128)(2,1)S(1)}, u32[]{:S(2)}, u32[]{:S(2)}) collective-permute-start(bf16[128,4096]{1,0:T(8,128)(2,1)} %collective-permute-done.8.refs_2_), channel_id=1, source_target_pairs={{0,32},{32,0},{64,96},{96,64},{128,160},{160,128},{192,224},{224,1... | collective-permute-start | bytes 3145736 | tf_op jit(solution)/shard_map/ppermute | solution.py:483
  50.8 42.5 %collective-permute-start.14 = (bf16[128,4096]{1,0:T(8,128)(2,1)}, bf16[128,4096]{1,0:T(8,128)(2,1)}, u32[]{:S(2)}, u32[]{:S(2)}) collective-permute-start(bf16[128,4096]{1,0:T(8,128)(2,1)} %constant_dynamic-update-slice_fusion.refs_3_), channel_id=1, source_target_pairs={{0,32},{32,0},{64,96},{96,64},{128,160},{160,128},{192,224},{224,1... | collective-permute-start | bytes 3145736 | tf_op jit(solution)/shard_map/ppermute | solution.py:483
  54.0 1.7 collective-permute-start.3
  55.7 25.2 %copy-start.18 = (bf16[128,768]{1,0:T(8,128)(2,1)}, bf16[128,768]{1,0:T(8,128)(2,1)S(1)}, u32[]{:S(2)}) copy-start(bf16[128,768]{1,0:T(8,128)(2,1)S(1)} %collective-permute-done.3.refs_4_) | copy-start | bytes 589828
  55.7 8.1 %collective-permute-start.4 = (bf16[128,768]{1,0:T(8,128)(2,1)}, bf16[128,768]{1,0:T(8,128)(2,1)S(1)}, u32[]{:S(2)}, u32[]{:S(2)}) collective-permute-start(bf16[128,768]{1,0:T(8,128)(2,1)} %get-tuple-element.41), channel_id=1, source_target_pairs={{0,96},{32,64},{64,160},{96,128},{128,224},{160,192},{192,32},{224... | collective-permute-start | bytes 589832 | tf_op jit(solution)/shard_map/ppermute | solution.py:483
  63.7 17.1 %copy-start.19 = (bf16[128,768]{1,0:T(8,128)(2,1)}, bf16[128,768]{1,0:T(8,128)(2,1)S(1)}, u32[]{:S(2)}) copy-start(bf16[128,768]{1,0:T(8,128)(2,1)S(1)} %collective-permute-done.4.refs_5_) | copy-start | bytes 589828
  63.7 8.5 %collective-permute-start.5 = (bf16[128,768]{1,0:T(8,128)(2,1)}, bf16[128,768]{1,0:T(8,128)(2,1)S(1)}, u32[]{:S(2)}, u32[]{:S(2)}) collective-permute-start(bf16[128,768]{1,0:T(8,128)(2,1)} %get-tuple-element.42), channel_id=1, source_target_pairs={{0,224},{32,192},{64,32},{96,0},{128,96},{160,64},{192,160},{224,1... | collective-permute-start | bytes 589832 | tf_op jit(solution)/shard_map/ppermute | solution.py:483
  72.2 8.6 %copy-start.20 = (bf16[128,768]{1,0:T(8,128)(2,1)}, bf16[128,768]{1,0:T(8,128)(2,1)S(1)}, u32[]{:S(2)}) copy-start(bf16[128,768]{1,0:T(8,128)(2,1)S(1)} %collective-permute-done.5.refs_6_) | copy-start | bytes 589828
  72.2 8.6 %collective-permute-start.6 = (bf16[128,768]{1,0:T(8,128)(2,1)}, bf16[128,768]{1,0:T(8,128)(2,1)S(1)}, u32[]{:S(2)}, u32[]{:S(2)}) collective-permute-start(bf16[128,768]{1,0:T(8,128)(2,1)} %get-tuple-element.43), channel_id=1, source_target_pairs={{0,160},{32,128},{64,224},{96,192},{128,32},{160,0},{192,96},{224,... | collective-permute-start | bytes 589832 | tf_op jit(solution)/shard_map/ppermute | solution.py:483
  80.8 0.7 copy-start.21
  89.8 15.1 %copy-start = (bf16[8,128,512]{2,1,0:T(8,128)(2,1)}, bf16[8,128,512]{2,1,0:T(8,128)(2,1)S(1)}, u32[]{:S(2)}) copy-start(bf16[8,128,512]{2,1,0:T(8,128)(2,1)S(1)} %all-to-all-done.refs_8_) | copy-start | bytes 3145732
  89.8 44.2 %collective-permute-start.15 = (bf16[8,128,512]{2,1,0:T(8,128)(2,1)S(1)}, bf16[8,128,512]{2,1,0:T(8,128)(2,1)}, u32[]{:S(2)}, u32[]{:S(2)}) collective-permute-start(bf16[8,128,512]{2,1,0:T(8,128)(2,1)S(1)} %all-to-all-done.refs_8_), channel_id=1, source_target_pairs={{0,1},{1,2},{2,3},{3,0},{4,5},{5,6},{6,7},{7,4},{8,9},{9,10},{10,1... | collective-permute-start | bytes 3145736 | tf_op jit(solution)/shard_map/ppermute | solution.py:466
  91.6 42.4 %collective-permute-start.16 = (bf16[8,128,512]{2,1,0:T(8,128)(2,1)S(1)}, bf16[8,128,512]{2,1,0:T(8,128)(2,1)}, u32[]{:S(2)}, u32[]{:S(2)}) collective-permute-start(bf16[8,128,512]{2,1,0:T(8,128)(2,1)S(1)} %all-to-all-done.refs_8_), channel_id=1, source_target_pairs={{0,3},{1,0},{2,1},{3,2},{4,7},{5,4},{6,5},{7,6},{8,11},{9,8},{10,9... | collective-permute-start | bytes 3145736 | tf_op jit(solution)/shard_map/ppermute | solution.py:466
  93.3 1.0 copy-start.16
  104.9 22.5 %collective-permute-start.26 = (bf16[4,512,128]{2,1,0:T(8,128)(2,1)}, bf16[4,512,128]{2,1,0:T(8,128)(2,1)S(1)}, u32[]{:S(2)}, u32[]{:S(2)}) collective-permute-start(bf16[4,512,128]{2,1,0:T(8,128)(2,1)} %get-tuple-element.44), channel_id=1, source_target_pairs={{0,1},{1,2},{2,3},{3,0},{4,5},{5,6},{6,7},{7,4},{8,9},{9,10},{10,1... | collective-permute-start | bytes 1572872 | tf_op jit(solution)/shard_map/ppermute | solution.py:466
  105.3 22.1 %collective-permute-start.27 = (bf16[4,512,128]{2,1,0:T(8,128)(2,1)}, bf16[4,512,128]{2,1,0:T(8,128)(2,1)S(1)}, u32[]{:S(2)}, u32[]{:S(2)}) collective-permute-start(bf16[4,512,128]{2,1,0:T(8,128)(2,1)} %get-tuple-element.63), channel_id=1, source_target_pairs={{0,3},{1,0},{2,1},{3,2},{4,7},{5,4},{6,5},{7,6},{8,11},{9,8},{10,9... | collective-permute-start | bytes 1572872 | tf_op jit(solution)/shard_map/ppermute | solution.py:466
  127.4 0.8 copy-start.4
  127.4 0.9 copy-start.5
  130.7 55.8 %collective-permute-start.28 = (bf16[8,512,128]{2,1,0:T(8,128)(2,1)}, bf16[8,512,128]{2,1,0:T(8,128)(2,1)S(1)}, u32[]{:S(2)}, u32[]{:S(2)}) collective-permute-start(bf16[8,512,128]{2,1,0:T(8,128)(2,1)} %get-tuple-element.64), channel_id=1, source_target_pairs={{0,1},{1,2},{2,3},{3,0},{4,5},{5,6},{6,7},{7,4},{8,9},{9,10},{10,1... | collective-permute-start | bytes 3145736 | tf_op jit(solution)/shard_map/ppermute | solution.py:466
  132.1 54.4 %collective-permute-start.29 = (bf16[8,512,128]{2,1,0:T(8,128)(2,1)}, bf16[8,512,128]{2,1,0:T(8,128)(2,1)S(1)}, u32[]{:S(2)}, u32[]{:S(2)}) collective-permute-start(bf16[8,512,128]{2,1,0:T(8,128)(2,1)} %get-tuple-element.65), channel_id=1, source_target_pairs={{0,3},{1,0},{2,1},{3,2},{4,7},{5,4},{6,5},{7,6},{8,11},{9,8},{10,9... | collective-permute-start | bytes 3145736 | tf_op jit(solution)/shard_map/ppermute | solution.py:466
  135.9 31.6 %collective-permute-start.17 = (bf16[4,128,512]{2,1,0:T(8,128)(2,1)}, bf16[4,128,512]{2,1,0:T(8,128)(2,1)S(1)}, u32[]{:S(2)}, u32[]{:S(2)}) collective-permute-start(bf16[4,128,512]{2,1,0:T(8,128)(2,1)} %slice.14), channel_id=1, source_target_pairs={{0,1},{1,2},{2,3},{3,0},{4,5},{5,6},{6,7},{7,4},{8,9},{9,10},{10,1... | collective-permute-start | bytes 1572872 | tf_op jit(solution)/shard_map/ppermute | solution.py:466
  137.9 29.5 %collective-permute-start.18 = (bf16[4,128,512]{2,1,0:T(8,128)(2,1)}, bf16[4,128,512]{2,1,0:T(8,128)(2,1)S(1)}, u32[]{:S(2)}, u32[]{:S(2)}) collective-permute-start(bf16[4,128,512]{2,1,0:T(8,128)(2,1)} %slice.15), channel_id=1, source_target_pairs={{0,3},{1,0},{2,1},{3,2},{4,7},{5,4},{6,5},{7,6},{8,11},{9,8},{10,9... | collective-permute-start | bytes 1572872 | tf_op jit(solution)/shard_map/ppermute | solution.py:466
  167.4 0.8 copy-start.2
  167.4 1.0 copy-start.3
  173.3 13.2 %copy-start.1 = (bf16[8,512,128]{2,1,0:T(8,128)(2,1)S(1)}, bf16[8,512,128]{2,1,0:T(8,128)(2,1)}, u32[]{:S(2)}) copy-start(bf16[8,512,128]{2,1,0:T(8,128)(2,1)} %get-tuple-element.60) | copy-start | bytes 3145732
  188.0 7.4 %copy-start.28 = (bf16[128,768]{1,0:T(8,128)(2,1)S(1)}, bf16[128,768]{1,0:T(8,128)(2,1)}, u32[]{:S(2)}) copy-start(bf16[128,768]{1,0:T(8,128)(2,1)} %get-tuple-element.50) | copy-start | bytes 589828
  188.0 8.3 %copy-start.27 = (bf16[128,768]{1,0:T(8,128)(2,1)S(1)}, bf16[128,768]{1,0:T(8,128)(2,1)}, u32[]{:S(2)}) copy-start(bf16[128,768]{1,0:T(8,128)(2,1)} %get-tuple-element.51) | copy-start | bytes 589828
  188.0 10.5 %copy-start.26 = (bf16[128,768]{1,0:T(8,128)(2,1)S(1)}, bf16[128,768]{1,0:T(8,128)(2,1)}, u32[]{:S(2)}) copy-start(bf16[128,768]{1,0:T(8,128)(2,1)} %get-tuple-element.52) | copy-start | bytes 589828
  188.0 12.6 %copy-start.25 = (bf16[128,768]{1,0:T(8,128)(2,1)S(1)}, bf16[128,768]{1,0:T(8,128)(2,1)}, u32[]{:S(2)}) copy-start(bf16[128,768]{1,0:T(8,128)(2,1)} %get-tuple-element.53) | copy-start | bytes 589828
  188.0 12.6 %copy-start.24 = (bf16[128,768]{1,0:T(8,128)(2,1)S(1)}, bf16[128,768]{1,0:T(8,128)(2,1)}, u32[]{:S(2)}) copy-start(bf16[128,768]{1,0:T(8,128)(2,1)} %get-tuple-element.54) | copy-start | bytes 589828
  188.0 15.5 %copy-start.23 = (bf16[128,768]{1,0:T(8,128)(2,1)S(1)}, bf16[128,768]{1,0:T(8,128)(2,1)}, u32[]{:S(2)}) copy-start(bf16[128,768]{1,0:T(8,128)(2,1)} %get-tuple-element.55) | copy-start | bytes 589828
  188.0 16.7 %copy-start.22 = (bf16[128,768]{1,0:T(8,128)(2,1)S(1)}, bf16[128,768]{1,0:T(8,128)(2,1)}, u32[]{:S(2)}) copy-start(bf16[128,768]{1,0:T(8,128)(2,1)} %get-tuple-element.56) | copy-start | bytes 589828
  188.0 34.7 %all-to-all-start.1 = ((bf16[8,512,128]{2,1,0:T(8,128)(2,1)}), bf16[8,512,128]{2,1,0:T(8,128)(2,1)S(1)}, u32[]{:S(2)}, u32[]{:S(2)}) async-start(bf16[8,512,128]{2,1,0:T(8,128)(2,1)} %add_convert_fusion), calls=%async_computation.1 | async-start | bytes 2097152 | tf_op jit(solution)/shard_map/all_to_all | solution.py:478
  195.4 8.1 %collective-permute-start.19 = (bf16[128,768]{1,0:T(8,128)(2,1)S(1)}, bf16[128,768]{1,0:T(8,128)(2,1)S(1)}, u32[]{:S(2)}, u32[]{:S(2)}) collective-permute-start(bf16[128,768]{1,0:T(8,128)(2,1)S(1)} %copy-done.28), channel_id=1, source_target_pairs={{0,64},{32,96},{64,128},{96,160},{128,192},{160,224},{192,0},{224,... | collective-permute-start | bytes 589832 | tf_op jit(solution)/shard_map/ppermute | solution.py:483
  196.3 8.4 %collective-permute-start.20 = (bf16[128,768]{1,0:T(8,128)(2,1)S(1)}, bf16[128,768]{1,0:T(8,128)(2,1)S(1)}, u32[]{:S(2)}, u32[]{:S(2)}) collective-permute-start(bf16[128,768]{1,0:T(8,128)(2,1)S(1)} %copy-done.27), channel_id=1, source_target_pairs={{0,192},{32,224},{64,0},{96,32},{128,64},{160,96},{192,128},{224,1... | collective-permute-start | bytes 589832 | tf_op jit(solution)/shard_map/ppermute | solution.py:483
  198.5 11.0 %collective-permute-start.21 = (bf16[128,768]{1,0:T(8,128)(2,1)S(1)}, bf16[128,768]{1,0:T(8,128)(2,1)S(1)}, u32[]{:S(2)}, u32[]{:S(2)}) collective-permute-start(bf16[128,768]{1,0:T(8,128)(2,1)S(1)} %copy-done.26), channel_id=1, source_target_pairs={{0,128},{32,160},{64,192},{96,224},{128,0},{160,32},{192,64},{224,... | collective-permute-start | bytes 589832 | tf_op jit(solution)/shard_map/ppermute | solution.py:483
  200.6 8.9 %collective-permute-start.22 = (bf16[128,768]{1,0:T(8,128)(2,1)S(1)}, bf16[128,768]{1,0:T(8,128)(2,1)S(1)}, u32[]{:S(2)}, u32[]{:S(2)}) collective-permute-start(bf16[128,768]{1,0:T(8,128)(2,1)S(1)} %copy-done.25), channel_id=1, source_target_pairs={{0,32},{32,0},{64,96},{96,64},{128,160},{160,128},{192,224},{224,1... | collective-permute-start | bytes 589832 | tf_op jit(solution)/shard_map/ppermute | solution.py:483
  200.6 9.6 %collective-permute-start.23 = (bf16[128,768]{1,0:T(8,128)(2,1)S(1)}, bf16[128,768]{1,0:T(8,128)(2,1)S(1)}, u32[]{:S(2)}, u32[]{:S(2)}) collective-permute-start(bf16[128,768]{1,0:T(8,128)(2,1)S(1)} %copy-done.24), channel_id=1, source_target_pairs={{0,96},{32,64},{64,160},{96,128},{128,224},{160,192},{192,32},{224... | collective-permute-start | bytes 589832 | tf_op jit(solution)/shard_map/ppermute | solution.py:483
  203.5 12.9 %copy-start.7 = (bf16[128,768]{1,0:T(8,128)(2,1)}, bf16[128,768]{1,0:T(8,128)(2,1)S(1)}, u32[]{:S(2)}) copy-start(bf16[128,768]{1,0:T(8,128)(2,1)S(1)} %collective-permute-done.19.refs_1_) | copy-start | bytes 589828
  203.5 12.9 %collective-permute-start.24 = (bf16[128,768]{1,0:T(8,128)(2,1)S(1)}, bf16[128,768]{1,0:T(8,128)(2,1)S(1)}, u32[]{:S(2)}, u32[]{:S(2)}) collective-permute-start(bf16[128,768]{1,0:T(8,128)(2,1)S(1)} %copy-done.23), channel_id=1, source_target_pairs={{0,224},{32,192},{64,32},{96,0},{128,96},{160,64},{192,160},{224,1... | collective-permute-start | bytes 589832 | tf_op jit(solution)/shard_map/ppermute | solution.py:483
  204.7 11.7 %copy-start.8 = (bf16[128,768]{1,0:T(8,128)(2,1)}, bf16[128,768]{1,0:T(8,128)(2,1)S(1)}, u32[]{:S(2)}) copy-start(bf16[128,768]{1,0:T(8,128)(2,1)S(1)} %collective-permute-done.20.refs_2_) | copy-start | bytes 589828
  204.7 11.7 %collective-permute-start.25 = (bf16[128,768]{1,0:T(8,128)(2,1)S(1)}, bf16[128,768]{1,0:T(8,128)(2,1)S(1)}, u32[]{:S(2)}, u32[]{:S(2)}) collective-permute-start(bf16[128,768]{1,0:T(8,128)(2,1)S(1)} %copy-done.22), channel_id=1, source_target_pairs={{0,160},{32,128},{64,224},{96,192},{128,32},{160,0},{192,96},{224,... | collective-permute-start | bytes 589832 | tf_op jit(solution)/shard_map/ppermute | solution.py:483
  209.5 6.9 %copy-start.9 = (bf16[128,768]{1,0:T(8,128)(2,1)}, bf16[128,768]{1,0:T(8,128)(2,1)S(1)}, u32[]{:S(2)}) copy-start(bf16[128,768]{1,0:T(8,128)(2,1)S(1)} %collective-permute-done.21.refs_3_) | copy-start | bytes 589828
  209.5 6.9 %copy-start.10 = (bf16[128,768]{1,0:T(8,128)(2,1)}, bf16[128,768]{1,0:T(8,128)(2,1)S(1)}, u32[]{:S(2)}) copy-start(bf16[128,768]{1,0:T(8,128)(2,1)S(1)} %collective-permute-done.22.refs_4_) | copy-start | bytes 589828
  210.2 6.2 %copy-start.11 = (bf16[128,768]{1,0:T(8,128)(2,1)}, bf16[128,768]{1,0:T(8,128)(2,1)S(1)}, u32[]{:S(2)}) copy-start(bf16[128,768]{1,0:T(8,128)(2,1)S(1)} %collective-permute-done.23.refs_5_) | copy-start | bytes 589828
  216.4 0.7 copy-start.12
  217.1 0.7 copy-start.13
